TPU v7x, 256 devices: a whole 4x4x8 slice. The times are simulated.
256 devices in a mesh: lat: 4 (over y), col: 64 (over z, x, core).
Axes of the slice: x: 4, y: 4, z: 8, core: 2. Of those that a mesh axis runs over, the one named last changes fastest.
Arguments:
- control: float32 [128, 16384], P('lat', 'col'), may hold values from -6 to 6
- perturbations: float32 [128, 16384, 128], P('lat', 'col'), may hold values from -6 to 6
- zonal_flow: float32 [128, 16384], P('lat', 'col'), may hold values from -0.25 to 0.25
- meridional_flow: float32 [128, 16384], P('lat', 'col'), may hold values from -0.25 to 0.25
- diffusivity: float32 [128, 16384], P('lat', 'col'), may hold values from 0.03 to 0.12
- send_cell: int32 [4, 64, 64, 128], P('lat', 'col'), may hold values from 0 to 8191
- send_station: int32 [4, 64, 64, 128], P('lat', 'col'), may hold values from 0 to 255
- send_weight: float32 [4, 64, 64, 128], P('lat', 'col'), may hold values from 0.2 to 1
- send_count: int32 [4, 64, 64], P('lat', 'col'), may hold values from 32 to 128, as said below
- obs_value: float32 [2, 65536], P(None, ('lat', 'col')), may hold values from -24 to 24
- obs_error: float32 [2, 65536], P(None, ('lat', 'col')), may hold values from 1.3 to 64, as said below
Outputs:
- analysis: float32 [128, 16384, 128], P('lat', 'col')
- obs_analysis: float32 [2, 65536, 128], P(None, ('lat', 'col'))
Inputs may be any that keep to these rules, and one draw needn't show every extreme that they name: send_count[l, e, d] counts the live leading slots that device e of latitude group l fills for device d of its group; in every group one device d receives all 128 slots from every source. obs_error is positive.
All inputs are finite; a program needn't handle non-finite values.
Results may differ from a plain program's by a relative error of at most 0.0003.
Values sent between devices are 32-bit elements; how exact they have to be, the bound alone decides.
No kernel may reach another device: no remote copies, remote signals or barrier semaphores. Data moves between devices by JAX's collectives and lax.ppermute only.
A program may use at most 128 MiB of HBM per device.

v0:
```python
import functools
import math

import jax
import jax.numpy as jnp
from jax import lax
from jax.experimental import pallas as pl
from jax.experimental.pallas import tpu as pltpu
from jax.sharding import Mesh
from jax.sharding import PartitionSpec as P

exact_mode = lax.Precision.HIGHEST
COL = ("z", "x", "core")
UNROLL = 16


def shift(value, axis, step):
    count = lax.axis_size(axis)
    return lax.ppermute(value, axis, [(i, (i + step) % count) for i in range(count)])


def edges(block):
    sides = []
    for axis, dim in (("lat", 0), (COL, 1)):
        names = axis if isinstance(axis, tuple) else (axis,)
        count = math.prod(lax.axis_size(name) for name in names)
        forward = [(i, i + 1) for i in range(count - 1)]
        backward = [(target, source) for source, target in forward]
        last = lax.slice_in_dim(block, block.shape[dim] - 1, None, axis=dim)
        first = lax.slice_in_dim(block, 0, 1, axis=dim)
        sides.append(lax.ppermute(last, axis, forward))
        sides.append(lax.ppermute(first, axis, backward))
    return sides


def advance_kernel(adds, rates, block, above, below, left, right, out, padded, turned):
    rows, cells, members = block.shape
    groups, lanes = rates.shape[0], rates.shape[1]
    per_group = rows // groups
    for group in range(groups):
        turned[group] = jnp.transpose(rates[group])
    padded[0, 8 : 8 + cells, :] = above[0]
    padded[rows + 1, 8 : 8 + cells, :] = below[0]

    def rate(i, kind):
        lane = (i % per_group) * (lanes // per_group) + kind
        index = jnp.full((cells, members), lane, jnp.int32)
        return jnp.take_along_axis(turned[i // per_group], index, axis=1)

    def fill(i, carry):
        value = block[i]
        padded[i + 1, 8 : 8 + cells, :] = value + rate(i, 4) if adds else value
        padded[i + 1, 7:8, :] = left[i]
        padded[i + 1, 8 + cells : 9 + cells, :] = right[i]
        return carry

    lax.fori_loop(0, rows, fill, 0)

    def row(i, carry):
        centre = padded[i + 1, 8 : 8 + cells, :]
        result = centre + rate(i, 0) * (padded[i + 2, 8 : 8 + cells, :] - centre)
        result = result + rate(i, 1) * (padded[i, 8 : 8 + cells, :] - centre)
        result = result + rate(i, 2) * (padded[i + 1, 9 : 9 + cells, :] - centre)
        out[i] = result + rate(i, 3) * (padded[i + 1, 7 : 7 + cells, :] - centre)
        return carry

    lax.fori_loop(0, rows, row, 0)


def advance(adds, rates, block, sides):
    rows, cells, members = block.shape
    whole = pl.BlockSpec(memory_space=pltpu.VMEM)
    return pl.pallas_call(
        functools.partial(advance_kernel, adds),
        in_specs=[whole] * 6,
        out_specs=whole,
        out_shape=pltpu.VMEM(block.shape, jnp.float32),
        scratch_shapes=[
            pltpu.VMEM((rows + 2, cells + 16, members), jnp.float32),
            pltpu.VMEM((rates.shape[0], cells, rates.shape[1]), jnp.float32),
        ],
        compiler_params=pltpu.CompilerParams(vmem_limit_bytes=24 * 2**20),
        cost_estimate=pl.CostEstimate(
            flops=12 * block.size, bytes_accessed=8 * block.size, transcendentals=0
        ),
    )(rates, block, *sides)


def bin_kernel(
    size_z, size_x, owned, place, cell, weight, count, station, *rest
):
    states, (out_a, out_b, picked) = rest[:4], rest[4:]
    width = out_a.shape[3]
    cut = out_a.shape[2] - owned
    receivers, slots = size_z * size_x, station.shape[1]
    picked[...] = jnp.zeros_like(picked)
    own = lax.broadcasted_iota(jnp.int32, (owned, slots), 0)

    def one(step, carry):
        ahead_z, ahead_x = step // size_x, step % size_x
        receiver = ((place[0] + ahead_z) % size_z) * size_x + (place[1] + ahead_x) % size_x
        hots = []
        for e in range(2):
            first, second = states[2 * e], states[2 * e + 1]
            entry = e * receivers + receiver

            def pick(group, inner):
                for j in range(UNROLL):
                    slot = entry * slots + group * UNROLL + j
                    row, factor = cell[slot], weight[slot]
                    tile, line = group * (UNROLL // 8) + j // 8, j % 8
                    picked[e, 0, tile, line : line + 1, :] = first[pl.ds(row, 1), :] * factor
                    picked[e, 1, tile, line : line + 1, :] = second[pl.ds(row, 1), :] * factor
                return inner

            lax.fori_loop(0, (count[entry] + UNROLL - 1) // UNROLL, pick, 0)
            hit = station[pl.ds(entry, 1), :] == own
            hots.append(jnp.where(hit, 1.0, 0.0).astype(jnp.bfloat16))
        value = jnp.concatenate(
            [
                jnp.concatenate([picked[e, k].reshape(slots, width) for k in range(2)], axis=1)
                for e in range(2)
            ],
            axis=0,
        )
        high = value.astype(jnp.bfloat16)
        low = (value - high.astype(jnp.float32)).astype(jnp.bfloat16)
        total = jnp.dot(
            jnp.concatenate(hots + hots, axis=1),
            jnp.concatenate([high, low], axis=0),
            preferred_element_type=jnp.float32,
        )
        out_a[ahead_x, ahead_z, :owned, :] = total[:, :width]
        out_a[ahead_x, ahead_z, owned:, :] = total[:cut, width:]
        out_b[ahead_z, ahead_x] = total[cut:, width:]
        return carry

    lax.fori_loop(0, receivers, one, 0)


def bin_rows(place, cell, weight, count, station, states, owned):
    size_z, size_x = lax.axis_size("z"), lax.axis_size("x")
    members, slots = states[0].shape[1], station.shape[1]
    rows_a = owned + owned // 8
    rows_b = 2 * owned - rows_a
    scalar = pl.BlockSpec(memory_space=pltpu.SMEM)
    whole = pl.BlockSpec(memory_space=pltpu.VMEM)
    return pl.pallas_call(
        functools.partial(bin_kernel, size_z, size_x, owned),
        in_specs=[scalar] * 4 + [whole] * 5,
        out_specs=[whole] * 2,
        out_shape=[
            pltpu.VMEM((size_x, size_z, rows_a, members), jnp.float32),
            pltpu.VMEM((size_z, size_x, rows_b, members), jnp.float32),
        ],
        scratch_shapes=[pltpu.VMEM((2, 2, slots // 8, 8, members), jnp.float32)],
        compiler_params=pltpu.CompilerParams(vmem_limit_bytes=48 * 2**20),
        cost_estimate=pl.CostEstimate(flops=10**9, bytes_accessed=30 * 2**20, transcendentals=0),
    )(place, cell, weight, count, station, *states)


def factor_kernel(root_scale, products, high, low):
    size = products.shape[1]
    lane = lax.broadcasted_iota(jnp.int32, (size, size), 1)
    line = lax.broadcasted_iota(jnp.int32, (size, size), 0)
    eye = jnp.where(lane == line, 1.0, 0.0)
    left, right = products[:size, :] + eye, eye
    width = 4
    done_left, done_right = [], []
    for start in range(0, size, width):
        top = start % 8
        columns = [
            jnp.broadcast_to(left[:, start + a : start + a + 1], left.shape) for a in range(width)
        ]
        pivots = [[columns[b][top + a : top + a + 1, :] for b in range(width)] for a in range(width)]
        upper = [[None] * width for _ in range(width)]
        inverse = []
        for a in range(width):
            lower = []
            for k in range(a):
                value = pivots[a][k]
                for m in range(k):
                    value = value - lower[m] * upper[m][k]
                lower.append(value * inverse[k])
            for b in range(a, width):
                value = pivots[a][b]
                for m in range(a):
                    value = value - lower[m] * upper[m][b]
                upper[a][b] = value
            inverse.append(1.0 / upper[a][a])
        below = line[: left.shape[0]]
        multipliers = []
        for a in range(width):
            value = columns[a]
            for m in range(a):
                value = value - multipliers[m] * upper[m][a]
            value = value * inverse[a]
            multipliers.append(jnp.where(below > top + a, value, 0.0))
        rows_left, rows_right = [], []
        for a in range(width):
            row_left = left[top + a : top + a + 1, :]
            row_right = right[top + a : top + a + 1, :]
            for m in range(a):
                scale = multipliers[m][top + a : top + a + 1, :]
                row_left = row_left - scale * rows_left[m]
                row_right = row_right - scale * rows_right[m]
            rows_left.append(row_left)
            rows_right.append(row_right)
        for m in range(width):
            left = left - multipliers[m] * rows_left[m]
            right = right - multipliers[m] * rows_right[m]
        if top + width == 8:
            done_left.append(left[:8])
            done_right.append(right[:8])
            left, right = left[8:], right[8:]
    left = jnp.concatenate(done_left, axis=0)
    right = jnp.concatenate(done_right, axis=0)
    pivot = jnp.sum(jnp.where(lane == line, left, 0.0), axis=1, keepdims=True)
    inverse = right * lax.rsqrt(pivot)
    push = products[size : size + 1, :]
    pushed = jnp.sum(inverse * push, axis=1, keepdims=True)
    offset = jnp.sum(inverse * pushed, axis=0, keepdims=True) * (1.0 / root_scale)
    weights = inverse + offset
    top_half = weights.astype(jnp.bfloat16)
    high[...] = top_half
    low[...] = (weights - top_half.astype(jnp.float32)).astype(jnp.bfloat16)


def transposed_weights(products, root_scale):
    size = products.shape[1]
    whole = pl.BlockSpec(memory_space=pltpu.VMEM)
    return pl.pallas_call(
        functools.partial(factor_kernel, root_scale),
        in_specs=[whole],
        out_specs=[whole] * 2,
        out_shape=[jax.ShapeDtypeStruct((size, size), jnp.bfloat16)] * 2,
    )(products)


def analysis_kernel(high, low, state, out):
    value = state[...]
    mean = jnp.mean(value, axis=1, keepdims=True)
    departure = value - mean
    near = departure.astype(jnp.bfloat16)
    rest = (departure - near.astype(jnp.float32)).astype(jnp.bfloat16)

    def times(a, b):
        return lax.dot_general(
            a, b[...], (((1,), (1,)), ((), ())), preferred_element_type=jnp.float32
        )

    out[...] = mean + (times(near, high) + (times(rest, high) + times(near, low)))


def analyse(high, low, state):
    rows, members = state.shape
    size = min(rows, 1024)
    block = pl.BlockSpec((size, members), lambda k: (k, 0))
    whole = pl.BlockSpec(memory_space=pltpu.VMEM)
    return pl.pallas_call(
        analysis_kernel,
        grid=(rows // size,),
        in_specs=[whole, whole, block],
        out_specs=block,
        out_shape=jax.ShapeDtypeStruct(state.shape, jnp.float32),
    )(high, low, state)


def ring_reduce(blocks, axis):
    count = len(blocks)
    half = count // 2
    cut = blocks[half].shape[-2] // 2
    up = shift(blocks[half][..., :cut, :], axis, 1)
    down = shift(blocks[half][..., cut:, :], axis, -1)
    ahead, behind = blocks[half - 1], blocks[count - half + 1]
    up = jnp.concatenate([ahead[..., :cut, :] + up, ahead[..., cut:, :]], axis=-2)
    down = jnp.concatenate([behind[..., :cut, :], behind[..., cut:, :] + down], axis=-2)
    for k in range(half - 1, 0, -1):
        up = shift(up, axis, 1)
        down = shift(down, axis, -1)
        if k > 1:
            up = blocks[k - 1] + up
            down = blocks[count - k + 1] + down
    return blocks[0] + up + down


def reduce_to_owner(block_a, block_b):
    size_x, size_z = block_a.shape[:2]
    part_a = ring_reduce([block_a[k] for k in range(size_x)], "x")
    part_b = ring_reduce([block_b[k] for k in range(size_z)], "z")
    part_a = ring_reduce([part_a[k] for k in range(size_z)], "z")
    part_b = ring_reduce([part_b[k] for k in range(size_x)], "x")
    return jnp.concatenate([part_a, part_b], axis=0)


def spread_sum(value, axis):
    count = lax.axis_size(axis)
    copies = jnp.broadcast_to(value[None], (count,) + value.shape)
    return jnp.sum(lax.all_to_all(copies, axis, split_axis=0, concat_axis=0, tiled=True), axis=0)


def sum_everywhere(value):
    core = lax.axis_index("core")
    rows = value.shape[0] // 2
    value = value + shift(value, "core", 1)
    part = lax.dynamic_slice_in_dim(value, core * rows, rows, 0)
    for axis in ("x", "lat", "z"):
        part = spread_sum(part, axis)
    other = shift(part, "core", 1)
    return jnp.where(
        core == 0, jnp.concatenate([part, other]), jnp.concatenate([other, part])
    )


def on_device(
    control,
    perturbations,
    zonal_flow,
    meridional_flow,
    diffusivity,
    send_cell,
    send_station,
    send_weight,
    send_count,
    obs_value,
    obs_error,
):
    member_count = perturbations.shape[2]
    step_total, owned_count = obs_value.shape
    slots = send_cell.shape[3]
    size_z, size_x, size_c = (lax.axis_size(name) for name in COL)
    core = lax.axis_index("core")
    place = jnp.stack([lax.axis_index("z"), lax.axis_index("x")]).astype(jnp.int32)

    live = lax.broadcasted_iota(jnp.int32, send_cell.shape[2:], 1) < send_count[0, 0][:, None]
    station_live = jnp.where(live, send_station[0, 0], -1)
    whole_tables = jnp.concatenate(
        [
            send_cell[0, 0],
            station_live,
            jnp.broadcast_to(send_count[0, 0][:, None], (send_cell.shape[2], slots)),
        ],
        axis=1,
    ).reshape(size_z * size_x, size_c, 3 * slots)
    whole_weights = send_weight[0, 0].reshape(size_z * size_x, size_c, slots)
    index_own = lax.dynamic_index_in_dim(whole_tables, core, 1, keepdims=False)
    index_pair = shift(
        lax.dynamic_index_in_dim(whole_tables, 1 - core, 1, keepdims=False), "core", 1
    )
    weight_own = lax.dynamic_index_in_dim(whole_weights, core, 1, keepdims=False)
    weight_pair = shift(
        lax.dynamic_index_in_dim(whole_weights, 1 - core, 1, keepdims=False), "core", 1
    )

    zero = jnp.zeros_like(control)
    rates = jnp.stack(
        [
            diffusivity + jnp.maximum(-zonal_flow, 0.0),
            diffusivity + jnp.maximum(zonal_flow, 0.0),
            diffusivity + jnp.maximum(-meridional_flow, 0.0),
            diffusivity + jnp.maximum(meridional_flow, 0.0),
            control,
            zero,
            zero,
            zero,
        ],
        axis=1,
    ).reshape(-1, member_count, control.shape[1])
    first = advance(True, rates, perturbations, edges(perturbations + control[:, :, None]))
    second = advance(False, rates, first, edges(first))
    flat = [state.reshape(-1, member_count) for state in (first, second)]
    paired = [shift(state, "core", 1) for state in flat]
    index = jnp.concatenate([index_own, index_pair], axis=0)
    weight = jnp.concatenate([weight_own, weight_pair], axis=0)
    blocks = bin_rows(
        place,
        index[:, :slots].reshape(-1),
        weight.reshape(-1),
        index[:, 2 * slots],
        index[:, slots : 2 * slots],
        flat + paired,
        owned_count,
    )
    observed = reduce_to_owner(*blocks).reshape(step_total, owned_count, member_count)

    root_scale = math.sqrt(member_count - 1.0)
    obs_mean = jnp.mean(observed, axis=2)
    spread = observed - obs_mean[:, :, None]
    scaled = (spread / (obs_error[:, :, None] * root_scale)).reshape(-1, member_count)
    innovation = ((obs_value - obs_mean) / obs_error).reshape(-1)
    products = jnp.dot(
        jnp.concatenate(
            [scaled, innovation[:, None], jnp.zeros((scaled.shape[0], 15), jnp.float32)], axis=1
        ).T,
        scaled,
        precision=exact_mode,
    )
    products = sum_everywhere(products)
    high, low = transposed_weights(products, root_scale)
    analysis = analyse(high, low, flat[-1])
    obs_analysis = analyse(high, low, observed.reshape(-1, member_count))
    return (analysis.reshape(perturbations.shape), obs_analysis.reshape(observed.shape))


def solution(mesh):
    sizes = (mesh.shape["lat"], mesh.shape["col"] // 8, 4, 2)
    fine = Mesh(mesh.devices.reshape(sizes), ("lat",) + COL)
    grid = P("lat", COL)
    return jax.shard_map(
        on_device,
        mesh=fine,
        in_specs=(
            grid,
            P("lat", COL, None),
            grid,
            grid,
            grid,
            P("lat", COL, None, None),
            P("lat", COL, None, None),
            P("lat", COL, None, None),
            P("lat", COL, None),
            P(None, ("lat",) + COL),
            P(None, ("lat",) + COL),
        ),
        out_specs=(P("lat", COL, None), P(None, ("lat",) + COL, None)),
        check_vma=False,
    )
```

profile of v0, /device:TPU:1, one launch (start us, length us, event | category | flops | bytes accessed | tf_op | source)
XLA Modules:
  0.0 247.9 jit_solution(12008177134213390104)
XLA Ops:
  0.7 3.8 %broadcast_add_fusion = f32[32,256,128]{2,1,0:T(8,128)S(1)} fusion(f32[32,256,128]{2,1,0:T(8,128)} %block.1, f32[32,256]{1,0:T(8,128)} %param.11), kind=kLoop, calls=%fused_computation | loop fusion | flops 1048576 | bytes 8421376 | tf_op jit(solution)/shard_map/add | solution.py:369
  4.5 4.0 %collective-permute-start.2 = (f32[1,256,128]{2,1,0:T(8,128)S(1)}, f32[1,256,128]{2,1,0:T(8,128)S(1)}, u32[]{:S(2)}, u32[]{:S(2)}) collective-permute-start(f32[1,256,128]{2,1,0:T(8,128)S(1)} %get-tuple-element.20), channel_id=1, source_target_pairs={{0,64},{64,128},{128,192},{1,65},{65,129},{129,193},{2,66},{66,130... | collective-permute-start | bytes 393224 | tf_op jit(solution)/shard_map/ppermute | solution.py:31
  8.6 1.3 collective-permute-start.3
  9.9 4.0 %collective-permute-start.4 = (f32[32,1,128]{2,1,0:T(1,128)S(1)}, f32[32,1,128]{2,1,0:T(1,128)S(1)}, u32[]{:S(2)}, u32[]{:S(2)}) collective-permute-start(f32[32,1,128]{2,1,0:T(1,128)S(1)} %get-tuple-element.18), channel_id=1, source_target_pairs={{0,1},{1,2},{2,3},{3,4},{4,5},{5,6},{6,7},{7,8},{8,9},{9,10},{10,1... | collective-permute-start | bytes 49160 | tf_op jit(solution)/shard_map/ppermute | solution.py:31
  13.9 1.9 collective-permute-start.5
  16.5 2.4 collective-permute-done.5.right
  18.9 2.2 copy-done
  21.1 12.6 %shard_map.122.block = f32[32,256,128]{2,1,0:T(8,128)} custom-call(f32[2,128,256]{2,1,0:T(8,128)S(1)} %bitcast.126, f32[32,256,128]{2,1,0:T(8,128)S(1)} %copy-done, f32[1,256,128]{2,1,0:T(8,128)S(1)} %collective-permute-done.2.above, f32[1,256,128]{2,1,0:T(8,128)S(1)} %collective-permute-done.3.below, f32[32,1,128]{2,1,0:T(1,128)S(1)} %collective-permute-done.4.left, ...), custom_call_target="tpu_custom_call" | custom-call | flops 12582912 | bytes 8388608 | tf_op jit(solution)/shard_map/pallas_call | solution.py:73
  33.7 1.0 fusion.28
  34.7 4.3 %collective-permute-start.6 = (f32[1,256,128]{2,1,0:T(8,128)S(1)}, f32[1,256,128]{2,1,0:T(8,128)S(1)}, u32[]{:S(2)}, u32[]{:S(2)}) collective-permute-start(f32[1,256,128]{2,1,0:T(8,128)S(1)} %get-tuple-element.16), channel_id=1, source_target_pairs={{0,64},{64,128},{128,192},{1,65},{65,129},{129,193},{2,66},{66,130... | collective-permute-start | bytes 393224 | tf_op jit(solution)/shard_map/ppermute | solution.py:31
  38.9 1.3 collective-permute-start.7
  40.2 1.0 fusion.27
  41.2 2.2 collective-permute-start.8
  43.5 2.1 collective-permute-start.9
  45.7 2.8 %collective-permute-done.9.right = f32[32,1,128]{2,1,0:T(1,128)S(1)} collective-permute-done((f32[32,1,128]{2,1,0:T(1,128)S(1)}, f32[32,1,128]{2,1,0:T(1,128)S(1)}, u32[]{:S(2)}, u32[]{:S(2)}) %collective-permute-start.9) | collective-permute-done | bytes 16416 | tf_op jit(solution)/shard_map/ppermute | solution.py:32
  48.5 11.7 %shard_map.123 = f32[32,256,128]{2,1,0:T(8,128)} custom-call(f32[2,128,256]{2,1,0:T(8,128)S(1)} %bitcast.127, f32[32,256,128]{2,1,0:T(8,128)} %shard_map.122.block, f32[1,256,128]{2,1,0:T(8,128)S(1)} %collective-permute-done.6.above, f32[1,256,128]{2,1,0:T(8,128)S(1)} %collective-permute-done.7.below, f32[32,1,128]{2,1,0:T(1,128)S(1)} %collective-permute-done.8.left, ...), custom_call_target="tpu_custom_call" | custom-call | flops 12582912 | bytes 8388608 | tf_op jit(solution)/shard_map/pallas_call | solution.py:73
  60.3 0.5 broadcast.37
  60.8 0.7 reduce.6
  61.8 0.6 collective-permute-start
  62.6 0.6 pad_add_fusion.2.place
  63.2 4.3 %collective-permute-done.1 = f32[32,128]{1,0:T(8,128)S(1)} collective-permute-done((f32[32,128]{1,0:T(8,128)S(1)}, f32[32,128]{1,0:T(8,128)S(1)}, u32[]{:S(2)}, u32[]{:S(2)}) %collective-permute-start.1) | collective-permute-done | bytes 16416 | tf_op jit(solution)/shard_map/ppermute | solution.py:19
  67.5 0.6 maximum_bitcast_fusion.weight
  68.1 0.6 fusion.21.count
  68.8 0.6 pad_add_fusion.1
  69.4 23.7 %shard_map.124 = (f32[4,8,288,128]{3,2,1,0:T(8,128)S(1)}, f32[8,4,224,128]{3,2,1,0:T(8,128)S(1)}) custom-call(s32[2]{0:T(128)} %pad_add_fusion.2.place, s32[8192]{0:T(1024)} %get-tuple-element.55.cell, f32[8192]{0:T(1024)} %maximum_bitcast_fusion.weight, s32[64]{0:T(128)} %fusion.21.count, s32[64,128]{1,0:T(8,128)} %get-tuple-element.54.station, ...), custom_call_target="tpu_custom_call" | custom-call | flops 1000000000 | bytes 31457280 | tf_op jit(solution)/shard_map/pallas_call | solution.py:148
  93.5 4.8 %collective-permute-start.24 = (f32[4,112,128]{2,1,0:T(8,128)S(1)}, f32[4,112,128]{2,1,0:T(8,128)S(1)}, u32[]{:S(2)}, u32[]{:S(2)}) collective-permute-start(f32[4,112,128]{2,1,0:T(8,128)S(1)} %get-tuple-element.48), channel_id=1, source_target_pairs={{0,8},{8,16},{16,24},{24,32},{32,40},{40,48},{48,56},{56,0},{1,9},... | collective-permute-start | bytes 688136 | tf_op jit(solution)/shard_map/ppermute | solution.py:19
  98.4 4.7 %collective-permute-start.14 = (f32[8,144,128]{2,1,0:T(8,128)S(1)}, f32[8,144,128]{2,1,0:T(8,128)S(1)}, u32[]{:S(2)}, u32[]{:S(2)}) collective-permute-start(f32[8,144,128]{2,1,0:T(8,128)S(1)} %get-tuple-element.37), channel_id=1, source_target_pairs={{0,6},{2,0},{4,2},{6,4},{1,7},{3,1},{5,3},{7,5},{8,14},{10,8},{12,... | collective-permute-start | bytes 1769480 | tf_op jit(solution)/shard_map/ppermute | solution.py:19
  103.1 2.2 collective-permute-start.28
  105.3 3.3 %collective-permute-done.24 = f32[4,112,128]{2,1,0:T(8,128)S(1)} collective-permute-done((f32[4,112,128]{2,1,0:T(8,128)S(1)}, f32[4,112,128]{2,1,0:T(8,128)S(1)}, u32[]{:S(2)}, u32[]{:S(2)}) %collective-permute-start.24) | collective-permute-done | bytes 229408 | tf_op jit(solution)/shard_map/ppermute | solution.py:19
  108.7 8.0 %collective-permute-done.12 = f32[8,144,128]{2,1,0:T(8,128)S(1)} collective-permute-done((f32[8,144,128]{2,1,0:T(8,128)S(1)}, f32[8,144,128]{2,1,0:T(8,128)S(1)}, u32[]{:S(2)}, u32[]{:S(2)}) %collective-permute-start.12) | collective-permute-done | bytes 589856 | tf_op jit(solution)/shard_map/ppermute | solution.py:19
  117.2 2.7 %collective-permute-start.15 = (f32[8,288,128]{2,1,0:T(8,128)S(1)}, f32[8,288,128]{2,1,0:T(8,128)S(1)}, u32[]{:S(2)}, u32[]{:S(2)}) collective-permute-start(f32[8,288,128]{2,1,0:T(8,128)S(1)} %pad_maximum_fusion.1), channel_id=1, source_target_pairs={{0,6},{2,0},{4,2},{6,4},{1,7},{3,1},{5,3},{7,5},{8,14},{10,8},{12,... | collective-permute-start | bytes 3538952 | tf_op jit(solution)/shard_map/ppermute | solution.py:19
  120.1 2.4 collective-permute-start.29
  122.7 8.6 %collective-permute-done.29 = f32[4,224,128]{2,1,0:T(8,128)S(1)} collective-permute-done((f32[4,224,128]{2,1,0:T(8,128)S(1)}, f32[4,224,128]{2,1,0:T(8,128)S(1)}, u32[]{:S(2)}, u32[]{:S(2)}) %collective-permute-start.29) | collective-permute-done | bytes 458784 | tf_op jit(solution)/shard_map/ppermute | solution.py:19
  131.3 3.1 %collective-permute-done.26 = f32[4,224,128]{2,1,0:T(8,128)S(1)} collective-permute-done((f32[4,224,128]{2,1,0:T(8,128)S(1)}, f32[4,224,128]{2,1,0:T(8,128)S(1)}, u32[]{:S(2)}, u32[]{:S(2)}) %collective-permute-start.26) | collective-permute-done | bytes 458784 | tf_op jit(solution)/shard_map/ppermute | solution.py:19
  134.7 1.8 collective-permute-start.27
  136.5 9.1 %collective-permute-done.13 = f32[8,288,128]{2,1,0:T(8,128)S(1)} collective-permute-done((f32[8,288,128]{2,1,0:T(8,128)S(1)}, f32[8,288,128]{2,1,0:T(8,128)S(1)}, u32[]{:S(2)}, u32[]{:S(2)}) %collective-permute-start.13) | collective-permute-done | bytes 1179680 | tf_op jit(solution)/shard_map/ppermute | solution.py:19
  145.8 0.6 collective-permute-start.16
  146.5 2.1 collective-permute-start.20
  148.7 0.6 collective-permute-start.31
  149.2 1.1 collective-permute-done.16
  150.3 3.1 %collective-permute-done.20 = f32[144,128]{1,0:T(8,128)S(1)} collective-permute-done((f32[144,128]{1,0:T(8,128)S(1)}, f32[144,128]{1,0:T(8,128)S(1)}, u32[]{:S(2)}, u32[]{:S(2)}) %collective-permute-start.20) | collective-permute-done | bytes 73760 | tf_op jit(solution)/shard_map/ppermute | solution.py:19
  153.6 1.5 collective-permute-start.17
  155.1 7.0 %collective-permute-done.31 = f32[4,224,128]{2,1,0:T(8,128)S(1)} collective-permute-done((f32[4,224,128]{2,1,0:T(8,128)S(1)}, f32[4,224,128]{2,1,0:T(8,128)S(1)}, u32[]{:S(2)}, u32[]{:S(2)}) %collective-permute-start.31) | collective-permute-done | bytes 458784 | tf_op jit(solution)/shard_map/ppermute | solution.py:19
  162.3 2.7 %collective-permute-start.34 = (f32[112,128]{1,0:T(8,128)S(1)}, f32[112,128]{1,0:T(8,128)S(1)}, u32[]{:S(2)}, u32[]{:S(2)}) collective-permute-start(f32[112,128]{1,0:T(8,128)S(1)} %get-tuple-element.43), channel_id=1, source_target_pairs={{0,6},{2,0},{4,2},{6,4},{1,7},{3,1},{5,3},{7,5},{8,14},{10,8},{12,... | collective-permute-start | bytes 172040 | tf_op jit(solution)/shard_map/ppermute | solution.py:19
  165.0 1.3 collective-permute-start.18
  166.6 3.7 %collective-permute-done.18 = f32[288,128]{1,0:T(8,128)S(1)} collective-permute-done((f32[288,128]{1,0:T(8,128)S(1)}, f32[288,128]{1,0:T(8,128)S(1)}, u32[]{:S(2)}, u32[]{:S(2)}) %collective-permute-start.18) | collective-permute-done | bytes 147488 | tf_op jit(solution)/shard_map/ppermute | solution.py:19
  170.6 2.7 %collective-permute-start.35 = (f32[224,128]{1,0:T(8,128)S(1)}, f32[224,128]{1,0:T(8,128)S(1)}, u32[]{:S(2)}, u32[]{:S(2)}) collective-permute-start(f32[224,128]{1,0:T(8,128)S(1)} %pad_maximum_fusion.8), channel_id=1, source_target_pairs={{0,6},{2,0},{4,2},{6,4},{1,7},{3,1},{5,3},{7,5},{8,14},{10,8},{12,... | collective-permute-start | bytes 344072 | tf_op jit(solution)/shard_map/ppermute | solution.py:19
  173.3 1.4 collective-permute-start.19
  174.8 1.5 collective-permute-start.23
  176.4 2.2 collective-permute-done.19
  178.5 1.3 collective-permute-done.23
  179.9 0.7 pad_maximum_fusion.4
  181.0 1.0 fusion.1
  182.0 7.5 %collective-permute-start.36 = (f32[144,128]{1,0:T(8,128)S(1)}, f32[144,128]{1,0:T(8,128)S(1)}, u32[]{:S(2)}, u32[]{:S(2)}) collective-permute-start(f32[144,128]{1,0:T(8,128)S(1)} %fusion.1), channel_id=1, source_target_pairs={{0,1},{1,0},{2,3},{3,2},{4,5},{5,4},{6,7},{7,6},{8,9},{9,8},{10,11... | collective-permute-start | bytes 221192 | tf_op jit(solution)/shard_map/ppermute | solution.py:19
  189.5 0.9 collective-permute-done.36
  190.4 7.3 %all_to_all.15 = f32[4,72,128]{2,1,0:T(8,128)S(1)} all-to-all(f32[4,72,128]{2,1,0:T(8,128)S(1)} %broadcast_in_dim.14), channel_id=1, replica_groups=mesh['lat'=4,'z'=8,'x'=4,'core'=2] {'x'}, dimensions={0} | all-to-all | bytes 294912 | tf_op jit(solution)/shard_map/all_to_all | solution.py:299
  197.7 11.7 %all_to_all.16 = f32[4,72,128]{2,1,0:T(8,128)S(1)} all-to-all(f32[4,72,128]{2,1,0:T(8,128)S(1)} %broadcast_in_dim.15), channel_id=1, replica_groups=mesh['lat'=4,'z'=8,'x'=4,'core'=2] {'lat'}, dimensions={0} | all-to-all | bytes 294912 | tf_op jit(solution)/shard_map/all_to_all | solution.py:299
  209.5 15.9 %all_to_all.17 = f32[8,72,128]{2,1,0:T(8,128)S(1)} all-to-all(f32[8,72,128]{2,1,0:T(8,128)S(1)} %broadcast_in_dim.16), channel_id=1, replica_groups=mesh['lat'=4,'z'=8,'x'=4,'core'=2] {'z'}, dimensions={0} | all-to-all | bytes 589824 | tf_op jit(solution)/shard_map/all_to_all | solution.py:299
  225.4 4.7 %collective-permute-start.37 = (f32[72,128]{1,0:T(8,128)S(1)}, f32[72,128]{1,0:T(8,128)S(1)}, u32[]{:S(2)}, u32[]{:S(2)}) collective-permute-start(f32[72,128]{1,0:T(8,128)S(1)} %reduce_sum.39), channel_id=1, source_target_pairs={{0,1},{1,0},{2,3},{3,2},{4,5},{5,4},{6,7},{7,6},{8,9},{9,8},{10,11... | collective-permute-start | bytes 110600 | tf_op jit(solution)/shard_map/ppermute | solution.py:19
  230.0 0.9 collective-permute-done.37
  230.9 0.6 maximum_select_fusion.products
  231.5 6.3 %shard_map.125 = (bf16[128,128]{1,0:T(8,128)(2,1)}, bf16[128,128]{1,0:T(8,128)(2,1)}) custom-call(f32[144,128]{1,0:T(8,128)} %maximum_select_fusion.products), custom_call_target="tpu_custom_call" | custom-call | tf_op jit(solution)/shard_map/pallas_call | solution.py:232
  237.9 8.0 %shard_map.126 = f32[8192,128]{1,0:T(8,128)} custom-call(bf16[128,128]{1,0:T(8,128)(2,1)} %get-tuple-element.8.high, bf16[128,128]{1,0:T(8,128)(2,1)} %get-tuple-element.9.low, f32[8192,128]{1,0:T(8,128)} %bitcast.18.rest_1_.state), custom_call_target="tpu_custom_call" | custom-call | tf_op jit(solution)/shard_map/pallas_call | solution.py:260
  245.8 2.0 shard_map.127
  (120 shorter events, 4.9 us)
Async XLA Ops:
  0.6 15.4 %copy-start.1 = (f32[32,256]{1,0:T(8,128)S(1)}, f32[32,256]{1,0:T(8,128)}, u32[]{:S(2)}) copy-start(f32[32,256]{1,0:T(8,128)} %param.11) | copy-start | bytes 98308
  0.6 15.1 %copy-start.4 = (f32[32,256]{1,0:T(8,128)S(1)}, f32[32,256]{1,0:T(8,128)}, u32[]{:S(2)}) copy-start(f32[32,256]{1,0:T(8,128)} %param.13) | copy-start | bytes 98308
  0.7 15.1 %copy-start.3 = (f32[32,256]{1,0:T(8,128)S(1)}, f32[32,256]{1,0:T(8,128)}, u32[]{:S(2)}) copy-start(f32[32,256]{1,0:T(8,128)} %param.14) | copy-start | bytes 98308
  0.7 15.1 %copy-start.2 = (f32[32,256]{1,0:T(8,128)S(1)}, f32[32,256]{1,0:T(8,128)}, u32[]{:S(2)}) copy-start(f32[32,256]{1,0:T(8,128)} %param.15) | copy-start | bytes 98308
  4.5 14.4 %collective-permute-start.2 = (f32[1,256,128]{2,1,0:T(8,128)S(1)}, f32[1,256,128]{2,1,0:T(8,128)S(1)}, u32[]{:S(2)}, u32[]{:S(2)}) collective-permute-start(f32[1,256,128]{2,1,0:T(8,128)S(1)} %get-tuple-element.20), channel_id=1, source_target_pairs={{0,64},{64,128},{128,192},{1,65},{65,129},{129,193},{2,66},{66,130... | collective-permute-start | bytes 393224 | tf_op jit(solution)/shard_map/ppermute | solution.py:31
  8.6 10.4 %collective-permute-start.3 = (f32[1,256,128]{2,1,0:T(8,128)S(1)}, f32[1,256,128]{2,1,0:T(8,128)S(1)}, u32[]{:S(2)}, u32[]{:S(2)}) collective-permute-start(f32[1,256,128]{2,1,0:T(8,128)S(1)} %get-tuple-element.19), channel_id=1, source_target_pairs={{64,0},{128,64},{192,128},{65,1},{129,65},{193,129},{66,2},{130,66... | collective-permute-start | bytes 393224 | tf_op jit(solution)/shard_map/ppermute | solution.py:32
  9.9 6.6 %collective-permute-start.4 = (f32[32,1,128]{2,1,0:T(1,128)S(1)}, f32[32,1,128]{2,1,0:T(1,128)S(1)}, u32[]{:S(2)}, u32[]{:S(2)}) collective-permute-start(f32[32,1,128]{2,1,0:T(1,128)S(1)} %get-tuple-element.18), channel_id=1, source_target_pairs={{0,1},{1,2},{2,3},{3,4},{4,5},{5,6},{6,7},{7,8},{8,9},{9,10},{10,1... | collective-permute-start | bytes 49160 | tf_op jit(solution)/shard_map/ppermute | solution.py:31
  13.9 5.1 %collective-permute-start.5 = (f32[32,1,128]{2,1,0:T(1,128)S(1)}, f32[32,1,128]{2,1,0:T(1,128)S(1)}, u32[]{:S(2)}, u32[]{:S(2)}) collective-permute-start(f32[32,1,128]{2,1,0:T(1,128)S(1)} %get-tuple-element.17), channel_id=1, source_target_pairs={{1,0},{2,1},{3,2},{4,3},{5,4},{6,5},{7,6},{8,7},{9,8},{10,9},{11,1... | collective-permute-start | bytes 49160 | tf_op jit(solution)/shard_map/ppermute | solution.py:32
  18.9 2.2 copy-start
  34.7 13.9 %collective-permute-start.6 = (f32[1,256,128]{2,1,0:T(8,128)S(1)}, f32[1,256,128]{2,1,0:T(8,128)S(1)}, u32[]{:S(2)}, u32[]{:S(2)}) collective-permute-start(f32[1,256,128]{2,1,0:T(8,128)S(1)} %get-tuple-element.16), channel_id=1, source_target_pairs={{0,64},{64,128},{128,192},{1,65},{65,129},{129,193},{2,66},{66,130... | collective-permute-start | bytes 393224 | tf_op jit(solution)/shard_map/ppermute | solution.py:31
  38.9 9.6 %collective-permute-start.7 = (f32[1,256,128]{2,1,0:T(8,128)S(1)}, f32[1,256,128]{2,1,0:T(8,128)S(1)}, u32[]{:S(2)}, u32[]{:S(2)}) collective-permute-start(f32[1,256,128]{2,1,0:T(8,128)S(1)} %get-tuple-element.15), channel_id=1, source_target_pairs={{64,0},{128,64},{192,128},{65,1},{129,65},{193,129},{66,2},{130,66... | collective-permute-start | bytes 393224 | tf_op jit(solution)/shard_map/ppermute | solution.py:32
  41.2 4.5 %collective-permute-start.8 = (f32[32,1,128]{2,1,0:T(1,128)S(1)}, f32[32,1,128]{2,1,0:T(1,128)S(1)}, u32[]{:S(2)}, u32[]{:S(2)}) collective-permute-start(f32[32,1,128]{2,1,0:T(1,128)S(1)} %get-tuple-element.14), channel_id=1, source_target_pairs={{0,1},{1,2},{2,3},{3,4},{4,5},{5,6},{6,7},{7,8},{8,9},{9,10},{10,1... | collective-permute-start | bytes 49160 | tf_op jit(solution)/shard_map/ppermute | solution.py:31
  43.5 5.1 %collective-permute-start.9 = (f32[32,1,128]{2,1,0:T(1,128)S(1)}, f32[32,1,128]{2,1,0:T(1,128)S(1)}, u32[]{:S(2)}, u32[]{:S(2)}) collective-permute-start(f32[32,1,128]{2,1,0:T(1,128)S(1)} %get-tuple-element.13), channel_id=1, source_target_pairs={{1,0},{2,1},{3,2},{4,3},{5,4},{6,5},{7,6},{8,7},{9,8},{10,9},{11,1... | collective-permute-start | bytes 49160 | tf_op jit(solution)/shard_map/ppermute | solution.py:32
  45.6 15.2 %copy-start.10 = (s32[1,1,64]{2,1,0:T(1,128)S(1)}, s32[1,1,64]{2,1,0:T(1,128)}, u32[]{:S(2)}) copy-start(s32[1,1,64]{2,1,0:T(1,128)} %param.19) | copy-start | bytes 772
  45.6 16.0 %copy-start.5 = (s32[1,1,64,128]{3,2,1,0:T(8,128)S(1)}, s32[1,1,64,128]{3,2,1,0:T(8,128)}, u32[]{:S(2)}) copy-start(s32[1,1,64,128]{3,2,1,0:T(8,128)} %param.16) | copy-start | bytes 98308
  45.6 16.0 %copy-start.6 = (s32[1,1,64,128]{3,2,1,0:T(8,128)S(1)}, s32[1,1,64,128]{3,2,1,0:T(8,128)}, u32[]{:S(2)}) copy-start(s32[1,1,64,128]{3,2,1,0:T(8,128)} %param.17) | copy-start | bytes 98308
  45.6 16.8 %copy-start.7 = (f32[1,1,64,128]{3,2,1,0:T(8,128)S(1)}, f32[1,1,64,128]{3,2,1,0:T(8,128)}, u32[]{:S(2)}) copy-start(f32[1,1,64,128]{3,2,1,0:T(8,128)} %param.18) | copy-start | bytes 98308
  45.6 23.8 %collective-permute-start.10 = (f32[8192,128]{1,0:T(8,128)}, f32[8192,128]{1,0:T(8,128)}, u32[]{:S(2)}, u32[]{:S(2)}) collective-permute-start(f32[8192,128]{1,0:T(8,128)} %bitcast.17.rest_0_), channel_id=1, source_target_pairs={{0,1},{1,0},{2,3},{3,2},{4,5},{5,4},{6,7},{7,6},{8,9},{9,8},{10,11... | collective-permute-start | bytes 12582920 | tf_op jit(solution)/shard_map/ppermute | solution.py:19
  60.3 9.1 %collective-permute-start.11 = (f32[8192,128]{1,0:T(8,128)}, f32[8192,128]{1,0:T(8,128)}, u32[]{:S(2)}, u32[]{:S(2)}) collective-permute-start(f32[8192,128]{1,0:T(8,128)} %bitcast.18.rest_1_.state), channel_id=1, source_target_pairs={{0,1},{1,0},{2,3},{3,2},{4,5},{5,4},{6,7},{7,6},{8,9},{9,8},{10,11... | collective-permute-start | bytes 12582920 | tf_op jit(solution)/shard_map/ppermute | solution.py:19
  61.8 6.3 %collective-permute-start = (s32[32,384]{1,0:T(8,128)S(1)}, s32[32,384]{1,0:T(8,128)S(1)}, u32[]{:S(2)}, u32[]{:S(2)}) collective-permute-start(s32[32,384]{1,0:T(8,128)S(1)} %get-tuple-element.56), channel_id=1, source_target_pairs={{0,1},{1,0},{2,3},{3,2},{4,5},{5,4},{6,7},{7,6},{8,9},{9,8},{10,11... | collective-permute-start | bytes 147464 | tf_op jit(solution)/shard_map/ppermute | solution.py:19
  62.5 5.0 %collective-permute-start.1 = (f32[32,128]{1,0:T(8,128)S(1)}, f32[32,128]{1,0:T(8,128)S(1)}, u32[]{:S(2)}, u32[]{:S(2)}) collective-permute-start(f32[32,128]{1,0:T(8,128)S(1)} %bitcast.136), channel_id=1, source_target_pairs={{0,1},{1,0},{2,3},{3,2},{4,5},{5,4},{6,7},{7,6},{8,9},{9,8},{10,11... | collective-permute-start | bytes 49160 | tf_op jit(solution)/shard_map/ppermute | solution.py:19
  93.5 15.1 %collective-permute-start.24 = (f32[4,112,128]{2,1,0:T(8,128)S(1)}, f32[4,112,128]{2,1,0:T(8,128)S(1)}, u32[]{:S(2)}, u32[]{:S(2)}) collective-permute-start(f32[4,112,128]{2,1,0:T(8,128)S(1)} %get-tuple-element.48), channel_id=1, source_target_pairs={{0,8},{8,16},{16,24},{24,32},{32,40},{40,48},{48,56},{56,0},{1,9},... | collective-permute-start | bytes 688136 | tf_op jit(solution)/shard_map/ppermute | solution.py:19
  98.3 18.4 %collective-permute-start.12 = (f32[8,144,128]{2,1,0:T(8,128)S(1)}, f32[8,144,128]{2,1,0:T(8,128)S(1)}, u32[]{:S(2)}, u32[]{:S(2)}) collective-permute-start(f32[8,144,128]{2,1,0:T(8,128)S(1)} %get-tuple-element.36), channel_id=1, source_target_pairs={{0,2},{2,4},{4,6},{6,0},{1,3},{3,5},{5,7},{7,1},{8,10},{10,12},{12... | collective-permute-start | bytes 1769480 | tf_op jit(solution)/shard_map/ppermute | solution.py:19
  98.4 18.6 %collective-permute-start.14 = (f32[8,144,128]{2,1,0:T(8,128)S(1)}, f32[8,144,128]{2,1,0:T(8,128)S(1)}, u32[]{:S(2)}, u32[]{:S(2)}) collective-permute-start(f32[8,144,128]{2,1,0:T(8,128)S(1)} %get-tuple-element.37), channel_id=1, source_target_pairs={{0,6},{2,0},{4,2},{6,4},{1,7},{3,1},{5,3},{7,5},{8,14},{10,8},{12,... | collective-permute-start | bytes 1769480 | tf_op jit(solution)/shard_map/ppermute | solution.py:19
  103.1 16.9 %collective-permute-start.28 = (f32[4,112,128]{2,1,0:T(8,128)S(1)}, f32[4,112,128]{2,1,0:T(8,128)S(1)}, u32[]{:S(2)}, u32[]{:S(2)}) collective-permute-start(f32[4,112,128]{2,1,0:T(8,128)S(1)} %get-tuple-element.49), channel_id=1, source_target_pairs={{0,56},{8,0},{16,8},{24,16},{32,24},{40,32},{48,40},{56,48},{1,57}... | collective-permute-start | bytes 688136 | tf_op jit(solution)/shard_map/ppermute | solution.py:19
  108.7 13.8 %collective-permute-start.25 = (f32[4,224,128]{2,1,0:T(8,128)S(1)}, f32[4,224,128]{2,1,0:T(8,128)S(1)}, u32[]{:S(2)}, u32[]{:S(2)}) collective-permute-start(f32[4,224,128]{2,1,0:T(8,128)S(1)} %pad_maximum_fusion.2), channel_id=1, source_target_pairs={{0,8},{8,16},{16,24},{24,32},{32,40},{40,48},{48,56},{56,0},{1,9},... | collective-permute-start | bytes 1376264 | tf_op jit(solution)/shard_map/ppermute | solution.py:19
  116.9 28.6 %collective-permute-start.13 = (f32[8,288,128]{2,1,0:T(8,128)S(1)}, f32[8,288,128]{2,1,0:T(8,128)S(1)}, u32[]{:S(2)}, u32[]{:S(2)}) collective-permute-start(f32[8,288,128]{2,1,0:T(8,128)S(1)} %pad_maximum_fusion), channel_id=1, source_target_pairs={{0,2},{2,4},{4,6},{6,0},{1,3},{3,5},{5,7},{7,1},{8,10},{10,12},{12... | collective-permute-start | bytes 3538952 | tf_op jit(solution)/shard_map/ppermute | solution.py:19
  117.2 28.3 %collective-permute-start.15 = (f32[8,288,128]{2,1,0:T(8,128)S(1)}, f32[8,288,128]{2,1,0:T(8,128)S(1)}, u32[]{:S(2)}, u32[]{:S(2)}) collective-permute-start(f32[8,288,128]{2,1,0:T(8,128)S(1)} %pad_maximum_fusion.1), channel_id=1, source_target_pairs={{0,6},{2,0},{4,2},{6,4},{1,7},{3,1},{5,3},{7,5},{8,14},{10,8},{12,... | collective-permute-start | bytes 3538952 | tf_op jit(solution)/shard_map/ppermute | solution.py:19
  120.1 11.3 %collective-permute-start.29 = (f32[4,224,128]{2,1,0:T(8,128)S(1)}, f32[4,224,128]{2,1,0:T(8,128)S(1)}, u32[]{:S(2)}, u32[]{:S(2)}) collective-permute-start(f32[4,224,128]{2,1,0:T(8,128)S(1)} %pad_maximum_fusion.3), channel_id=1, source_target_pairs={{0,56},{8,0},{16,8},{24,16},{32,24},{40,32},{48,40},{56,48},{1,57}... | collective-permute-start | bytes 1376264 | tf_op jit(solution)/shard_map/ppermute | solution.py:19
  122.6 11.8 %collective-permute-start.26 = (f32[4,224,128]{2,1,0:T(8,128)S(1)}, f32[4,224,128]{2,1,0:T(8,128)S(1)}, u32[]{:S(2)}, u32[]{:S(2)}) collective-permute-start(f32[4,224,128]{2,1,0:T(8,128)S(1)} %bitcast_add_fusion.3), channel_id=1, source_target_pairs={{0,8},{8,16},{16,24},{24,32},{32,40},{40,48},{48,56},{56,0},{1,9},... | collective-permute-start | bytes 1376264 | tf_op jit(solution)/shard_map/ppermute | solution.py:19
  134.5 14.1 %collective-permute-start.30 = (f32[4,224,128]{2,1,0:T(8,128)S(1)}, f32[4,224,128]{2,1,0:T(8,128)S(1)}, u32[]{:S(2)}, u32[]{:S(2)}) collective-permute-start(f32[4,224,128]{2,1,0:T(8,128)S(1)} %get-tuple-element.22), channel_id=1, source_target_pairs={{0,56},{8,0},{16,8},{24,16},{32,24},{40,32},{48,40},{56,48},{1,57}... | collective-permute-start | bytes 1376264 | tf_op jit(solution)/shard_map/ppermute | solution.py:19
  134.7 20.4 %collective-permute-start.27 = (f32[4,224,128]{2,1,0:T(8,128)S(1)}, f32[4,224,128]{2,1,0:T(8,128)S(1)}, u32[]{:S(2)}, u32[]{:S(2)}) collective-permute-start(f32[4,224,128]{2,1,0:T(8,128)S(1)} %get-tuple-element.21), channel_id=1, source_target_pairs={{0,8},{8,16},{16,24},{24,32},{32,40},{40,48},{48,56},{56,0},{1,9},... | collective-permute-start | bytes 1376264 | tf_op jit(solution)/shard_map/ppermute | solution.py:19
  145.8 4.5 %collective-permute-start.16 = (f32[144,128]{1,0:T(8,128)S(1)}, f32[144,128]{1,0:T(8,128)S(1)}, u32[]{:S(2)}, u32[]{:S(2)}) collective-permute-start(f32[144,128]{1,0:T(8,128)S(1)} %get-tuple-element.30), channel_id=1, source_target_pairs={{0,8},{8,16},{16,24},{24,32},{32,40},{40,48},{48,56},{56,0},{1,9},... | collective-permute-start | bytes 221192 | tf_op jit(solution)/shard_map/ppermute | solution.py:19
  146.5 6.9 %collective-permute-start.20 = (f32[144,128]{1,0:T(8,128)S(1)}, f32[144,128]{1,0:T(8,128)S(1)}, u32[]{:S(2)}, u32[]{:S(2)}) collective-permute-start(f32[144,128]{1,0:T(8,128)S(1)} %get-tuple-element.31), channel_id=1, source_target_pairs={{0,56},{8,0},{16,8},{24,16},{32,24},{40,32},{48,40},{56,48},{1,57}... | collective-permute-start | bytes 221192 | tf_op jit(solution)/shard_map/ppermute | solution.py:19
  148.7 13.5 %collective-permute-start.31 = (f32[4,224,128]{2,1,0:T(8,128)S(1)}, f32[4,224,128]{2,1,0:T(8,128)S(1)}, u32[]{:S(2)}, u32[]{:S(2)}) collective-permute-start(f32[4,224,128]{2,1,0:T(8,128)S(1)} %bitcast_add_fusion.2), channel_id=1, source_target_pairs={{0,56},{8,0},{16,8},{24,16},{32,24},{40,32},{48,40},{56,48},{1,57}... | collective-permute-start | bytes 1376264 | tf_op jit(solution)/shard_map/ppermute | solution.py:19
  153.5 13.1 %collective-permute-start.21 = (f32[288,128]{1,0:T(8,128)S(1)}, f32[288,128]{1,0:T(8,128)S(1)}, u32[]{:S(2)}, u32[]{:S(2)}) collective-permute-start(f32[288,128]{1,0:T(8,128)S(1)} %pad_maximum_fusion.6), channel_id=1, source_target_pairs={{0,56},{8,0},{16,8},{24,16},{32,24},{40,32},{48,40},{56,48},{1,57}... | collective-permute-start | bytes 442376 | tf_op jit(solution)/shard_map/ppermute | solution.py:19
  153.6 11.4 %collective-permute-start.17 = (f32[288,128]{1,0:T(8,128)S(1)}, f32[288,128]{1,0:T(8,128)S(1)}, u32[]{:S(2)}, u32[]{:S(2)}) collective-permute-start(f32[288,128]{1,0:T(8,128)S(1)} %pad_maximum_fusion.5), channel_id=1, source_target_pairs={{0,8},{8,16},{16,24},{24,32},{32,40},{40,48},{48,56},{56,0},{1,9},... | collective-permute-start | bytes 442376 | tf_op jit(solution)/shard_map/ppermute | solution.py:19
  162.3 4.3 %collective-permute-start.32 = (f32[112,128]{1,0:T(8,128)S(1)}, f32[112,128]{1,0:T(8,128)S(1)}, u32[]{:S(2)}, u32[]{:S(2)}) collective-permute-start(f32[112,128]{1,0:T(8,128)S(1)} %get-tuple-element.42), channel_id=1, source_target_pairs={{0,2},{2,4},{4,6},{6,0},{1,3},{3,5},{5,7},{7,1},{8,10},{10,12},{12... | collective-permute-start | bytes 172040 | tf_op jit(solution)/shard_map/ppermute | solution.py:19
  162.3 4.2 %collective-permute-start.34 = (f32[112,128]{1,0:T(8,128)S(1)}, f32[112,128]{1,0:T(8,128)S(1)}, u32[]{:S(2)}, u32[]{:S(2)}) collective-permute-start(f32[112,128]{1,0:T(8,128)S(1)} %get-tuple-element.43), channel_id=1, source_target_pairs={{0,6},{2,0},{4,2},{6,4},{1,7},{3,1},{5,3},{7,5},{8,14},{10,8},{12,... | collective-permute-start | bytes 172040 | tf_op jit(solution)/shard_map/ppermute | solution.py:19
  165.0 5.3 %collective-permute-start.18 = (f32[288,128]{1,0:T(8,128)S(1)}, f32[288,128]{1,0:T(8,128)S(1)}, u32[]{:S(2)}, u32[]{:S(2)}) collective-permute-start(f32[288,128]{1,0:T(8,128)S(1)} %fusion.10), channel_id=1, source_target_pairs={{0,8},{8,16},{16,24},{24,32},{32,40},{40,48},{48,56},{56,0},{1,9},... | collective-permute-start | bytes 442376 | tf_op jit(solution)/shard_map/ppermute | solution.py:19
  170.4 4.4 %collective-permute-start.22 = (f32[288,128]{1,0:T(8,128)S(1)}, f32[288,128]{1,0:T(8,128)S(1)}, u32[]{:S(2)}, u32[]{:S(2)}) collective-permute-start(f32[288,128]{1,0:T(8,128)S(1)} %get-tuple-element.27), channel_id=1, source_target_pairs={{0,56},{8,0},{16,8},{24,16},{32,24},{40,32},{48,40},{56,48},{1,57}... | collective-permute-start | bytes 442376 | tf_op jit(solution)/shard_map/ppermute | solution.py:19
  170.5 10.1 %copy-start.8 = (f32[2,256]{1,0:T(2,128)S(1)}, f32[2,256]{1,0:T(2,128)}, u32[]{:S(2)}) copy-start(f32[2,256]{1,0:T(2,128)} %param.21) | copy-start | bytes 6148
  170.5 10.1 %copy-start.9 = (f32[2,256]{1,0:T(2,128)S(1)}, f32[2,256]{1,0:T(2,128)}, u32[]{:S(2)}) copy-start(f32[2,256]{1,0:T(2,128)} %param.20) | copy-start | bytes 6148
  170.5 5.8 %collective-permute-start.33 = (f32[224,128]{1,0:T(8,128)S(1)}, f32[224,128]{1,0:T(8,128)S(1)}, u32[]{:S(2)}, u32[]{:S(2)}) collective-permute-start(f32[224,128]{1,0:T(8,128)S(1)} %pad_maximum_fusion.7), channel_id=1, source_target_pairs={{0,2},{2,4},{4,6},{6,0},{1,3},{3,5},{5,7},{7,1},{8,10},{10,12},{12... | collective-permute-start | bytes 344072 | tf_op jit(solution)/shard_map/ppermute | solution.py:19
  170.6 5.7 %collective-permute-start.35 = (f32[224,128]{1,0:T(8,128)S(1)}, f32[224,128]{1,0:T(8,128)S(1)}, u32[]{:S(2)}, u32[]{:S(2)}) collective-permute-start(f32[224,128]{1,0:T(8,128)S(1)} %pad_maximum_fusion.8), channel_id=1, source_target_pairs={{0,6},{2,0},{4,2},{6,4},{1,7},{3,1},{5,3},{7,5},{8,14},{10,8},{12,... | collective-permute-start | bytes 344072 | tf_op jit(solution)/shard_map/ppermute | solution.py:19
  173.3 5.2 %collective-permute-start.19 = (f32[288,128]{1,0:T(8,128)S(1)}, f32[288,128]{1,0:T(8,128)S(1)}, u32[]{:S(2)}, u32[]{:S(2)}) collective-permute-start(f32[288,128]{1,0:T(8,128)S(1)} %get-tuple-element.26), channel_id=1, source_target_pairs={{0,8},{8,16},{16,24},{24,32},{32,40},{40,48},{48,56},{56,0},{1,9},... | collective-permute-start | bytes 442376 | tf_op jit(solution)/shard_map/ppermute | solution.py:19
  174.8 5.0 %collective-permute-start.23 = (f32[288,128]{1,0:T(8,128)S(1)}, f32[288,128]{1,0:T(8,128)S(1)}, u32[]{:S(2)}, u32[]{:S(2)}) collective-permute-start(f32[288,128]{1,0:T(8,128)S(1)} %fusion.9), channel_id=1, source_target_pairs={{0,56},{8,0},{16,8},{24,16},{32,24},{40,32},{48,40},{56,48},{1,57}... | collective-permute-start | bytes 442376 | tf_op jit(solution)/shard_map/ppermute | solution.py:19
  182.0 8.4 %collective-permute-start.36 = (f32[144,128]{1,0:T(8,128)S(1)}, f32[144,128]{1,0:T(8,128)S(1)}, u32[]{:S(2)}, u32[]{:S(2)}) collective-permute-start(f32[144,128]{1,0:T(8,128)S(1)} %fusion.1), channel_id=1, source_target_pairs={{0,1},{1,0},{2,3},{3,2},{4,5},{5,4},{6,7},{7,6},{8,9},{9,8},{10,11... | collective-permute-start | bytes 221192 | tf_op jit(solution)/shard_map/ppermute | solution.py:19
  225.4 5.6 %collective-permute-start.37 = (f32[72,128]{1,0:T(8,128)S(1)}, f32[72,128]{1,0:T(8,128)S(1)}, u32[]{:S(2)}, u32[]{:S(2)}) collective-permute-start(f32[72,128]{1,0:T(8,128)S(1)} %reduce_sum.39), channel_id=1, source_target_pairs={{0,1},{1,0},{2,3},{3,2},{4,5},{5,4},{6,7},{7,6},{8,9},{9,8},{10,11... | collective-permute-start | bytes 110600 | tf_op jit(solution)/shard_map/ppermute | solution.py:19
where the time goes:
time: 248 us
  starting transfers between devices  68.1 us (27%)
  Pallas kernels  64.3 us (26%)
  waiting for transfers between devices  62 us (25%)
  blocking collectives  34.8 us (14%)
  other arithmetic  9.96 us (4%)
  local copies, waits for them, and re-layouts  6.42 us (3%)
    ppermute x30, waiting for transfers between devices, shift(): lax.ppermute(value, axis, [(i, (i + step) % count) for i in range(count)])  56.8 us
    ppermute x30, starting transfers between devices, shift(): lax.ppermute(value, axis, [(i, (i + step) % count) for i in range(count)])  47 us
    all_to_all x3, blocking collectives, spread_sum(): lax.all_to_all(copies, axis, split_axis=0, concat_axis=0, tiled=True)  34.8 us
    pallas_call x2, Pallas kernels, advance(): pl.pallas_call(functools.partial(advance_kernel, adds), in_specs=[whole]...  24.3 us
    pallas_call x1, Pallas kernels, bin_rows(): pl.pallas_call(functools.partial(bin_kernel, size_z, size_x, owned), in_s...  23.7 us
    ppermute x4, starting transfers between devices, edges(): sides.append(lax.ppermute(last, axis, forward))  14.5 us
    pallas_call x2, Pallas kernels, analyse(): pl.pallas_call(analysis_kernel, grid=(rows // size,), in_specs=[whole, wh...  9.98 us
    ppermute x4, starting transfers between devices, edges(): sides.append(lax.ppermute(first, axis, backward))  6.61 us
  transfers between devices with their start and end apart: 38, of which 17 were waited for; matrix products, arithmetic and copies ran while one was open for 3% of the time, Pallas kernels for 5%

commit v1 on v0

--- a/solution.py
+++ b/solution.py
@@ -19,28 +19,38 @@
     return lax.ppermute(value, axis, [(i, (i + step) % count) for i in range(count)])
 
 
-def edges(block):
+def neighbours(first_row, last_row, first_cell, last_cell):
     sides = []
-    for axis, dim in (("lat", 0), (COL, 1)):
+    for axis, ends in (("lat", (last_row, first_row)), (COL, (last_cell, first_cell))):
         names = axis if isinstance(axis, tuple) else (axis,)
         count = math.prod(lax.axis_size(name) for name in names)
         forward = [(i, i + 1) for i in range(count - 1)]
         backward = [(target, source) for source, target in forward]
-        last = lax.slice_in_dim(block, block.shape[dim] - 1, None, axis=dim)
-        first = lax.slice_in_dim(block, 0, 1, axis=dim)
-        sides.append(lax.ppermute(last, axis, forward))
-        sides.append(lax.ppermute(first, axis, backward))
+        sides.append(lax.ppermute(ends[0], axis, forward))
+        sides.append(lax.ppermute(ends[1], axis, backward))
     return sides
 
 
-def advance_kernel(adds, rates, block, above, below, left, right, out, padded, turned):
+def ends_of(block, offset=None):
+    parts = []
+    for dim in (0, 1):
+        for start in (0, block.shape[dim] - 1):
+            part = lax.slice_in_dim(block, start, start + 1, axis=dim)
+            if offset is not None:
+                part = part + lax.slice_in_dim(offset, start, start + 1, axis=dim)[:, :, None]
+            parts.append(part)
+    return parts
+
+
+def advance_kernel(adds, rates, block, out, padded, turned):
     rows, cells, members = block.shape
     groups, lanes = rates.shape[0], rates.shape[1]
     per_group = rows // groups
     for group in range(groups):
         turned[group] = jnp.transpose(rates[group])
-    padded[0, 8 : 8 + cells, :] = above[0]
-    padded[rows + 1, 8 : 8 + cells, :] = below[0]
+    nothing = jnp.zeros((cells, members), jnp.float32)
+    padded[0, 8 : 8 + cells, :] = nothing
+    padded[rows + 1, 8 : 8 + cells, :] = nothing
 
     def rate(i, kind):
         lane = (i % per_group) * (lanes // per_group) + kind
@@ -50,8 +60,8 @@
     def fill(i, carry):
         value = block[i]
         padded[i + 1, 8 : 8 + cells, :] = value + rate(i, 4) if adds else value
-        padded[i + 1, 7:8, :] = left[i]
-        padded[i + 1, 8 + cells : 9 + cells, :] = right[i]
+        padded[i + 1, 0:8, :] = nothing[:8]
+        padded[i + 1, 8 + cells : 16 + cells, :] = nothing[:8]
         return carry
 
     lax.fori_loop(0, rows, fill, 0)
@@ -67,31 +77,62 @@
     lax.fori_loop(0, rows, row, 0)
 
 
-def advance(adds, rates, block, sides):
+def advance(adds, rates, block):
     rows, cells, members = block.shape
     whole = pl.BlockSpec(memory_space=pltpu.VMEM)
     return pl.pallas_call(
         functools.partial(advance_kernel, adds),
-        in_specs=[whole] * 6,
+        in_specs=[whole] * 2,
         out_specs=whole,
         out_shape=pltpu.VMEM(block.shape, jnp.float32),
         scratch_shapes=[
             pltpu.VMEM((rows + 2, cells + 16, members), jnp.float32),
             pltpu.VMEM((rates.shape[0], cells, rates.shape[1]), jnp.float32),
         ],
-        compiler_params=pltpu.CompilerParams(vmem_limit_bytes=24 * 2**20),
+        compiler_params=pltpu.CompilerParams(vmem_limit_bytes=16 * 2**20),
         cost_estimate=pl.CostEstimate(
             flops=12 * block.size, bytes_accessed=8 * block.size, transcendentals=0
         ),
-    )(rates, block, *sides)
-
-
-def bin_kernel(
-    size_z, size_x, owned, place, cell, weight, count, station, *rest
-):
-    states, (out_a, out_b, picked) = rest[:4], rest[4:]
-    width = out_a.shape[3]
-    cut = out_a.shape[2] - owned
+    )(rates, block)
+
+
+def border_kernel(rates, above, below, left, right, block, out, lines):
+    rows, cells, members = block.shape
+    lanes = rates.shape[1]
+    per_row = rates.shape[0] * lanes // rows
+    first = jnp.transpose(rates[0, :per_row, :])
+    last = jnp.transpose(rates[rates.shape[0] - 1, lanes - per_row :, :])
+    out[0] = out[0] + first[:, 1:2] * above[0]
+    out[rows - 1] = out[rows - 1] + last[:, 0:1] * below[0]
+    flat = rates[...].reshape(rows * per_row, cells)
+    lines[0] = jnp.broadcast_to(flat[:, 0:1], (rows * per_row, members))
+    lines[1] = jnp.broadcast_to(flat[:, cells - 1 : cells], (rows * per_row, members))
+    for i in range(rows):
+        west, east = i * per_row + 3, i * per_row + 2
+        out[i, 0:1, :] = out[i, 0:1, :] + lines[0, west : west + 1, :] * left[i]
+        out[i, cells - 1 : cells, :] = (
+            out[i, cells - 1 : cells, :] + lines[1, east : east + 1, :] * right[i]
+        )
+
+
+def with_border(rates, block, sides):
+    whole = pl.BlockSpec(memory_space=pltpu.VMEM)
+    lines = rates.shape[0] * rates.shape[1]
+    return pl.pallas_call(
+        border_kernel,
+        in_specs=[whole] * 6,
+        out_specs=whole,
+        out_shape=pltpu.VMEM(block.shape, jnp.float32),
+        input_output_aliases={5: 0},
+        scratch_shapes=[pltpu.VMEM((2, lines, block.shape[2]), jnp.float32)],
+        compiler_params=pltpu.CompilerParams(vmem_limit_bytes=4 * 2**20),
+        cost_estimate=pl.CostEstimate(flops=10**6, bytes_accessed=2**20, transcendentals=0),
+    )(rates, *sides, block)
+
+
+def bin_kernel(x_major, size_z, size_x, owned, place, cell, weight, count, station, *rest):
+    states, (out, picked) = rest[:2], rest[2:]
+    width = out.shape[3]
     receivers, slots = size_z * size_x, station.shape[1]
     picked[...] = jnp.zeros_like(picked)
     own = lax.broadcasted_iota(jnp.int32, (owned, slots), 0)
@@ -101,61 +142,55 @@
         receiver = ((place[0] + ahead_z) % size_z) * size_x + (place[1] + ahead_x) % size_x
         hots = []
         for e in range(2):
-            first, second = states[2 * e], states[2 * e + 1]
             entry = e * receivers + receiver
 
             def pick(group, inner):
                 for j in range(UNROLL):
                     slot = entry * slots + group * UNROLL + j
-                    row, factor = cell[slot], weight[slot]
                     tile, line = group * (UNROLL // 8) + j // 8, j % 8
-                    picked[e, 0, tile, line : line + 1, :] = first[pl.ds(row, 1), :] * factor
-                    picked[e, 1, tile, line : line + 1, :] = second[pl.ds(row, 1), :] * factor
+                    picked[e, tile, line : line + 1, :] = (
+                        states[e][pl.ds(cell[slot], 1), :] * weight[slot]
+                    )
                 return inner
 
             lax.fori_loop(0, (count[entry] + UNROLL - 1) // UNROLL, pick, 0)
             hit = station[pl.ds(entry, 1), :] == own
             hots.append(jnp.where(hit, 1.0, 0.0).astype(jnp.bfloat16))
-        value = jnp.concatenate(
-            [
-                jnp.concatenate([picked[e, k].reshape(slots, width) for k in range(2)], axis=1)
-                for e in range(2)
-            ],
-            axis=0,
-        )
+        value = picked[...].reshape(2 * slots, width)
         high = value.astype(jnp.bfloat16)
         low = (value - high.astype(jnp.float32)).astype(jnp.bfloat16)
         total = jnp.dot(
-            jnp.concatenate(hots + hots, axis=1),
-            jnp.concatenate([high, low], axis=0),
+            jnp.concatenate(hots, axis=1),
+            jnp.concatenate([high, low], axis=1),
             preferred_element_type=jnp.float32,
         )
-        out_a[ahead_x, ahead_z, :owned, :] = total[:, :width]
-        out_a[ahead_x, ahead_z, owned:, :] = total[:cut, width:]
-        out_b[ahead_z, ahead_x] = total[cut:, width:]
+        total = total[:, :width] + total[:, width:]
+        if x_major:
+            out[ahead_x, ahead_z] = total
+        else:
+            out[ahead_z, ahead_x] = total
         return carry
 
     lax.fori_loop(0, receivers, one, 0)
 
 
-def bin_rows(place, cell, weight, count, station, states, owned):
+def bin_rows(x_major, tables, states, owned):
+    place, cell, weight, count, station = tables
     size_z, size_x = lax.axis_size("z"), lax.axis_size("x")
     members, slots = states[0].shape[1], station.shape[1]
-    rows_a = owned + owned // 8
-    rows_b = 2 * owned - rows_a
     scalar = pl.BlockSpec(memory_space=pltpu.SMEM)
     whole = pl.BlockSpec(memory_space=pltpu.VMEM)
+    sizes = (size_x, size_z) if x_major else (size_z, size_x)
     return pl.pallas_call(
-        functools.partial(bin_kernel, size_z, size_x, owned),
-        in_specs=[scalar] * 4 + [whole] * 5,
-        out_specs=[whole] * 2,
-        out_shape=[
-            pltpu.VMEM((size_x, size_z, rows_a, members), jnp.float32),
-            pltpu.VMEM((size_z, size_x, rows_b, members), jnp.float32),
-        ],
-        scratch_shapes=[pltpu.VMEM((2, 2, slots // 8, 8, members), jnp.float32)],
-        compiler_params=pltpu.CompilerParams(vmem_limit_bytes=48 * 2**20),
-        cost_estimate=pl.CostEstimate(flops=10**9, bytes_accessed=30 * 2**20, transcendentals=0),
+        functools.partial(bin_kernel, x_major, size_z, size_x, owned),
+        in_specs=[scalar] * 4 + [whole] * 3,
+        out_specs=whole,
+        out_shape=pltpu.VMEM(sizes + (owned, members), jnp.float32),
+        scratch_shapes=[pltpu.VMEM((2, slots // 8, 8, members), jnp.float32)],
+        compiler_params=pltpu.CompilerParams(vmem_limit_bytes=8 * 2**20),
+        cost_estimate=pl.CostEstimate(
+            flops=10**9, bytes_accessed=30 * 2**20, transcendentals=0
+        ),
     )(place, cell, weight, count, station, *states)
 
 
@@ -221,6 +256,7 @@
     pushed = jnp.sum(inverse * push, axis=1, keepdims=True)
     offset = jnp.sum(inverse * pushed, axis=0, keepdims=True) * (1.0 / root_scale)
     weights = inverse + offset
+    weights = weights - jnp.mean(weights, axis=1, keepdims=True) + 1.0 / size
     top_half = weights.astype(jnp.bfloat16)
     high[...] = top_half
     low[...] = (weights - top_half.astype(jnp.float32)).astype(jnp.bfloat16)
@@ -237,33 +273,44 @@
     )(products)
 
 
-def analysis_kernel(high, low, state, out):
-    value = state[...]
-    mean = jnp.mean(value, axis=1, keepdims=True)
-    departure = value - mean
-    near = departure.astype(jnp.bfloat16)
-    rest = (departure - near.astype(jnp.float32)).astype(jnp.bfloat16)
-
-    def times(a, b):
-        return lax.dot_general(
-            a, b[...], (((1,), (1,)), ((), ())), preferred_element_type=jnp.float32
-        )
-
-    out[...] = mean + (times(near, high) + (times(rest, high) + times(near, low)))
-
-
-def analyse(high, low, state):
+def analysis_kernel(size, high, low, state, observed, out, out_observed):
+    def update(value):
+        near = value.astype(jnp.bfloat16)
+        rest = (value - near.astype(jnp.float32)).astype(jnp.bfloat16)
+
+        def times(a, b):
+            return lax.dot_general(
+                a, b[...], (((1,), (1,)), ((), ())), preferred_element_type=jnp.float32
+            )
+
+        return times(near, high) + (times(rest, high) + times(near, low))
+
+    step = pl.program_id(0)
+    out[...] = update(state[pl.ds(pl.multiple_of(step * size, size), size), :])
+
+    @pl.when(step == 0)
+    def _():
+        out_observed[...] = update(observed[...])
+
+
+def analyse(high, low, state, observed):
     rows, members = state.shape
-    size = min(rows, 1024)
-    block = pl.BlockSpec((size, members), lambda k: (k, 0))
+    size = rows // 8
     whole = pl.BlockSpec(memory_space=pltpu.VMEM)
     return pl.pallas_call(
-        analysis_kernel,
+        functools.partial(analysis_kernel, size),
         grid=(rows // size,),
-        in_specs=[whole, whole, block],
-        out_specs=block,
-        out_shape=jax.ShapeDtypeStruct(state.shape, jnp.float32),
-    )(high, low, state)
+        in_specs=[whole] * 4,
+        out_specs=[
+            pl.BlockSpec((size, members), lambda k: (k, 0)),
+            pl.BlockSpec(observed.shape, lambda k: (0, 0)),
+        ],
+        out_shape=[
+            jax.ShapeDtypeStruct(state.shape, jnp.float32),
+            jax.ShapeDtypeStruct(observed.shape, jnp.float32),
+        ],
+        compiler_params=pltpu.CompilerParams(vmem_limit_bytes=16 * 2**20),
+    )(high, low, state, observed)
 
 
 def ring_reduce(blocks, axis):
@@ -284,13 +331,23 @@
     return blocks[0] + up + down
 
 
-def reduce_to_owner(block_a, block_b):
-    size_x, size_z = block_a.shape[:2]
-    part_a = ring_reduce([block_a[k] for k in range(size_x)], "x")
-    part_b = ring_reduce([block_b[k] for k in range(size_z)], "z")
-    part_a = ring_reduce([part_a[k] for k in range(size_z)], "z")
-    part_b = ring_reduce([part_b[k] for k in range(size_x)], "x")
-    return jnp.concatenate([part_a, part_b], axis=0)
+def reduce_x_then_z(blocks):
+    part = ring_reduce([blocks[k] for k in range(blocks.shape[0])], "x")
+    return ring_reduce([part[k] for k in range(part.shape[0])], "z")
+
+
+def reduce_z_then_x(blocks):
+    part = ring_reduce([blocks[k] for k in range(blocks.shape[0])], "z")
+    return ring_reduce([part[k] for k in range(part.shape[0])], "x")
+
+
+def member_products(observed, value, error, root_scale):
+    mean = jnp.mean(observed, axis=1)
+    scaled = (observed - mean[:, None]) / (error[:, None] * root_scale)
+    innovation = (value - mean) / error
+    padding = jnp.zeros((scaled.shape[0], 15), jnp.float32)
+    left = jnp.concatenate([scaled, innovation[:, None], padding], axis=1)
+    return jnp.dot(left.T, scaled, precision=exact_mode)
 
 
 def spread_sum(value, axis):
@@ -366,40 +423,42 @@
         ],
         axis=1,
     ).reshape(-1, member_count, control.shape[1])
-    first = advance(True, rates, perturbations, edges(perturbations + control[:, :, None]))
-    second = advance(False, rates, first, edges(first))
-    flat = [state.reshape(-1, member_count) for state in (first, second)]
-    paired = [shift(state, "core", 1) for state in flat]
     index = jnp.concatenate([index_own, index_pair], axis=0)
     weight = jnp.concatenate([weight_own, weight_pair], axis=0)
-    blocks = bin_rows(
+    tables = (
         place,
         index[:, :slots].reshape(-1),
         weight.reshape(-1),
         index[:, 2 * slots],
         index[:, slots : 2 * slots],
-        flat + paired,
-        owned_count,
-    )
-    observed = reduce_to_owner(*blocks).reshape(step_total, owned_count, member_count)
+    )
+    sides = neighbours(*ends_of(perturbations, control))
+    first = advance(True, rates, perturbations)
+    first, tables, sides = lax.optimization_barrier((first, tables, sides))
+    first = with_border(rates, first, sides)
+    flat_first = first.reshape(-1, member_count)
+    pair_first = shift(flat_first, "core", 1)
+    sides = neighbours(*ends_of(first))
+    second = with_border(rates, advance(False, rates, first), sides)
+    flat_second = second.reshape(-1, member_count)
+    pair_second = shift(flat_second, "core", 1)
 
     root_scale = math.sqrt(member_count - 1.0)
-    obs_mean = jnp.mean(observed, axis=2)
-    spread = observed - obs_mean[:, :, None]
-    scaled = (spread / (obs_error[:, :, None] * root_scale)).reshape(-1, member_count)
-    innovation = ((obs_value - obs_mean) / obs_error).reshape(-1)
-    products = jnp.dot(
-        jnp.concatenate(
-            [scaled, innovation[:, None], jnp.zeros((scaled.shape[0], 15), jnp.float32)], axis=1
-        ).T,
-        scaled,
-        precision=exact_mode,
-    )
-    products = sum_everywhere(products)
-    high, low = transposed_weights(products, root_scale)
-    analysis = analyse(high, low, flat[-1])
-    obs_analysis = analyse(high, low, observed.reshape(-1, member_count))
-    return (analysis.reshape(perturbations.shape), obs_analysis.reshape(observed.shape))
+    blocks_first = bin_rows(True, tables, (flat_first, pair_first), owned_count)
+    blocks_second = bin_rows(False, tables, (flat_second, pair_second), owned_count)
+    observed_first = reduce_x_then_z(blocks_first)
+    observed_second = reduce_z_then_x(blocks_second)
+    products = member_products(observed_first, obs_value[0], obs_error[0], root_scale)
+    products = products + member_products(
+        observed_second, obs_value[1], obs_error[1], root_scale
+    )
+    high, low = transposed_weights(sum_everywhere(products), root_scale)
+    observed = jnp.concatenate([observed_first, observed_second], axis=0)
+    analysis, obs_analysis = analyse(high, low, flat_second, observed)
+    return (
+        analysis.reshape(perturbations.shape),
+        obs_analysis.reshape(step_total, owned_count, member_count),
+    )
 
 
 def solution(mesh):

time: 248 us -> 259 us (1.044)
  starting transfers between devices: 68.1 us -> 82.3 us
  blocking collectives: 34.8 us -> 21.1 us
  local copies, waits for them, and re-layouts: 6.42 us -> 13.3 us
    all_to_all x3 -> x2, blocking collectives: 34.8 us -> 21.1 us  [spread_sum(): lax.all_to_all(copies, axis, split_axis=0, concat_axis=0, tiled=True)]
    all_to_all x0 -> x1, waiting for transfers between devices: none -> 9.79 us  [spread_sum(): lax.all_to_all(copies, axis, split_axis=0, concat_axis=0, tiled=True)]
    all_to_all x0 -> x1, starting transfers between devices: none -> 9.05 us  [spread_sum(): lax.all_to_all(copies, axis, split_axis=0, concat_axis=0, tiled=True)]
    pallas_call x3 -> x5, Pallas kernels: 33.7 us -> 41.6 us  [the longest x2 35.5 us: bin_rows(): pl.pallas_call(functools.partial(bin_kernel, x_major, size_z, size_x, own...]
    ppermute x30, starting transfers between devices: 47 us -> 53.6 us  [shift(): lax.ppermute(value, axis, [(i, (i + step) % count) for i in range(count)])]
    ppermute x30, waiting for transfers between devices: 56.8 us -> 50.5 us  [shift(): lax.ppermute(value, axis, [(i, (i + step) % count) for i in range(count)])]
    pallas_call x2, Pallas kernels: 24.3 us -> 18 us  [advance(): pl.pallas_call(functools.partial(advance_kernel, adds), in_specs=[whole]...]
    unnamed x26 -> x17, local copies, waits for them, and re-layouts: 2.91 us -> 6.42 us
  transfers between devices with their start and end apart: 38 -> 39, of which waited for: 17 -> 14; matrix products, arithmetic and copies ran while one was open for 3% -> 4% of each run, Pallas kernels for 5% -> 21%
where the time goes in v1:
time: 259 us
  starting transfers between devices  82.3 us (32%)
  Pallas kernels  66.1 us (26%)
  waiting for transfers between devices  63.3 us (24%)
  blocking collectives  21.1 us (8%)
  local copies, waits for them, and re-layouts  13.3 us (5%)
  other arithmetic  10.5 us (4%)
    ppermute x30, starting transfers between devices, shift(): lax.ppermute(value, axis, [(i, (i + step) % count) for i in range(count)])  53.6 us
    ppermute x30, waiting for transfers between devices, shift(): lax.ppermute(value, axis, [(i, (i + step) % count) for i in range(count)])  50.5 us
    pallas_call x2, Pallas kernels, bin_rows(): pl.pallas_call(functools.partial(bin_kernel, x_major, size_z, size_x, own...  35.5 us
    all_to_all x2, blocking collectives, spread_sum(): lax.all_to_all(copies, axis, split_axis=0, concat_axis=0, tiled=True)  21.1 us
    pallas_call x2, Pallas kernels, advance(): pl.pallas_call(functools.partial(advance_kernel, adds), in_specs=[whole]...  18 us
    ppermute x4, starting transfers between devices, neighbours(): sides.append(lax.ppermute(ends[0], axis, forward))  13.3 us
    all_to_all x1, waiting for transfers between devices, spread_sum(): lax.all_to_all(copies, axis, split_axis=0, concat_axis=0, tiled=True)  9.79 us
    all_to_all x1, starting transfers between devices, spread_sum(): lax.all_to_all(copies, axis, split_axis=0, concat_axis=0, tiled=True)  9.05 us
  transfers between devices with their start and end apart: 39, of which 14 were waited for; matrix products, arithmetic and copies ran while one was open for 4% of the time, Pallas kernels for 21%

profile of v1, /device:TPU:1, one launch (start us, length us, event | category | flops | bytes accessed | tf_op | source)
XLA Modules:
  0.0 259.1 jit_solution(8189947601169718190)
XLA Ops:
  1.1 1.3 reduce.9
  2.6 0.8 copy.58
  3.4 0.8 copy_select_fusion
  4.4 3.3 %collective-permute-start = (s32[32,384]{1,0:T(8,128)S(1)}, s32[32,384]{1,0:T(8,128)S(1)}, u32[]{:S(2)}, u32[]{:S(2)}) collective-permute-start(s32[32,384]{1,0:T(8,128)S(1)} %get-tuple-element.80), channel_id=1, source_target_pairs={{0,1},{1,0},{2,3},{3,2},{4,5},{5,4},{6,7},{7,6},{8,9},{9,8},{10,11... | collective-permute-start | bytes 147464 | tf_op jit(solution)/shard_map/ppermute | solution.py:19
  7.7 0.9 constant_dynamic-slice_fusion.1
  8.7 0.7 fusion.47
  9.4 1.1 slice_add_fusion.4
  10.5 1.5 collective-permute-start.2
  12.0 1.3 collective-permute-start.3
  13.3 0.9 slice_reduce_fusion
  14.2 1.1 slice_add_fusion.6
  15.3 3.8 %collective-permute-start.4 = (f32[32,1,128]{2,1,0:T(1,128)S(1)}, f32[32,1,128]{2,1,0:T(1,128)S(1)}, u32[]{:S(2)}, u32[]{:S(2)}) collective-permute-start(f32[32,1,128]{2,1,0:T(1,128)S(1)} %get-tuple-element.49), channel_id=1, source_target_pairs={{0,1},{1,2},{2,3},{3,4},{4,5},{5,6},{6,7},{7,8},{8,9},{9,10},{10,1... | collective-permute-start | bytes 49160 | tf_op jit(solution)/shard_map/ppermute | solution.py:29
  19.1 0.8 add_bitcast_fusion
  20.1 0.8 copy.55
  21.4 2.2 copy-done.3
  23.5 10.5 %shard_map.122.block = f32[32,256,128]{2,1,0:T(8,128)S(1)} custom-call(f32[2,128,256]{2,1,0:T(8,128)S(1)} %bitcast.152, f32[32,256,128]{2,1,0:T(8,128)S(1)} %copy-done.3), custom_call_target="tpu_custom_call" | custom-call | flops 12582912 | bytes 8388608 | tf_op jit(solution)/shard_map/pallas_call | solution.py:83
  34.1 1.9 collective-permute-start.5
  36.2 3.0 %collective-permute-done.5.right = f32[32,1,128]{2,1,0:T(1,128)S(1)} collective-permute-done((f32[32,1,128]{2,1,0:T(1,128)S(1)}, f32[32,1,128]{2,1,0:T(1,128)S(1)}, u32[]{:S(2)}, u32[]{:S(2)}) %collective-permute-start.5) | collective-permute-done | bytes 16416 | tf_op jit(solution)/shard_map/ppermute | solution.py:30
  39.6 4.3 %collective-permute-start.19 = (f32[1,256,128]{2,1,0:T(8,128)S(1)}, f32[1,256,128]{2,1,0:T(8,128)S(1)}, u32[]{:S(2)}, u32[]{:S(2)}) collective-permute-start(f32[1,256,128]{2,1,0:T(8,128)S(1)} %get-tuple-element.47), channel_id=1, source_target_pairs={{0,64},{64,128},{128,192},{1,65},{65,129},{129,193},{2,66},{66,130... | collective-permute-start | bytes 393224 | tf_op jit(solution)/shard_map/ppermute | solution.py:29
  43.9 1.3 collective-permute-start.20
  45.2 3.8 %collective-permute-start.21 = (f32[32,1,128]{2,1,0:T(1,128)S(1)}, f32[32,1,128]{2,1,0:T(1,128)S(1)}, u32[]{:S(2)}, u32[]{:S(2)}) collective-permute-start(f32[32,1,128]{2,1,0:T(1,128)S(1)} %get-tuple-element.45), channel_id=1, source_target_pairs={{0,1},{1,2},{2,3},{3,4},{4,5},{5,6},{6,7},{7,8},{8,9},{9,10},{10,1... | collective-permute-start | bytes 49160 | tf_op jit(solution)/shard_map/ppermute | solution.py:29
  49.0 1.9 collective-permute-start.22
  51.0 7.5 %shard_map.125.block = f32[32,256,128]{2,1,0:T(8,128)S(1)} custom-call(f32[2,128,256]{2,1,0:T(8,128)S(1)} %bitcast.154, f32[32,256,128]{2,1,0:T(8,128)S(1)} %shard_map.123.block), custom_call_target="tpu_custom_call" | custom-call | flops 12582912 | bytes 8388608 | tf_op jit(solution)/shard_map/pallas_call | solution.py:83
  59.0 17.8 %shard_map.124 = f32[4,8,256,128]{3,2,1,0:T(8,128)S(1)} custom-call(s32[2]{0:T(128)S(1)} %pad_add_fusion.2.place, s32[8192]{0:T(1024)S(1)} %get-tuple-element.17.cell, f32[8192]{0:T(1024)S(1)} %maximum_bitcast_fusion.weight, s32[64]{0:T(128)S(1)} %fusion.32.count, s32[64,128]{1,0:T(8,128)S(1)} %get-tuple-element.20.station, f32[8192,128]{1,0:T(8,128)S(1)} %bitcast.148, ...), custom_call_target="tpu_custom_call" | custom-call | flops 1000000000 | bytes 31457280 | tf_op jit(solution)/shard_map/pallas_call | solution.py:184
  77.2 2.1 collective-permute-start.7
  79.3 3.7 %collective-permute-start.9 = (f32[8,128,128]{2,1,0:T(8,128)S(1)}, f32[8,128,128]{2,1,0:T(8,128)S(1)}, u32[]{:S(2)}, u32[]{:S(2)}) collective-permute-start(f32[8,128,128]{2,1,0:T(8,128)S(1)} %get-tuple-element.63), channel_id=1, source_target_pairs={{0,6},{2,0},{4,2},{6,4},{1,7},{3,1},{5,3},{7,5},{8,14},{10,8},{12,... | collective-permute-start | bytes 1572872 | tf_op jit(solution)/shard_map/ppermute | solution.py:19
  83.0 17.8 %shard_map.127 = f32[8,4,256,128]{3,2,1,0:T(8,128)S(1)} custom-call(s32[2]{0:T(128)S(1)} %pad_add_fusion.2.place, s32[8192]{0:T(1024)S(1)} %get-tuple-element.17.cell, f32[8192]{0:T(1024)S(1)} %maximum_bitcast_fusion.weight, s32[64]{0:T(128)S(1)} %fusion.32.count, s32[64,128]{1,0:T(8,128)S(1)} %get-tuple-element.20.station, f32[8192,128]{1,0:T(8,128)S(1)} %bitcast.150, ...), custom_call_target="tpu_custom_call" | custom-call | flops 1000000000 | bytes 31457280 | tf_op jit(solution)/shard_map/pallas_call | solution.py:184
  100.9 6.6 %collective-permute-start.28 = (f32[4,128,128]{2,1,0:T(8,128)S(1)}, f32[4,128,128]{2,1,0:T(8,128)S(1)}, u32[]{:S(2)}, u32[]{:S(2)}) collective-permute-start(f32[4,128,128]{2,1,0:T(8,128)S(1)} %get-tuple-element.75), channel_id=1, source_target_pairs={{0,56},{8,0},{16,8},{24,16},{32,24},{40,32},{48,40},{56,48},{1,57}... | collective-permute-start | bytes 786440 | tf_op jit(solution)/shard_map/ppermute | solution.py:19
  108.0 2.7 %collective-permute-start.10 = (f32[8,256,128]{2,1,0:T(8,128)S(1)}, f32[8,256,128]{2,1,0:T(8,128)S(1)}, u32[]{:S(2)}, u32[]{:S(2)}) collective-permute-start(f32[8,256,128]{2,1,0:T(8,128)S(1)} %pad_maximum_fusion.1), channel_id=1, source_target_pairs={{0,6},{2,0},{4,2},{6,4},{1,7},{3,1},{5,3},{7,5},{8,14},{10,8},{12,... | collective-permute-start | bytes 3145736 | tf_op jit(solution)/shard_map/ppermute | solution.py:19
  110.7 5.0 %collective-permute-done.24 = f32[4,128,128]{2,1,0:T(8,128)S(1)} collective-permute-done((f32[4,128,128]{2,1,0:T(8,128)S(1)}, f32[4,128,128]{2,1,0:T(8,128)S(1)}, u32[]{:S(2)}, u32[]{:S(2)}) %collective-permute-start.24) | collective-permute-done | bytes 262176 | tf_op jit(solution)/shard_map/ppermute | solution.py:19
  116.0 2.9 %collective-permute-start.29 = (f32[4,256,128]{2,1,0:T(8,128)S(1)}, f32[4,256,128]{2,1,0:T(8,128)S(1)}, u32[]{:S(2)}, u32[]{:S(2)}) collective-permute-start(f32[4,256,128]{2,1,0:T(8,128)S(1)} %pad_maximum_fusion.3), channel_id=1, source_target_pairs={{0,56},{8,0},{16,8},{24,16},{32,24},{40,32},{48,40},{56,48},{1,57}... | collective-permute-start | bytes 1572872 | tf_op jit(solution)/shard_map/ppermute | solution.py:19
  119.0 9.9 %collective-permute-done.25 = f32[4,256,128]{2,1,0:T(8,128)S(1)} collective-permute-done((f32[4,256,128]{2,1,0:T(8,128)S(1)}, f32[4,256,128]{2,1,0:T(8,128)S(1)}, u32[]{:S(2)}, u32[]{:S(2)}) %collective-permute-start.25) | collective-permute-done | bytes 524320 | tf_op jit(solution)/shard_map/ppermute | solution.py:19
  129.0 3.9 %collective-permute-done.8 = f32[8,256,128]{2,1,0:T(8,128)S(1)} collective-permute-done((f32[8,256,128]{2,1,0:T(8,128)S(1)}, f32[8,256,128]{2,1,0:T(8,128)S(1)}, u32[]{:S(2)}, u32[]{:S(2)}) %collective-permute-start.8) | collective-permute-done | bytes 1048608 | tf_op jit(solution)/shard_map/ppermute | solution.py:19
  133.2 2.7 %collective-permute-start.15 = (f32[128,128]{1,0:T(8,128)S(1)}, f32[128,128]{1,0:T(8,128)S(1)}, u32[]{:S(2)}, u32[]{:S(2)}) collective-permute-start(f32[128,128]{1,0:T(8,128)S(1)} %get-tuple-element.57), channel_id=1, source_target_pairs={{0,56},{8,0},{16,8},{24,16},{32,24},{40,32},{48,40},{56,48},{1,57}... | collective-permute-start | bytes 196616 | tf_op jit(solution)/shard_map/ppermute | solution.py:19
  135.8 6.6 %collective-permute-done.11 = f32[128,128]{1,0:T(8,128)S(1)} collective-permute-done((f32[128,128]{1,0:T(8,128)S(1)}, f32[128,128]{1,0:T(8,128)S(1)}, u32[]{:S(2)}, u32[]{:S(2)}) %collective-permute-start.11) | collective-permute-done | bytes 65568 | tf_op jit(solution)/shard_map/ppermute | solution.py:19
  142.7 2.7 %collective-permute-start.30 = (f32[4,256,128]{2,1,0:T(8,128)S(1)}, f32[4,256,128]{2,1,0:T(8,128)S(1)}, u32[]{:S(2)}, u32[]{:S(2)}) collective-permute-start(f32[4,256,128]{2,1,0:T(8,128)S(1)} %get-tuple-element.40), channel_id=1, source_target_pairs={{0,56},{8,0},{16,8},{24,16},{32,24},{40,32},{48,40},{56,48},{1,57}... | collective-permute-start | bytes 1572872 | tf_op jit(solution)/shard_map/ppermute | solution.py:19
  145.6 2.0 collective-permute-done.12
  147.8 7.9 %collective-permute-done.16 = f32[256,128]{1,0:T(8,128)S(1)} collective-permute-done((f32[256,128]{1,0:T(8,128)S(1)}, f32[256,128]{1,0:T(8,128)S(1)}, u32[]{:S(2)}, u32[]{:S(2)}) %collective-permute-start.16) | collective-permute-done | bytes 131104 | tf_op jit(solution)/shard_map/ppermute | solution.py:19
  155.7 0.7 fusion.22
  156.3 3.4 %collective-permute-start.17 = (f32[256,128]{1,0:T(8,128)S(1)}, f32[256,128]{1,0:T(8,128)S(1)}, u32[]{:S(2)}, u32[]{:S(2)}) collective-permute-start(f32[256,128]{1,0:T(8,128)S(1)} %get-tuple-element.53), channel_id=1, source_target_pairs={{0,56},{8,0},{16,8},{24,16},{32,24},{40,32},{48,40},{56,48},{1,57}... | collective-permute-start | bytes 393224 | tf_op jit(solution)/shard_map/ppermute | solution.py:19
  159.8 2.7 %collective-permute-start.31 = (f32[4,256,128]{2,1,0:T(8,128)S(1)}, f32[4,256,128]{2,1,0:T(8,128)S(1)}, u32[]{:S(2)}, u32[]{:S(2)}) collective-permute-start(f32[4,256,128]{2,1,0:T(8,128)S(1)} %fusion.3), channel_id=1, source_target_pairs={{0,56},{8,0},{16,8},{24,16},{32,24},{40,32},{48,40},{56,48},{1,57}... | collective-permute-start | bytes 1572872 | tf_op jit(solution)/shard_map/ppermute | solution.py:19
  162.6 2.3 collective-permute-start.18
  165.3 1.5 collective-permute-done.14
  166.8 7.4 %collective-permute-done.18 = f32[256,128]{1,0:T(8,128)} collective-permute-done((f32[256,128]{1,0:T(8,128)S(1)}, f32[256,128]{1,0:T(8,128)}, u32[]{:S(2)}, u32[]{:S(2)}) %collective-permute-start.18) | collective-permute-done | bytes 131104 | tf_op jit(solution)/shard_map/ppermute | solution.py:19
  174.1 1.1 fusion.37
  175.2 1.1 fusion.7
  176.5 2.7 %collective-permute-start.34 = (f32[128,128]{1,0:T(8,128)S(1)}, f32[128,128]{1,0:T(8,128)S(1)}, u32[]{:S(2)}, u32[]{:S(2)}) collective-permute-start(f32[128,128]{1,0:T(8,128)S(1)} %get-tuple-element.69), channel_id=1, source_target_pairs={{0,6},{2,0},{4,2},{6,4},{1,7},{3,1},{5,3},{7,5},{8,14},{10,8},{12,... | collective-permute-start | bytes 196616 | tf_op jit(solution)/shard_map/ppermute | solution.py:19
  179.1 1.6 collective-permute-done.32
  181.1 2.8 %collective-permute-start.35 = (f32[256,128]{1,0:T(8,128)S(1)}, f32[256,128]{1,0:T(8,128)S(1)}, u32[]{:S(2)}, u32[]{:S(2)}) collective-permute-start(f32[256,128]{1,0:T(8,128)S(1)} %pad_maximum_fusion.8), channel_id=1, source_target_pairs={{0,6},{2,0},{4,2},{6,4},{1,7},{3,1},{5,3},{7,5},{8,14},{10,8},{12,... | collective-permute-start | bytes 393224 | tf_op jit(solution)/shard_map/ppermute | solution.py:19
  184.0 3.0 %collective-permute-done.33 = f32[256,128]{1,0:T(8,128)S(1)} collective-permute-done((f32[256,128]{1,0:T(8,128)S(1)}, f32[256,128]{1,0:T(8,128)S(1)}, u32[]{:S(2)}, u32[]{:S(2)}) %collective-permute-start.33) | collective-permute-done | bytes 131104 | tf_op jit(solution)/shard_map/ppermute | solution.py:19
  188.8 7.0 %collective-permute-start.36 = (f32[144,128]{1,0:T(8,128)S(1)}, f32[144,128]{1,0:T(8,128)S(1)}, u32[]{:S(2)}, u32[]{:S(2)}) collective-permute-start(f32[144,128]{1,0:T(8,128)S(1)} %convolution_add_fusion), channel_id=1, source_target_pairs={{0,1},{1,0},{2,3},{3,2},{4,5},{5,4},{6,7},{7,6},{8,9},{9,8},{10,11... | collective-permute-start | bytes 221192 | tf_op jit(solution)/shard_map/ppermute | solution.py:19
  195.8 0.9 collective-permute-done.36
  196.7 9.2 %all_to_all.15 = f32[4,72,128]{2,1,0:T(8,128)S(1)} all-to-all(f32[4,72,128]{2,1,0:T(8,128)S(1)} %broadcast_in_dim.11), channel_id=1, replica_groups=mesh['lat'=4,'z'=8,'x'=4,'core'=2] {'x'}, dimensions={0} | all-to-all | bytes 294912 | tf_op jit(solution)/shard_map/all_to_all | solution.py:356
  206.0 11.9 %all_to_all.16 = f32[4,72,128]{2,1,0:T(8,128)S(1)} all-to-all(f32[4,72,128]{2,1,0:T(8,128)S(1)} %broadcast_in_dim.12), channel_id=1, replica_groups=mesh['lat'=4,'z'=8,'x'=4,'core'=2] {'lat'}, dimensions={0} | all-to-all | bytes 294912 | tf_op jit(solution)/shard_map/all_to_all | solution.py:356
  217.9 0.7 broadcast_in_dim.13
  218.6 9.1 %all-to-all-start.2 = ((f32[8,72,128]{2,1,0:T(8,128)}), f32[8,72,128]{2,1,0:T(8,128)S(1)}, u32[]{:S(2)}, u32[]{:S(2)}) async-start(f32[8,72,128]{2,1,0:T(8,128)} %broadcast_in_dim.13), calls=%async_computation.2 | async-start | bytes 589824 | tf_op jit(solution)/shard_map/all_to_all | solution.py:356
  227.7 9.8 %all-to-all-done.2 = f32[8,72,128]{2,1,0:T(8,128)S(1)} async-done(((f32[8,72,128]{2,1,0:T(8,128)}), f32[8,72,128]{2,1,0:T(8,128)S(1)}, u32[]{:S(2)}, u32[]{:S(2)}) %all-to-all-start.2) | async-done | bytes 294944 | tf_op jit(solution)/shard_map/all_to_all | solution.py:356
  237.5 4.6 %collective-permute-start.37 = (f32[72,128]{1,0:T(8,128)S(1)}, f32[72,128]{1,0:T(8,128)S(1)}, u32[]{:S(2)}, u32[]{:S(2)}) collective-permute-start(f32[72,128]{1,0:T(8,128)S(1)} %reduce_sum.49), channel_id=1, source_target_pairs={{0,1},{1,0},{2,3},{3,2},{4,5},{5,4},{6,7},{7,6},{8,9},{9,8},{10,11... | collective-permute-start | bytes 110600 | tf_op jit(solution)/shard_map/ppermute | solution.py:19
  242.1 0.8 collective-permute-done.37
  243.6 6.4 %shard_map.128 = (bf16[128,128]{1,0:T(8,128)(2,1)}, bf16[128,128]{1,0:T(8,128)(2,1)}) custom-call(f32[144,128]{1,0:T(8,128)} %maximum_select_fusion.products), custom_call_target="tpu_custom_call" | custom-call | tf_op jit(solution)/shard_map/pallas_call | solution.py:268
  250.0 2.2 copy-done.1
  252.2 0.8 copy-done.4
  253.0 0.8 copy-done.5
  253.7 5.4 %shard_map.129 = (f32[8192,128]{1,0:T(8,128)}, f32[512,128]{1,0:T(8,128)}) custom-call(bf16[128,128]{1,0:T(8,128)(2,1)S(1)} %copy-done.4, bf16[128,128]{1,0:T(8,128)(2,1)S(1)} %copy-done.5, f32[8192,128]{1,0:T(8,128)S(1)} %bitcast.151, f32[512,128]{1,0:T(8,128)S(1)} %pad_maximum_fusion.4.observed), custom_call_target="tpu_custom_call" | custom-call | tf_op jit(solution)/shard_map/pallas_call | solution.py:300
  (124 shorter events, 8.3 us)
Async XLA Ops:
  4.4 31.7 %collective-permute-start = (s32[32,384]{1,0:T(8,128)S(1)}, s32[32,384]{1,0:T(8,128)S(1)}, u32[]{:S(2)}, u32[]{:S(2)}) collective-permute-start(s32[32,384]{1,0:T(8,128)S(1)} %get-tuple-element.80), channel_id=1, source_target_pairs={{0,1},{1,0},{2,3},{3,2},{4,5},{5,4},{6,7},{7,6},{8,9},{9,8},{10,11... | collective-permute-start | bytes 147464 | tf_op jit(solution)/shard_map/ppermute | solution.py:19
  8.6 25.5 %collective-permute-start.1 = (f32[32,128]{1,0:T(8,128)S(1)}, f32[32,128]{1,0:T(8,128)S(1)}, u32[]{:S(2)}, u32[]{:S(2)}) collective-permute-start(f32[32,128]{1,0:T(8,128)S(1)} %bitcast.161), channel_id=1, source_target_pairs={{0,1},{1,0},{2,3},{3,2},{4,5},{5,4},{6,7},{7,6},{8,9},{9,8},{10,11... | collective-permute-start | bytes 49160 | tf_op jit(solution)/shard_map/ppermute | solution.py:19
  10.5 28.6 %collective-permute-start.2 = (f32[1,256,128]{2,1,0:T(8,128)S(1)}, f32[1,256,128]{2,1,0:T(8,128)S(1)}, u32[]{:S(2)}, u32[]{:S(2)}) collective-permute-start(f32[1,256,128]{2,1,0:T(8,128)S(1)} %get-tuple-element.51), channel_id=1, source_target_pairs={{0,64},{64,128},{128,192},{1,65},{65,129},{129,193},{2,66},{66,130... | collective-permute-start | bytes 393224 | tf_op jit(solution)/shard_map/ppermute | solution.py:29
  12.0 27.2 %collective-permute-start.3 = (f32[1,256,128]{2,1,0:T(8,128)S(1)}, f32[1,256,128]{2,1,0:T(8,128)S(1)}, u32[]{:S(2)}, u32[]{:S(2)}) collective-permute-start(f32[1,256,128]{2,1,0:T(8,128)S(1)} %get-tuple-element.50), channel_id=1, source_target_pairs={{64,0},{128,64},{192,128},{65,1},{129,65},{193,129},{66,2},{130,66... | collective-permute-start | bytes 393224 | tf_op jit(solution)/shard_map/ppermute | solution.py:30
  15.3 20.8 %collective-permute-start.4 = (f32[32,1,128]{2,1,0:T(1,128)S(1)}, f32[32,1,128]{2,1,0:T(1,128)S(1)}, u32[]{:S(2)}, u32[]{:S(2)}) collective-permute-start(f32[32,1,128]{2,1,0:T(1,128)S(1)} %get-tuple-element.49), channel_id=1, source_target_pairs={{0,1},{1,2},{2,3},{3,4},{4,5},{5,6},{6,7},{7,8},{8,9},{9,10},{10,1... | collective-permute-start | bytes 49160 | tf_op jit(solution)/shard_map/ppermute | solution.py:29
  21.3 2.2 copy-start.3
  34.1 5.1 %collective-permute-start.5 = (f32[32,1,128]{2,1,0:T(1,128)S(1)}, f32[32,1,128]{2,1,0:T(1,128)S(1)}, u32[]{:S(2)}, u32[]{:S(2)}) collective-permute-start(f32[32,1,128]{2,1,0:T(1,128)S(1)} %get-tuple-element.48), channel_id=1, source_target_pairs={{1,0},{2,1},{3,2},{4,3},{5,4},{6,5},{7,6},{8,7},{9,8},{10,9},{11,1... | collective-permute-start | bytes 49160 | tf_op jit(solution)/shard_map/ppermute | solution.py:30
  39.5 19.5 %collective-permute-start.6 = (f32[8192,128]{1,0:T(8,128)S(1)}, f32[8192,128]{1,0:T(8,128)S(1)}, u32[]{:S(2)}, u32[]{:S(2)}) collective-permute-start(f32[8192,128]{1,0:T(8,128)S(1)} %bitcast.147), channel_id=1, source_target_pairs={{0,1},{1,0},{2,3},{3,2},{4,5},{5,4},{6,7},{7,6},{8,9},{9,8},{10,11... | collective-permute-start | bytes 12582920 | tf_op jit(solution)/shard_map/ppermute | solution.py:19
  39.6 18.9 %collective-permute-start.19 = (f32[1,256,128]{2,1,0:T(8,128)S(1)}, f32[1,256,128]{2,1,0:T(8,128)S(1)}, u32[]{:S(2)}, u32[]{:S(2)}) collective-permute-start(f32[1,256,128]{2,1,0:T(8,128)S(1)} %get-tuple-element.47), channel_id=1, source_target_pairs={{0,64},{64,128},{128,192},{1,65},{65,129},{129,193},{2,66},{66,130... | collective-permute-start | bytes 393224 | tf_op jit(solution)/shard_map/ppermute | solution.py:29
  43.9 14.6 %collective-permute-start.20 = (f32[1,256,128]{2,1,0:T(8,128)S(1)}, f32[1,256,128]{2,1,0:T(8,128)S(1)}, u32[]{:S(2)}, u32[]{:S(2)}) collective-permute-start(f32[1,256,128]{2,1,0:T(8,128)S(1)} %get-tuple-element.46), channel_id=1, source_target_pairs={{64,0},{128,64},{192,128},{65,1},{129,65},{193,129},{66,2},{130,66... | collective-permute-start | bytes 393224 | tf_op jit(solution)/shard_map/ppermute | solution.py:30
  45.2 13.2 %collective-permute-start.21 = (f32[32,1,128]{2,1,0:T(1,128)S(1)}, f32[32,1,128]{2,1,0:T(1,128)S(1)}, u32[]{:S(2)}, u32[]{:S(2)}) collective-permute-start(f32[32,1,128]{2,1,0:T(1,128)S(1)} %get-tuple-element.45), channel_id=1, source_target_pairs={{0,1},{1,2},{2,3},{3,4},{4,5},{5,6},{6,7},{7,8},{8,9},{9,10},{10,1... | collective-permute-start | bytes 49160 | tf_op jit(solution)/shard_map/ppermute | solution.py:29
  49.0 9.5 %collective-permute-start.22 = (f32[32,1,128]{2,1,0:T(1,128)S(1)}, f32[32,1,128]{2,1,0:T(1,128)S(1)}, u32[]{:S(2)}, u32[]{:S(2)}) collective-permute-start(f32[32,1,128]{2,1,0:T(1,128)S(1)} %get-tuple-element.44), channel_id=1, source_target_pairs={{1,0},{2,1},{3,2},{4,3},{5,4},{6,5},{7,6},{8,7},{9,8},{10,9},{11,1... | collective-permute-start | bytes 49160 | tf_op jit(solution)/shard_map/ppermute | solution.py:30
  58.9 24.1 %copy-start = (f32[32,256,128]{2,1,0:T(8,128)}, f32[32,256,128]{2,1,0:T(8,128)S(1)}, u32[]{:S(2)}) copy-start(f32[32,256,128]{2,1,0:T(8,128)S(1)} %shard_map.126) | copy-start | bytes 12582916
  58.9 24.1 %collective-permute-start.23 = (f32[8192,128]{1,0:T(8,128)S(1)}, f32[8192,128]{1,0:T(8,128)S(1)}, u32[]{:S(2)}, u32[]{:S(2)}) collective-permute-start(f32[8192,128]{1,0:T(8,128)S(1)} %bitcast.149), channel_id=1, source_target_pairs={{0,1},{1,0},{2,3},{3,2},{4,5},{5,4},{6,7},{7,6},{8,9},{9,8},{10,11... | collective-permute-start | bytes 12582920 | tf_op jit(solution)/shard_map/ppermute | solution.py:19
  77.2 30.3 %collective-permute-start.7 = (f32[8,128,128]{2,1,0:T(8,128)S(1)}, f32[8,128,128]{2,1,0:T(8,128)S(1)}, u32[]{:S(2)}, u32[]{:S(2)}) collective-permute-start(f32[8,128,128]{2,1,0:T(8,128)S(1)} %get-tuple-element.62), channel_id=1, source_target_pairs={{0,2},{2,4},{4,6},{6,0},{1,3},{3,5},{5,7},{7,1},{8,10},{10,12},{12... | collective-permute-start | bytes 1572872 | tf_op jit(solution)/shard_map/ppermute | solution.py:19
  79.3 28.5 %collective-permute-start.9 = (f32[8,128,128]{2,1,0:T(8,128)S(1)}, f32[8,128,128]{2,1,0:T(8,128)S(1)}, u32[]{:S(2)}, u32[]{:S(2)}) collective-permute-start(f32[8,128,128]{2,1,0:T(8,128)S(1)} %get-tuple-element.63), channel_id=1, source_target_pairs={{0,6},{2,0},{4,2},{6,4},{1,7},{3,1},{5,3},{7,5},{8,14},{10,8},{12,... | collective-permute-start | bytes 1572872 | tf_op jit(solution)/shard_map/ppermute | solution.py:19
  100.7 59.0 %copy-start.2 = (f32[8,4,256,128]{3,2,1,0:T(8,128)}, f32[8,4,256,128]{3,2,1,0:T(8,128)S(1)}, u32[]{:S(2)}) copy-start(f32[8,4,256,128]{3,2,1,0:T(8,128)S(1)} %shard_map.127) | copy-start | bytes 12582916
  100.9 15.0 %collective-permute-start.28 = (f32[4,128,128]{2,1,0:T(8,128)S(1)}, f32[4,128,128]{2,1,0:T(8,128)S(1)}, u32[]{:S(2)}, u32[]{:S(2)}) collective-permute-start(f32[4,128,128]{2,1,0:T(8,128)S(1)} %get-tuple-element.75), channel_id=1, source_target_pairs={{0,56},{8,0},{16,8},{24,16},{32,24},{40,32},{48,40},{56,48},{1,57}... | collective-permute-start | bytes 786440 | tf_op jit(solution)/shard_map/ppermute | solution.py:19
  107.5 8.2 %collective-permute-start.24 = (f32[4,128,128]{2,1,0:T(8,128)S(1)}, f32[4,128,128]{2,1,0:T(8,128)S(1)}, u32[]{:S(2)}, u32[]{:S(2)}) collective-permute-start(f32[4,128,128]{2,1,0:T(8,128)S(1)} %get-tuple-element.74), channel_id=1, source_target_pairs={{0,8},{8,16},{16,24},{24,32},{32,40},{40,48},{48,56},{56,0},{1,9},... | collective-permute-start | bytes 786440 | tf_op jit(solution)/shard_map/ppermute | solution.py:19
  107.7 25.2 %collective-permute-start.8 = (f32[8,256,128]{2,1,0:T(8,128)S(1)}, f32[8,256,128]{2,1,0:T(8,128)S(1)}, u32[]{:S(2)}, u32[]{:S(2)}) collective-permute-start(f32[8,256,128]{2,1,0:T(8,128)S(1)} %pad_maximum_fusion), channel_id=1, source_target_pairs={{0,2},{2,4},{4,6},{6,0},{1,3},{3,5},{5,7},{7,1},{8,10},{10,12},{12... | collective-permute-start | bytes 3145736 | tf_op jit(solution)/shard_map/ppermute | solution.py:19
  108.0 24.9 %collective-permute-start.10 = (f32[8,256,128]{2,1,0:T(8,128)S(1)}, f32[8,256,128]{2,1,0:T(8,128)S(1)}, u32[]{:S(2)}, u32[]{:S(2)}) collective-permute-start(f32[8,256,128]{2,1,0:T(8,128)S(1)} %pad_maximum_fusion.1), channel_id=1, source_target_pairs={{0,6},{2,0},{4,2},{6,4},{1,7},{3,1},{5,3},{7,5},{8,14},{10,8},{12,... | collective-permute-start | bytes 3145736 | tf_op jit(solution)/shard_map/ppermute | solution.py:19
  115.8 13.0 %collective-permute-start.25 = (f32[4,256,128]{2,1,0:T(8,128)S(1)}, f32[4,256,128]{2,1,0:T(8,128)S(1)}, u32[]{:S(2)}, u32[]{:S(2)}) collective-permute-start(f32[4,256,128]{2,1,0:T(8,128)S(1)} %pad_maximum_fusion.2), channel_id=1, source_target_pairs={{0,8},{8,16},{16,24},{24,32},{32,40},{40,48},{48,56},{56,0},{1,9},... | collective-permute-start | bytes 1572872 | tf_op jit(solution)/shard_map/ppermute | solution.py:19
  116.0 26.5 %collective-permute-start.29 = (f32[4,256,128]{2,1,0:T(8,128)S(1)}, f32[4,256,128]{2,1,0:T(8,128)S(1)}, u32[]{:S(2)}, u32[]{:S(2)}) collective-permute-start(f32[4,256,128]{2,1,0:T(8,128)S(1)} %pad_maximum_fusion.3), channel_id=1, source_target_pairs={{0,56},{8,0},{16,8},{24,16},{32,24},{40,32},{48,40},{56,48},{1,57}... | collective-permute-start | bytes 1572872 | tf_op jit(solution)/shard_map/ppermute | solution.py:19
  128.9 13.6 %collective-permute-start.26 = (f32[4,256,128]{2,1,0:T(8,128)S(1)}, f32[4,256,128]{2,1,0:T(8,128)S(1)}, u32[]{:S(2)}, u32[]{:S(2)}) collective-permute-start(f32[4,256,128]{2,1,0:T(8,128)S(1)} %fusion.4), channel_id=1, source_target_pairs={{0,8},{8,16},{16,24},{24,32},{32,40},{40,48},{48,56},{56,0},{1,9},... | collective-permute-start | bytes 1572872 | tf_op jit(solution)/shard_map/ppermute | solution.py:19
  133.0 31.9 %copy-start.6 = (f32[2,256]{1,0:T(2,128)S(1)}, f32[2,256]{1,0:T(2,128)}, u32[]{:S(2)}) copy-start(f32[2,256]{1,0:T(2,128)} %param.21) | copy-start | bytes 6148
  133.1 9.3 %collective-permute-start.11 = (f32[128,128]{1,0:T(8,128)S(1)}, f32[128,128]{1,0:T(8,128)S(1)}, u32[]{:S(2)}, u32[]{:S(2)}) collective-permute-start(f32[128,128]{1,0:T(8,128)S(1)} %get-tuple-element.56), channel_id=1, source_target_pairs={{0,8},{8,16},{16,24},{24,32},{32,40},{40,48},{48,56},{56,0},{1,9},... | collective-permute-start | bytes 196616 | tf_op jit(solution)/shard_map/ppermute | solution.py:19
  133.2 9.3 %collective-permute-start.15 = (f32[128,128]{1,0:T(8,128)S(1)}, f32[128,128]{1,0:T(8,128)S(1)}, u32[]{:S(2)}, u32[]{:S(2)}) collective-permute-start(f32[128,128]{1,0:T(8,128)S(1)} %get-tuple-element.57), channel_id=1, source_target_pairs={{0,56},{8,0},{16,8},{24,16},{32,24},{40,32},{48,40},{56,48},{1,57}... | collective-permute-start | bytes 196616 | tf_op jit(solution)/shard_map/ppermute | solution.py:19
  142.5 5.1 %collective-permute-start.12 = (f32[256,128]{1,0:T(8,128)S(1)}, f32[256,128]{1,0:T(8,128)S(1)}, u32[]{:S(2)}, u32[]{:S(2)}) collective-permute-start(f32[256,128]{1,0:T(8,128)S(1)} %pad_maximum_fusion.5), channel_id=1, source_target_pairs={{0,8},{8,16},{16,24},{24,32},{32,40},{40,48},{48,56},{56,0},{1,9},... | collective-permute-start | bytes 393224 | tf_op jit(solution)/shard_map/ppermute | solution.py:19
  142.7 17.0 %collective-permute-start.30 = (f32[4,256,128]{2,1,0:T(8,128)S(1)}, f32[4,256,128]{2,1,0:T(8,128)S(1)}, u32[]{:S(2)}, u32[]{:S(2)}) collective-permute-start(f32[4,256,128]{2,1,0:T(8,128)S(1)} %get-tuple-element.40), channel_id=1, source_target_pairs={{0,56},{8,0},{16,8},{24,16},{32,24},{40,32},{48,40},{56,48},{1,57}... | collective-permute-start | bytes 1572872 | tf_op jit(solution)/shard_map/ppermute | solution.py:19
  145.5 41.7 %copy-start.7 = (f32[2,256]{1,0:T(2,128)S(1)}, f32[2,256]{1,0:T(2,128)}, u32[]{:S(2)}) copy-start(f32[2,256]{1,0:T(2,128)} %param.20) | copy-start | bytes 6148
  145.5 10.2 %collective-permute-start.16 = (f32[256,128]{1,0:T(8,128)S(1)}, f32[256,128]{1,0:T(8,128)S(1)}, u32[]{:S(2)}, u32[]{:S(2)}) collective-permute-start(f32[256,128]{1,0:T(8,128)S(1)} %pad_maximum_fusion.6), channel_id=1, source_target_pairs={{0,56},{8,0},{16,8},{24,16},{32,24},{40,32},{48,40},{56,48},{1,57}... | collective-permute-start | bytes 393224 | tf_op jit(solution)/shard_map/ppermute | solution.py:19
  147.6 8.1 %collective-permute-start.13 = (f32[256,128]{1,0:T(8,128)S(1)}, f32[256,128]{1,0:T(8,128)S(1)}, u32[]{:S(2)}, u32[]{:S(2)}) collective-permute-start(f32[256,128]{1,0:T(8,128)S(1)} %fusion.21), channel_id=1, source_target_pairs={{0,8},{8,16},{16,24},{24,32},{32,40},{40,48},{48,56},{56,0},{1,9},... | collective-permute-start | bytes 393224 | tf_op jit(solution)/shard_map/ppermute | solution.py:19
  147.7 27.5 %collective-permute-start.27 = (f32[4,256,128]{2,1,0:T(8,128)S(1)}, f32[4,256,128]{2,1,0:T(8,128)S(1)}, u32[]{:S(2)}, u32[]{:S(2)}) collective-permute-start(f32[4,256,128]{2,1,0:T(8,128)S(1)} %get-tuple-element.39), channel_id=1, source_target_pairs={{0,8},{8,16},{16,24},{24,32},{32,40},{40,48},{48,56},{56,0},{1,9},... | collective-permute-start | bytes 1572872 | tf_op jit(solution)/shard_map/ppermute | solution.py:19
  156.3 6.2 %collective-permute-start.17 = (f32[256,128]{1,0:T(8,128)S(1)}, f32[256,128]{1,0:T(8,128)S(1)}, u32[]{:S(2)}, u32[]{:S(2)}) collective-permute-start(f32[256,128]{1,0:T(8,128)S(1)} %get-tuple-element.53), channel_id=1, source_target_pairs={{0,56},{8,0},{16,8},{24,16},{32,24},{40,32},{48,40},{56,48},{1,57}... | collective-permute-start | bytes 393224 | tf_op jit(solution)/shard_map/ppermute | solution.py:19
  159.8 7.0 %collective-permute-start.14 = (f32[256,128]{1,0:T(8,128)}, f32[256,128]{1,0:T(8,128)}, u32[]{:S(2)}, u32[]{:S(2)}) collective-permute-start(f32[256,128]{1,0:T(8,128)} %get-tuple-element.52), channel_id=1, source_target_pairs={{0,8},{8,16},{16,24},{24,32},{32,40},{40,48},{48,56},{56,0},{1,9},... | collective-permute-start | bytes 393224 | tf_op jit(solution)/shard_map/ppermute | solution.py:19
  159.8 15.4 %collective-permute-start.31 = (f32[4,256,128]{2,1,0:T(8,128)S(1)}, f32[4,256,128]{2,1,0:T(8,128)S(1)}, u32[]{:S(2)}, u32[]{:S(2)}) collective-permute-start(f32[4,256,128]{2,1,0:T(8,128)S(1)} %fusion.3), channel_id=1, source_target_pairs={{0,56},{8,0},{16,8},{24,16},{32,24},{40,32},{48,40},{56,48},{1,57}... | collective-permute-start | bytes 1572872 | tf_op jit(solution)/shard_map/ppermute | solution.py:19
  162.6 11.5 %collective-permute-start.18 = (f32[256,128]{1,0:T(8,128)S(1)}, f32[256,128]{1,0:T(8,128)}, u32[]{:S(2)}, u32[]{:S(2)}) collective-permute-start(f32[256,128]{1,0:T(8,128)S(1)} %fusion.20), channel_id=1, source_target_pairs={{0,56},{8,0},{16,8},{24,16},{32,24},{40,32},{48,40},{56,48},{1,57}... | collective-permute-start | bytes 393224 | tf_op jit(solution)/shard_map/ppermute | solution.py:19
  176.4 4.4 %collective-permute-start.32 = (f32[128,128]{1,0:T(8,128)S(1)}, f32[128,128]{1,0:T(8,128)S(1)}, u32[]{:S(2)}, u32[]{:S(2)}) collective-permute-start(f32[128,128]{1,0:T(8,128)S(1)} %get-tuple-element.68), channel_id=1, source_target_pairs={{0,2},{2,4},{4,6},{6,0},{1,3},{3,5},{5,7},{7,1},{8,10},{10,12},{12... | collective-permute-start | bytes 196616 | tf_op jit(solution)/shard_map/ppermute | solution.py:19
  176.5 4.3 %collective-permute-start.34 = (f32[128,128]{1,0:T(8,128)S(1)}, f32[128,128]{1,0:T(8,128)S(1)}, u32[]{:S(2)}, u32[]{:S(2)}) collective-permute-start(f32[128,128]{1,0:T(8,128)S(1)} %get-tuple-element.69), channel_id=1, source_target_pairs={{0,6},{2,0},{4,2},{6,4},{1,7},{3,1},{5,3},{7,5},{8,14},{10,8},{12,... | collective-permute-start | bytes 196616 | tf_op jit(solution)/shard_map/ppermute | solution.py:19
  180.8 6.2 %collective-permute-start.33 = (f32[256,128]{1,0:T(8,128)S(1)}, f32[256,128]{1,0:T(8,128)S(1)}, u32[]{:S(2)}, u32[]{:S(2)}) collective-permute-start(f32[256,128]{1,0:T(8,128)S(1)} %pad_maximum_fusion.7), channel_id=1, source_target_pairs={{0,2},{2,4},{4,6},{6,0},{1,3},{3,5},{5,7},{7,1},{8,10},{10,12},{12... | collective-permute-start | bytes 393224 | tf_op jit(solution)/shard_map/ppermute | solution.py:19
  181.1 5.9 %collective-permute-start.35 = (f32[256,128]{1,0:T(8,128)S(1)}, f32[256,128]{1,0:T(8,128)S(1)}, u32[]{:S(2)}, u32[]{:S(2)}) collective-permute-start(f32[256,128]{1,0:T(8,128)S(1)} %pad_maximum_fusion.8), channel_id=1, source_target_pairs={{0,6},{2,0},{4,2},{6,4},{1,7},{3,1},{5,3},{7,5},{8,14},{10,8},{12,... | collective-permute-start | bytes 393224 | tf_op jit(solution)/shard_map/ppermute | solution.py:19
  188.8 7.9 %collective-permute-start.36 = (f32[144,128]{1,0:T(8,128)S(1)}, f32[144,128]{1,0:T(8,128)S(1)}, u32[]{:S(2)}, u32[]{:S(2)}) collective-permute-start(f32[144,128]{1,0:T(8,128)S(1)} %convolution_add_fusion), channel_id=1, source_target_pairs={{0,1},{1,0},{2,3},{3,2},{4,5},{5,4},{6,7},{7,6},{8,9},{9,8},{10,11... | collective-permute-start | bytes 221192 | tf_op jit(solution)/shard_map/ppermute | solution.py:19
  218.6 18.8 %all-to-all-start.2 = ((f32[8,72,128]{2,1,0:T(8,128)}), f32[8,72,128]{2,1,0:T(8,128)S(1)}, u32[]{:S(2)}, u32[]{:S(2)}) async-start(f32[8,72,128]{2,1,0:T(8,128)} %broadcast_in_dim.13), calls=%async_computation.2 | async-start | bytes 589824 | tf_op jit(solution)/shard_map/all_to_all | solution.py:356
  237.5 5.5 %collective-permute-start.37 = (f32[72,128]{1,0:T(8,128)S(1)}, f32[72,128]{1,0:T(8,128)S(1)}, u32[]{:S(2)}, u32[]{:S(2)}) collective-permute-start(f32[72,128]{1,0:T(8,128)S(1)} %reduce_sum.49), channel_id=1, source_target_pairs={{0,1},{1,0},{2,3},{3,2},{4,5},{5,4},{6,7},{7,6},{8,9},{9,8},{10,11... | collective-permute-start | bytes 110600 | tf_op jit(solution)/shard_map/ppermute | solution.py:19
  250.0 2.2 copy-start.1
  252.2 0.8 copy-start.4
  253.0 0.8 copy-start.5

commit v2 on v1

v2 whole, which is shorter than its diff:
```python
import functools
import math

import jax
import jax.numpy as jnp
import numpy as np
from jax import lax
from jax.experimental import pallas as pl
from jax.experimental.pallas import tpu as pltpu
from jax.sharding import Mesh
from jax.sharding import PartitionSpec as P

exact_mode = lax.Precision.HIGHEST
COL = ("z", "x", "core")
UNROLL = 16


def shift(value, axis, step):
    count = lax.axis_size(axis)
    return lax.ppermute(value, axis, [(i, (i + step) % count) for i in range(count)])


def swap(value):
    return shift(value, "core", 1)


def onward(value, axis):
    count = lax.axis_size(axis)
    pairs = []
    for i in range(count):
        pairs += [(2 * i, 2 * ((i + 1) % count)), (2 * i + 1, 2 * ((i - 1) % count) + 1)]
    return lax.ppermute(value, (axis, "core"), pairs)


def neighbours(first_row, last_row, first_cell, last_cell):
    sides = []
    for axis, ends in (("lat", (last_row, first_row)), (COL, (last_cell, first_cell))):
        names = axis if isinstance(axis, tuple) else (axis,)
        count = math.prod(lax.axis_size(name) for name in names)
        forward = [(i, i + 1) for i in range(count - 1)]
        backward = [(target, source) for source, target in forward]
        sides.append(lax.ppermute(ends[0], axis, forward))
        sides.append(lax.ppermute(ends[1], axis, backward))
    return sides


def ends_of(block, offset=None):
    parts = []
    for dim in (0, 1):
        for start in (0, block.shape[dim] - 1):
            part = lax.slice_in_dim(block, start, start + 1, axis=dim)
            if offset is not None:
                part = part + lax.slice_in_dim(offset, start, start + 1, axis=dim)[:, :, None]
            parts.append(part)
    return parts


def upwind_rates(zonal, meridional, diffusion):
    return [
        diffusion + jnp.maximum(-zonal, 0.0),
        diffusion + jnp.maximum(zonal, 0.0),
        diffusion + jnp.maximum(-meridional, 0.0),
        diffusion + jnp.maximum(meridional, 0.0),
    ]


def advance_kernel(adds, control, zonal, meridional, diffusion, block, out, padded, turned):
    rows, cells, members = block.shape
    rates = upwind_rates(zonal[...], meridional[...], diffusion[...])
    turned[0] = jnp.transpose(jnp.concatenate(rates, axis=0))
    if adds:
        turned[1] = jnp.transpose(jnp.concatenate([control[...]] * 4, axis=0))
    nothing = jnp.zeros((cells, members), jnp.float32)
    padded[0, 8 : 8 + cells, :] = nothing
    padded[rows + 1, 8 : 8 + cells, :] = nothing

    def rate(i, kind):
        lane = (kind % 4) * rows + i
        index = jnp.full((cells, members), lane, jnp.int32)
        return jnp.take_along_axis(turned[kind // 4], index, axis=1)

    def fill(i, carry):
        value = block[i]
        padded[i + 1, 8 : 8 + cells, :] = value + rate(i, 4) if adds else value
        padded[i + 1, 0:8, :] = nothing[:8]
        padded[i + 1, 8 + cells : 16 + cells, :] = nothing[:8]
        return carry

    lax.fori_loop(0, rows, fill, 0)

    def row(i, carry):
        centre = padded[i + 1, 8 : 8 + cells, :]
        result = centre + rate(i, 0) * (padded[i + 2, 8 : 8 + cells, :] - centre)
        result = result + rate(i, 1) * (padded[i, 8 : 8 + cells, :] - centre)
        result = result + rate(i, 2) * (padded[i + 1, 9 : 9 + cells, :] - centre)
        out[i] = result + rate(i, 3) * (padded[i + 1, 7 : 7 + cells, :] - centre)
        return carry

    lax.fori_loop(0, rows, row, 0)


def advance(adds, fields, block):
    rows, cells, members = block.shape
    whole = pl.BlockSpec(memory_space=pltpu.VMEM)
    return pl.pallas_call(
        functools.partial(advance_kernel, adds),
        in_specs=[whole] * 5,
        out_specs=whole,
        out_shape=pltpu.VMEM(block.shape, jnp.float32),
        scratch_shapes=[
            pltpu.VMEM((rows + 2, cells + 16, members), jnp.float32),
            pltpu.VMEM((2, cells, 4 * rows), jnp.float32),
        ],
        compiler_params=pltpu.CompilerParams(vmem_limit_bytes=16 * 2**20),
        cost_estimate=pl.CostEstimate(
            flops=12 * block.size, bytes_accessed=8 * block.size, transcendentals=0
        ),
    )(*fields, block)


def border_kernel(zonal, meridional, diffusion, above, below, left, right, block, out, lines):
    rows, cells, members = block.shape

    def copy(i, carry):
        out[i] = block[i]
        return carry

    lax.fori_loop(0, rows, copy, 0)
    east, west, north, south = upwind_rates(zonal[...], meridional[...], diffusion[...])
    first = jnp.transpose(west[0:8, :])
    last = jnp.transpose(east[rows - 8 : rows, :])
    out[0] = out[0] + first[:, 0:1] * above[0]
    out[rows - 1] = out[rows - 1] + last[:, 7:8] * below[0]
    lines[0] = jnp.broadcast_to(south[:, 0:1], (rows, members))
    lines[1] = jnp.broadcast_to(north[:, cells - 1 : cells], (rows, members))
    for i in range(rows):
        out[i, 0:1, :] = out[i, 0:1, :] + lines[0, i : i + 1, :] * left[i]
        out[i, cells - 1 : cells, :] = (
            out[i, cells - 1 : cells, :] + lines[1, i : i + 1, :] * right[i]
        )


def with_border(fields, block, sides):
    whole = pl.BlockSpec(memory_space=pltpu.VMEM)
    return pl.pallas_call(
        border_kernel,
        in_specs=[whole] * 8,
        out_specs=whole,
        out_shape=pltpu.VMEM(block.shape, jnp.float32),
        scratch_shapes=[pltpu.VMEM((2, block.shape[0], block.shape[2]), jnp.float32)],
        compiler_params=pltpu.CompilerParams(vmem_limit_bytes=12 * 2**20),
        cost_estimate=pl.CostEstimate(flops=10**6, bytes_accessed=2**20, transcendentals=0),
    )(*fields[1:], *sides, block)


def bin_kernel(owned, receivers, cells, weights, counts, *refs):
    stations, states, (out, picked) = refs[:2], refs[2:4], refs[4:]
    width, slots = out.shape[2], stations[0].shape[1]
    picked[...] = jnp.zeros_like(picked)
    own = lax.broadcasted_iota(jnp.int32, (owned, slots), 0)
    order = lax.broadcasted_iota(jnp.int32, (1, slots), 1)

    def one(step, carry):
        receiver = receivers[step]
        hots = []
        for e in range(2):
            entry = e * stations[e].shape[0] + receiver
            live = counts[entry]

            def pick(group, inner):
                for j in range(UNROLL):
                    slot = entry * slots + group * UNROLL + j
                    tile, line = group * (UNROLL // 8) + j // 8, j % 8
                    picked[e, tile, line : line + 1, :] = (
                        states[e][pl.ds(cells[slot], 1), :] * weights[slot]
                    )
                return inner

            lax.fori_loop(0, (live + UNROLL - 1) // UNROLL, pick, 0)
            station = jnp.where(order < live, stations[e][pl.ds(receiver, 1), :], -1)
            hots.append(jnp.where(station == own, 1.0, 0.0).astype(jnp.bfloat16))
        value = picked[...].reshape(2 * slots, width)
        high = value.astype(jnp.bfloat16)
        low = (value - high.astype(jnp.float32)).astype(jnp.bfloat16)
        total = jnp.dot(
            jnp.concatenate(hots, axis=1),
            jnp.concatenate([high, low], axis=1),
            preferred_element_type=jnp.float32,
        )
        out[step] = total[:, :width] + total[:, width:]
        return carry

    lax.fori_loop(0, out.shape[0], one, 0)


def bin_rows(receivers, tables, states, owned):
    members, slots = states[0].shape[1], tables[-1].shape[1]
    scalar = pl.BlockSpec(memory_space=pltpu.SMEM)
    whole = pl.BlockSpec(memory_space=pltpu.VMEM)
    return pl.pallas_call(
        functools.partial(bin_kernel, owned),
        in_specs=[scalar] * 4 + [whole] * 4,
        out_specs=whole,
        out_shape=pltpu.VMEM((receivers.shape[0], owned, members), jnp.float32),
        scratch_shapes=[pltpu.VMEM((2, slots // 8, 8, members), jnp.float32)],
        compiler_params=pltpu.CompilerParams(vmem_limit_bytes=14 * 2**20),
        cost_estimate=pl.CostEstimate(
            flops=10**9, bytes_accessed=30 * 2**20, transcendentals=0
        ),
    )(receivers, *tables, *states)


def factor_kernel(root_scale, products, high, low):
    size = products.shape[1]
    lane = lax.broadcasted_iota(jnp.int32, (size, size), 1)
    line = lax.broadcasted_iota(jnp.int32, (size, size), 0)
    eye = jnp.where(lane == line, 1.0, 0.0)
    left, right = products[:size, :] + eye, eye
    width = 4
    done_left, done_right = [], []
    for start in range(0, size, width):
        top = start % 8
        columns = [
            jnp.broadcast_to(left[:, start + a : start + a + 1], left.shape) for a in range(width)
        ]
        pivots = [[columns[b][top + a : top + a + 1, :] for b in range(width)] for a in range(width)]
        upper = [[None] * width for _ in range(width)]
        inverse = []
        for a in range(width):
            lower = []
            for k in range(a):
                value = pivots[a][k]
                for m in range(k):
                    value = value - lower[m] * upper[m][k]
                lower.append(value * inverse[k])
            for b in range(a, width):
                value = pivots[a][b]
                for m in range(a):
                    value = value - lower[m] * upper[m][b]
                upper[a][b] = value
            inverse.append(1.0 / upper[a][a])
        below = line[: left.shape[0]]
        multipliers = []
        for a in range(width):
            value = columns[a]
            for m in range(a):
                value = value - multipliers[m] * upper[m][a]
            value = value * inverse[a]
            multipliers.append(jnp.where(below > top + a, value, 0.0))
        rows_left, rows_right = [], []
        for a in range(width):
            row_left = left[top + a : top + a + 1, :]
            row_right = right[top + a : top + a + 1, :]
            for m in range(a):
                scale = multipliers[m][top + a : top + a + 1, :]
                row_left = row_left - scale * rows_left[m]
                row_right = row_right - scale * rows_right[m]
            rows_left.append(row_left)
            rows_right.append(row_right)
        for m in range(width):
            left = left - multipliers[m] * rows_left[m]
            right = right - multipliers[m] * rows_right[m]
        if top + width == 8:
            done_left.append(left[:8])
            done_right.append(right[:8])
            left, right = left[8:], right[8:]
    left = jnp.concatenate(done_left, axis=0)
    right = jnp.concatenate(done_right, axis=0)
    pivot = jnp.sum(jnp.where(lane == line, left, 0.0), axis=1, keepdims=True)
    inverse = right * lax.rsqrt(pivot)
    push = products[size : size + 1, :]
    pushed = jnp.sum(inverse * push, axis=1, keepdims=True)
    offset = jnp.sum(inverse * pushed, axis=0, keepdims=True) * (1.0 / root_scale)
    weights = inverse + offset
    weights = weights - jnp.mean(weights, axis=1, keepdims=True) + 1.0 / size
    top_half = weights.astype(jnp.bfloat16)
    high[...] = top_half
    low[...] = (weights - top_half.astype(jnp.float32)).astype(jnp.bfloat16)


def transposed_weights(products, root_scale):
    size = products.shape[1]
    whole = pl.BlockSpec(memory_space=pltpu.VMEM)
    return pl.pallas_call(
        functools.partial(factor_kernel, root_scale),
        in_specs=[whole],
        out_specs=[whole] * 2,
        out_shape=[pltpu.VMEM((size, size), jnp.bfloat16)] * 2,
    )(products)


def analysis_kernel(high, low, state, observed, out, out_observed):
    def update(value):
        near = value.astype(jnp.bfloat16)
        rest = (value - near.astype(jnp.float32)).astype(jnp.bfloat16)

        def times(a, b):
            return lax.dot_general(
                a, b[...], (((1,), (1,)), ((), ())), preferred_element_type=jnp.float32
            )

        return times(near, high) + (times(rest, high) + times(near, low))

    size = out.shape[0]
    start = pl.multiple_of(pl.program_id(0) * size, size)
    out[...] = update(state[pl.ds(start, size), :])

    @pl.when(pl.program_id(0) == 0)
    def _():
        out_observed[...] = update(observed[...])


def analyse(high, low, state, observed):
    rows, members = state.shape
    size = rows // 8
    whole = pl.BlockSpec(memory_space=pltpu.VMEM)
    block = pl.BlockSpec((size, members), lambda k: (k, 0))
    return pl.pallas_call(
        analysis_kernel,
        grid=(rows // size,),
        in_specs=[whole] * 4,
        out_specs=[block, pl.BlockSpec(observed.shape, lambda k: (0, 0))],
        out_shape=[
            jax.ShapeDtypeStruct(state.shape, jnp.float32),
            jax.ShapeDtypeStruct(observed.shape, jnp.float32),
        ],
        compiler_params=pltpu.CompilerParams(vmem_limit_bytes=16 * 2**20),
    )(high, low, state, observed)


def stage_entries(count):
    entries = [(count // 2, 0)]
    for distance in range(count // 2 - 1, 0, -1):
        entries += [(distance, 0), (distance, 1)]
    return entries + [(0, 0)]


def stage(held, axis):
    count = lax.axis_size(axis)
    moving = onward(held[0], axis)
    for distance in range(count // 2 - 1, 0, -1):
        start = 2 * (count // 2 - 1 - distance) + 1
        pair = held[start : start + 2]
        if distance == count // 2 - 1:
            pair = jnp.stack([pair[0] + moving, pair[1]])
        else:
            pair = pair + moving
        moving = onward(pair, axis)
    return moving[0] + held[-1], moving[1]


def reduce_to_owner(blocks, first_axis, second_axis):
    count = lax.axis_size(second_axis)
    mine, others = stage(blocks.reshape((-1, count) + blocks.shape[1:]), first_axis)
    keep, give = [], []
    for distance, whose in stage_entries(count):
        keep.append((mine, others)[whose][distance])
        give.append((others, mine)[whose][-distance % count])
    held = jnp.stack(keep) + swap(jnp.stack(give))
    mine, others = stage(held, second_axis)
    return mine + swap(others)


def receiver_list(first_axis, second_axis):
    core = lax.axis_index("core")
    direction = 1 - 2 * core
    at = {name: lax.axis_index(name) for name in COL}
    size = {name: lax.axis_size(name) for name in COL}
    entries = stage_entries(size[first_axis])
    count = size[second_axis]
    ahead = np.repeat([entry[0] for entry in entries], count)
    whose = np.repeat([entry[1] for entry in entries], count)
    along = np.tile(np.arange(count), len(entries))
    place = {
        first_axis: (at[first_axis] + direction * ahead) % size[first_axis],
        second_axis: (at[second_axis] + direction * along) % size[second_axis],
    }
    chip = place["z"] * size["x"] + place["x"]
    return (chip * size["core"] + (core + whose) % 2).astype(jnp.int32)


def member_products(observed, value, error, root_scale):
    mean = jnp.mean(observed, axis=1)
    scaled = (observed - mean[:, None]) / (error[:, None] * root_scale)
    innovation = (value - mean) / error
    padding = jnp.zeros((scaled.shape[0], 15), jnp.float32)
    left = jnp.concatenate([scaled, innovation[:, None], padding], axis=1)
    return jnp.dot(left.T, scaled, precision=exact_mode)


def spread_sum(value, axis):
    count = lax.axis_size(axis)
    copies = jnp.broadcast_to(value[None], (count,) + value.shape)
    return jnp.sum(lax.all_to_all(copies, axis, split_axis=0, concat_axis=0, tiled=True), axis=0)


def sum_everywhere(value):
    core = lax.axis_index("core")
    rows = value.shape[0] // 2
    value = value + shift(value, "core", 1)
    part = lax.dynamic_slice_in_dim(value, core * rows, rows, 0)
    for axis in ("x", "lat", "z"):
        part = spread_sum(part, axis)
    other = shift(part, "core", 1)
    return jnp.where(
        core == 0, jnp.concatenate([part, other]), jnp.concatenate([other, part])
    )


def on_device(
    control,
    perturbations,
    zonal_flow,
    meridional_flow,
    diffusivity,
    send_cell,
    send_station,
    send_weight,
    send_count,
    obs_value,
    obs_error,
):
    member_count = perturbations.shape[2]
    step_total, owned_count = obs_value.shape
    fields = (control, zonal_flow, meridional_flow, diffusivity)

    sides = neighbours(*ends_of(perturbations, control))
    tables = [
        jnp.concatenate([table[0, 0], swap(table[0, 0])], axis=0).reshape(-1)
        for table in (send_cell, send_weight, send_count)
    ]
    tables += [send_station[0, 0], swap(send_station[0, 0])]
    first = advance(True, fields, perturbations)
    first, tables, sides = lax.optimization_barrier((first, tables, sides))
    first = with_border(fields, first, sides)
    flat_first = first.reshape(-1, member_count)
    pair_first = swap(flat_first)
    sides = neighbours(*ends_of(first))
    second = with_border(fields, advance(False, fields, first), sides)
    flat_second = second.reshape(-1, member_count)
    pair_second = swap(flat_second)

    root_scale = math.sqrt(member_count - 1.0)
    blocks = bin_rows(receiver_list("x", "z"), tables, (flat_first, pair_first), owned_count)
    observed_first = reduce_to_owner(blocks, "x", "z")
    blocks = bin_rows(receiver_list("z", "x"), tables, (flat_second, pair_second), owned_count)
    observed_second = reduce_to_owner(blocks, "z", "x")
    products = member_products(observed_first, obs_value[0], obs_error[0], root_scale)
    products = products + member_products(
        observed_second, obs_value[1], obs_error[1], root_scale
    )
    high, low = transposed_weights(sum_everywhere(products), root_scale)
    observed = jnp.concatenate([observed_first, observed_second], axis=0)
    analysis, obs_analysis = analyse(high, low, flat_second, observed)
    return (
        analysis.reshape(perturbations.shape),
        obs_analysis.reshape(step_total, owned_count, member_count),
    )


def solution(mesh):
    sizes = (mesh.shape["lat"], mesh.shape["col"] // 8, 4, 2)
    fine = Mesh(mesh.devices.reshape(sizes), ("lat",) + COL)
    grid = P("lat", COL)
    return jax.shard_map(
        on_device,
        mesh=fine,
        in_specs=(
            grid,
            P("lat", COL, None),
            grid,
            grid,
            grid,
            P("lat", COL, None, None),
            P("lat", COL, None, None),
            P("lat", COL, None, None),
            P("lat", COL, None),
            P(None, ("lat",) + COL),
            P(None, ("lat",) + COL),
        ),
        out_specs=(P("lat", COL, None), P(None, ("lat",) + COL, None)),
        check_vma=False,
    )
```

time: 259 us -> 261 us (level)
  Pallas kernels: 66.1 us -> 76.4 us
  other arithmetic: 10.5 us -> 4.96 us
  starting transfers between devices: 82.3 us -> 85.5 us
  blocking collectives: 21.1 us -> 18.2 us
    ppermute x0 -> x12, waiting for transfers between devices: none -> 45.3 us  [onward(): return lax.ppermute(value, (axis, 'core'), pairs)]
    ppermute x30 -> x12, waiting for transfers between devices: 50.5 us -> 6.34 us  [shift(): lax.ppermute(value, axis, [(i, (i + step) % count) for i in range(count)])]
    ppermute x0 -> x12, starting transfers between devices: none -> 32.2 us  [onward(): return lax.ppermute(value, (axis, 'core'), pairs)]
    ppermute x30 -> x12, starting transfers between devices: 53.6 us -> 22.7 us  [shift(): lax.ppermute(value, axis, [(i, (i + step) % count) for i in range(count)])]
    pallas_call x5, Pallas kernels: 41.6 us -> 50.3 us  [the longest x2 37.5 us: bin_rows(): pl.pallas_call(functools.partial(bin_kernel, owned), in_specs=[scalar] *...]
    ppermute x4, waiting for transfers between devices: 2.98 us -> 0.01 us  [neighbours(): sides.append(lax.ppermute(ends[1], axis, backward))]
    ppermute x4, starting transfers between devices: 13.3 us -> 16.2 us  [neighbours(): sides.append(lax.ppermute(ends[0], axis, forward))]
    all_to_all x2, blocking collectives: 21.1 us -> 18.2 us  [spread_sum(): lax.all_to_all(copies, axis, split_axis=0, concat_axis=0, tiled=True)]
  transfers between devices with their start and end apart: 39 -> 33, of which waited for: 14 -> 16; matrix products, arithmetic and copies ran while one was open for 4% -> 3% of each run, Pallas kernels for 21% -> 23%
where the time goes in v2:
time: 261 us; the launch traced here: 260 us
  starting transfers between devices  85.5 us (33%)
  Pallas kernels  76.4 us (29%)
  waiting for transfers between devices  61.4 us (24%)
  blocking collectives  18.2 us (7%)
  local copies, waits for them, and re-layouts  10.9 us (4%)
  other arithmetic  4.96 us (2%)
    ppermute x12, waiting for transfers between devices, onward(): return lax.ppermute(value, (axis, 'core'), pairs)  45.3 us
    pallas_call x2, Pallas kernels, bin_rows(): pl.pallas_call(functools.partial(bin_kernel, owned), in_specs=[scalar] *...  37.5 us
    ppermute x12, starting transfers between devices, onward(): return lax.ppermute(value, (axis, 'core'), pairs)  32.2 us
    ppermute x12, starting transfers between devices, shift(): lax.ppermute(value, axis, [(i, (i + step) % count) for i in range(count)])  22.7 us
    pallas_call x2, Pallas kernels, advance(): pl.pallas_call(functools.partial(advance_kernel, adds), in_specs=[whole]...  20.3 us
    all_to_all x2, blocking collectives, spread_sum(): lax.all_to_all(copies, axis, split_axis=0, concat_axis=0, tiled=True)  18.2 us
    ppermute x4, starting transfers between devices, neighbours(): sides.append(lax.ppermute(ends[0], axis, forward))  16.2 us
    all_to_all x1, waiting for transfers between devices, spread_sum(): lax.all_to_all(copies, axis, split_axis=0, concat_axis=0, tiled=True)  9.79 us
  transfers between devices with their start and end apart: 33, of which 16 were waited for; matrix products, arithmetic and copies ran while one was open for 3% of the time, Pallas kernels for 23%

profile of v2, /device:TPU:1, one launch (start us, length us, event | category | flops | bytes accessed | tf_op | source)
XLA Modules:
  0.0 259.9 jit_solution(8733039214709016223)
XLA Ops:
  0.6 0.7 fusion.51
  1.4 1.1 slice_add_fusion.8
  2.5 4.0 %collective-permute-start.4 = (f32[1,256,128]{2,1,0:T(8,128)S(1)}, f32[1,256,128]{2,1,0:T(8,128)S(1)}, u32[]{:S(2)}, u32[]{:S(2)}) collective-permute-start(f32[1,256,128]{2,1,0:T(8,128)S(1)} %get-tuple-element.49), channel_id=1, source_target_pairs={{0,64},{64,128},{128,192},{1,65},{65,129},{129,193},{2,66},{66,130... | collective-permute-start | bytes 393224 | tf_op jit(solution)/shard_map/ppermute | solution.py:42
  6.5 1.3 collective-permute-start.5
  7.8 0.9 slice_reduce_fusion
  8.7 1.1 slice_add_fusion.10
  9.8 4.0 %collective-permute-start.6 = (f32[32,1,128]{2,1,0:T(1,128)S(1)}, f32[32,1,128]{2,1,0:T(1,128)S(1)}, u32[]{:S(2)}, u32[]{:S(2)}) collective-permute-start(f32[32,1,128]{2,1,0:T(1,128)S(1)} %get-tuple-element.47), channel_id=1, source_target_pairs={{0,1},{1,2},{2,3},{3,4},{4,5},{5,6},{6,7},{7,8},{8,9},{9,10},{10,1... | collective-permute-start | bytes 49160 | tf_op jit(solution)/shard_map/ppermute | solution.py:42
  13.8 1.9 collective-permute-start.7
  15.8 2.2 copy-done
  18.0 0.8 copy-done.1
  18.8 0.8 copy-done.2
  19.5 0.8 copy-done.3
  20.3 0.8 copy-done.5
  21.1 10.6 %shard_map.176.block = f32[32,256,128]{2,1,0:T(8,128)S(1)} custom-call(f32[32,256]{1,0:T(8,128)S(1)} %copy-done.5, f32[32,256]{1,0:T(8,128)S(1)} %copy-done.1, f32[32,256]{1,0:T(8,128)S(1)} %copy-done.2, f32[32,256]{1,0:T(8,128)S(1)} %copy-done.3, f32[32,256,128]{2,1,0:T(8,128)S(1)} %copy-done), custom_call_target="tpu_custom_call" | custom-call | flops 12582912 | bytes 8388608 | tf_op jit(solution)/shard_map/pallas_call | solution.py:105
  31.7 0.6 collective-permute-start
  32.3 0.8 collective-permute-done
  33.5 0.9 collective-permute-done.1
  34.7 0.8 collective-permute-done.3.refs_1_
  35.5 2.6 %shard_map.177.block = f32[32,256,128]{2,1,0:T(8,128)} custom-call(f32[32,256]{1,0:T(8,128)S(1)} %copy-done.1, f32[32,256]{1,0:T(8,128)S(1)} %copy-done.2, f32[32,256]{1,0:T(8,128)S(1)} %copy-done.4, f32[1,256,128]{2,1,0:T(8,128)S(1)} %collective-permute-done.4.above, f32[1,256,128]{2,1,0:T(8,128)S(1)} %collective-permute-done.5.below, ...), custom_call_target="tpu_custom_call" | custom-call | flops 1000000 | bytes 1048576 | tf_op jit(solution)/shard_map/pallas_call | solution.py:145
  38.5 1.0 fusion.49
  39.5 4.3 %collective-permute-start.17 = (f32[1,256,128]{2,1,0:T(8,128)S(1)}, f32[1,256,128]{2,1,0:T(8,128)S(1)}, u32[]{:S(2)}, u32[]{:S(2)}) collective-permute-start(f32[1,256,128]{2,1,0:T(8,128)S(1)} %get-tuple-element.45), channel_id=1, source_target_pairs={{0,64},{64,128},{128,192},{1,65},{65,129},{129,193},{2,66},{66,130... | collective-permute-start | bytes 393224 | tf_op jit(solution)/shard_map/ppermute | solution.py:42
  43.8 1.3 collective-permute-start.18
  45.1 1.0 fusion.48
  46.1 3.9 %collective-permute-start.19 = (f32[32,1,128]{2,1,0:T(1,128)S(1)}, f32[32,1,128]{2,1,0:T(1,128)S(1)}, u32[]{:S(2)}, u32[]{:S(2)}) collective-permute-start(f32[32,1,128]{2,1,0:T(1,128)S(1)} %get-tuple-element.43), channel_id=1, source_target_pairs={{0,1},{1,2},{2,3},{3,4},{4,5},{5,6},{6,7},{7,8},{8,9},{9,10},{10,1... | collective-permute-start | bytes 49160 | tf_op jit(solution)/shard_map/ppermute | solution.py:42
  50.0 1.9 collective-permute-start.20
  52.0 9.7 %shard_map.179.block = f32[32,256,128]{2,1,0:T(8,128)S(1)} custom-call(f32[32,256]{1,0:T(8,128)S(1)} %copy-done.5, f32[32,256]{1,0:T(8,128)S(1)} %copy-done.1, f32[32,256]{1,0:T(8,128)S(1)} %copy-done.2, f32[32,256]{1,0:T(8,128)S(1)} %copy-done.4, f32[32,256,128]{2,1,0:T(8,128)} %shard_map.177.block), custom_call_target="tpu_custom_call" | custom-call | flops 12582912 | bytes 8388608 | tf_op jit(solution)/shard_map/pallas_call | solution.py:105
  61.8 2.6 %shard_map.180 = f32[32,256,128]{2,1,0:T(8,128)} custom-call(f32[32,256]{1,0:T(8,128)S(1)} %copy-done.1, f32[32,256]{1,0:T(8,128)S(1)} %copy-done.2, f32[32,256]{1,0:T(8,128)S(1)} %copy-done.4, f32[1,256,128]{2,1,0:T(8,128)S(1)} %collective-permute-done.17.above, f32[1,256,128]{2,1,0:T(8,128)S(1)} %collective-permute-done.18.below, ...), custom_call_target="tpu_custom_call" | custom-call | flops 1000000 | bytes 1048576 | tf_op jit(solution)/shard_map/pallas_call | solution.py:145
  64.5 18.8 %shard_map.178 = f32[32,256,128]{2,1,0:T(8,128)S(1)} custom-call(s32[32]{0:T(128)S(1)} %fusion.30.receivers, s32[16384]{0:T(1024)S(1)} %add_bitcast_fusion.cells, f32[16384]{0:T(1024)S(1)} %maximum_bitcast_fusion.weights, s32[128]{0:T(128)S(1)} %pad_add_fusion.counts, s32[64,128]{1,0:T(8,128)S(1)} %bitcast.121, ...), custom_call_target="tpu_custom_call" | custom-call | flops 1000000000 | bytes 31457280 | tf_op jit(solution)/shard_map/pallas_call | solution.py:200
  83.3 5.4 %collective-permute-start.9 = (f32[8,256,128]{2,1,0:T(8,128)S(1)}, f32[8,256,128]{2,1,0:T(8,128)S(1)}, u32[]{:S(2)}, u32[]{:S(2)}) collective-permute-start(f32[8,256,128]{2,1,0:T(8,128)S(1)} %slice.363), channel_id=1, source_target_pairs={{0,2},{1,7},{2,4},{3,1},{4,6},{5,3},{6,0},{7,5},{8,10},{9,15},{10,... | collective-permute-start | bytes 3145736 | tf_op jit(solution)/shard_map/ppermute | solution.py:32
  88.8 18.7 %shard_map.181 = f32[32,256,128]{2,1,0:T(8,128)S(1)} custom-call(s32[32]{0:T(128)S(1)} %fusion.32.receivers, s32[16384]{0:T(1024)S(1)} %add_bitcast_fusion.cells, f32[16384]{0:T(1024)S(1)} %maximum_bitcast_fusion.weights, s32[128]{0:T(128)S(1)} %pad_add_fusion.counts, s32[64,128]{1,0:T(8,128)S(1)} %bitcast.122, ...), custom_call_target="tpu_custom_call" | custom-call | flops 1000000000 | bytes 31457280 | tf_op jit(solution)/shard_map/pallas_call | solution.py:200
  107.5 5.5 %collective-permute-start.22 = (f32[4,256,128]{2,1,0:T(8,128)S(1)}, f32[4,256,128]{2,1,0:T(8,128)S(1)}, u32[]{:S(2)}, u32[]{:S(2)}) collective-permute-start(f32[4,256,128]{2,1,0:T(8,128)S(1)} %slice.398), channel_id=1, source_target_pairs={{0,8},{1,57},{8,16},{9,1},{16,24},{17,9},{24,32},{25,17},{32,40},{... | collective-permute-start | bytes 1572872 | tf_op jit(solution)/shard_map/ppermute | solution.py:32
  113.0 6.1 %collective-permute-done.22 = f32[4,256,128]{2,1,0:T(8,128)S(1)} collective-permute-done((f32[4,256,128]{2,1,0:T(8,128)S(1)}, f32[4,256,128]{2,1,0:T(8,128)S(1)}, u32[]{:S(2)}, u32[]{:S(2)}) %collective-permute-start.22) | collective-permute-done | bytes 524320 | tf_op jit(solution)/shard_map/ppermute | solution.py:32
  119.3 3.2 %collective-permute-start.23 = (f32[2,4,256,128]{3,2,1,0:T(8,128)S(1)}, f32[2,4,256,128]{3,2,1,0:T(8,128)S(1)}, u32[]{:S(2)}, u32[]{:S(2)}) collective-permute-start(f32[2,4,256,128]{3,2,1,0:T(8,128)S(1)} %pad_maximum_fusion.1), channel_id=1, source_target_pairs={{0,8},{1,57},{8,16},{9,1},{16,24},{17,9},{24,32},{25,17},{32,40},{... | collective-permute-start | bytes 3145736 | tf_op jit(solution)/shard_map/ppermute | solution.py:32
  123.1 11.1 %collective-permute-done.23 = f32[2,4,256,128]{3,2,1,0:T(8,128)S(1)} collective-permute-done((f32[2,4,256,128]{3,2,1,0:T(8,128)S(1)}, f32[2,4,256,128]{3,2,1,0:T(8,128)S(1)}, u32[]{:S(2)}, u32[]{:S(2)}) %collective-permute-start.23) | collective-permute-done | bytes 1048608 | tf_op jit(solution)/shard_map/ppermute | solution.py:32
  134.4 3.5 %collective-permute-start.24 = (f32[2,4,256,128]{3,2,1,0:T(8,128)S(1)}, f32[2,4,256,128]{3,2,1,0:T(8,128)S(1)}, u32[]{:S(2)}, u32[]{:S(2)}) collective-permute-start(f32[2,4,256,128]{3,2,1,0:T(8,128)S(1)} %add.212), channel_id=1, source_target_pairs={{0,8},{1,57},{8,16},{9,1},{16,24},{17,9},{24,32},{25,17},{32,40},{... | collective-permute-start | bytes 3145736 | tf_op jit(solution)/shard_map/ppermute | solution.py:32
  137.9 11.7 %collective-permute-done.24 = f32[2,4,256,128]{3,2,1,0:T(8,128)S(1)} collective-permute-done((f32[2,4,256,128]{3,2,1,0:T(8,128)S(1)}, f32[2,4,256,128]{3,2,1,0:T(8,128)S(1)}, u32[]{:S(2)}, u32[]{:S(2)}) %collective-permute-start.24) | collective-permute-done | bytes 1048608 | tf_op jit(solution)/shard_map/ppermute | solution.py:32
  149.8 3.2 %collective-permute-start.25 = (f32[2,4,256,128]{3,2,1,0:T(8,128)S(1)}, f32[2,4,256,128]{3,2,1,0:T(8,128)S(1)}, u32[]{:S(2)}, u32[]{:S(2)}) collective-permute-start(f32[2,4,256,128]{3,2,1,0:T(8,128)S(1)} %add.213), channel_id=1, source_target_pairs={{0,8},{1,57},{8,16},{9,1},{16,24},{17,9},{24,32},{25,17},{32,40},{... | collective-permute-start | bytes 3145736 | tf_op jit(solution)/shard_map/ppermute | solution.py:32
  153.8 10.9 %collective-permute-done.25 = f32[2,4,256,128]{3,2,1,0:T(8,128)S(1)} collective-permute-done((f32[2,4,256,128]{3,2,1,0:T(8,128)S(1)}, f32[2,4,256,128]{3,2,1,0:T(8,128)S(1)}, u32[]{:S(2)}, u32[]{:S(2)}) %collective-permute-start.25) | collective-permute-done | bytes 1048608 | tf_op jit(solution)/shard_map/ppermute | solution.py:32
  165.0 4.5 %collective-permute-start.26 = (f32[4,256,128]{2,1,0:T(8,128)S(1)}, f32[4,256,128]{2,1,0:T(8,128)S(1)}, u32[]{:S(2)}, u32[]{:S(2)}) collective-permute-start(f32[4,256,128]{2,1,0:T(8,128)S(1)} %pad_maximum_fusion.2), channel_id=1, source_target_pairs={{0,1},{1,0},{2,3},{3,2},{4,5},{5,4},{6,7},{7,6},{8,9},{9,8},{10,11... | collective-permute-start | bytes 1572872 | tf_op jit(solution)/shard_map/ppermute | solution.py:20
  169.7 1.3 collective-permute-done.26
  171.1 3.0 %collective-permute-start.27 = (f32[256,128]{1,0:T(8,128)S(1)}, f32[256,128]{1,0:T(8,128)S(1)}, u32[]{:S(2)}, u32[]{:S(2)}) collective-permute-start(f32[256,128]{1,0:T(8,128)S(1)} %get-tuple-element.68), channel_id=1, source_target_pairs={{0,2},{1,7},{2,4},{3,1},{4,6},{5,3},{6,0},{7,5},{8,10},{9,15},{10,... | collective-permute-start | bytes 393224 | tf_op jit(solution)/shard_map/ppermute | solution.py:32
  174.2 0.7 collective-permute-start.13
  174.9 1.2 collective-permute-done.27
  176.1 3.2 %collective-permute-start.28 = (f32[2,256,128]{2,1,0:T(8,128)S(1)}, f32[2,256,128]{2,1,0:T(8,128)S(1)}, u32[]{:S(2)}, u32[]{:S(2)}) collective-permute-start(f32[2,256,128]{2,1,0:T(8,128)S(1)} %pad_maximum_fusion.4), channel_id=1, source_target_pairs={{0,2},{1,7},{2,4},{3,1},{4,6},{5,3},{6,0},{7,5},{8,10},{9,15},{10,... | collective-permute-start | bytes 786440 | tf_op jit(solution)/shard_map/ppermute | solution.py:32
  179.5 1.9 collective-permute-start.14
  181.8 0.8 collective-permute-done.28
  182.6 2.9 %collective-permute-start.29 = (f32[256,128]{1,0:T(8,128)S(1)}, f32[256,128]{1,0:T(8,128)S(1)}, u32[]{:S(2)}, u32[]{:S(2)}) collective-permute-start(f32[256,128]{1,0:T(8,128)S(1)} %slice_bitcast_fusion.4), channel_id=1, source_target_pairs={{0,1},{1,0},{2,3},{3,2},{4,5},{5,4},{6,7},{7,6},{8,9},{9,8},{10,11... | collective-permute-start | bytes 393224 | tf_op jit(solution)/shard_map/ppermute | solution.py:20
  185.6 2.4 collective-permute-start.15
  188.1 3.2 %collective-permute-done.15 = f32[2,256,128]{2,1,0:T(8,128)S(1)} collective-permute-done((f32[2,256,128]{2,1,0:T(8,128)S(1)}, f32[2,256,128]{2,1,0:T(8,128)S(1)}, u32[]{:S(2)}, u32[]{:S(2)}) %collective-permute-start.15) | collective-permute-done | bytes 262176 | tf_op jit(solution)/shard_map/ppermute | solution.py:32
  191.3 7.8 %collective-permute-start.16 = (f32[256,128]{1,0:T(8,128)S(1)}, f32[256,128]{1,0:T(8,128)S(1)}, u32[]{:S(2)}, u32[]{:S(2)}) collective-permute-start(f32[256,128]{1,0:T(8,128)S(1)} %slice_bitcast_fusion.11), channel_id=1, source_target_pairs={{0,1},{1,0},{2,3},{3,2},{4,5},{5,4},{6,7},{7,6},{8,9},{9,8},{10,11... | collective-permute-start | bytes 393224 | tf_op jit(solution)/shard_map/ppermute | solution.py:20
  199.3 0.8 collective-permute-done.16
  200.8 0.6 fusion.6
  201.3 0.6 convolution_add_fusion
  202.3 0.9 collective-permute-done.30
  203.3 8.9 %all_to_all.15 = f32[4,72,128]{2,1,0:T(8,128)S(1)} all-to-all(f32[4,72,128]{2,1,0:T(8,128)S(1)} %broadcast_in_dim.6), channel_id=1, replica_groups=mesh['lat'=4,'z'=8,'x'=4,'core'=2] {'x'}, dimensions={0} | all-to-all | bytes 294912 | tf_op jit(solution)/shard_map/all_to_all | solution.py:394
  212.2 9.3 %all_to_all.16 = f32[4,72,128]{2,1,0:T(8,128)S(1)} all-to-all(f32[4,72,128]{2,1,0:T(8,128)S(1)} %broadcast_in_dim.7), channel_id=1, replica_groups=mesh['lat'=4,'z'=8,'x'=4,'core'=2] {'lat'}, dimensions={0} | all-to-all | bytes 294912 | tf_op jit(solution)/shard_map/all_to_all | solution.py:394
  221.5 0.7 broadcast_in_dim.8
  222.3 8.1 %all-to-all-start.2 = ((f32[8,72,128]{2,1,0:T(8,128)}), f32[8,72,128]{2,1,0:T(8,128)S(1)}, u32[]{:S(2)}, u32[]{:S(2)}) async-start(f32[8,72,128]{2,1,0:T(8,128)} %broadcast_in_dim.8), calls=%async_computation.2 | async-start | bytes 589824 | tf_op jit(solution)/shard_map/all_to_all | solution.py:394
  230.3 9.8 %all-to-all-done.2 = f32[8,72,128]{2,1,0:T(8,128)S(1)} async-done(((f32[8,72,128]{2,1,0:T(8,128)}), f32[8,72,128]{2,1,0:T(8,128)S(1)}, u32[]{:S(2)}, u32[]{:S(2)}) %all-to-all-start.2) | async-done | bytes 294944 | tf_op jit(solution)/shard_map/all_to_all | solution.py:394
  240.1 4.8 %collective-permute-start.31 = (f32[72,128]{1,0:T(8,128)S(1)}, f32[72,128]{1,0:T(8,128)S(1)}, u32[]{:S(2)}, u32[]{:S(2)}) collective-permute-start(f32[72,128]{1,0:T(8,128)S(1)} %reduce_sum.49), channel_id=1, source_target_pairs={{0,1},{1,0},{2,3},{3,2},{4,5},{5,4},{6,7},{7,6},{8,9},{9,8},{10,11... | collective-permute-start | bytes 110600 | tf_op jit(solution)/shard_map/ppermute | solution.py:20
  245.0 0.8 collective-permute-done.31
  245.8 0.6 maximum_select_fusion.products
  246.5 5.8 %shard_map.182 = (bf16[128,128]{1,0:T(8,128)(2,1)S(1)}, bf16[128,128]{1,0:T(8,128)(2,1)S(1)}) custom-call(f32[144,128]{1,0:T(8,128)} %maximum_select_fusion.products), custom_call_target="tpu_custom_call" | custom-call | tf_op jit(solution)/shard_map/pallas_call | solution.py:284
  252.3 7.6 %shard_map.183 = (f32[8192,128]{1,0:T(8,128)}, f32[512,128]{1,0:T(8,128)}) custom-call(bf16[128,128]{1,0:T(8,128)(2,1)S(1)} %get-tuple-element.26.high, bf16[128,128]{1,0:T(8,128)(2,1)S(1)} %get-tuple-element.27.low, f32[8192,128]{1,0:T(8,128)} %bitcast.29.refs_2_.state, f32[512,128]{1,0:T(8,128)S(1)} %pad_maximum_fusion.5.observed), custom_call_target="tpu_custom_call" | custom-call | tf_op jit(solution)/shard_map/pallas_call | solution.py:318
  (121 shorter events, 5.8 us)
Async XLA Ops:
  2.5 33.1 %collective-permute-start.4 = (f32[1,256,128]{2,1,0:T(8,128)S(1)}, f32[1,256,128]{2,1,0:T(8,128)S(1)}, u32[]{:S(2)}, u32[]{:S(2)}) collective-permute-start(f32[1,256,128]{2,1,0:T(8,128)S(1)} %get-tuple-element.49), channel_id=1, source_target_pairs={{0,64},{64,128},{128,192},{1,65},{65,129},{129,193},{2,66},{66,130... | collective-permute-start | bytes 393224 | tf_op jit(solution)/shard_map/ppermute | solution.py:42
  6.5 29.0 %collective-permute-start.5 = (f32[1,256,128]{2,1,0:T(8,128)S(1)}, f32[1,256,128]{2,1,0:T(8,128)S(1)}, u32[]{:S(2)}, u32[]{:S(2)}) collective-permute-start(f32[1,256,128]{2,1,0:T(8,128)S(1)} %get-tuple-element.48), channel_id=1, source_target_pairs={{64,0},{128,64},{192,128},{65,1},{129,65},{193,129},{66,2},{130,66... | collective-permute-start | bytes 393224 | tf_op jit(solution)/shard_map/ppermute | solution.py:43
  9.8 24.8 %collective-permute-start.6 = (f32[32,1,128]{2,1,0:T(1,128)S(1)}, f32[32,1,128]{2,1,0:T(1,128)S(1)}, u32[]{:S(2)}, u32[]{:S(2)}) collective-permute-start(f32[32,1,128]{2,1,0:T(1,128)S(1)} %get-tuple-element.47), channel_id=1, source_target_pairs={{0,1},{1,2},{2,3},{3,4},{4,5},{5,6},{6,7},{7,8},{8,9},{9,10},{10,1... | collective-permute-start | bytes 49160 | tf_op jit(solution)/shard_map/ppermute | solution.py:42
  13.8 20.9 %collective-permute-start.7 = (f32[32,1,128]{2,1,0:T(1,128)S(1)}, f32[32,1,128]{2,1,0:T(1,128)S(1)}, u32[]{:S(2)}, u32[]{:S(2)}) collective-permute-start(f32[32,1,128]{2,1,0:T(1,128)S(1)} %get-tuple-element.46), channel_id=1, source_target_pairs={{1,0},{2,1},{3,2},{4,3},{5,4},{6,5},{7,6},{8,7},{9,8},{10,9},{11,1... | collective-permute-start | bytes 49160 | tf_op jit(solution)/shard_map/ppermute | solution.py:43
  15.7 15.9 %collective-permute-start.2 = (s32[64]{0:T(128)}, s32[64]{0:T(128)S(1)}, u32[]{:S(2)}, u32[]{:S(2)}) collective-permute-start(s32[64]{0:T(128)} %bitcast.137), channel_id=1, source_target_pairs={{0,1},{1,0},{2,3},{3,2},{4,5},{5,4},{6,7},{7,6},{8,9},{9,8},{10,11... | collective-permute-start | bytes 776 | tf_op jit(solution)/shard_map/ppermute | solution.py:20
  15.8 2.2 copy-start
  18.0 0.8 copy-start.1
  18.8 0.8 copy-start.2
  19.5 0.8 copy-start.3
  20.3 0.8 copy-start.5
  21.1 10.6 %copy-start.7 = (s32[1,1,64,128]{3,2,1,0:T(8,128)S(1)}, s32[1,1,64,128]{3,2,1,0:T(8,128)}, u32[]{:S(2)}) copy-start(s32[1,1,64,128]{3,2,1,0:T(8,128)} %param.22) | copy-start | bytes 98308
  21.1 11.2 %copy-start.17 = (s32[1,1,64]{2,1,0:T(1,128)S(1)}, s32[1,1,64]{2,1,0:T(1,128)}, u32[]{:S(2)}) copy-start(s32[1,1,64]{2,1,0:T(1,128)} %param.25) | copy-start | bytes 772
  21.1 12.0 %copy-start.8 = (f32[1,1,64,128]{3,2,1,0:T(8,128)S(1)}, f32[1,1,64,128]{3,2,1,0:T(8,128)}, u32[]{:S(2)}) copy-start(f32[1,1,64,128]{3,2,1,0:T(8,128)} %param.24) | copy-start | bytes 98308
  21.1 13.3 %copy-start.6 = (s32[1,1,64,128]{3,2,1,0:T(8,128)S(1)}, s32[1,1,64,128]{3,2,1,0:T(8,128)}, u32[]{:S(2)}) copy-start(s32[1,1,64,128]{3,2,1,0:T(8,128)} %param.23) | copy-start | bytes 98308
  21.1 14.5 %copy-start.4 = (f32[32,256]{1,0:T(8,128)S(1)}, f32[32,256]{1,0:T(8,128)}, u32[]{:S(2)}) copy-start(f32[32,256]{1,0:T(8,128)} %diffusion.7) | copy-start | bytes 98308
  31.7 1.4 collective-permute-start
  33.1 1.2 collective-permute-start.1
  34.3 1.2 collective-permute-start.3
  38.2 26.3 %collective-permute-start.8 = (f32[8192,128]{1,0:T(8,128)}, f32[8192,128]{1,0:T(8,128)}, u32[]{:S(2)}, u32[]{:S(2)}) collective-permute-start(f32[8192,128]{1,0:T(8,128)} %bitcast.8.refs_2_), channel_id=1, source_target_pairs={{0,1},{1,0},{2,3},{3,2},{4,5},{5,4},{6,7},{7,6},{8,9},{9,8},{10,11... | collective-permute-start | bytes 12582920 | tf_op jit(solution)/shard_map/ppermute | solution.py:20
  39.5 22.2 %collective-permute-start.17 = (f32[1,256,128]{2,1,0:T(8,128)S(1)}, f32[1,256,128]{2,1,0:T(8,128)S(1)}, u32[]{:S(2)}, u32[]{:S(2)}) collective-permute-start(f32[1,256,128]{2,1,0:T(8,128)S(1)} %get-tuple-element.45), channel_id=1, source_target_pairs={{0,64},{64,128},{128,192},{1,65},{65,129},{129,193},{2,66},{66,130... | collective-permute-start | bytes 393224 | tf_op jit(solution)/shard_map/ppermute | solution.py:42
  43.8 17.9 %collective-permute-start.18 = (f32[1,256,128]{2,1,0:T(8,128)S(1)}, f32[1,256,128]{2,1,0:T(8,128)S(1)}, u32[]{:S(2)}, u32[]{:S(2)}) collective-permute-start(f32[1,256,128]{2,1,0:T(8,128)S(1)} %get-tuple-element.44), channel_id=1, source_target_pairs={{64,0},{128,64},{192,128},{65,1},{129,65},{193,129},{66,2},{130,66... | collective-permute-start | bytes 393224 | tf_op jit(solution)/shard_map/ppermute | solution.py:43
  46.1 15.6 %collective-permute-start.19 = (f32[32,1,128]{2,1,0:T(1,128)S(1)}, f32[32,1,128]{2,1,0:T(1,128)S(1)}, u32[]{:S(2)}, u32[]{:S(2)}) collective-permute-start(f32[32,1,128]{2,1,0:T(1,128)S(1)} %get-tuple-element.43), channel_id=1, source_target_pairs={{0,1},{1,2},{2,3},{3,4},{4,5},{5,6},{6,7},{7,8},{8,9},{9,10},{10,1... | collective-permute-start | bytes 49160 | tf_op jit(solution)/shard_map/ppermute | solution.py:42
  50.0 11.7 %collective-permute-start.20 = (f32[32,1,128]{2,1,0:T(1,128)S(1)}, f32[32,1,128]{2,1,0:T(1,128)S(1)}, u32[]{:S(2)}, u32[]{:S(2)}) collective-permute-start(f32[32,1,128]{2,1,0:T(1,128)S(1)} %get-tuple-element.42), channel_id=1, source_target_pairs={{1,0},{2,1},{3,2},{4,3},{5,4},{6,5},{7,6},{8,7},{9,8},{10,9},{11,1... | collective-permute-start | bytes 49160 | tf_op jit(solution)/shard_map/ppermute | solution.py:43
  61.7 2.7 %copy-start.14 = (s32[32]{0:T(128)S(1)}, s32[32]{0:T(128)}, u32[]{:S(2)}) copy-start(s32[32]{0:T(128)} %constant.93.clone) | copy-start | bytes 388
  61.7 2.7 %copy-start.15 = (s32[32]{0:T(128)S(1)}, s32[32]{0:T(128)}, u32[]{:S(2)}) copy-start(s32[32]{0:T(128)} %constant.94.clone) | copy-start | bytes 388
  61.7 2.7 %copy-start.16 = (s32[32]{0:T(128)S(1)}, s32[32]{0:T(128)}, u32[]{:S(2)}) copy-start(s32[32]{0:T(128)} %constant.95.clone) | copy-start | bytes 388
  64.4 24.4 %collective-permute-start.21 = (f32[8192,128]{1,0:T(8,128)}, f32[8192,128]{1,0:T(8,128)}, u32[]{:S(2)}, u32[]{:S(2)}) collective-permute-start(f32[8192,128]{1,0:T(8,128)} %bitcast.29.refs_2_.state), channel_id=1, source_target_pairs={{0,1},{1,0},{2,3},{3,2},{4,5},{5,4},{6,7},{7,6},{8,9},{9,8},{10,11... | collective-permute-start | bytes 12582920 | tf_op jit(solution)/shard_map/ppermute | solution.py:20
  64.4 24.3 %copy-start.11 = (s32[32]{0:T(128)S(1)}, s32[32]{0:T(128)}, u32[]{:S(2)}) copy-start(s32[32]{0:T(128)} %constant.96.clone) | copy-start | bytes 388
  64.4 24.3 %copy-start.12 = (s32[32]{0:T(128)S(1)}, s32[32]{0:T(128)}, u32[]{:S(2)}) copy-start(s32[32]{0:T(128)} %constant.97.clone) | copy-start | bytes 388
  64.5 24.3 %copy-start.13 = (s32[32]{0:T(128)S(1)}, s32[32]{0:T(128)}, u32[]{:S(2)}) copy-start(s32[32]{0:T(128)} %constant.98.clone) | copy-start | bytes 388
  83.3 39.2 %collective-permute-start.9 = (f32[8,256,128]{2,1,0:T(8,128)S(1)}, f32[8,256,128]{2,1,0:T(8,128)S(1)}, u32[]{:S(2)}, u32[]{:S(2)}) collective-permute-start(f32[8,256,128]{2,1,0:T(8,128)S(1)} %slice.363), channel_id=1, source_target_pairs={{0,2},{1,7},{2,4},{3,1},{4,6},{5,3},{6,0},{7,5},{8,10},{9,15},{10,... | collective-permute-start | bytes 3145736 | tf_op jit(solution)/shard_map/ppermute | solution.py:32
  107.5 11.6 %collective-permute-start.22 = (f32[4,256,128]{2,1,0:T(8,128)S(1)}, f32[4,256,128]{2,1,0:T(8,128)S(1)}, u32[]{:S(2)}, u32[]{:S(2)}) collective-permute-start(f32[4,256,128]{2,1,0:T(8,128)S(1)} %slice.398), channel_id=1, source_target_pairs={{0,8},{1,57},{8,16},{9,1},{16,24},{17,9},{24,32},{25,17},{32,40},{... | collective-permute-start | bytes 1572872 | tf_op jit(solution)/shard_map/ppermute | solution.py:32
  119.3 14.9 %collective-permute-start.23 = (f32[2,4,256,128]{3,2,1,0:T(8,128)S(1)}, f32[2,4,256,128]{3,2,1,0:T(8,128)S(1)}, u32[]{:S(2)}, u32[]{:S(2)}) collective-permute-start(f32[2,4,256,128]{3,2,1,0:T(8,128)S(1)} %pad_maximum_fusion.1), channel_id=1, source_target_pairs={{0,8},{1,57},{8,16},{9,1},{16,24},{17,9},{24,32},{25,17},{32,40},{... | collective-permute-start | bytes 3145736 | tf_op jit(solution)/shard_map/ppermute | solution.py:32
  122.9 30.2 %collective-permute-start.10 = (f32[2,8,256,128]{3,2,1,0:T(8,128)S(1)}, f32[2,8,256,128]{3,2,1,0:T(8,128)S(1)}, u32[]{:S(2)}, u32[]{:S(2)}) collective-permute-start(f32[2,8,256,128]{3,2,1,0:T(8,128)S(1)} %pad_maximum_fusion), channel_id=1, source_target_pairs={{0,2},{1,7},{2,4},{3,1},{4,6},{5,3},{6,0},{7,5},{8,10},{9,15},{10,... | collective-permute-start | bytes 6291464 | tf_op jit(solution)/shard_map/ppermute | solution.py:32
  134.4 15.2 %collective-permute-start.24 = (f32[2,4,256,128]{3,2,1,0:T(8,128)S(1)}, f32[2,4,256,128]{3,2,1,0:T(8,128)S(1)}, u32[]{:S(2)}, u32[]{:S(2)}) collective-permute-start(f32[2,4,256,128]{3,2,1,0:T(8,128)S(1)} %add.212), channel_id=1, source_target_pairs={{0,8},{1,57},{8,16},{9,1},{16,24},{17,9},{24,32},{25,17},{32,40},{... | collective-permute-start | bytes 3145736 | tf_op jit(solution)/shard_map/ppermute | solution.py:32
  149.8 14.9 %collective-permute-start.25 = (f32[2,4,256,128]{3,2,1,0:T(8,128)S(1)}, f32[2,4,256,128]{3,2,1,0:T(8,128)S(1)}, u32[]{:S(2)}, u32[]{:S(2)}) collective-permute-start(f32[2,4,256,128]{3,2,1,0:T(8,128)S(1)} %add.213), channel_id=1, source_target_pairs={{0,8},{1,57},{8,16},{9,1},{16,24},{17,9},{24,32},{25,17},{32,40},{... | collective-permute-start | bytes 3145736 | tf_op jit(solution)/shard_map/ppermute | solution.py:32
  153.4 16.1 %collective-permute-start.11 = (f32[8,256,128]{2,1,0:T(8,128)S(1)}, f32[8,256,128]{2,1,0:T(8,128)S(1)}, u32[]{:S(2)}, u32[]{:S(2)}) collective-permute-start(f32[8,256,128]{2,1,0:T(8,128)S(1)} %get-tuple-element.50), channel_id=1, source_target_pairs={{0,1},{1,0},{2,3},{3,2},{4,5},{5,4},{6,7},{7,6},{8,9},{9,8},{10,11... | collective-permute-start | bytes 3145736 | tf_op jit(solution)/shard_map/ppermute | solution.py:20
  165.0 6.0 %collective-permute-start.26 = (f32[4,256,128]{2,1,0:T(8,128)S(1)}, f32[4,256,128]{2,1,0:T(8,128)S(1)}, u32[]{:S(2)}, u32[]{:S(2)}) collective-permute-start(f32[4,256,128]{2,1,0:T(8,128)S(1)} %pad_maximum_fusion.2), channel_id=1, source_target_pairs={{0,1},{1,0},{2,3},{3,2},{4,5},{5,4},{6,7},{7,6},{8,9},{9,8},{10,11... | collective-permute-start | bytes 1572872 | tf_op jit(solution)/shard_map/ppermute | solution.py:20
  169.5 12.0 %copy-start.9 = (f32[2,256]{1,0:T(2,128)S(1)}, f32[2,256]{1,0:T(2,128)}, u32[]{:S(2)}) copy-start(f32[2,256]{1,0:T(2,128)} %param.27) | copy-start | bytes 6148
  169.6 30.6 %copy-start.10 = (f32[2,256]{1,0:T(2,128)S(1)}, f32[2,256]{1,0:T(2,128)}, u32[]{:S(2)}) copy-start(f32[2,256]{1,0:T(2,128)} %param.26) | copy-start | bytes 6148
  169.6 4.5 %collective-permute-start.12 = (f32[256,128]{1,0:T(8,128)S(1)}, f32[256,128]{1,0:T(8,128)S(1)}, u32[]{:S(2)}, u32[]{:S(2)}) collective-permute-start(f32[256,128]{1,0:T(8,128)S(1)} %get-tuple-element.56), channel_id=1, source_target_pairs={{0,8},{1,57},{8,16},{9,1},{16,24},{17,9},{24,32},{25,17},{32,40},{... | collective-permute-start | bytes 393224 | tf_op jit(solution)/shard_map/ppermute | solution.py:32
  171.1 5.0 %collective-permute-start.27 = (f32[256,128]{1,0:T(8,128)S(1)}, f32[256,128]{1,0:T(8,128)S(1)}, u32[]{:S(2)}, u32[]{:S(2)}) collective-permute-start(f32[256,128]{1,0:T(8,128)S(1)} %get-tuple-element.68), channel_id=1, source_target_pairs={{0,2},{1,7},{2,4},{3,1},{4,6},{5,3},{6,0},{7,5},{8,10},{9,15},{10,... | collective-permute-start | bytes 393224 | tf_op jit(solution)/shard_map/ppermute | solution.py:32
  174.2 5.3 %collective-permute-start.13 = (f32[2,256,128]{2,1,0:T(8,128)S(1)}, f32[2,256,128]{2,1,0:T(8,128)S(1)}, u32[]{:S(2)}, u32[]{:S(2)}) collective-permute-start(f32[2,256,128]{2,1,0:T(8,128)S(1)} %pad_maximum_fusion.3), channel_id=1, source_target_pairs={{0,8},{1,57},{8,16},{9,1},{16,24},{17,9},{24,32},{25,17},{32,40},{... | collective-permute-start | bytes 786440 | tf_op jit(solution)/shard_map/ppermute | solution.py:32
  176.1 6.5 %collective-permute-start.28 = (f32[2,256,128]{2,1,0:T(8,128)S(1)}, f32[2,256,128]{2,1,0:T(8,128)S(1)}, u32[]{:S(2)}, u32[]{:S(2)}) collective-permute-start(f32[2,256,128]{2,1,0:T(8,128)S(1)} %pad_maximum_fusion.4), channel_id=1, source_target_pairs={{0,2},{1,7},{2,4},{3,1},{4,6},{5,3},{6,0},{7,5},{8,10},{9,15},{10,... | collective-permute-start | bytes 786440 | tf_op jit(solution)/shard_map/ppermute | solution.py:32
  179.5 6.0 %collective-permute-start.14 = (f32[2,256,128]{2,1,0:T(8,128)S(1)}, f32[2,256,128]{2,1,0:T(8,128)S(1)}, u32[]{:S(2)}, u32[]{:S(2)}) collective-permute-start(f32[2,256,128]{2,1,0:T(8,128)S(1)} %slice_add_fusion.4), channel_id=1, source_target_pairs={{0,8},{1,57},{8,16},{9,1},{16,24},{17,9},{24,32},{25,17},{32,40},{... | collective-permute-start | bytes 786440 | tf_op jit(solution)/shard_map/ppermute | solution.py:32
  182.6 5.4 %collective-permute-start.29 = (f32[256,128]{1,0:T(8,128)S(1)}, f32[256,128]{1,0:T(8,128)S(1)}, u32[]{:S(2)}, u32[]{:S(2)}) collective-permute-start(f32[256,128]{1,0:T(8,128)S(1)} %slice_bitcast_fusion.4), channel_id=1, source_target_pairs={{0,1},{1,0},{2,3},{3,2},{4,5},{5,4},{6,7},{7,6},{8,9},{9,8},{10,11... | collective-permute-start | bytes 393224 | tf_op jit(solution)/shard_map/ppermute | solution.py:20
  185.6 5.7 %collective-permute-start.15 = (f32[2,256,128]{2,1,0:T(8,128)S(1)}, f32[2,256,128]{2,1,0:T(8,128)S(1)}, u32[]{:S(2)}, u32[]{:S(2)}) collective-permute-start(f32[2,256,128]{2,1,0:T(8,128)S(1)} %slice_add_fusion.5), channel_id=1, source_target_pairs={{0,8},{1,57},{8,16},{9,1},{16,24},{17,9},{24,32},{25,17},{32,40},{... | collective-permute-start | bytes 786440 | tf_op jit(solution)/shard_map/ppermute | solution.py:32
  191.3 8.8 %collective-permute-start.16 = (f32[256,128]{1,0:T(8,128)S(1)}, f32[256,128]{1,0:T(8,128)S(1)}, u32[]{:S(2)}, u32[]{:S(2)}) collective-permute-start(f32[256,128]{1,0:T(8,128)S(1)} %slice_bitcast_fusion.11), channel_id=1, source_target_pairs={{0,1},{1,0},{2,3},{3,2},{4,5},{5,4},{6,7},{7,6},{8,9},{9,8},{10,11... | collective-permute-start | bytes 393224 | tf_op jit(solution)/shard_map/ppermute | solution.py:20
  201.9 1.3 collective-permute-start.30
  222.3 17.9 %all-to-all-start.2 = ((f32[8,72,128]{2,1,0:T(8,128)}), f32[8,72,128]{2,1,0:T(8,128)S(1)}, u32[]{:S(2)}, u32[]{:S(2)}) async-start(f32[8,72,128]{2,1,0:T(8,128)} %broadcast_in_dim.8), calls=%async_computation.2 | async-start | bytes 589824 | tf_op jit(solution)/shard_map/all_to_all | solution.py:394
  240.1 5.7 %collective-permute-start.31 = (f32[72,128]{1,0:T(8,128)S(1)}, f32[72,128]{1,0:T(8,128)S(1)}, u32[]{:S(2)}, u32[]{:S(2)}) collective-permute-start(f32[72,128]{1,0:T(8,128)S(1)} %reduce_sum.49), channel_id=1, source_target_pairs={{0,1},{1,0},{2,3},{3,2},{4,5},{5,4},{6,7},{7,6},{8,9},{9,8},{10,11... | collective-permute-start | bytes 110600 | tf_op jit(solution)/shard_map/ppermute | solution.py:20

commit v3 on v2

--- a/solution.py
+++ b/solution.py
@@ -337,7 +337,7 @@
 
 def stage(held, axis):
     count = lax.axis_size(axis)
-    moving = onward(held[0], axis)
+    moving = onward((yield held[0]), axis)
     for distance in range(count // 2 - 1, 0, -1):
         start = 2 * (count // 2 - 1 - distance) + 1
         pair = held[start : start + 2]
@@ -345,20 +345,47 @@
             pair = jnp.stack([pair[0] + moving, pair[1]])
         else:
             pair = pair + moving
-        moving = onward(pair, axis)
+        moving = onward((yield pair), axis)
     return moving[0] + held[-1], moving[1]
 
 
 def reduce_to_owner(blocks, first_axis, second_axis):
     count = lax.axis_size(second_axis)
-    mine, others = stage(blocks.reshape((-1, count) + blocks.shape[1:]), first_axis)
+    mine, others = yield from stage(
+        blocks.reshape((-1, count) + blocks.shape[1:]), first_axis
+    )
     keep, give = [], []
     for distance, whose in stage_entries(count):
         keep.append((mine, others)[whose][distance])
         give.append((others, mine)[whose][-distance % count])
-    held = jnp.stack(keep) + swap(jnp.stack(give))
-    mine, others = stage(held, second_axis)
-    return mine + swap(others)
+    held = jnp.stack(keep) + swap((yield jnp.stack(give)))
+    mine, others = yield from stage(held, second_axis)
+    return mine + swap((yield others))
+
+
+def reduce_together(ahead, behind, ties):
+    runs = [ahead, behind]
+    pending, done, results = [next(ahead), next(behind)], [0, 0], [None, None]
+
+    def send(k):
+        try:
+            pending[k] = runs[k].send(pending[k])
+            done[k] += 1
+        except StopIteration as stop:
+            pending[k], results[k] = None, stop.value
+
+    for i, j in ties:
+        while done[0] < i:
+            send(0)
+        while done[1] < j:
+            send(1)
+        pending[0], pending[1] = lax.optimization_barrier((pending[0], pending[1]))
+        send(0)
+        send(1)
+    for k in range(2):
+        while pending[k] is not None:
+            send(k)
+    return results
 
 
 def receiver_list(first_axis, second_axis):
@@ -442,9 +469,12 @@
 
     root_scale = math.sqrt(member_count - 1.0)
     blocks = bin_rows(receiver_list("x", "z"), tables, (flat_first, pair_first), owned_count)
-    observed_first = reduce_to_owner(blocks, "x", "z")
+    first_run = reduce_to_owner(blocks, "x", "z")
     blocks = bin_rows(receiver_list("z", "x"), tables, (flat_second, pair_second), owned_count)
-    observed_second = reduce_to_owner(blocks, "z", "x")
+    second_run = reduce_to_owner(blocks, "z", "x")
+    observed_first, observed_second = reduce_together(
+        first_run, second_run, ((1, 0), (3, 2), (4, 3), (6, 5), (7, 6))
+    )
     products = member_products(observed_first, obs_value[0], obs_error[0], root_scale)
     products = products + member_products(
         observed_second, obs_value[1], obs_error[1], root_scale

time: 261 us -> 262 us (level)
  waiting for transfers between devices: 61.4 us -> 70.7 us
  starting transfers between devices: 85.5 us -> 77.7 us
    ppermute x12, waiting for transfers between devices: 45.3 us -> 52.9 us  [onward(): return lax.ppermute(value, (axis, 'core'), pairs)]
    ppermute x12, starting transfers between devices: 22.7 us -> 17.1 us  [shift(): lax.ppermute(value, axis, [(i, (i + step) % count) for i in range(count)])]
    ppermute x4, waiting for transfers between devices: 0.01 us -> 3.1 us  [neighbours(): sides.append(lax.ppermute(ends[1], axis, backward))]
    ppermute x4, starting transfers between devices: 16.2 us -> 13.2 us  [neighbours(): sides.append(lax.ppermute(ends[0], axis, forward))]
  transfers between devices with their start and end apart: 33 -> 33, of which waited for: 16 -> 13; matrix products, arithmetic and copies ran while one was open for 3% -> 3% of each run, Pallas kernels for 23% -> 23%
where the time goes in v3:
time: 262 us; the launch traced here: 261 us
  starting transfers between devices  77.7 us (30%)
  Pallas kernels  76.2 us (29%)
  waiting for transfers between devices  70.7 us (27%)
  blocking collectives  17.5 us (7%)
  local copies, waits for them, and re-layouts  10.9 us (4%)
  other arithmetic  4.98 us (2%)
    ppermute x12, waiting for transfers between devices, onward(): return lax.ppermute(value, (axis, 'core'), pairs)  52.9 us
    pallas_call x2, Pallas kernels, bin_rows(): pl.pallas_call(functools.partial(bin_kernel, owned), in_specs=[scalar] *...  37.3 us
    ppermute x12, starting transfers between devices, onward(): return lax.ppermute(value, (axis, 'core'), pairs)  32 us
    pallas_call x2, Pallas kernels, advance(): pl.pallas_call(functools.partial(advance_kernel, adds), in_specs=[whole]...  20.3 us
    all_to_all x2, blocking collectives, spread_sum(): lax.all_to_all(copies, axis, split_axis=0, concat_axis=0, tiled=True)  17.5 us
    ppermute x12, starting transfers between devices, shift(): lax.ppermute(value, axis, [(i, (i + step) % count) for i in range(count)])  17.1 us
    ppermute x4, starting transfers between devices, neighbours(): sides.append(lax.ppermute(ends[0], axis, forward))  13.2 us
    all_to_all x1, waiting for transfers between devices, spread_sum(): lax.all_to_all(copies, axis, split_axis=0, concat_axis=0, tiled=True)  9.78 us
  transfers between devices with their start and end apart: 33, of which 13 were waited for; matrix products, arithmetic and copies ran while one was open for 3% of the time, Pallas kernels for 23%

profile of v3, /device:TPU:1, one launch (start us, length us, event | category | flops | bytes accessed | tf_op | source)
XLA Modules:
  0.0 260.5 jit_solution(13364270232378921012)
XLA Ops:
  0.6 3.3 %collective-permute-start = (s32[64,128]{1,0:T(8,128)}, s32[64,128]{1,0:T(8,128)S(1)}, u32[]{:S(2)}, u32[]{:S(2)}) collective-permute-start(s32[64,128]{1,0:T(8,128)} %bitcast.125), channel_id=1, source_target_pairs={{0,1},{1,0},{2,3},{3,2},{4,5},{5,4},{6,7},{7,6},{8,9},{9,8},{10,11... | collective-permute-start | bytes 98312 | tf_op jit(solution)/shard_map/ppermute | solution.py:20
  4.1 0.4 collective-permute-start.2
  4.6 0.7 fusion.52
  5.3 1.1 slice_add_fusion.8
  6.4 1.5 collective-permute-start.4
  7.9 0.9 slice_reduce_fusion
  8.8 1.1 slice_add_fusion.10
  9.9 2.2 copy-done
  12.1 0.8 copy-done.1
  12.9 0.8 copy-done.2
  13.6 0.8 copy-done.3
  14.4 0.8 copy-done.5
  15.1 10.6 %shard_map.176.block = f32[32,256,128]{2,1,0:T(8,128)S(1)} custom-call(f32[32,256]{1,0:T(8,128)S(1)} %copy-done.5, f32[32,256]{1,0:T(8,128)S(1)} %copy-done.1, f32[32,256]{1,0:T(8,128)S(1)} %copy-done.2, f32[32,256]{1,0:T(8,128)S(1)} %copy-done.3, f32[32,256,128]{2,1,0:T(8,128)S(1)} %copy-done), custom_call_target="tpu_custom_call" | custom-call | flops 12582912 | bytes 8388608 | tf_op jit(solution)/shard_map/pallas_call | solution.py:105
  25.7 1.3 collective-permute-start.5
  27.1 3.7 %collective-permute-start.6 = (f32[32,1,128]{2,1,0:T(1,128)S(1)}, f32[32,1,128]{2,1,0:T(1,128)S(1)}, u32[]{:S(2)}, u32[]{:S(2)}) collective-permute-start(f32[32,1,128]{2,1,0:T(1,128)S(1)} %get-tuple-element.67), channel_id=1, source_target_pairs={{0,1},{1,2},{2,3},{3,4},{4,5},{5,6},{6,7},{7,8},{8,9},{9,10},{10,1... | collective-permute-start | bytes 49160 | tf_op jit(solution)/shard_map/ppermute | solution.py:42
  30.8 1.9 collective-permute-start.7
  32.8 3.1 %collective-permute-done.7.right = f32[32,1,128]{2,1,0:T(1,128)S(1)} collective-permute-done((f32[32,1,128]{2,1,0:T(1,128)S(1)}, f32[32,1,128]{2,1,0:T(1,128)S(1)}, u32[]{:S(2)}, u32[]{:S(2)}) %collective-permute-start.7) | collective-permute-done | bytes 16416 | tf_op jit(solution)/shard_map/ppermute | solution.py:43
  35.9 2.6 %shard_map.177.block = f32[32,256,128]{2,1,0:T(8,128)} custom-call(f32[32,256]{1,0:T(8,128)S(1)} %copy-done.1, f32[32,256]{1,0:T(8,128)S(1)} %copy-done.2, f32[32,256]{1,0:T(8,128)S(1)} %copy-done.4, f32[1,256,128]{2,1,0:T(8,128)S(1)} %collective-permute-done.4.above, f32[1,256,128]{2,1,0:T(8,128)S(1)} %collective-permute-done.5.below, ...), custom_call_target="tpu_custom_call" | custom-call | flops 1000000 | bytes 1048576 | tf_op jit(solution)/shard_map/pallas_call | solution.py:145
  38.6 1.0 fusion.49
  39.5 4.3 %collective-permute-start.10 = (f32[1,256,128]{2,1,0:T(8,128)S(1)}, f32[1,256,128]{2,1,0:T(8,128)S(1)}, u32[]{:S(2)}, u32[]{:S(2)}) collective-permute-start(f32[1,256,128]{2,1,0:T(8,128)S(1)} %get-tuple-element.63), channel_id=1, source_target_pairs={{0,64},{64,128},{128,192},{1,65},{65,129},{129,193},{2,66},{66,130... | collective-permute-start | bytes 393224 | tf_op jit(solution)/shard_map/ppermute | solution.py:42
  43.8 1.3 collective-permute-start.11
  45.1 1.0 fusion.48
  46.1 3.8 %collective-permute-start.12 = (f32[32,1,128]{2,1,0:T(1,128)S(1)}, f32[32,1,128]{2,1,0:T(1,128)S(1)}, u32[]{:S(2)}, u32[]{:S(2)}) collective-permute-start(f32[32,1,128]{2,1,0:T(1,128)S(1)} %get-tuple-element.61), channel_id=1, source_target_pairs={{0,1},{1,2},{2,3},{3,4},{4,5},{5,6},{6,7},{7,8},{8,9},{9,10},{10,1... | collective-permute-start | bytes 49160 | tf_op jit(solution)/shard_map/ppermute | solution.py:42
  49.9 1.9 collective-permute-start.13
  51.9 9.7 %shard_map.179.block = f32[32,256,128]{2,1,0:T(8,128)S(1)} custom-call(f32[32,256]{1,0:T(8,128)S(1)} %copy-done.5, f32[32,256]{1,0:T(8,128)S(1)} %copy-done.1, f32[32,256]{1,0:T(8,128)S(1)} %copy-done.2, f32[32,256]{1,0:T(8,128)S(1)} %copy-done.4, f32[32,256,128]{2,1,0:T(8,128)} %shard_map.177.block), custom_call_target="tpu_custom_call" | custom-call | flops 12582912 | bytes 8388608 | tf_op jit(solution)/shard_map/pallas_call | solution.py:105
  61.7 2.6 %shard_map.180 = f32[32,256,128]{2,1,0:T(8,128)} custom-call(f32[32,256]{1,0:T(8,128)S(1)} %copy-done.1, f32[32,256]{1,0:T(8,128)S(1)} %copy-done.2, f32[32,256]{1,0:T(8,128)S(1)} %copy-done.4, f32[1,256,128]{2,1,0:T(8,128)S(1)} %collective-permute-done.10.above, f32[1,256,128]{2,1,0:T(8,128)S(1)} %collective-permute-done.11.below, ...), custom_call_target="tpu_custom_call" | custom-call | flops 1000000 | bytes 1048576 | tf_op jit(solution)/shard_map/pallas_call | solution.py:145
  64.4 18.5 %shard_map.178 = f32[32,256,128]{2,1,0:T(8,128)S(1)} custom-call(s32[32]{0:T(128)S(1)} %fusion.30.receivers, s32[16384]{0:T(1024)S(1)} %add_bitcast_fusion.cells, f32[16384]{0:T(1024)S(1)} %maximum_bitcast_fusion.weights, s32[128]{0:T(128)S(1)} %pad_add_fusion.counts, s32[64,128]{1,0:T(8,128)S(1)} %bitcast.121, ...), custom_call_target="tpu_custom_call" | custom-call | flops 1000000000 | bytes 31457280 | tf_op jit(solution)/shard_map/pallas_call | solution.py:200
  83.0 5.9 %collective-permute-start.9 = (f32[8,256,128]{2,1,0:T(8,128)S(1)}, f32[8,256,128]{2,1,0:T(8,128)S(1)}, u32[]{:S(2)}, u32[]{:S(2)}) collective-permute-start(f32[8,256,128]{2,1,0:T(8,128)S(1)} %slice.363), channel_id=1, source_target_pairs={{0,2},{1,7},{2,4},{3,1},{4,6},{5,3},{6,0},{7,5},{8,10},{9,15},{10,... | collective-permute-start | bytes 3145736 | tf_op jit(solution)/shard_map/ppermute | solution.py:32
  88.9 18.8 %shard_map.181 = f32[32,256,128]{2,1,0:T(8,128)S(1)} custom-call(s32[32]{0:T(128)S(1)} %fusion.32.receivers, s32[16384]{0:T(1024)S(1)} %add_bitcast_fusion.cells, f32[16384]{0:T(1024)S(1)} %maximum_bitcast_fusion.weights, s32[128]{0:T(128)S(1)} %pad_add_fusion.counts, s32[64,128]{1,0:T(8,128)S(1)} %bitcast.122, ...), custom_call_target="tpu_custom_call" | custom-call | flops 1000000000 | bytes 31457280 | tf_op jit(solution)/shard_map/pallas_call | solution.py:200
  108.2 2.4 collective-permute-start.17
  110.5 6.1 %collective-permute-done.17 = f32[4,256,128]{2,1,0:T(8,128)S(1)} collective-permute-done((f32[4,256,128]{2,1,0:T(8,128)S(1)}, f32[4,256,128]{2,1,0:T(8,128)S(1)}, u32[]{:S(2)}, u32[]{:S(2)}) %collective-permute-start.17) | collective-permute-done | bytes 524320 | tf_op jit(solution)/shard_map/ppermute | solution.py:32
  116.8 3.5 %collective-permute-start.18 = (f32[2,4,256,128]{3,2,1,0:T(8,128)S(1)}, f32[2,4,256,128]{3,2,1,0:T(8,128)S(1)}, u32[]{:S(2)}, u32[]{:S(2)}) collective-permute-start(f32[2,4,256,128]{3,2,1,0:T(8,128)S(1)} %pad_maximum_fusion.1), channel_id=1, source_target_pairs={{0,8},{1,57},{8,16},{9,1},{16,24},{17,9},{24,32},{25,17},{32,40},{... | collective-permute-start | bytes 3145736 | tf_op jit(solution)/shard_map/ppermute | solution.py:32
  120.3 13.0 %collective-permute-done.15 = f32[2,8,256,128]{3,2,1,0:T(8,128)S(1)} collective-permute-done((f32[2,8,256,128]{3,2,1,0:T(8,128)S(1)}, f32[2,8,256,128]{3,2,1,0:T(8,128)S(1)}, u32[]{:S(2)}, u32[]{:S(2)}) %collective-permute-start.15) | collective-permute-done | bytes 2097184 | tf_op jit(solution)/shard_map/ppermute | solution.py:32
  134.2 2.3 collective-permute-done.16
  136.6 5.4 %collective-permute-start.20 = (f32[2,4,256,128]{3,2,1,0:T(8,128)S(1)}, f32[2,4,256,128]{3,2,1,0:T(8,128)S(1)}, u32[]{:S(2)}, u32[]{:S(2)}) collective-permute-start(f32[2,4,256,128]{3,2,1,0:T(8,128)S(1)} %add.206), channel_id=1, source_target_pairs={{0,8},{1,57},{8,16},{9,1},{16,24},{17,9},{24,32},{25,17},{32,40},{... | collective-permute-start | bytes 3145736 | tf_op jit(solution)/shard_map/ppermute | solution.py:32
  142.0 0.8 collective-permute-start.19
  142.8 12.3 %collective-permute-done.19 = f32[256,128]{1,0:T(8,128)S(1)} collective-permute-done((f32[256,128]{1,0:T(8,128)S(1)}, f32[256,128]{1,0:T(8,128)S(1)}, u32[]{:S(2)}, u32[]{:S(2)}) %collective-permute-start.19) | collective-permute-done | bytes 131104 | tf_op jit(solution)/shard_map/ppermute | solution.py:32
  155.4 3.2 %collective-permute-start.23 = (f32[2,4,256,128]{3,2,1,0:T(8,128)S(1)}, f32[2,4,256,128]{3,2,1,0:T(8,128)S(1)}, u32[]{:S(2)}, u32[]{:S(2)}) collective-permute-start(f32[2,4,256,128]{3,2,1,0:T(8,128)S(1)} %add.208), channel_id=1, source_target_pairs={{0,8},{1,57},{8,16},{9,1},{16,24},{17,9},{24,32},{25,17},{32,40},{... | collective-permute-start | bytes 3145736 | tf_op jit(solution)/shard_map/ppermute | solution.py:32
  158.6 11.7 %collective-permute-done.23 = f32[2,4,256,128]{3,2,1,0:T(8,128)S(1)} collective-permute-done((f32[2,4,256,128]{3,2,1,0:T(8,128)S(1)}, f32[2,4,256,128]{3,2,1,0:T(8,128)S(1)}, u32[]{:S(2)}, u32[]{:S(2)}) %collective-permute-start.23) | collective-permute-done | bytes 1048608 | tf_op jit(solution)/shard_map/ppermute | solution.py:32
  170.5 2.9 %collective-permute-start.24 = (f32[4,256,128]{2,1,0:T(8,128)S(1)}, f32[4,256,128]{2,1,0:T(8,128)S(1)}, u32[]{:S(2)}, u32[]{:S(2)}) collective-permute-start(f32[4,256,128]{2,1,0:T(8,128)S(1)} %pad_maximum_fusion.2), channel_id=1, source_target_pairs={{0,1},{1,0},{2,3},{3,2},{4,5},{5,4},{6,7},{7,6},{8,9},{9,8},{10,11... | collective-permute-start | bytes 1572872 | tf_op jit(solution)/shard_map/ppermute | solution.py:20
  173.5 2.8 %collective-permute-start.22 = (f32[2,256,128]{2,1,0:T(8,128)S(1)}, f32[2,256,128]{2,1,0:T(8,128)S(1)}, u32[]{:S(2)}, u32[]{:S(2)}) collective-permute-start(f32[2,256,128]{2,1,0:T(8,128)S(1)} %slice_add_fusion.4), channel_id=1, source_target_pairs={{0,8},{1,57},{8,16},{9,1},{16,24},{17,9},{24,32},{25,17},{32,40},{... | collective-permute-start | bytes 786440 | tf_op jit(solution)/shard_map/ppermute | solution.py:32
  176.3 3.3 %collective-permute-done.22 = f32[2,256,128]{2,1,0:T(8,128)S(1)} collective-permute-done((f32[2,256,128]{2,1,0:T(8,128)S(1)}, f32[2,256,128]{2,1,0:T(8,128)S(1)}, u32[]{:S(2)}, u32[]{:S(2)}) %collective-permute-start.22) | collective-permute-done | bytes 262176 | tf_op jit(solution)/shard_map/ppermute | solution.py:32
  179.8 1.8 collective-permute-start.26
  181.6 3.1 %collective-permute-start.25 = (f32[2,256,128]{2,1,0:T(8,128)S(1)}, f32[2,256,128]{2,1,0:T(8,128)S(1)}, u32[]{:S(2)}, u32[]{:S(2)}) collective-permute-start(f32[2,256,128]{2,1,0:T(8,128)S(1)} %slice_add_fusion.5), channel_id=1, source_target_pairs={{0,8},{1,57},{8,16},{9,1},{16,24},{17,9},{24,32},{25,17},{32,40},{... | collective-permute-start | bytes 786440 | tf_op jit(solution)/shard_map/ppermute | solution.py:32
  184.8 3.3 %collective-permute-done.25 = f32[2,256,128]{2,1,0:T(8,128)S(1)} collective-permute-done((f32[2,256,128]{2,1,0:T(8,128)S(1)}, f32[2,256,128]{2,1,0:T(8,128)S(1)}, u32[]{:S(2)}, u32[]{:S(2)}) %collective-permute-start.25) | collective-permute-done | bytes 262176 | tf_op jit(solution)/shard_map/ppermute | solution.py:32
  188.1 3.6 %collective-permute-start.27 = (f32[256,128]{1,0:T(8,128)S(1)}, f32[256,128]{1,0:T(8,128)S(1)}, u32[]{:S(2)}, u32[]{:S(2)}) collective-permute-start(f32[256,128]{1,0:T(8,128)S(1)} %slice_bitcast_fusion.6), channel_id=1, source_target_pairs={{0,1},{1,0},{2,3},{3,2},{4,5},{5,4},{6,7},{7,6},{8,9},{9,8},{10,11... | collective-permute-start | bytes 393224 | tf_op jit(solution)/shard_map/ppermute | solution.py:20
  192.0 2.9 %collective-permute-start.28 = (f32[2,256,128]{2,1,0:T(8,128)S(1)}, f32[2,256,128]{2,1,0:T(8,128)S(1)}, u32[]{:S(2)}, u32[]{:S(2)}) collective-permute-start(f32[2,256,128]{2,1,0:T(8,128)S(1)} %pad_maximum_fusion.4), channel_id=1, source_target_pairs={{0,2},{1,7},{2,4},{3,1},{4,6},{5,3},{6,0},{7,5},{8,10},{9,15},{10,... | collective-permute-start | bytes 786440 | tf_op jit(solution)/shard_map/ppermute | solution.py:32
  195.0 3.2 %collective-permute-done.28 = f32[2,256,128]{2,1,0:T(8,128)S(1)} collective-permute-done((f32[2,256,128]{2,1,0:T(8,128)S(1)}, f32[2,256,128]{2,1,0:T(8,128)S(1)}, u32[]{:S(2)}, u32[]{:S(2)}) %collective-permute-start.28) | collective-permute-done | bytes 262176 | tf_op jit(solution)/shard_map/ppermute | solution.py:32
  198.2 1.5 collective-permute-start.29
  199.9 0.8 collective-permute-done.29
  201.4 0.6 fusion.6
  202.0 0.6 convolution_add_fusion
  202.5 0.4 collective-permute-start.30
  203.0 0.9 collective-permute-done.30
  203.9 8.0 %all_to_all.15 = f32[4,72,128]{2,1,0:T(8,128)S(1)} all-to-all(f32[4,72,128]{2,1,0:T(8,128)S(1)} %broadcast_in_dim.6), channel_id=1, replica_groups=mesh['lat'=4,'z'=8,'x'=4,'core'=2] {'x'}, dimensions={0} | all-to-all | bytes 294912 | tf_op jit(solution)/shard_map/all_to_all | solution.py:421
  211.9 9.5 %all_to_all.16 = f32[4,72,128]{2,1,0:T(8,128)S(1)} all-to-all(f32[4,72,128]{2,1,0:T(8,128)S(1)} %broadcast_in_dim.7), channel_id=1, replica_groups=mesh['lat'=4,'z'=8,'x'=4,'core'=2] {'lat'}, dimensions={0} | all-to-all | bytes 294912 | tf_op jit(solution)/shard_map/all_to_all | solution.py:421
  221.5 0.7 broadcast_in_dim.8
  222.2 8.9 %all-to-all-start.2 = ((f32[8,72,128]{2,1,0:T(8,128)}), f32[8,72,128]{2,1,0:T(8,128)S(1)}, u32[]{:S(2)}, u32[]{:S(2)}) async-start(f32[8,72,128]{2,1,0:T(8,128)} %broadcast_in_dim.8), calls=%async_computation.2 | async-start | bytes 589824 | tf_op jit(solution)/shard_map/all_to_all | solution.py:421
  231.1 9.8 %all-to-all-done.2 = f32[8,72,128]{2,1,0:T(8,128)S(1)} async-done(((f32[8,72,128]{2,1,0:T(8,128)}), f32[8,72,128]{2,1,0:T(8,128)S(1)}, u32[]{:S(2)}, u32[]{:S(2)}) %all-to-all-start.2) | async-done | bytes 294944 | tf_op jit(solution)/shard_map/all_to_all | solution.py:421
  240.9 4.7 %collective-permute-start.31 = (f32[72,128]{1,0:T(8,128)S(1)}, f32[72,128]{1,0:T(8,128)S(1)}, u32[]{:S(2)}, u32[]{:S(2)}) collective-permute-start(f32[72,128]{1,0:T(8,128)S(1)} %reduce_sum.49), channel_id=1, source_target_pairs={{0,1},{1,0},{2,3},{3,2},{4,5},{5,4},{6,7},{7,6},{8,9},{9,8},{10,11... | collective-permute-start | bytes 110600 | tf_op jit(solution)/shard_map/ppermute | solution.py:20
  245.6 0.8 collective-permute-done.31
  246.5 0.6 maximum_select_fusion.products
  247.1 5.8 %shard_map.182 = (bf16[128,128]{1,0:T(8,128)(2,1)S(1)}, bf16[128,128]{1,0:T(8,128)(2,1)S(1)}) custom-call(f32[144,128]{1,0:T(8,128)} %maximum_select_fusion.products), custom_call_target="tpu_custom_call" | custom-call | tf_op jit(solution)/shard_map/pallas_call | solution.py:284
  252.9 7.6 %shard_map.183 = (f32[8192,128]{1,0:T(8,128)}, f32[512,128]{1,0:T(8,128)}) custom-call(bf16[128,128]{1,0:T(8,128)(2,1)S(1)} %get-tuple-element.46.high, bf16[128,128]{1,0:T(8,128)(2,1)S(1)} %get-tuple-element.47.low, f32[8192,128]{1,0:T(8,128)} %bitcast.11.refs_2_.state, f32[512,128]{1,0:T(8,128)S(1)} %pad_maximum_fusion.5.observed), custom_call_target="tpu_custom_call" | custom-call | tf_op jit(solution)/shard_map/pallas_call | solution.py:318
  (121 shorter events, 4.0 us)
Async XLA Ops:
  0.6 26.5 %collective-permute-start = (s32[64,128]{1,0:T(8,128)}, s32[64,128]{1,0:T(8,128)S(1)}, u32[]{:S(2)}, u32[]{:S(2)}) collective-permute-start(s32[64,128]{1,0:T(8,128)} %bitcast.125), channel_id=1, source_target_pairs={{0,1},{1,0},{2,3},{3,2},{4,5},{5,4},{6,7},{7,6},{8,9},{9,8},{10,11... | collective-permute-start | bytes 98312 | tf_op jit(solution)/shard_map/ppermute | solution.py:20
  4.0 26.9 %collective-permute-start.1 = (f32[64,128]{1,0:T(8,128)}, f32[64,128]{1,0:T(8,128)S(1)}, u32[]{:S(2)}, u32[]{:S(2)}) collective-permute-start(f32[64,128]{1,0:T(8,128)} %bitcast.127), channel_id=1, source_target_pairs={{0,1},{1,0},{2,3},{3,2},{4,5},{5,4},{6,7},{7,6},{8,9},{9,8},{10,11... | collective-permute-start | bytes 98312 | tf_op jit(solution)/shard_map/ppermute | solution.py:20
  4.1 21.6 %collective-permute-start.2 = (s32[64]{0:T(128)}, s32[64]{0:T(128)S(1)}, u32[]{:S(2)}, u32[]{:S(2)}) collective-permute-start(s32[64]{0:T(128)} %bitcast.137), channel_id=1, source_target_pairs={{0,1},{1,0},{2,3},{3,2},{4,5},{5,4},{6,7},{7,6},{8,9},{9,8},{10,11... | collective-permute-start | bytes 776 | tf_op jit(solution)/shard_map/ppermute | solution.py:20
  4.5 31.4 %collective-permute-start.3 = (s32[64,128]{1,0:T(8,128)}, s32[64,128]{1,0:T(8,128)S(1)}, u32[]{:S(2)}, u32[]{:S(2)}) collective-permute-start(s32[64,128]{1,0:T(8,128)} %bitcast.120), channel_id=1, source_target_pairs={{0,1},{1,0},{2,3},{3,2},{4,5},{5,4},{6,7},{7,6},{8,9},{9,8},{10,11... | collective-permute-start | bytes 98312 | tf_op jit(solution)/shard_map/ppermute | solution.py:20
  6.4 29.5 %collective-permute-start.4 = (f32[1,256,128]{2,1,0:T(8,128)S(1)}, f32[1,256,128]{2,1,0:T(8,128)S(1)}, u32[]{:S(2)}, u32[]{:S(2)}) collective-permute-start(f32[1,256,128]{2,1,0:T(8,128)S(1)} %get-tuple-element.69), channel_id=1, source_target_pairs={{0,64},{64,128},{128,192},{1,65},{65,129},{129,193},{2,66},{66,130... | collective-permute-start | bytes 393224 | tf_op jit(solution)/shard_map/ppermute | solution.py:42
  9.9 2.2 copy-start
  12.1 0.8 copy-start.1
  12.8 0.8 copy-start.2
  13.6 0.8 copy-start.3
  14.4 0.8 copy-start.5
  15.1 11.9 %copy-start.17 = (s32[1,1,64]{2,1,0:T(1,128)S(1)}, s32[1,1,64]{2,1,0:T(1,128)}, u32[]{:S(2)}) copy-start(s32[1,1,64]{2,1,0:T(1,128)} %param.25) | copy-start | bytes 772
  15.1 15.7 %copy-start.7 = (s32[1,1,64,128]{3,2,1,0:T(8,128)S(1)}, s32[1,1,64,128]{3,2,1,0:T(8,128)}, u32[]{:S(2)}) copy-start(s32[1,1,64,128]{3,2,1,0:T(8,128)} %param.22) | copy-start | bytes 98308
  15.1 17.6 %copy-start.8 = (f32[1,1,64,128]{3,2,1,0:T(8,128)S(1)}, f32[1,1,64,128]{3,2,1,0:T(8,128)}, u32[]{:S(2)}) copy-start(f32[1,1,64,128]{3,2,1,0:T(8,128)} %param.24) | copy-start | bytes 98308
  15.1 20.8 %copy-start.4 = (f32[32,256]{1,0:T(8,128)S(1)}, f32[32,256]{1,0:T(8,128)}, u32[]{:S(2)}) copy-start(f32[32,256]{1,0:T(8,128)} %diffusion.7) | copy-start | bytes 98308
  25.7 10.2 %collective-permute-start.5 = (f32[1,256,128]{2,1,0:T(8,128)S(1)}, f32[1,256,128]{2,1,0:T(8,128)S(1)}, u32[]{:S(2)}, u32[]{:S(2)}) collective-permute-start(f32[1,256,128]{2,1,0:T(8,128)S(1)} %get-tuple-element.68), channel_id=1, source_target_pairs={{64,0},{128,64},{192,128},{65,1},{129,65},{193,129},{66,2},{130,66... | collective-permute-start | bytes 393224 | tf_op jit(solution)/shard_map/ppermute | solution.py:43
  27.1 5.7 %collective-permute-start.6 = (f32[32,1,128]{2,1,0:T(1,128)S(1)}, f32[32,1,128]{2,1,0:T(1,128)S(1)}, u32[]{:S(2)}, u32[]{:S(2)}) collective-permute-start(f32[32,1,128]{2,1,0:T(1,128)S(1)} %get-tuple-element.67), channel_id=1, source_target_pairs={{0,1},{1,2},{2,3},{3,4},{4,5},{5,6},{6,7},{7,8},{8,9},{9,10},{10,1... | collective-permute-start | bytes 49160 | tf_op jit(solution)/shard_map/ppermute | solution.py:42
  30.8 5.1 %collective-permute-start.7 = (f32[32,1,128]{2,1,0:T(1,128)S(1)}, f32[32,1,128]{2,1,0:T(1,128)S(1)}, u32[]{:S(2)}, u32[]{:S(2)}) collective-permute-start(f32[32,1,128]{2,1,0:T(1,128)S(1)} %get-tuple-element.66), channel_id=1, source_target_pairs={{1,0},{2,1},{3,2},{4,3},{5,4},{6,5},{7,6},{8,7},{9,8},{10,9},{11,1... | collective-permute-start | bytes 49160 | tf_op jit(solution)/shard_map/ppermute | solution.py:43
  38.6 25.8 %collective-permute-start.8 = (f32[8192,128]{1,0:T(8,128)}, f32[8192,128]{1,0:T(8,128)}, u32[]{:S(2)}, u32[]{:S(2)}) collective-permute-start(f32[8192,128]{1,0:T(8,128)} %bitcast.8.refs_2_), channel_id=1, source_target_pairs={{0,1},{1,0},{2,3},{3,2},{4,5},{5,4},{6,7},{7,6},{8,9},{9,8},{10,11... | collective-permute-start | bytes 12582920 | tf_op jit(solution)/shard_map/ppermute | solution.py:20
  39.5 22.1 %collective-permute-start.10 = (f32[1,256,128]{2,1,0:T(8,128)S(1)}, f32[1,256,128]{2,1,0:T(8,128)S(1)}, u32[]{:S(2)}, u32[]{:S(2)}) collective-permute-start(f32[1,256,128]{2,1,0:T(8,128)S(1)} %get-tuple-element.63), channel_id=1, source_target_pairs={{0,64},{64,128},{128,192},{1,65},{65,129},{129,193},{2,66},{66,130... | collective-permute-start | bytes 393224 | tf_op jit(solution)/shard_map/ppermute | solution.py:42
  43.8 17.8 %collective-permute-start.11 = (f32[1,256,128]{2,1,0:T(8,128)S(1)}, f32[1,256,128]{2,1,0:T(8,128)S(1)}, u32[]{:S(2)}, u32[]{:S(2)}) collective-permute-start(f32[1,256,128]{2,1,0:T(8,128)S(1)} %get-tuple-element.62), channel_id=1, source_target_pairs={{64,0},{128,64},{192,128},{65,1},{129,65},{193,129},{66,2},{130,66... | collective-permute-start | bytes 393224 | tf_op jit(solution)/shard_map/ppermute | solution.py:43
  46.1 15.5 %collective-permute-start.12 = (f32[32,1,128]{2,1,0:T(1,128)S(1)}, f32[32,1,128]{2,1,0:T(1,128)S(1)}, u32[]{:S(2)}, u32[]{:S(2)}) collective-permute-start(f32[32,1,128]{2,1,0:T(1,128)S(1)} %get-tuple-element.61), channel_id=1, source_target_pairs={{0,1},{1,2},{2,3},{3,4},{4,5},{5,6},{6,7},{7,8},{8,9},{9,10},{10,1... | collective-permute-start | bytes 49160 | tf_op jit(solution)/shard_map/ppermute | solution.py:42
  49.9 11.7 %collective-permute-start.13 = (f32[32,1,128]{2,1,0:T(1,128)S(1)}, f32[32,1,128]{2,1,0:T(1,128)S(1)}, u32[]{:S(2)}, u32[]{:S(2)}) collective-permute-start(f32[32,1,128]{2,1,0:T(1,128)S(1)} %get-tuple-element.60), channel_id=1, source_target_pairs={{1,0},{2,1},{3,2},{4,3},{5,4},{6,5},{7,6},{8,7},{9,8},{10,9},{11,1... | collective-permute-start | bytes 49160 | tf_op jit(solution)/shard_map/ppermute | solution.py:43
  61.6 2.7 %copy-start.14 = (s32[32]{0:T(128)S(1)}, s32[32]{0:T(128)}, u32[]{:S(2)}) copy-start(s32[32]{0:T(128)} %constant.95.clone) | copy-start | bytes 388
  61.6 2.7 %copy-start.15 = (s32[32]{0:T(128)S(1)}, s32[32]{0:T(128)}, u32[]{:S(2)}) copy-start(s32[32]{0:T(128)} %constant.93.clone) | copy-start | bytes 388
  61.6 2.7 %copy-start.16 = (s32[32]{0:T(128)S(1)}, s32[32]{0:T(128)}, u32[]{:S(2)}) copy-start(s32[32]{0:T(128)} %constant.94.clone) | copy-start | bytes 388
  61.6 2.8 %copy-start.6 = (s32[1,1,64,128]{3,2,1,0:T(8,128)S(1)}, s32[1,1,64,128]{3,2,1,0:T(8,128)}, u32[]{:S(2)}) copy-start(s32[1,1,64,128]{3,2,1,0:T(8,128)} %param.23) | copy-start | bytes 98308
  64.3 24.6 %collective-permute-start.14 = (f32[8192,128]{1,0:T(8,128)}, f32[8192,128]{1,0:T(8,128)}, u32[]{:S(2)}, u32[]{:S(2)}) collective-permute-start(f32[8192,128]{1,0:T(8,128)} %bitcast.11.refs_2_.state), channel_id=1, source_target_pairs={{0,1},{1,0},{2,3},{3,2},{4,5},{5,4},{6,7},{7,6},{8,9},{9,8},{10,11... | collective-permute-start | bytes 12582920 | tf_op jit(solution)/shard_map/ppermute | solution.py:20
  64.3 24.5 %copy-start.11 = (s32[32]{0:T(128)S(1)}, s32[32]{0:T(128)}, u32[]{:S(2)}) copy-start(s32[32]{0:T(128)} %constant.98.clone) | copy-start | bytes 388
  64.3 24.5 %copy-start.12 = (s32[32]{0:T(128)S(1)}, s32[32]{0:T(128)}, u32[]{:S(2)}) copy-start(s32[32]{0:T(128)} %constant.97.clone) | copy-start | bytes 388
  64.4 24.5 %copy-start.13 = (s32[32]{0:T(128)S(1)}, s32[32]{0:T(128)}, u32[]{:S(2)}) copy-start(s32[32]{0:T(128)} %constant.96.clone) | copy-start | bytes 388
  83.0 24.7 %collective-permute-start.9 = (f32[8,256,128]{2,1,0:T(8,128)S(1)}, f32[8,256,128]{2,1,0:T(8,128)S(1)}, u32[]{:S(2)}, u32[]{:S(2)}) collective-permute-start(f32[8,256,128]{2,1,0:T(8,128)S(1)} %slice.363), channel_id=1, source_target_pairs={{0,2},{1,7},{2,4},{3,1},{4,6},{5,3},{6,0},{7,5},{8,10},{9,15},{10,... | collective-permute-start | bytes 3145736 | tf_op jit(solution)/shard_map/ppermute | solution.py:32
  108.1 25.3 %collective-permute-start.15 = (f32[2,8,256,128]{3,2,1,0:T(8,128)S(1)}, f32[2,8,256,128]{3,2,1,0:T(8,128)S(1)}, u32[]{:S(2)}, u32[]{:S(2)}) collective-permute-start(f32[2,8,256,128]{3,2,1,0:T(8,128)S(1)} %pad_maximum_fusion), channel_id=1, source_target_pairs={{0,2},{1,7},{2,4},{3,1},{4,6},{5,3},{6,0},{7,5},{8,10},{9,15},{10,... | collective-permute-start | bytes 6291464 | tf_op jit(solution)/shard_map/ppermute | solution.py:32
  108.2 8.5 %collective-permute-start.17 = (f32[4,256,128]{2,1,0:T(8,128)S(1)}, f32[4,256,128]{2,1,0:T(8,128)S(1)}, u32[]{:S(2)}, u32[]{:S(2)}) collective-permute-start(f32[4,256,128]{2,1,0:T(8,128)S(1)} %slice.369), channel_id=1, source_target_pairs={{0,8},{1,57},{8,16},{9,1},{16,24},{17,9},{24,32},{25,17},{32,40},{... | collective-permute-start | bytes 1572872 | tf_op jit(solution)/shard_map/ppermute | solution.py:32
  116.8 17.1 %collective-permute-start.18 = (f32[2,4,256,128]{3,2,1,0:T(8,128)S(1)}, f32[2,4,256,128]{3,2,1,0:T(8,128)S(1)}, u32[]{:S(2)}, u32[]{:S(2)}) collective-permute-start(f32[2,4,256,128]{3,2,1,0:T(8,128)S(1)} %pad_maximum_fusion.1), channel_id=1, source_target_pairs={{0,8},{1,57},{8,16},{9,1},{16,24},{17,9},{24,32},{25,17},{32,40},{... | collective-permute-start | bytes 3145736 | tf_op jit(solution)/shard_map/ppermute | solution.py:32
  133.7 2.7 %collective-permute-start.16 = (f32[8,256,128]{2,1,0:T(8,128)S(1)}, f32[8,256,128]{2,1,0:T(8,128)S(1)}, u32[]{:S(2)}, u32[]{:S(2)}) collective-permute-start(f32[8,256,128]{2,1,0:T(8,128)S(1)} %get-tuple-element.70), channel_id=1, source_target_pairs={{0,1},{1,0},{2,3},{3,2},{4,5},{5,4},{6,7},{7,6},{8,9},{9,8},{10,11... | collective-permute-start | bytes 3145736 | tf_op jit(solution)/shard_map/ppermute | solution.py:20
  136.6 18.6 %collective-permute-start.20 = (f32[2,4,256,128]{3,2,1,0:T(8,128)S(1)}, f32[2,4,256,128]{3,2,1,0:T(8,128)S(1)}, u32[]{:S(2)}, u32[]{:S(2)}) collective-permute-start(f32[2,4,256,128]{3,2,1,0:T(8,128)S(1)} %add.206), channel_id=1, source_target_pairs={{0,8},{1,57},{8,16},{9,1},{16,24},{17,9},{24,32},{25,17},{32,40},{... | collective-permute-start | bytes 3145736 | tf_op jit(solution)/shard_map/ppermute | solution.py:32
  142.0 13.1 %collective-permute-start.19 = (f32[256,128]{1,0:T(8,128)S(1)}, f32[256,128]{1,0:T(8,128)S(1)}, u32[]{:S(2)}, u32[]{:S(2)}) collective-permute-start(f32[256,128]{1,0:T(8,128)S(1)} %get-tuple-element.38), channel_id=1, source_target_pairs={{0,8},{1,57},{8,16},{9,1},{16,24},{17,9},{24,32},{25,17},{32,40},{... | collective-permute-start | bytes 393224 | tf_op jit(solution)/shard_map/ppermute | solution.py:32
  155.4 14.9 %collective-permute-start.23 = (f32[2,4,256,128]{3,2,1,0:T(8,128)S(1)}, f32[2,4,256,128]{3,2,1,0:T(8,128)S(1)}, u32[]{:S(2)}, u32[]{:S(2)}) collective-permute-start(f32[2,4,256,128]{3,2,1,0:T(8,128)S(1)} %add.208), channel_id=1, source_target_pairs={{0,8},{1,57},{8,16},{9,1},{16,24},{17,9},{24,32},{25,17},{32,40},{... | collective-permute-start | bytes 3145736 | tf_op jit(solution)/shard_map/ppermute | solution.py:32
  158.5 14.9 %collective-permute-start.21 = (f32[2,256,128]{2,1,0:T(8,128)S(1)}, f32[2,256,128]{2,1,0:T(8,128)S(1)}, u32[]{:S(2)}, u32[]{:S(2)}) collective-permute-start(f32[2,256,128]{2,1,0:T(8,128)S(1)} %pad_maximum_fusion.3), channel_id=1, source_target_pairs={{0,8},{1,57},{8,16},{9,1},{16,24},{17,9},{24,32},{25,17},{32,40},{... | collective-permute-start | bytes 786440 | tf_op jit(solution)/shard_map/ppermute | solution.py:32
  170.4 21.3 %copy-start.9 = (f32[2,256]{1,0:T(2,128)S(1)}, f32[2,256]{1,0:T(2,128)}, u32[]{:S(2)}) copy-start(f32[2,256]{1,0:T(2,128)} %param.27) | copy-start | bytes 6148
  170.4 30.4 %copy-start.10 = (f32[2,256]{1,0:T(2,128)S(1)}, f32[2,256]{1,0:T(2,128)}, u32[]{:S(2)}) copy-start(f32[2,256]{1,0:T(2,128)} %param.26) | copy-start | bytes 6148
  170.5 9.2 %collective-permute-start.24 = (f32[4,256,128]{2,1,0:T(8,128)S(1)}, f32[4,256,128]{2,1,0:T(8,128)S(1)}, u32[]{:S(2)}, u32[]{:S(2)}) collective-permute-start(f32[4,256,128]{2,1,0:T(8,128)S(1)} %pad_maximum_fusion.2), channel_id=1, source_target_pairs={{0,1},{1,0},{2,3},{3,2},{4,5},{5,4},{6,7},{7,6},{8,9},{9,8},{10,11... | collective-permute-start | bytes 1572872 | tf_op jit(solution)/shard_map/ppermute | solution.py:20
  173.5 6.1 %collective-permute-start.22 = (f32[2,256,128]{2,1,0:T(8,128)S(1)}, f32[2,256,128]{2,1,0:T(8,128)S(1)}, u32[]{:S(2)}, u32[]{:S(2)}) collective-permute-start(f32[2,256,128]{2,1,0:T(8,128)S(1)} %slice_add_fusion.4), channel_id=1, source_target_pairs={{0,8},{1,57},{8,16},{9,1},{16,24},{17,9},{24,32},{25,17},{32,40},{... | collective-permute-start | bytes 786440 | tf_op jit(solution)/shard_map/ppermute | solution.py:32
  179.8 4.9 %collective-permute-start.26 = (f32[256,128]{1,0:T(8,128)S(1)}, f32[256,128]{1,0:T(8,128)S(1)}, u32[]{:S(2)}, u32[]{:S(2)}) collective-permute-start(f32[256,128]{1,0:T(8,128)S(1)} %get-tuple-element.43), channel_id=1, source_target_pairs={{0,2},{1,7},{2,4},{3,1},{4,6},{5,3},{6,0},{7,5},{8,10},{9,15},{10,... | collective-permute-start | bytes 393224 | tf_op jit(solution)/shard_map/ppermute | solution.py:32
  181.6 6.4 %collective-permute-start.25 = (f32[2,256,128]{2,1,0:T(8,128)S(1)}, f32[2,256,128]{2,1,0:T(8,128)S(1)}, u32[]{:S(2)}, u32[]{:S(2)}) collective-permute-start(f32[2,256,128]{2,1,0:T(8,128)S(1)} %slice_add_fusion.5), channel_id=1, source_target_pairs={{0,8},{1,57},{8,16},{9,1},{16,24},{17,9},{24,32},{25,17},{32,40},{... | collective-permute-start | bytes 786440 | tf_op jit(solution)/shard_map/ppermute | solution.py:32
  188.1 6.8 %collective-permute-start.27 = (f32[256,128]{1,0:T(8,128)S(1)}, f32[256,128]{1,0:T(8,128)S(1)}, u32[]{:S(2)}, u32[]{:S(2)}) collective-permute-start(f32[256,128]{1,0:T(8,128)S(1)} %slice_bitcast_fusion.6), channel_id=1, source_target_pairs={{0,1},{1,0},{2,3},{3,2},{4,5},{5,4},{6,7},{7,6},{8,9},{9,8},{10,11... | collective-permute-start | bytes 393224 | tf_op jit(solution)/shard_map/ppermute | solution.py:20
  192.0 6.2 %collective-permute-start.28 = (f32[2,256,128]{2,1,0:T(8,128)S(1)}, f32[2,256,128]{2,1,0:T(8,128)S(1)}, u32[]{:S(2)}, u32[]{:S(2)}) collective-permute-start(f32[2,256,128]{2,1,0:T(8,128)S(1)} %pad_maximum_fusion.4), channel_id=1, source_target_pairs={{0,2},{1,7},{2,4},{3,1},{4,6},{5,3},{6,0},{7,5},{8,10},{9,15},{10,... | collective-permute-start | bytes 786440 | tf_op jit(solution)/shard_map/ppermute | solution.py:32
  198.2 2.5 collective-permute-start.29
  202.5 1.3 collective-permute-start.30
  222.2 18.7 %all-to-all-start.2 = ((f32[8,72,128]{2,1,0:T(8,128)}), f32[8,72,128]{2,1,0:T(8,128)S(1)}, u32[]{:S(2)}, u32[]{:S(2)}) async-start(f32[8,72,128]{2,1,0:T(8,128)} %broadcast_in_dim.8), calls=%async_computation.2 | async-start | bytes 589824 | tf_op jit(solution)/shard_map/all_to_all | solution.py:421
  240.9 5.5 %collective-permute-start.31 = (f32[72,128]{1,0:T(8,128)S(1)}, f32[72,128]{1,0:T(8,128)S(1)}, u32[]{:S(2)}, u32[]{:S(2)}) collective-permute-start(f32[72,128]{1,0:T(8,128)S(1)} %reduce_sum.49), channel_id=1, source_target_pairs={{0,1},{1,0},{2,3},{3,2},{4,5},{5,4},{6,7},{7,6},{8,9},{9,8},{10,11... | collective-permute-start | bytes 110600 | tf_op jit(solution)/shard_map/ppermute | solution.py:20

commit v4 on v0

--- a/solution.py
+++ b/solution.py
@@ -19,7 +19,7 @@
     return lax.ppermute(value, axis, [(i, (i + step) % count) for i in range(count)])
 
 
-def edges(block):
+def edges(block, offset=None):
     sides = []
     for axis, dim in (("lat", 0), (COL, 1)):
         names = axis if isinstance(axis, tuple) else (axis,)
@@ -28,6 +28,10 @@
         backward = [(target, source) for source, target in forward]
         last = lax.slice_in_dim(block, block.shape[dim] - 1, None, axis=dim)
         first = lax.slice_in_dim(block, 0, 1, axis=dim)
+        if offset is not None:
+            count = offset.shape[dim]
+            last = last + lax.slice_in_dim(offset, count - 1, None, axis=dim)[:, :, None]
+            first = first + lax.slice_in_dim(offset, 0, 1, axis=dim)[:, :, None]
         sides.append(lax.ppermute(last, axis, forward))
         sides.append(lax.ppermute(first, axis, backward))
     return sides
@@ -86,10 +90,40 @@
     )(rates, block, *sides)
 
 
+def receiver_of(step, place, size_z, size_x):
+    ahead_z, ahead_x = step // size_x, step % size_x
+    return ((place[0] + ahead_z) % size_z) * size_x + (place[1] + ahead_x) % size_x
+
+
+def pick_rows(out, entry, slots, cell, weight, count, states):
+    def pick(group, carry):
+        for j in range(UNROLL):
+            slot = entry * slots + group * UNROLL + j
+            row, factor = cell[slot], weight[slot]
+            tile, line = group * (UNROLL // 8) + j // 8, j % 8
+            for k in range(2):
+                out[k, tile, line : line + 1, :] = states[k][pl.ds(row, 1), :] * factor
+        return carry
+
+    lax.fori_loop(0, (count[entry] + UNROLL - 1) // UNROLL, pick, 0)
+
+
+def own_kernel(size_z, size_x, place, cell, weight, count, first, second, out):
+    slots = 8 * out.shape[2]
+
+    def one(step, carry):
+        out[step] = jnp.zeros(out.shape[1:], jnp.float32)
+        receiver = receiver_of(step, place, size_z, size_x)
+        pick_rows(out.at[step], receiver, slots, cell, weight, count, (first, second))
+        return carry
+
+    lax.fori_loop(0, out.shape[0], one, 0)
+
+
 def bin_kernel(
-    size_z, size_x, owned, place, cell, weight, count, station, *rest
+    size_z, size_x, owned, place, cell, weight, count, station, held, first, second, *rest
 ):
-    states, (out_a, out_b, picked) = rest[:4], rest[4:]
+    out_a, out_b, picked = rest
     width = out_a.shape[3]
     cut = out_a.shape[2] - owned
     receivers, slots = size_z * size_x, station.shape[1]
@@ -97,32 +131,15 @@
     own = lax.broadcasted_iota(jnp.int32, (owned, slots), 0)
 
     def one(step, carry):
-        ahead_z, ahead_x = step // size_x, step % size_x
-        receiver = ((place[0] + ahead_z) % size_z) * size_x + (place[1] + ahead_x) % size_x
+        receiver = receiver_of(step, place, size_z, size_x)
+        pick_rows(picked, receivers + receiver, slots, cell, weight, count, (first, second))
         hots = []
         for e in range(2):
-            first, second = states[2 * e], states[2 * e + 1]
-            entry = e * receivers + receiver
-
-            def pick(group, inner):
-                for j in range(UNROLL):
-                    slot = entry * slots + group * UNROLL + j
-                    row, factor = cell[slot], weight[slot]
-                    tile, line = group * (UNROLL // 8) + j // 8, j % 8
-                    picked[e, 0, tile, line : line + 1, :] = first[pl.ds(row, 1), :] * factor
-                    picked[e, 1, tile, line : line + 1, :] = second[pl.ds(row, 1), :] * factor
-                return inner
-
-            lax.fori_loop(0, (count[entry] + UNROLL - 1) // UNROLL, pick, 0)
-            hit = station[pl.ds(entry, 1), :] == own
+            hit = station[pl.ds(e * receivers + receiver, 1), :] == own
             hots.append(jnp.where(hit, 1.0, 0.0).astype(jnp.bfloat16))
-        value = jnp.concatenate(
-            [
-                jnp.concatenate([picked[e, k].reshape(slots, width) for k in range(2)], axis=1)
-                for e in range(2)
-            ],
-            axis=0,
-        )
+        rows = [[held[step, k].reshape(slots, width) for k in range(2)]]
+        rows.append([picked[k].reshape(slots, width) for k in range(2)])
+        value = jnp.concatenate([jnp.concatenate(pair, axis=1) for pair in rows], axis=0)
         high = value.astype(jnp.bfloat16)
         low = (value - high.astype(jnp.float32)).astype(jnp.bfloat16)
         total = jnp.dot(
@@ -130,6 +147,7 @@
             jnp.concatenate([high, low], axis=0),
             preferred_element_type=jnp.float32,
         )
+        ahead_z, ahead_x = step // size_x, step % size_x
         out_a[ahead_x, ahead_z, :owned, :] = total[:, :width]
         out_a[ahead_x, ahead_z, owned:, :] = total[:cut, width:]
         out_b[ahead_z, ahead_x] = total[cut:, width:]
@@ -145,18 +163,28 @@
     rows_b = 2 * owned - rows_a
     scalar = pl.BlockSpec(memory_space=pltpu.SMEM)
     whole = pl.BlockSpec(memory_space=pltpu.VMEM)
+    held = pl.pallas_call(
+        functools.partial(own_kernel, size_z, size_x),
+        in_specs=[scalar] * 4 + [whole] * 2,
+        out_specs=whole,
+        out_shape=pltpu.VMEM((size_z * size_x, 2, slots // 8, 8, members), jnp.float32),
+        compiler_params=pltpu.CompilerParams(vmem_limit_bytes=24 * 2**20),
+        cost_estimate=pl.CostEstimate(
+            flops=10**8, bytes_accessed=20 * 2**20, transcendentals=0
+        ),
+    )(place, cell, weight, count, *states[:2])
     return pl.pallas_call(
         functools.partial(bin_kernel, size_z, size_x, owned),
-        in_specs=[scalar] * 4 + [whole] * 5,
+        in_specs=[scalar] * 4 + [whole] * 4,
         out_specs=[whole] * 2,
         out_shape=[
             pltpu.VMEM((size_x, size_z, rows_a, members), jnp.float32),
             pltpu.VMEM((size_z, size_x, rows_b, members), jnp.float32),
         ],
-        scratch_shapes=[pltpu.VMEM((2, 2, slots // 8, 8, members), jnp.float32)],
-        compiler_params=pltpu.CompilerParams(vmem_limit_bytes=48 * 2**20),
+        scratch_shapes=[pltpu.VMEM((2, slots // 8, 8, members), jnp.float32)],
+        compiler_params=pltpu.CompilerParams(vmem_limit_bytes=32 * 2**20),
         cost_estimate=pl.CostEstimate(flops=10**9, bytes_accessed=30 * 2**20, transcendentals=0),
-    )(place, cell, weight, count, station, *states)
+    )(place, cell, weight, count, station, held, *states[2:])
 
 
 def factor_kernel(root_scale, products, high, low):
@@ -221,6 +249,7 @@
     pushed = jnp.sum(inverse * push, axis=1, keepdims=True)
     offset = jnp.sum(inverse * pushed, axis=0, keepdims=True) * (1.0 / root_scale)
     weights = inverse + offset
+    weights = weights - jnp.mean(weights, axis=1, keepdims=True) + 1.0 / size
     top_half = weights.astype(jnp.bfloat16)
     high[...] = top_half
     low[...] = (weights - top_half.astype(jnp.float32)).astype(jnp.bfloat16)
@@ -233,37 +262,43 @@
         functools.partial(factor_kernel, root_scale),
         in_specs=[whole],
         out_specs=[whole] * 2,
-        out_shape=[jax.ShapeDtypeStruct((size, size), jnp.bfloat16)] * 2,
+        out_shape=[pltpu.VMEM((size, size), jnp.bfloat16)] * 2,
     )(products)
 
 
-def analysis_kernel(high, low, state, out):
-    value = state[...]
-    mean = jnp.mean(value, axis=1, keepdims=True)
-    departure = value - mean
-    near = departure.astype(jnp.bfloat16)
-    rest = (departure - near.astype(jnp.float32)).astype(jnp.bfloat16)
-
-    def times(a, b):
-        return lax.dot_general(
-            a, b[...], (((1,), (1,)), ((), ())), preferred_element_type=jnp.float32
-        )
-
-    out[...] = mean + (times(near, high) + (times(rest, high) + times(near, low)))
-
-
-def analyse(high, low, state):
+def analysis_kernel(high, low, state, observed, out, out_observed):
+    def update(value):
+        near = value.astype(jnp.bfloat16)
+        rest = (value - near.astype(jnp.float32)).astype(jnp.bfloat16)
+
+        def times(a, b):
+            return lax.dot_general(
+                a, b[...], (((1,), (1,)), ((), ())), preferred_element_type=jnp.float32
+            )
+
+        return times(near, high) + (times(rest, high) + times(near, low))
+
+    out[...] = update(state[...])
+
+    @pl.when(pl.program_id(0) == 0)
+    def _():
+        out_observed[...] = update(observed[...])
+
+
+def analyse(high, low, state, observed):
     rows, members = state.shape
-    size = min(rows, 1024)
-    block = pl.BlockSpec((size, members), lambda k: (k, 0))
     whole = pl.BlockSpec(memory_space=pltpu.VMEM)
+    block = pl.BlockSpec((rows // 8, members), lambda k: (k, 0))
     return pl.pallas_call(
         analysis_kernel,
-        grid=(rows // size,),
-        in_specs=[whole, whole, block],
-        out_specs=block,
-        out_shape=jax.ShapeDtypeStruct(state.shape, jnp.float32),
-    )(high, low, state)
+        grid=(8,),
+        in_specs=[whole, whole, block, whole],
+        out_specs=[block, pl.BlockSpec(observed.shape, lambda k: (0, 0))],
+        out_shape=[
+            jax.ShapeDtypeStruct(state.shape, jnp.float32),
+            jax.ShapeDtypeStruct(observed.shape, jnp.float32),
+        ],
+    )(high, low, state, observed)
 
 
 def ring_reduce(blocks, axis):
@@ -366,21 +401,20 @@
         ],
         axis=1,
     ).reshape(-1, member_count, control.shape[1])
-    first = advance(True, rates, perturbations, edges(perturbations + control[:, :, None]))
-    second = advance(False, rates, first, edges(first))
-    flat = [state.reshape(-1, member_count) for state in (first, second)]
-    paired = [shift(state, "core", 1) for state in flat]
+    first = advance(True, rates, perturbations, edges(perturbations, control))
     index = jnp.concatenate([index_own, index_pair], axis=0)
     weight = jnp.concatenate([weight_own, weight_pair], axis=0)
-    blocks = bin_rows(
-        place,
+    tables = (
         index[:, :slots].reshape(-1),
         weight.reshape(-1),
         index[:, 2 * slots],
         index[:, slots : 2 * slots],
-        flat + paired,
-        owned_count,
-    )
+    )
+    sides, tables = lax.optimization_barrier((edges(first), tables))
+    second = advance(False, rates, first, sides)
+    flat = [state.reshape(-1, member_count) for state in (first, second)]
+    paired = [shift(state, "core", 1) for state in flat]
+    blocks = bin_rows(place, *tables, flat + paired, owned_count)
     observed = reduce_to_owner(*blocks).reshape(step_total, owned_count, member_count)
 
     root_scale = math.sqrt(member_count - 1.0)
@@ -397,8 +431,9 @@
     )
     products = sum_everywhere(products)
     high, low = transposed_weights(products, root_scale)
-    analysis = analyse(high, low, flat[-1])
-    obs_analysis = analyse(high, low, observed.reshape(-1, member_count))
+    analysis, obs_analysis = analyse(
+        high, low, flat[-1], observed.reshape(-1, member_count)
+    )
     return (analysis.reshape(perturbations.shape), obs_analysis.reshape(observed.shape))
 
 

time: 248 us -> 244 us (0.984)
  waiting for transfers between devices: 62 us -> 53.9 us
  starting transfers between devices: 68.1 us -> 72.9 us
  local copies, waits for them, and re-layouts: 6.42 us -> 10 us
  other arithmetic: 9.96 us -> 7.36 us
    ppermute x30, waiting for transfers between devices: 56.8 us -> 48.1 us  [shift(): lax.ppermute(value, axis, [(i, (i + step) % count) for i in range(count)])]
    ppermute x30, starting transfers between devices: 47 us -> 54.5 us  [shift(): lax.ppermute(value, axis, [(i, (i + step) % count) for i in range(count)])]
    pallas_call x1, Pallas kernels: 23.7 us -> 16.6 us  [bin_rows(): pl.pallas_call(functools.partial(bin_kernel, size_z, size_x, owned), in_s...]
    pallas_call x2, Pallas kernels: 9.98 us -> 16.9 us  [the longest x1 8.72 us: bin_rows(): pl.pallas_call(functools.partial(own_kernel, size_z, size_x), in_specs=[s...]
    ppermute x4, starting transfers between devices: 14.5 us -> 11.7 us  [edges(): sides.append(lax.ppermute(last, axis, forward))]
  transfers between devices with their start and end apart: 38 -> 38, of which waited for: 17 -> 16; matrix products, arithmetic and copies ran while one was open for 3% -> 3% of each run, Pallas kernels for 5% -> 14%
where the time goes in v4:
time: 244 us; the launch traced here: 243 us
  starting transfers between devices  72.9 us (30%)
  Pallas kernels  63.6 us (26%)
  waiting for transfers between devices  53.9 us (22%)
  blocking collectives  32.8 us (13%)
  local copies, waits for them, and re-layouts  10 us (4%)
  other arithmetic  7.36 us (3%)
    ppermute x30, starting transfers between devices, shift(): lax.ppermute(value, axis, [(i, (i + step) % count) for i in range(count)])  54.5 us
    ppermute x30, waiting for transfers between devices, shift(): lax.ppermute(value, axis, [(i, (i + step) % count) for i in range(count)])  48.1 us
    all_to_all x3, blocking collectives, spread_sum(): lax.all_to_all(copies, axis, split_axis=0, concat_axis=0, tiled=True)  32.8 us
    pallas_call x2, Pallas kernels, advance(): pl.pallas_call(functools.partial(advance_kernel, adds), in_specs=[whole]...  24.3 us
    pallas_call x1, Pallas kernels, bin_rows(): pl.pallas_call(functools.partial(bin_kernel, size_z, size_x, owned), in_s...  16.6 us
    ppermute x4, starting transfers between devices, edges(): sides.append(lax.ppermute(last, axis, forward))  11.7 us
    pallas_call x1, Pallas kernels, bin_rows(): pl.pallas_call(functools.partial(own_kernel, size_z, size_x), in_specs=[s...  8.72 us
    pallas_call x1, Pallas kernels, analyse(): pl.pallas_call(analysis_kernel, grid=(8,), in_specs=[whole, whole, block,...  8.18 us
  transfers between devices with their start and end apart: 38, of which 16 were waited for; matrix products, arithmetic and copies ran while one was open for 3% of the time, Pallas kernels for 14%

profile of v4, /device:TPU:1, one launch (start us, length us, event | category | flops | bytes accessed | tf_op | source)
XLA Modules:
  0.0 242.8 jit_solution(9027488412084002013)
XLA Ops:
  1.2 1.3 reduce.10
  2.7 0.8 copy.37
  3.5 0.8 copy_select_fusion
  4.4 3.3 %collective-permute-start.8 = (s32[32,384]{1,0:T(8,128)S(1)}, s32[32,384]{1,0:T(8,128)S(1)}, u32[]{:S(2)}, u32[]{:S(2)}) collective-permute-start(s32[32,384]{1,0:T(8,128)S(1)} %get-tuple-element.78), channel_id=1, source_target_pairs={{0,1},{1,0},{2,3},{3,2},{4,5},{5,4},{6,7},{7,6},{8,9},{9,8},{10,11... | collective-permute-start | bytes 147464 | tf_op jit(solution)/shard_map/ppermute | solution.py:19
  7.7 0.9 constant_dynamic-slice_fusion.1
  8.7 0.7 fusion.33
  9.4 1.1 slice_add_fusion.4
  10.5 1.5 collective-permute-start
  12.0 1.3 collective-permute-start.1
  13.5 1.1 slice_add_fusion.6
  14.6 3.8 %collective-permute-start.2 = (f32[32,1,128]{2,1,0:T(1,128)S(1)}, f32[32,1,128]{2,1,0:T(1,128)S(1)}, u32[]{:S(2)}, u32[]{:S(2)}) collective-permute-start(f32[32,1,128]{2,1,0:T(1,128)S(1)} %get-tuple-element.40), channel_id=1, source_target_pairs={{0,1},{1,2},{2,3},{3,4},{4,5},{5,6},{6,7},{7,8},{8,9},{9,10},{10,1... | collective-permute-start | bytes 49160 | tf_op jit(solution)/shard_map/ppermute | solution.py:35
  19.1 1.9 collective-permute-start.3
  21.0 3.1 %collective-permute-done.3.right = f32[32,1,128]{2,1,0:T(1,128)S(1)} collective-permute-done((f32[32,1,128]{2,1,0:T(1,128)S(1)}, f32[32,1,128]{2,1,0:T(1,128)S(1)}, u32[]{:S(2)}, u32[]{:S(2)}) %collective-permute-start.3) | collective-permute-done | bytes 16416 | tf_op jit(solution)/shard_map/ppermute | solution.py:36
  24.1 2.2 copy-done
  26.3 12.6 %shard_map.122.block = f32[32,256,128]{2,1,0:T(8,128)} custom-call(f32[2,128,256]{2,1,0:T(8,128)S(1)} %bitcast.128, f32[32,256,128]{2,1,0:T(8,128)S(1)} %copy-done, f32[1,256,128]{2,1,0:T(8,128)S(1)} %collective-permute-done.above, f32[1,256,128]{2,1,0:T(8,128)S(1)} %collective-permute-done.1.below, f32[32,1,128]{2,1,0:T(1,128)S(1)} %collective-permute-done.2.left, ...), custom_call_target="tpu_custom_call" | custom-call | flops 12582912 | bytes 8388608 | tf_op jit(solution)/shard_map/pallas_call | solution.py:77
  38.9 1.0 fusion.28
  39.9 4.3 %collective-permute-start.4 = (f32[1,256,128]{2,1,0:T(8,128)S(1)}, f32[1,256,128]{2,1,0:T(8,128)S(1)}, u32[]{:S(2)}, u32[]{:S(2)}) collective-permute-start(f32[1,256,128]{2,1,0:T(8,128)S(1)} %get-tuple-element.38), channel_id=1, source_target_pairs={{0,64},{64,128},{128,192},{1,65},{65,129},{129,193},{2,66},{66,130... | collective-permute-start | bytes 393224 | tf_op jit(solution)/shard_map/ppermute | solution.py:35
  44.2 1.3 collective-permute-start.5
  45.5 1.0 fusion.27
  46.5 2.2 collective-permute-start.6
  48.7 2.1 collective-permute-start.7
  51.0 2.7 %collective-permute-done.7.right = f32[32,1,128]{2,1,0:T(1,128)S(1)} collective-permute-done((f32[32,1,128]{2,1,0:T(1,128)S(1)}, f32[32,1,128]{2,1,0:T(1,128)S(1)}, u32[]{:S(2)}, u32[]{:S(2)}) %collective-permute-start.7) | collective-permute-done | bytes 16416 | tf_op jit(solution)/shard_map/ppermute | solution.py:36
  53.7 11.7 %shard_map.123 = f32[32,256,128]{2,1,0:T(8,128)} custom-call(f32[2,128,256]{2,1,0:T(8,128)S(1)} %bitcast.129, f32[32,256,128]{2,1,0:T(8,128)} %shard_map.122.block, f32[1,256,128]{2,1,0:T(8,128)S(1)} %collective-permute-done.4.above, f32[1,256,128]{2,1,0:T(8,128)S(1)} %collective-permute-done.5.below, f32[32,1,128]{2,1,0:T(1,128)S(1)} %collective-permute-done.6.left, ...), custom_call_target="tpu_custom_call" | custom-call | flops 12582912 | bytes 8388608 | tf_op jit(solution)/shard_map/pallas_call | solution.py:77
  65.5 8.7 %shard_map.124.held = f32[32,2,16,8,128]{4,3,2,1,0:T(8,128)S(1)} custom-call(s32[2]{0:T(128)S(1)} %pad_add_fusion.2.place, s32[8192]{0:T(1024)S(1)} %get-tuple-element.16.cell, f32[8192]{0:T(1024)S(1)} %maximum_bitcast_fusion.weight, s32[64]{0:T(128)S(1)} %fusion.21.count, f32[8192,128]{1,0:T(8,128)} %bitcast.19.first, f32[8192,128]{1,0:T(8,128)} %bitcast.20.second.state), custom_call_target="tpu_custom_call" | custom-call | flops 100000000 | bytes 20971520 | tf_op jit(solution)/shard_map/pallas_call | solution.py:166
  74.3 16.6 %shard_map.125 = (f32[4,8,288,128]{3,2,1,0:T(8,128)S(1)}, f32[8,4,224,128]{3,2,1,0:T(8,128)S(1)}) custom-call(s32[2]{0:T(128)S(1)} %pad_add_fusion.2.place, s32[8192]{0:T(1024)S(1)} %get-tuple-element.16.cell, f32[8192]{0:T(1024)S(1)} %maximum_bitcast_fusion.weight, s32[64]{0:T(128)S(1)} %fusion.21.count, s32[64,128]{1,0:T(8,128)S(1)} %get-tuple-element.19.station, ...), custom_call_target="tpu_custom_call" | custom-call | flops 1000000000 | bytes 31457280 | tf_op jit(solution)/shard_map/pallas_call | solution.py:176
  91.2 5.5 %collective-permute-start.24 = (f32[4,112,128]{2,1,0:T(8,128)S(1)}, f32[4,112,128]{2,1,0:T(8,128)S(1)}, u32[]{:S(2)}, u32[]{:S(2)}) collective-permute-start(f32[4,112,128]{2,1,0:T(8,128)S(1)} %get-tuple-element.70), channel_id=1, source_target_pairs={{0,8},{8,16},{16,24},{24,32},{32,40},{40,48},{48,56},{56,0},{1,9},... | collective-permute-start | bytes 688136 | tf_op jit(solution)/shard_map/ppermute | solution.py:19
  96.9 3.5 %collective-permute-start.14 = (f32[8,144,128]{2,1,0:T(8,128)S(1)}, f32[8,144,128]{2,1,0:T(8,128)S(1)}, u32[]{:S(2)}, u32[]{:S(2)}) collective-permute-start(f32[8,144,128]{2,1,0:T(8,128)S(1)} %get-tuple-element.59), channel_id=1, source_target_pairs={{0,6},{2,0},{4,2},{6,4},{1,7},{3,1},{5,3},{7,5},{8,14},{10,8},{12,... | collective-permute-start | bytes 1769480 | tf_op jit(solution)/shard_map/ppermute | solution.py:19
  100.4 2.5 %collective-permute-start.28 = (f32[4,112,128]{2,1,0:T(8,128)S(1)}, f32[4,112,128]{2,1,0:T(8,128)S(1)}, u32[]{:S(2)}, u32[]{:S(2)}) collective-permute-start(f32[4,112,128]{2,1,0:T(8,128)S(1)} %get-tuple-element.71), channel_id=1, source_target_pairs={{0,56},{8,0},{16,8},{24,16},{32,24},{40,32},{48,40},{56,48},{1,57}... | collective-permute-start | bytes 688136 | tf_op jit(solution)/shard_map/ppermute | solution.py:19
  102.9 2.5 %collective-permute-done.24 = f32[4,112,128]{2,1,0:T(8,128)S(1)} collective-permute-done((f32[4,112,128]{2,1,0:T(8,128)S(1)}, f32[4,112,128]{2,1,0:T(8,128)S(1)}, u32[]{:S(2)}, u32[]{:S(2)}) %collective-permute-start.24) | collective-permute-done | bytes 229408 | tf_op jit(solution)/shard_map/ppermute | solution.py:19
  105.6 6.9 %collective-permute-done.12 = f32[8,144,128]{2,1,0:T(8,128)S(1)} collective-permute-done((f32[8,144,128]{2,1,0:T(8,128)S(1)}, f32[8,144,128]{2,1,0:T(8,128)S(1)}, u32[]{:S(2)}, u32[]{:S(2)}) %collective-permute-start.12) | collective-permute-done | bytes 589856 | tf_op jit(solution)/shard_map/ppermute | solution.py:19
  113.0 2.7 %collective-permute-start.15 = (f32[8,288,128]{2,1,0:T(8,128)S(1)}, f32[8,288,128]{2,1,0:T(8,128)S(1)}, u32[]{:S(2)}, u32[]{:S(2)}) collective-permute-start(f32[8,288,128]{2,1,0:T(8,128)S(1)} %pad_maximum_fusion.1), channel_id=1, source_target_pairs={{0,6},{2,0},{4,2},{6,4},{1,7},{3,1},{5,3},{7,5},{8,14},{10,8},{12,... | collective-permute-start | bytes 3538952 | tf_op jit(solution)/shard_map/ppermute | solution.py:19
  115.8 3.3 %collective-permute-start.29 = (f32[4,224,128]{2,1,0:T(8,128)S(1)}, f32[4,224,128]{2,1,0:T(8,128)S(1)}, u32[]{:S(2)}, u32[]{:S(2)}) collective-permute-start(f32[4,224,128]{2,1,0:T(8,128)S(1)} %pad_maximum_fusion.3), channel_id=1, source_target_pairs={{0,56},{8,0},{16,8},{24,16},{32,24},{40,32},{48,40},{56,48},{1,57}... | collective-permute-start | bytes 1376264 | tf_op jit(solution)/shard_map/ppermute | solution.py:19
  119.7 9.2 %collective-permute-done.29 = f32[4,224,128]{2,1,0:T(8,128)S(1)} collective-permute-done((f32[4,224,128]{2,1,0:T(8,128)S(1)}, f32[4,224,128]{2,1,0:T(8,128)S(1)}, u32[]{:S(2)}, u32[]{:S(2)}) %collective-permute-start.29) | collective-permute-done | bytes 458784 | tf_op jit(solution)/shard_map/ppermute | solution.py:19
  128.8 1.5 collective-permute-done.26
  130.5 4.2 %collective-permute-start.27 = (f32[4,224,128]{2,1,0:T(8,128)S(1)}, f32[4,224,128]{2,1,0:T(8,128)S(1)}, u32[]{:S(2)}, u32[]{:S(2)}) collective-permute-start(f32[4,224,128]{2,1,0:T(8,128)S(1)} %get-tuple-element.43), channel_id=1, source_target_pairs={{0,8},{8,16},{16,24},{24,32},{32,40},{40,48},{48,56},{56,0},{1,9},... | collective-permute-start | bytes 1376264 | tf_op jit(solution)/shard_map/ppermute | solution.py:19
  134.7 4.6 %collective-permute-done.13 = f32[8,288,128]{2,1,0:T(8,128)S(1)} collective-permute-done((f32[8,288,128]{2,1,0:T(8,128)S(1)}, f32[8,288,128]{2,1,0:T(8,128)S(1)}, u32[]{:S(2)}, u32[]{:S(2)}) %collective-permute-start.13) | collective-permute-done | bytes 1179680 | tf_op jit(solution)/shard_map/ppermute | solution.py:19
  139.5 4.9 %collective-permute-start.16 = (f32[144,128]{1,0:T(8,128)S(1)}, f32[144,128]{1,0:T(8,128)S(1)}, u32[]{:S(2)}, u32[]{:S(2)}) collective-permute-start(f32[144,128]{1,0:T(8,128)S(1)} %get-tuple-element.52), channel_id=1, source_target_pairs={{0,8},{8,16},{16,24},{24,32},{32,40},{40,48},{48,56},{56,0},{1,9},... | collective-permute-start | bytes 221192 | tf_op jit(solution)/shard_map/ppermute | solution.py:19
  144.5 0.5 collective-permute-start.31
  145.1 0.8 collective-permute-done.16
  145.9 5.9 %collective-permute-done.20 = f32[144,128]{1,0:T(8,128)S(1)} collective-permute-done((f32[144,128]{1,0:T(8,128)S(1)}, f32[144,128]{1,0:T(8,128)S(1)}, u32[]{:S(2)}, u32[]{:S(2)}) %collective-permute-start.20) | collective-permute-done | bytes 73760 | tf_op jit(solution)/shard_map/ppermute | solution.py:19
  151.9 1.5 collective-permute-start.17
  153.4 7.2 %collective-permute-done.31 = f32[4,224,128]{2,1,0:T(8,128)S(1)} collective-permute-done((f32[4,224,128]{2,1,0:T(8,128)S(1)}, f32[4,224,128]{2,1,0:T(8,128)S(1)}, u32[]{:S(2)}, u32[]{:S(2)}) %collective-permute-start.31) | collective-permute-done | bytes 458784 | tf_op jit(solution)/shard_map/ppermute | solution.py:19
  160.9 2.7 %collective-permute-start.34 = (f32[112,128]{1,0:T(8,128)S(1)}, f32[112,128]{1,0:T(8,128)S(1)}, u32[]{:S(2)}, u32[]{:S(2)}) collective-permute-start(f32[112,128]{1,0:T(8,128)S(1)} %get-tuple-element.65), channel_id=1, source_target_pairs={{0,6},{2,0},{4,2},{6,4},{1,7},{3,1},{5,3},{7,5},{8,14},{10,8},{12,... | collective-permute-start | bytes 172040 | tf_op jit(solution)/shard_map/ppermute | solution.py:19
  163.6 1.3 collective-permute-start.18
  165.1 3.7 %collective-permute-done.18 = f32[288,128]{1,0:T(8,128)S(1)} collective-permute-done((f32[288,128]{1,0:T(8,128)S(1)}, f32[288,128]{1,0:T(8,128)S(1)}, u32[]{:S(2)}, u32[]{:S(2)}) %collective-permute-start.18) | collective-permute-done | bytes 147488 | tf_op jit(solution)/shard_map/ppermute | solution.py:19
  169.1 2.7 %collective-permute-start.35 = (f32[224,128]{1,0:T(8,128)S(1)}, f32[224,128]{1,0:T(8,128)S(1)}, u32[]{:S(2)}, u32[]{:S(2)}) collective-permute-start(f32[224,128]{1,0:T(8,128)S(1)} %pad_maximum_fusion.8), channel_id=1, source_target_pairs={{0,6},{2,0},{4,2},{6,4},{1,7},{3,1},{5,3},{7,5},{8,14},{10,8},{12,... | collective-permute-start | bytes 344072 | tf_op jit(solution)/shard_map/ppermute | solution.py:19
  171.9 1.4 collective-permute-start.19
  173.3 1.5 collective-permute-start.23
  174.9 2.2 collective-permute-done.19
  177.1 1.5 collective-permute-done.23
  178.6 0.7 pad_maximum_fusion.4
  179.7 1.0 fusion.1
  180.7 7.1 %collective-permute-start.36 = (f32[144,128]{1,0:T(8,128)S(1)}, f32[144,128]{1,0:T(8,128)S(1)}, u32[]{:S(2)}, u32[]{:S(2)}) collective-permute-start(f32[144,128]{1,0:T(8,128)S(1)} %fusion.1), channel_id=1, source_target_pairs={{0,1},{1,0},{2,3},{3,2},{4,5},{5,4},{6,7},{7,6},{8,9},{9,8},{10,11... | collective-permute-start | bytes 221192 | tf_op jit(solution)/shard_map/ppermute | solution.py:19
  187.8 0.9 collective-permute-done.36
  188.8 7.3 %all_to_all.15 = f32[4,72,128]{2,1,0:T(8,128)S(1)} all-to-all(f32[4,72,128]{2,1,0:T(8,128)S(1)} %broadcast_in_dim.14), channel_id=1, replica_groups=mesh['lat'=4,'z'=8,'x'=4,'core'=2] {'x'}, dimensions={0} | all-to-all | bytes 294912 | tf_op jit(solution)/shard_map/all_to_all | solution.py:334
  196.1 8.8 %all_to_all.16 = f32[4,72,128]{2,1,0:T(8,128)S(1)} all-to-all(f32[4,72,128]{2,1,0:T(8,128)S(1)} %broadcast_in_dim.15), channel_id=1, replica_groups=mesh['lat'=4,'z'=8,'x'=4,'core'=2] {'lat'}, dimensions={0} | all-to-all | bytes 294912 | tf_op jit(solution)/shard_map/all_to_all | solution.py:334
  204.9 16.7 %all_to_all.17 = f32[8,72,128]{2,1,0:T(8,128)S(1)} all-to-all(f32[8,72,128]{2,1,0:T(8,128)S(1)} %broadcast_in_dim.16), channel_id=1, replica_groups=mesh['lat'=4,'z'=8,'x'=4,'core'=2] {'z'}, dimensions={0} | all-to-all | bytes 589824 | tf_op jit(solution)/shard_map/all_to_all | solution.py:334
  221.7 4.4 %collective-permute-start.37 = (f32[72,128]{1,0:T(8,128)S(1)}, f32[72,128]{1,0:T(8,128)S(1)}, u32[]{:S(2)}, u32[]{:S(2)}) collective-permute-start(f32[72,128]{1,0:T(8,128)S(1)} %reduce_sum.39), channel_id=1, source_target_pairs={{0,1},{1,0},{2,3},{3,2},{4,5},{5,4},{6,7},{7,6},{8,9},{9,8},{10,11... | collective-permute-start | bytes 110600 | tf_op jit(solution)/shard_map/ppermute | solution.py:19
  226.1 0.9 collective-permute-done.37
  227.0 0.6 maximum_select_fusion.products
  227.6 5.8 %shard_map.126 = (bf16[128,128]{1,0:T(8,128)(2,1)S(1)}, bf16[128,128]{1,0:T(8,128)(2,1)S(1)}) custom-call(f32[144,128]{1,0:T(8,128)} %maximum_select_fusion.products), custom_call_target="tpu_custom_call" | custom-call | tf_op jit(solution)/shard_map/pallas_call | solution.py:261
  233.4 0.6 copy-done.1
  234.0 0.6 copy-done.2
  234.7 8.2 %shard_map.127 = (f32[8192,128]{1,0:T(8,128)}, f32[512,128]{1,0:T(8,128)}) custom-call(bf16[128,128]{1,0:T(8,128)(2,1)} %copy-done.1, bf16[128,128]{1,0:T(8,128)(2,1)} %copy-done.2, f32[8192,128]{1,0:T(8,128)} %bitcast.20.second.state, f32[512,128]{1,0:T(8,128)} %get-tuple-element.74.observed), custom_call_target="tpu_custom_call" | custom-call | tf_op jit(solution)/shard_map/pallas_call | solution.py:292
  (117 shorter events, 5.6 us)
Async XLA Ops:
  0.6 12.7 %copy-start.3 = (f32[32,256]{1,0:T(8,128)S(1)}, f32[32,256]{1,0:T(8,128)}, u32[]{:S(2)}) copy-start(f32[32,256]{1,0:T(8,128)} %param.11) | copy-start | bytes 98308
  0.6 17.8 %copy-start.6 = (f32[32,256]{1,0:T(8,128)S(1)}, f32[32,256]{1,0:T(8,128)}, u32[]{:S(2)}) copy-start(f32[32,256]{1,0:T(8,128)} %param.13) | copy-start | bytes 98308
  0.7 17.8 %copy-start.5 = (f32[32,256]{1,0:T(8,128)S(1)}, f32[32,256]{1,0:T(8,128)}, u32[]{:S(2)}) copy-start(f32[32,256]{1,0:T(8,128)} %param.14) | copy-start | bytes 98308
  0.7 17.8 %copy-start.4 = (f32[32,256]{1,0:T(8,128)S(1)}, f32[32,256]{1,0:T(8,128)}, u32[]{:S(2)}) copy-start(f32[32,256]{1,0:T(8,128)} %param.15) | copy-start | bytes 98308
  4.4 46.4 %collective-permute-start.8 = (s32[32,384]{1,0:T(8,128)S(1)}, s32[32,384]{1,0:T(8,128)S(1)}, u32[]{:S(2)}, u32[]{:S(2)}) collective-permute-start(s32[32,384]{1,0:T(8,128)S(1)} %get-tuple-element.78), channel_id=1, source_target_pairs={{0,1},{1,0},{2,3},{3,2},{4,5},{5,4},{6,7},{7,6},{8,9},{9,8},{10,11... | collective-permute-start | bytes 147464 | tf_op jit(solution)/shard_map/ppermute | solution.py:19
  8.6 10.5 %collective-permute-start.9 = (f32[32,128]{1,0:T(8,128)S(1)}, f32[32,128]{1,0:T(8,128)S(1)}, u32[]{:S(2)}, u32[]{:S(2)}) collective-permute-start(f32[32,128]{1,0:T(8,128)S(1)} %bitcast.136), channel_id=1, source_target_pairs={{0,1},{1,0},{2,3},{3,2},{4,5},{5,4},{6,7},{7,6},{8,9},{9,8},{10,11... | collective-permute-start | bytes 49160 | tf_op jit(solution)/shard_map/ppermute | solution.py:19
  10.5 13.6 %collective-permute-start = (f32[1,256,128]{2,1,0:T(8,128)S(1)}, f32[1,256,128]{2,1,0:T(8,128)S(1)}, u32[]{:S(2)}, u32[]{:S(2)}) collective-permute-start(f32[1,256,128]{2,1,0:T(8,128)S(1)} %get-tuple-element.42), channel_id=1, source_target_pairs={{0,64},{64,128},{128,192},{1,65},{65,129},{129,193},{2,66},{66,130... | collective-permute-start | bytes 393224 | tf_op jit(solution)/shard_map/ppermute | solution.py:35
  12.0 12.1 %collective-permute-start.1 = (f32[1,256,128]{2,1,0:T(8,128)S(1)}, f32[1,256,128]{2,1,0:T(8,128)S(1)}, u32[]{:S(2)}, u32[]{:S(2)}) collective-permute-start(f32[1,256,128]{2,1,0:T(8,128)S(1)} %get-tuple-element.41), channel_id=1, source_target_pairs={{64,0},{128,64},{192,128},{65,1},{129,65},{193,129},{66,2},{130,66... | collective-permute-start | bytes 393224 | tf_op jit(solution)/shard_map/ppermute | solution.py:36
  14.6 6.4 %collective-permute-start.2 = (f32[32,1,128]{2,1,0:T(1,128)S(1)}, f32[32,1,128]{2,1,0:T(1,128)S(1)}, u32[]{:S(2)}, u32[]{:S(2)}) collective-permute-start(f32[32,1,128]{2,1,0:T(1,128)S(1)} %get-tuple-element.40), channel_id=1, source_target_pairs={{0,1},{1,2},{2,3},{3,4},{4,5},{5,6},{6,7},{7,8},{8,9},{9,10},{10,1... | collective-permute-start | bytes 49160 | tf_op jit(solution)/shard_map/ppermute | solution.py:35
  19.1 5.1 %collective-permute-start.3 = (f32[32,1,128]{2,1,0:T(1,128)S(1)}, f32[32,1,128]{2,1,0:T(1,128)S(1)}, u32[]{:S(2)}, u32[]{:S(2)}) collective-permute-start(f32[32,1,128]{2,1,0:T(1,128)S(1)} %get-tuple-element.39), channel_id=1, source_target_pairs={{1,0},{2,1},{3,2},{4,3},{5,4},{6,5},{7,6},{8,7},{9,8},{10,9},{11,1... | collective-permute-start | bytes 49160 | tf_op jit(solution)/shard_map/ppermute | solution.py:36
  24.1 2.2 copy-start
  39.9 13.9 %collective-permute-start.4 = (f32[1,256,128]{2,1,0:T(8,128)S(1)}, f32[1,256,128]{2,1,0:T(8,128)S(1)}, u32[]{:S(2)}, u32[]{:S(2)}) collective-permute-start(f32[1,256,128]{2,1,0:T(8,128)S(1)} %get-tuple-element.38), channel_id=1, source_target_pairs={{0,64},{64,128},{128,192},{1,65},{65,129},{129,193},{2,66},{66,130... | collective-permute-start | bytes 393224 | tf_op jit(solution)/shard_map/ppermute | solution.py:35
  44.2 9.6 %collective-permute-start.5 = (f32[1,256,128]{2,1,0:T(8,128)S(1)}, f32[1,256,128]{2,1,0:T(8,128)S(1)}, u32[]{:S(2)}, u32[]{:S(2)}) collective-permute-start(f32[1,256,128]{2,1,0:T(8,128)S(1)} %get-tuple-element.37), channel_id=1, source_target_pairs={{64,0},{128,64},{192,128},{65,1},{129,65},{193,129},{66,2},{130,66... | collective-permute-start | bytes 393224 | tf_op jit(solution)/shard_map/ppermute | solution.py:36
  46.5 4.6 %collective-permute-start.6 = (f32[32,1,128]{2,1,0:T(1,128)S(1)}, f32[32,1,128]{2,1,0:T(1,128)S(1)}, u32[]{:S(2)}, u32[]{:S(2)}) collective-permute-start(f32[32,1,128]{2,1,0:T(1,128)S(1)} %get-tuple-element.36), channel_id=1, source_target_pairs={{0,1},{1,2},{2,3},{3,4},{4,5},{5,6},{6,7},{7,8},{8,9},{9,10},{10,1... | collective-permute-start | bytes 49160 | tf_op jit(solution)/shard_map/ppermute | solution.py:35
  48.7 5.1 %collective-permute-start.7 = (f32[32,1,128]{2,1,0:T(1,128)S(1)}, f32[32,1,128]{2,1,0:T(1,128)S(1)}, u32[]{:S(2)}, u32[]{:S(2)}) collective-permute-start(f32[32,1,128]{2,1,0:T(1,128)S(1)} %get-tuple-element.35), channel_id=1, source_target_pairs={{1,0},{2,1},{3,2},{4,3},{5,4},{6,5},{7,6},{8,7},{9,8},{10,9},{11,1... | collective-permute-start | bytes 49160 | tf_op jit(solution)/shard_map/ppermute | solution.py:36
  50.9 23.3 %collective-permute-start.10 = (f32[8192,128]{1,0:T(8,128)}, f32[8192,128]{1,0:T(8,128)}, u32[]{:S(2)}, u32[]{:S(2)}) collective-permute-start(f32[8192,128]{1,0:T(8,128)} %bitcast.19.first), channel_id=1, source_target_pairs={{0,1},{1,0},{2,3},{3,2},{4,5},{5,4},{6,7},{7,6},{8,9},{9,8},{10,11... | collective-permute-start | bytes 12582920 | tf_op jit(solution)/shard_map/ppermute | solution.py:19
  65.5 8.8 %collective-permute-start.11 = (f32[8192,128]{1,0:T(8,128)}, f32[8192,128]{1,0:T(8,128)}, u32[]{:S(2)}, u32[]{:S(2)}) collective-permute-start(f32[8192,128]{1,0:T(8,128)} %bitcast.20.second.state), channel_id=1, source_target_pairs={{0,1},{1,0},{2,3},{3,2},{4,5},{5,4},{6,7},{7,6},{8,9},{9,8},{10,11... | collective-permute-start | bytes 12582920 | tf_op jit(solution)/shard_map/ppermute | solution.py:19
  91.2 14.2 %collective-permute-start.24 = (f32[4,112,128]{2,1,0:T(8,128)S(1)}, f32[4,112,128]{2,1,0:T(8,128)S(1)}, u32[]{:S(2)}, u32[]{:S(2)}) collective-permute-start(f32[4,112,128]{2,1,0:T(8,128)S(1)} %get-tuple-element.70), channel_id=1, source_target_pairs={{0,8},{8,16},{16,24},{24,32},{32,40},{40,48},{48,56},{56,0},{1,9},... | collective-permute-start | bytes 688136 | tf_op jit(solution)/shard_map/ppermute | solution.py:19
  96.8 15.7 %collective-permute-start.12 = (f32[8,144,128]{2,1,0:T(8,128)S(1)}, f32[8,144,128]{2,1,0:T(8,128)S(1)}, u32[]{:S(2)}, u32[]{:S(2)}) collective-permute-start(f32[8,144,128]{2,1,0:T(8,128)S(1)} %get-tuple-element.58), channel_id=1, source_target_pairs={{0,2},{2,4},{4,6},{6,0},{1,3},{3,5},{5,7},{7,1},{8,10},{10,12},{12... | collective-permute-start | bytes 1769480 | tf_op jit(solution)/shard_map/ppermute | solution.py:19
  96.9 15.9 %collective-permute-start.14 = (f32[8,144,128]{2,1,0:T(8,128)S(1)}, f32[8,144,128]{2,1,0:T(8,128)S(1)}, u32[]{:S(2)}, u32[]{:S(2)}) collective-permute-start(f32[8,144,128]{2,1,0:T(8,128)S(1)} %get-tuple-element.59), channel_id=1, source_target_pairs={{0,6},{2,0},{4,2},{6,4},{1,7},{3,1},{5,3},{7,5},{8,14},{10,8},{12,... | collective-permute-start | bytes 1769480 | tf_op jit(solution)/shard_map/ppermute | solution.py:19
  100.4 15.3 %collective-permute-start.28 = (f32[4,112,128]{2,1,0:T(8,128)S(1)}, f32[4,112,128]{2,1,0:T(8,128)S(1)}, u32[]{:S(2)}, u32[]{:S(2)}) collective-permute-start(f32[4,112,128]{2,1,0:T(8,128)S(1)} %get-tuple-element.71), channel_id=1, source_target_pairs={{0,56},{8,0},{16,8},{24,16},{32,24},{40,32},{48,40},{56,48},{1,57}... | collective-permute-start | bytes 688136 | tf_op jit(solution)/shard_map/ppermute | solution.py:19
  105.5 13.5 %collective-permute-start.25 = (f32[4,224,128]{2,1,0:T(8,128)S(1)}, f32[4,224,128]{2,1,0:T(8,128)S(1)}, u32[]{:S(2)}, u32[]{:S(2)}) collective-permute-start(f32[4,224,128]{2,1,0:T(8,128)S(1)} %pad_maximum_fusion.2), channel_id=1, source_target_pairs={{0,8},{8,16},{16,24},{24,32},{32,40},{40,48},{48,56},{56,0},{1,9},... | collective-permute-start | bytes 1376264 | tf_op jit(solution)/shard_map/ppermute | solution.py:19
  112.7 26.6 %collective-permute-start.13 = (f32[8,288,128]{2,1,0:T(8,128)S(1)}, f32[8,288,128]{2,1,0:T(8,128)S(1)}, u32[]{:S(2)}, u32[]{:S(2)}) collective-permute-start(f32[8,288,128]{2,1,0:T(8,128)S(1)} %pad_maximum_fusion), channel_id=1, source_target_pairs={{0,2},{2,4},{4,6},{6,0},{1,3},{3,5},{5,7},{7,1},{8,10},{10,12},{12... | collective-permute-start | bytes 3538952 | tf_op jit(solution)/shard_map/ppermute | solution.py:19
  113.0 26.3 %collective-permute-start.15 = (f32[8,288,128]{2,1,0:T(8,128)S(1)}, f32[8,288,128]{2,1,0:T(8,128)S(1)}, u32[]{:S(2)}, u32[]{:S(2)}) collective-permute-start(f32[8,288,128]{2,1,0:T(8,128)S(1)} %pad_maximum_fusion.1), channel_id=1, source_target_pairs={{0,6},{2,0},{4,2},{6,4},{1,7},{3,1},{5,3},{7,5},{8,14},{10,8},{12,... | collective-permute-start | bytes 3538952 | tf_op jit(solution)/shard_map/ppermute | solution.py:19
  115.8 13.0 %collective-permute-start.29 = (f32[4,224,128]{2,1,0:T(8,128)S(1)}, f32[4,224,128]{2,1,0:T(8,128)S(1)}, u32[]{:S(2)}, u32[]{:S(2)}) collective-permute-start(f32[4,224,128]{2,1,0:T(8,128)S(1)} %pad_maximum_fusion.3), channel_id=1, source_target_pairs={{0,56},{8,0},{16,8},{24,16},{32,24},{40,32},{48,40},{56,48},{1,57}... | collective-permute-start | bytes 1376264 | tf_op jit(solution)/shard_map/ppermute | solution.py:19
  119.1 11.2 %collective-permute-start.26 = (f32[4,224,128]{2,1,0:T(8,128)S(1)}, f32[4,224,128]{2,1,0:T(8,128)S(1)}, u32[]{:S(2)}, u32[]{:S(2)}) collective-permute-start(f32[4,224,128]{2,1,0:T(8,128)S(1)} %bitcast_add_fusion.3), channel_id=1, source_target_pairs={{0,8},{8,16},{16,24},{24,32},{32,40},{40,48},{48,56},{56,0},{1,9},... | collective-permute-start | bytes 1376264 | tf_op jit(solution)/shard_map/ppermute | solution.py:19
  130.4 14.1 %collective-permute-start.30 = (f32[4,224,128]{2,1,0:T(8,128)S(1)}, f32[4,224,128]{2,1,0:T(8,128)S(1)}, u32[]{:S(2)}, u32[]{:S(2)}) collective-permute-start(f32[4,224,128]{2,1,0:T(8,128)S(1)} %get-tuple-element.44), channel_id=1, source_target_pairs={{0,56},{8,0},{16,8},{24,16},{32,24},{40,32},{48,40},{56,48},{1,57}... | collective-permute-start | bytes 1376264 | tf_op jit(solution)/shard_map/ppermute | solution.py:19
  130.5 23.0 %collective-permute-start.27 = (f32[4,224,128]{2,1,0:T(8,128)S(1)}, f32[4,224,128]{2,1,0:T(8,128)S(1)}, u32[]{:S(2)}, u32[]{:S(2)}) collective-permute-start(f32[4,224,128]{2,1,0:T(8,128)S(1)} %get-tuple-element.43), channel_id=1, source_target_pairs={{0,8},{8,16},{16,24},{24,32},{32,40},{40,48},{48,56},{56,0},{1,9},... | collective-permute-start | bytes 1376264 | tf_op jit(solution)/shard_map/ppermute | solution.py:19
  139.5 6.3 %collective-permute-start.16 = (f32[144,128]{1,0:T(8,128)S(1)}, f32[144,128]{1,0:T(8,128)S(1)}, u32[]{:S(2)}, u32[]{:S(2)}) collective-permute-start(f32[144,128]{1,0:T(8,128)S(1)} %get-tuple-element.52), channel_id=1, source_target_pairs={{0,8},{8,16},{16,24},{24,32},{32,40},{40,48},{48,56},{56,0},{1,9},... | collective-permute-start | bytes 221192 | tf_op jit(solution)/shard_map/ppermute | solution.py:19
  144.4 7.3 %collective-permute-start.20 = (f32[144,128]{1,0:T(8,128)S(1)}, f32[144,128]{1,0:T(8,128)S(1)}, u32[]{:S(2)}, u32[]{:S(2)}) collective-permute-start(f32[144,128]{1,0:T(8,128)S(1)} %get-tuple-element.53), channel_id=1, source_target_pairs={{0,56},{8,0},{16,8},{24,16},{32,24},{40,32},{48,40},{56,48},{1,57}... | collective-permute-start | bytes 221192 | tf_op jit(solution)/shard_map/ppermute | solution.py:19
  144.5 16.2 %collective-permute-start.31 = (f32[4,224,128]{2,1,0:T(8,128)S(1)}, f32[4,224,128]{2,1,0:T(8,128)S(1)}, u32[]{:S(2)}, u32[]{:S(2)}) collective-permute-start(f32[4,224,128]{2,1,0:T(8,128)S(1)} %bitcast_add_fusion.2), channel_id=1, source_target_pairs={{0,56},{8,0},{16,8},{24,16},{32,24},{40,32},{48,40},{56,48},{1,57}... | collective-permute-start | bytes 1376264 | tf_op jit(solution)/shard_map/ppermute | solution.py:19
  151.8 13.3 %collective-permute-start.21 = (f32[288,128]{1,0:T(8,128)S(1)}, f32[288,128]{1,0:T(8,128)S(1)}, u32[]{:S(2)}, u32[]{:S(2)}) collective-permute-start(f32[288,128]{1,0:T(8,128)S(1)} %pad_maximum_fusion.6), channel_id=1, source_target_pairs={{0,56},{8,0},{16,8},{24,16},{32,24},{40,32},{48,40},{56,48},{1,57}... | collective-permute-start | bytes 442376 | tf_op jit(solution)/shard_map/ppermute | solution.py:19
  151.9 11.6 %collective-permute-start.17 = (f32[288,128]{1,0:T(8,128)S(1)}, f32[288,128]{1,0:T(8,128)S(1)}, u32[]{:S(2)}, u32[]{:S(2)}) collective-permute-start(f32[288,128]{1,0:T(8,128)S(1)} %pad_maximum_fusion.5), channel_id=1, source_target_pairs={{0,8},{8,16},{16,24},{24,32},{32,40},{40,48},{48,56},{56,0},{1,9},... | collective-permute-start | bytes 442376 | tf_op jit(solution)/shard_map/ppermute | solution.py:19
  160.8 4.3 %collective-permute-start.32 = (f32[112,128]{1,0:T(8,128)S(1)}, f32[112,128]{1,0:T(8,128)S(1)}, u32[]{:S(2)}, u32[]{:S(2)}) collective-permute-start(f32[112,128]{1,0:T(8,128)S(1)} %get-tuple-element.64), channel_id=1, source_target_pairs={{0,2},{2,4},{4,6},{6,0},{1,3},{3,5},{5,7},{7,1},{8,10},{10,12},{12... | collective-permute-start | bytes 172040 | tf_op jit(solution)/shard_map/ppermute | solution.py:19
  160.9 4.2 %collective-permute-start.34 = (f32[112,128]{1,0:T(8,128)S(1)}, f32[112,128]{1,0:T(8,128)S(1)}, u32[]{:S(2)}, u32[]{:S(2)}) collective-permute-start(f32[112,128]{1,0:T(8,128)S(1)} %get-tuple-element.65), channel_id=1, source_target_pairs={{0,6},{2,0},{4,2},{6,4},{1,7},{3,1},{5,3},{7,5},{8,14},{10,8},{12,... | collective-permute-start | bytes 172040 | tf_op jit(solution)/shard_map/ppermute | solution.py:19
  163.6 5.3 %collective-permute-start.18 = (f32[288,128]{1,0:T(8,128)S(1)}, f32[288,128]{1,0:T(8,128)S(1)}, u32[]{:S(2)}, u32[]{:S(2)}) collective-permute-start(f32[288,128]{1,0:T(8,128)S(1)} %fusion.10), channel_id=1, source_target_pairs={{0,8},{8,16},{16,24},{24,32},{32,40},{40,48},{48,56},{56,0},{1,9},... | collective-permute-start | bytes 442376 | tf_op jit(solution)/shard_map/ppermute | solution.py:19
  168.9 4.4 %collective-permute-start.22 = (f32[288,128]{1,0:T(8,128)S(1)}, f32[288,128]{1,0:T(8,128)S(1)}, u32[]{:S(2)}, u32[]{:S(2)}) collective-permute-start(f32[288,128]{1,0:T(8,128)S(1)} %get-tuple-element.49), channel_id=1, source_target_pairs={{0,56},{8,0},{16,8},{24,16},{32,24},{40,32},{48,40},{56,48},{1,57}... | collective-permute-start | bytes 442376 | tf_op jit(solution)/shard_map/ppermute | solution.py:19
  169.0 10.3 %copy-start.7 = (f32[2,256]{1,0:T(2,128)S(1)}, f32[2,256]{1,0:T(2,128)}, u32[]{:S(2)}) copy-start(f32[2,256]{1,0:T(2,128)} %param.21) | copy-start | bytes 6148
  169.0 10.3 %copy-start.8 = (f32[2,256]{1,0:T(2,128)S(1)}, f32[2,256]{1,0:T(2,128)}, u32[]{:S(2)}) copy-start(f32[2,256]{1,0:T(2,128)} %param.20) | copy-start | bytes 6148
  169.0 5.8 %collective-permute-start.33 = (f32[224,128]{1,0:T(8,128)S(1)}, f32[224,128]{1,0:T(8,128)S(1)}, u32[]{:S(2)}, u32[]{:S(2)}) collective-permute-start(f32[224,128]{1,0:T(8,128)S(1)} %pad_maximum_fusion.7), channel_id=1, source_target_pairs={{0,2},{2,4},{4,6},{6,0},{1,3},{3,5},{5,7},{7,1},{8,10},{10,12},{12... | collective-permute-start | bytes 344072 | tf_op jit(solution)/shard_map/ppermute | solution.py:19
  169.1 5.7 %collective-permute-start.35 = (f32[224,128]{1,0:T(8,128)S(1)}, f32[224,128]{1,0:T(8,128)S(1)}, u32[]{:S(2)}, u32[]{:S(2)}) collective-permute-start(f32[224,128]{1,0:T(8,128)S(1)} %pad_maximum_fusion.8), channel_id=1, source_target_pairs={{0,6},{2,0},{4,2},{6,4},{1,7},{3,1},{5,3},{7,5},{8,14},{10,8},{12,... | collective-permute-start | bytes 344072 | tf_op jit(solution)/shard_map/ppermute | solution.py:19
  171.9 5.2 %collective-permute-start.19 = (f32[288,128]{1,0:T(8,128)S(1)}, f32[288,128]{1,0:T(8,128)S(1)}, u32[]{:S(2)}, u32[]{:S(2)}) collective-permute-start(f32[288,128]{1,0:T(8,128)S(1)} %get-tuple-element.48), channel_id=1, source_target_pairs={{0,8},{8,16},{16,24},{24,32},{32,40},{40,48},{48,56},{56,0},{1,9},... | collective-permute-start | bytes 442376 | tf_op jit(solution)/shard_map/ppermute | solution.py:19
  173.3 5.2 %collective-permute-start.23 = (f32[288,128]{1,0:T(8,128)S(1)}, f32[288,128]{1,0:T(8,128)S(1)}, u32[]{:S(2)}, u32[]{:S(2)}) collective-permute-start(f32[288,128]{1,0:T(8,128)S(1)} %fusion.9), channel_id=1, source_target_pairs={{0,56},{8,0},{16,8},{24,16},{32,24},{40,32},{48,40},{56,48},{1,57}... | collective-permute-start | bytes 442376 | tf_op jit(solution)/shard_map/ppermute | solution.py:19
  180.7 8.0 %collective-permute-start.36 = (f32[144,128]{1,0:T(8,128)S(1)}, f32[144,128]{1,0:T(8,128)S(1)}, u32[]{:S(2)}, u32[]{:S(2)}) collective-permute-start(f32[144,128]{1,0:T(8,128)S(1)} %fusion.1), channel_id=1, source_target_pairs={{0,1},{1,0},{2,3},{3,2},{4,5},{5,4},{6,7},{7,6},{8,9},{9,8},{10,11... | collective-permute-start | bytes 221192 | tf_op jit(solution)/shard_map/ppermute | solution.py:19
  221.7 5.3 %collective-permute-start.37 = (f32[72,128]{1,0:T(8,128)S(1)}, f32[72,128]{1,0:T(8,128)S(1)}, u32[]{:S(2)}, u32[]{:S(2)}) collective-permute-start(f32[72,128]{1,0:T(8,128)S(1)} %reduce_sum.39), channel_id=1, source_target_pairs={{0,1},{1,0},{2,3},{3,2},{4,5},{5,4},{6,7},{7,6},{8,9},{9,8},{10,11... | collective-permute-start | bytes 110600 | tf_op jit(solution)/shard_map/ppermute | solution.py:19
  233.4 0.6 copy-start.1
  234.0 0.6 copy-start.2

commit v5 on v4

--- a/solution.py
+++ b/solution.py
@@ -19,19 +19,24 @@
     return lax.ppermute(value, axis, [(i, (i + step) % count) for i in range(count)])
 
 
-def edges(block, offset=None):
+def ends_of(block, offset=None):
+    parts = []
+    for dim in (0, 1):
+        for start in (block.shape[dim] - 1, 0):
+            part = lax.slice_in_dim(block, start, start + 1, axis=dim)
+            if offset is not None:
+                part = part + lax.slice_in_dim(offset, start, start + 1, axis=dim)[:, :, None]
+            parts.append(part)
+    return parts
+
+
+def edges(parts):
     sides = []
-    for axis, dim in (("lat", 0), (COL, 1)):
+    for axis, (last, first) in (("lat", parts[:2]), (COL, parts[2:])):
         names = axis if isinstance(axis, tuple) else (axis,)
         count = math.prod(lax.axis_size(name) for name in names)
         forward = [(i, i + 1) for i in range(count - 1)]
         backward = [(target, source) for source, target in forward]
-        last = lax.slice_in_dim(block, block.shape[dim] - 1, None, axis=dim)
-        first = lax.slice_in_dim(block, 0, 1, axis=dim)
-        if offset is not None:
-            count = offset.shape[dim]
-            last = last + lax.slice_in_dim(offset, count - 1, None, axis=dim)[:, :, None]
-            first = first + lax.slice_in_dim(offset, 0, 1, axis=dim)[:, :, None]
         sides.append(lax.ppermute(last, axis, forward))
         sides.append(lax.ppermute(first, axis, backward))
     return sides
@@ -92,7 +97,8 @@
 
 def receiver_of(step, place, size_z, size_x):
     ahead_z, ahead_x = step // size_x, step % size_x
-    return ((place[0] + ahead_z) % size_z) * size_x + (place[1] + ahead_x) % size_x
+    chip = ((place[0] + ahead_z) % size_z) * size_x + (place[1] + ahead_x) % size_x
+    return 2 * chip + place[2]
 
 
 def pick_rows(out, entry, slots, cell, weight, count, states):
@@ -121,12 +127,13 @@
 
 
 def bin_kernel(
-    size_z, size_x, owned, place, cell, weight, count, station, held, first, second, *rest
+    size_z, size_x, owned, place, cell, weight, count, station_own, station_pair, held, first, second, *rest
 ):
     out_a, out_b, picked = rest
     width = out_a.shape[3]
     cut = out_a.shape[2] - owned
-    receivers, slots = size_z * size_x, station.shape[1]
+    receivers, slots = station_own.shape
+    order = lax.broadcasted_iota(jnp.int32, (1, slots), 1)
     picked[...] = jnp.zeros_like(picked)
     own = lax.broadcasted_iota(jnp.int32, (owned, slots), 0)
 
@@ -135,7 +142,9 @@
         pick_rows(picked, receivers + receiver, slots, cell, weight, count, (first, second))
         hots = []
         for e in range(2):
-            hit = station[pl.ds(e * receivers + receiver, 1), :] == own
+            station = (station_own, station_pair)[e][pl.ds(receiver, 1), :]
+            live = order < count[e * receivers + receiver]
+            hit = jnp.where(live, station, -1) == own
             hots.append(jnp.where(hit, 1.0, 0.0).astype(jnp.bfloat16))
         rows = [[held[step, k].reshape(slots, width) for k in range(2)]]
         rows.append([picked[k].reshape(slots, width) for k in range(2)])
@@ -153,12 +162,12 @@
         out_b[ahead_z, ahead_x] = total[cut:, width:]
         return carry
 
-    lax.fori_loop(0, receivers, one, 0)
-
-
-def bin_rows(place, cell, weight, count, station, states, owned):
+    lax.fori_loop(0, size_z * size_x, one, 0)
+
+
+def bin_rows(place, cell, weight, count, station_own, station_pair, states, owned):
     size_z, size_x = lax.axis_size("z"), lax.axis_size("x")
-    members, slots = states[0].shape[1], station.shape[1]
+    members, slots = states[0].shape[1], station_own.shape[1]
     rows_a = owned + owned // 8
     rows_b = 2 * owned - rows_a
     scalar = pl.BlockSpec(memory_space=pltpu.SMEM)
@@ -175,7 +184,7 @@
     )(place, cell, weight, count, *states[:2])
     return pl.pallas_call(
         functools.partial(bin_kernel, size_z, size_x, owned),
-        in_specs=[scalar] * 4 + [whole] * 4,
+        in_specs=[scalar] * 4 + [whole] * 5,
         out_specs=[whole] * 2,
         out_shape=[
             pltpu.VMEM((size_x, size_z, rows_a, members), jnp.float32),
@@ -184,7 +193,7 @@
         scratch_shapes=[pltpu.VMEM((2, slots // 8, 8, members), jnp.float32)],
         compiler_params=pltpu.CompilerParams(vmem_limit_bytes=32 * 2**20),
         cost_estimate=pl.CostEstimate(flops=10**9, bytes_accessed=30 * 2**20, transcendentals=0),
-    )(place, cell, weight, count, station, held, *states[2:])
+    )(place, cell, weight, count, station_own, station_pair, held, *states[2:])
 
 
 def factor_kernel(root_scale, products, high, low):
@@ -329,7 +338,7 @@
 
 
 def spread_sum(value, axis):
-    count = lax.axis_size(axis)
+    count = math.prod(lax.axis_size(name) for name in axis)
     copies = jnp.broadcast_to(value[None], (count,) + value.shape)
     return jnp.sum(lax.all_to_all(copies, axis, split_axis=0, concat_axis=0, tiled=True), axis=0)
 
@@ -339,7 +348,7 @@
     rows = value.shape[0] // 2
     value = value + shift(value, "core", 1)
     part = lax.dynamic_slice_in_dim(value, core * rows, rows, 0)
-    for axis in ("x", "lat", "z"):
+    for axis in (("lat", "x"), ("z",)):
         part = spread_sum(part, axis)
     other = shift(part, "core", 1)
     return jnp.where(
@@ -362,30 +371,11 @@
 ):
     member_count = perturbations.shape[2]
     step_total, owned_count = obs_value.shape
-    slots = send_cell.shape[3]
-    size_z, size_x, size_c = (lax.axis_size(name) for name in COL)
-    core = lax.axis_index("core")
-    place = jnp.stack([lax.axis_index("z"), lax.axis_index("x")]).astype(jnp.int32)
-
-    live = lax.broadcasted_iota(jnp.int32, send_cell.shape[2:], 1) < send_count[0, 0][:, None]
-    station_live = jnp.where(live, send_station[0, 0], -1)
-    whole_tables = jnp.concatenate(
-        [
-            send_cell[0, 0],
-            station_live,
-            jnp.broadcast_to(send_count[0, 0][:, None], (send_cell.shape[2], slots)),
-        ],
-        axis=1,
-    ).reshape(size_z * size_x, size_c, 3 * slots)
-    whole_weights = send_weight[0, 0].reshape(size_z * size_x, size_c, slots)
-    index_own = lax.dynamic_index_in_dim(whole_tables, core, 1, keepdims=False)
-    index_pair = shift(
-        lax.dynamic_index_in_dim(whole_tables, 1 - core, 1, keepdims=False), "core", 1
-    )
-    weight_own = lax.dynamic_index_in_dim(whole_weights, core, 1, keepdims=False)
-    weight_pair = shift(
-        lax.dynamic_index_in_dim(whole_weights, 1 - core, 1, keepdims=False), "core", 1
-    )
+    place = jnp.stack([lax.axis_index(name) for name in COL]).astype(jnp.int32)
+    swapped = [
+        shift(table[0, 0], "core", 1)
+        for table in (send_cell, send_weight, send_count, send_station)
+    ]
 
     zero = jnp.zeros_like(control)
     rates = jnp.stack(
@@ -401,16 +391,12 @@
         ],
         axis=1,
     ).reshape(-1, member_count, control.shape[1])
-    first = advance(True, rates, perturbations, edges(perturbations, control))
-    index = jnp.concatenate([index_own, index_pair], axis=0)
-    weight = jnp.concatenate([weight_own, weight_pair], axis=0)
-    tables = (
-        index[:, :slots].reshape(-1),
-        weight.reshape(-1),
-        index[:, 2 * slots],
-        index[:, slots : 2 * slots],
-    )
-    sides, tables = lax.optimization_barrier((edges(first), tables))
+    first = advance(True, rates, perturbations, edges(ends_of(perturbations, control)))
+    tables = [
+        jnp.concatenate([table[0, 0], other], axis=0).reshape(-1)
+        for table, other in zip((send_cell, send_weight, send_count), swapped)
+    ] + [send_station[0, 0], swapped[3]]
+    sides, tables = lax.optimization_barrier((edges(ends_of(first)), tables))
     second = advance(False, rates, first, sides)
     flat = [state.reshape(-1, member_count) for state in (first, second)]
     paired = [shift(state, "core", 1) for state in flat]

time: 244 us -> 243 us (level)
  waiting for transfers between devices: 53.9 us -> 48.3 us
  blocking collectives: 32.8 us -> 35.8 us
  starting transfers between devices: 72.9 us -> 75.9 us
    ppermute x4, starting transfers between devices: 11.7 us -> 16.2 us  [edges(): sides.append(lax.ppermute(last, axis, forward))]
    all_to_all x3 -> x2, blocking collectives: 32.8 us -> 35.8 us  [spread_sum(): lax.all_to_all(copies, axis, split_axis=0, concat_axis=0, tiled=True)]
    ppermute x4, waiting for transfers between devices: 5.81 us -> 3 us  [edges(): sides.append(lax.ppermute(first, axis, backward))]
    ppermute x30 -> x32, waiting for transfers between devices: 48.1 us -> 45.3 us  [shift(): lax.ppermute(value, axis, [(i, (i + step) % count) for i in range(count)])]
    ppermute x30 -> x32, starting transfers between devices: 54.5 us -> 53.3 us  [shift(): lax.ppermute(value, axis, [(i, (i + step) % count) for i in range(count)])]
  transfers between devices with their start and end apart: 38 -> 40, of which waited for: 16 -> 15; matrix products, arithmetic and copies ran while one was open for 3% -> 3% of each run, Pallas kernels for 14% -> 14%
where the time goes in v5:
time: 243 us; the launch traced here: 242 us
  starting transfers between devices  75.9 us (31%)
  Pallas kernels  64.2 us (26%)
  waiting for transfers between devices  48.3 us (20%)
  blocking collectives  35.8 us (15%)
  local copies, waits for them, and re-layouts  9.17 us (4%)
  other arithmetic  6.18 us (3%)
    ppermute x32, starting transfers between devices, shift(): lax.ppermute(value, axis, [(i, (i + step) % count) for i in range(count)])  53.3 us
    ppermute x32, waiting for transfers between devices, shift(): lax.ppermute(value, axis, [(i, (i + step) % count) for i in range(count)])  45.3 us
    all_to_all x2, blocking collectives, spread_sum(): lax.all_to_all(copies, axis, split_axis=0, concat_axis=0, tiled=True)  35.8 us
    pallas_call x2, Pallas kernels, advance(): pl.pallas_call(functools.partial(advance_kernel, adds), in_specs=[whole]...  24.3 us
    pallas_call x1, Pallas kernels, bin_rows(): pl.pallas_call(functools.partial(bin_kernel, size_z, size_x, owned), in_s...  16.7 us
    ppermute x4, starting transfers between devices, edges(): sides.append(lax.ppermute(last, axis, forward))  16.2 us
    pallas_call x1, Pallas kernels, bin_rows(): pl.pallas_call(functools.partial(own_kernel, size_z, size_x), in_specs=[s...  9.2 us
    pallas_call x1, Pallas kernels, analyse(): pl.pallas_call(analysis_kernel, grid=(8,), in_specs=[whole, whole, block,...  8.18 us
  transfers between devices with their start and end apart: 40, of which 15 were waited for; matrix products, arithmetic and copies ran while one was open for 3% of the time, Pallas kernels for 14%

profile of v5, /device:TPU:1, one launch (start us, length us, event | category | flops | bytes accessed | tf_op | source)
XLA Modules:
  0.0 241.8 jit_solution(8565714210412625481)
XLA Ops:
  0.7 0.7 fusion.29
  1.4 1.1 slice_add_fusion.4
  2.5 4.0 %collective-permute-start = (f32[1,256,128]{2,1,0:T(8,128)S(1)}, f32[1,256,128]{2,1,0:T(8,128)S(1)}, u32[]{:S(2)}, u32[]{:S(2)}) collective-permute-start(f32[1,256,128]{2,1,0:T(8,128)S(1)} %get-tuple-element.44), channel_id=1, source_target_pairs={{0,64},{64,128},{128,192},{1,65},{65,129},{129,193},{2,66},{66,130... | collective-permute-start | bytes 393224 | tf_op jit(solution)/shard_map/ppermute | solution.py:40
  6.6 1.3 collective-permute-start.1
  7.9 0.9 slice_reduce_fusion
  8.8 1.1 slice_add_fusion.6
  9.9 4.0 %collective-permute-start.2 = (f32[32,1,128]{2,1,0:T(1,128)S(1)}, f32[32,1,128]{2,1,0:T(1,128)S(1)}, u32[]{:S(2)}, u32[]{:S(2)}) collective-permute-start(f32[32,1,128]{2,1,0:T(1,128)S(1)} %get-tuple-element.42), channel_id=1, source_target_pairs={{0,1},{1,2},{2,3},{3,4},{4,5},{5,6},{6,7},{7,8},{8,9},{9,10},{10,1... | collective-permute-start | bytes 49160 | tf_op jit(solution)/shard_map/ppermute | solution.py:40
  13.9 1.9 collective-permute-start.3
  15.9 0.8 add_bitcast_fusion.1
  16.9 0.8 copy.28
  18.1 0.6 collective-permute-start.8
  18.7 0.8 collective-permute-done.8
  19.5 0.3 collective-permute-start.9
  20.2 2.2 copy-done
  22.4 12.6 %shard_map.122.block = f32[32,256,128]{2,1,0:T(8,128)} custom-call(f32[2,128,256]{2,1,0:T(8,128)S(1)} %bitcast.124, f32[32,256,128]{2,1,0:T(8,128)S(1)} %copy-done, f32[1,256,128]{2,1,0:T(8,128)S(1)} %collective-permute-done.above, f32[1,256,128]{2,1,0:T(8,128)S(1)} %collective-permute-done.1.below, f32[32,1,128]{2,1,0:T(1,128)S(1)} %collective-permute-done.2.left, ...), custom_call_target="tpu_custom_call" | custom-call | flops 12582912 | bytes 8388608 | tf_op jit(solution)/shard_map/pallas_call | solution.py:82
  34.9 1.0 fusion.24
  35.9 1.0 fusion.23
  36.9 4.3 %collective-permute-start.4 = (f32[1,256,128]{2,1,0:T(8,128)S(1)}, f32[1,256,128]{2,1,0:T(8,128)S(1)}, u32[]{:S(2)}, u32[]{:S(2)}) collective-permute-start(f32[1,256,128]{2,1,0:T(8,128)S(1)} %get-tuple-element.40), channel_id=1, source_target_pairs={{0,64},{64,128},{128,192},{1,65},{65,129},{129,193},{2,66},{66,130... | collective-permute-start | bytes 393224 | tf_op jit(solution)/shard_map/ppermute | solution.py:40
  41.2 1.3 collective-permute-start.5
  42.5 3.9 %collective-permute-start.6 = (f32[32,1,128]{2,1,0:T(1,128)S(1)}, f32[32,1,128]{2,1,0:T(1,128)S(1)}, u32[]{:S(2)}, u32[]{:S(2)}) collective-permute-start(f32[32,1,128]{2,1,0:T(1,128)S(1)} %get-tuple-element.38), channel_id=1, source_target_pairs={{0,1},{1,2},{2,3},{3,4},{4,5},{5,6},{6,7},{7,8},{8,9},{9,10},{10,1... | collective-permute-start | bytes 49160 | tf_op jit(solution)/shard_map/ppermute | solution.py:40
  46.4 1.9 collective-permute-start.7
  48.5 3.0 %collective-permute-done.7.right = f32[32,1,128]{2,1,0:T(1,128)S(1)} collective-permute-done((f32[32,1,128]{2,1,0:T(1,128)S(1)}, f32[32,1,128]{2,1,0:T(1,128)S(1)}, u32[]{:S(2)}, u32[]{:S(2)}) %collective-permute-start.7) | collective-permute-done | bytes 16416 | tf_op jit(solution)/shard_map/ppermute | solution.py:41
  51.5 11.7 %shard_map.123 = f32[32,256,128]{2,1,0:T(8,128)} custom-call(f32[2,128,256]{2,1,0:T(8,128)S(1)} %bitcast.125, f32[32,256,128]{2,1,0:T(8,128)} %shard_map.122.block, f32[1,256,128]{2,1,0:T(8,128)S(1)} %collective-permute-done.4.above, f32[1,256,128]{2,1,0:T(8,128)S(1)} %collective-permute-done.5.below, f32[32,1,128]{2,1,0:T(1,128)S(1)} %collective-permute-done.6.left, ...), custom_call_target="tpu_custom_call" | custom-call | flops 12582912 | bytes 8388608 | tf_op jit(solution)/shard_map/pallas_call | solution.py:82
  63.3 9.2 %shard_map.124.held = f32[32,2,16,8,128]{4,3,2,1,0:T(8,128)S(1)} custom-call(s32[3]{0:T(128)S(1)} %pad_add_fusion.place, s32[16384]{0:T(1024)S(1)} %add_bitcast_fusion.cell, f32[16384]{0:T(1024)S(1)} %maximum_bitcast_fusion.weight, s32[128]{0:T(128)S(1)} %pad_add_fusion.1.count, f32[8192,128]{1,0:T(8,128)} %bitcast.17.first, f32[8192,128]{1,0:T(8,128)} %bitcast.18.second.state), custom_call_target="tpu_custom_call" | custom-call | flops 100000000 | bytes 20971520 | tf_op jit(solution)/shard_map/pallas_call | solution.py:175
  72.5 16.7 %shard_map.125 = (f32[4,8,288,128]{3,2,1,0:T(8,128)S(1)}, f32[8,4,224,128]{3,2,1,0:T(8,128)S(1)}) custom-call(s32[3]{0:T(128)S(1)} %pad_add_fusion.place, s32[16384]{0:T(1024)S(1)} %add_bitcast_fusion.cell, f32[16384]{0:T(1024)S(1)} %maximum_bitcast_fusion.weight, s32[128]{0:T(128)S(1)} %pad_add_fusion.1.count, s32[64,128]{1,0:T(8,128)S(1)} %bitcast.127, ...), custom_call_target="tpu_custom_call" | custom-call | flops 1000000000 | bytes 31457280 | tf_op jit(solution)/shard_map/pallas_call | solution.py:185
  89.6 4.4 %collective-permute-start.26 = (f32[4,112,128]{2,1,0:T(8,128)S(1)}, f32[4,112,128]{2,1,0:T(8,128)S(1)}, u32[]{:S(2)}, u32[]{:S(2)}) collective-permute-start(f32[4,112,128]{2,1,0:T(8,128)S(1)} %get-tuple-element.72), channel_id=1, source_target_pairs={{0,8},{8,16},{16,24},{24,32},{32,40},{40,48},{48,56},{56,0},{1,9},... | collective-permute-start | bytes 688136 | tf_op jit(solution)/shard_map/ppermute | solution.py:19
  94.2 4.1 %collective-permute-start.16 = (f32[8,144,128]{2,1,0:T(8,128)S(1)}, f32[8,144,128]{2,1,0:T(8,128)S(1)}, u32[]{:S(2)}, u32[]{:S(2)}) collective-permute-start(f32[8,144,128]{2,1,0:T(8,128)S(1)} %get-tuple-element.61), channel_id=1, source_target_pairs={{0,6},{2,0},{4,2},{6,4},{1,7},{3,1},{5,3},{7,5},{8,14},{10,8},{12,... | collective-permute-start | bytes 1769480 | tf_op jit(solution)/shard_map/ppermute | solution.py:19
  98.3 3.0 %collective-permute-start.30 = (f32[4,112,128]{2,1,0:T(8,128)S(1)}, f32[4,112,128]{2,1,0:T(8,128)S(1)}, u32[]{:S(2)}, u32[]{:S(2)}) collective-permute-start(f32[4,112,128]{2,1,0:T(8,128)S(1)} %get-tuple-element.73), channel_id=1, source_target_pairs={{0,56},{8,0},{16,8},{24,16},{32,24},{40,32},{48,40},{56,48},{1,57}... | collective-permute-start | bytes 688136 | tf_op jit(solution)/shard_map/ppermute | solution.py:19
  101.3 3.1 %collective-permute-done.26 = f32[4,112,128]{2,1,0:T(8,128)S(1)} collective-permute-done((f32[4,112,128]{2,1,0:T(8,128)S(1)}, f32[4,112,128]{2,1,0:T(8,128)S(1)}, u32[]{:S(2)}, u32[]{:S(2)}) %collective-permute-start.26) | collective-permute-done | bytes 229408 | tf_op jit(solution)/shard_map/ppermute | solution.py:19
  104.7 6.8 %collective-permute-done.14 = f32[8,144,128]{2,1,0:T(8,128)S(1)} collective-permute-done((f32[8,144,128]{2,1,0:T(8,128)S(1)}, f32[8,144,128]{2,1,0:T(8,128)S(1)}, u32[]{:S(2)}, u32[]{:S(2)}) %collective-permute-start.14) | collective-permute-done | bytes 589856 | tf_op jit(solution)/shard_map/ppermute | solution.py:19
  111.9 2.9 %collective-permute-start.17 = (f32[8,288,128]{2,1,0:T(8,128)S(1)}, f32[8,288,128]{2,1,0:T(8,128)S(1)}, u32[]{:S(2)}, u32[]{:S(2)}) collective-permute-start(f32[8,288,128]{2,1,0:T(8,128)S(1)} %pad_maximum_fusion.1), channel_id=1, source_target_pairs={{0,6},{2,0},{4,2},{6,4},{1,7},{3,1},{5,3},{7,5},{8,14},{10,8},{12,... | collective-permute-start | bytes 3538952 | tf_op jit(solution)/shard_map/ppermute | solution.py:19
  114.9 3.8 %collective-permute-start.31 = (f32[4,224,128]{2,1,0:T(8,128)S(1)}, f32[4,224,128]{2,1,0:T(8,128)S(1)}, u32[]{:S(2)}, u32[]{:S(2)}) collective-permute-start(f32[4,224,128]{2,1,0:T(8,128)S(1)} %pad_maximum_fusion.3), channel_id=1, source_target_pairs={{0,56},{8,0},{16,8},{24,16},{32,24},{40,32},{48,40},{56,48},{1,57}... | collective-permute-start | bytes 1376264 | tf_op jit(solution)/shard_map/ppermute | solution.py:19
  118.9 8.5 %collective-permute-done.31 = f32[4,224,128]{2,1,0:T(8,128)S(1)} collective-permute-done((f32[4,224,128]{2,1,0:T(8,128)S(1)}, f32[4,224,128]{2,1,0:T(8,128)S(1)}, u32[]{:S(2)}, u32[]{:S(2)}) %collective-permute-start.31) | collective-permute-done | bytes 458784 | tf_op jit(solution)/shard_map/ppermute | solution.py:19
  127.4 3.3 %collective-permute-done.28 = f32[4,224,128]{2,1,0:T(8,128)S(1)} collective-permute-done((f32[4,224,128]{2,1,0:T(8,128)S(1)}, f32[4,224,128]{2,1,0:T(8,128)S(1)}, u32[]{:S(2)}, u32[]{:S(2)}) %collective-permute-start.28) | collective-permute-done | bytes 458784 | tf_op jit(solution)/shard_map/ppermute | solution.py:19
  131.0 1.3 collective-permute-start.29
  132.4 6.9 %collective-permute-done.15 = f32[8,288,128]{2,1,0:T(8,128)S(1)} collective-permute-done((f32[8,288,128]{2,1,0:T(8,128)S(1)}, f32[8,288,128]{2,1,0:T(8,128)S(1)}, u32[]{:S(2)}, u32[]{:S(2)}) %collective-permute-start.15) | collective-permute-done | bytes 1179680 | tf_op jit(solution)/shard_map/ppermute | solution.py:19
  139.5 1.0 collective-permute-start.18
  140.6 3.5 %collective-permute-start.22 = (f32[144,128]{1,0:T(8,128)S(1)}, f32[144,128]{1,0:T(8,128)S(1)}, u32[]{:S(2)}, u32[]{:S(2)}) collective-permute-start(f32[144,128]{1,0:T(8,128)S(1)} %get-tuple-element.55), channel_id=1, source_target_pairs={{0,56},{8,0},{16,8},{24,16},{32,24},{40,32},{48,40},{56,48},{1,57}... | collective-permute-start | bytes 221192 | tf_op jit(solution)/shard_map/ppermute | solution.py:19
  144.1 1.5 collective-permute-start.33
  145.7 1.7 collective-permute-done.22
  147.4 1.2 collective-permute-start.23
  148.6 1.0 collective-permute-start.19
  149.6 5.5 %collective-permute-done.33 = f32[4,224,128]{2,1,0:T(8,128)S(1)} collective-permute-done((f32[4,224,128]{2,1,0:T(8,128)S(1)}, f32[4,224,128]{2,1,0:T(8,128)S(1)}, u32[]{:S(2)}, u32[]{:S(2)}) %collective-permute-start.33) | collective-permute-done | bytes 458784 | tf_op jit(solution)/shard_map/ppermute | solution.py:19
  155.3 2.7 %collective-permute-start.36 = (f32[112,128]{1,0:T(8,128)S(1)}, f32[112,128]{1,0:T(8,128)S(1)}, u32[]{:S(2)}, u32[]{:S(2)}) collective-permute-start(f32[112,128]{1,0:T(8,128)S(1)} %get-tuple-element.67), channel_id=1, source_target_pairs={{0,6},{2,0},{4,2},{6,4},{1,7},{3,1},{5,3},{7,5},{8,14},{10,8},{12,... | collective-permute-start | bytes 172040 | tf_op jit(solution)/shard_map/ppermute | solution.py:19
  157.9 2.6 %collective-permute-start.20 = (f32[288,128]{1,0:T(8,128)S(1)}, f32[288,128]{1,0:T(8,128)S(1)}, u32[]{:S(2)}, u32[]{:S(2)}) collective-permute-start(f32[288,128]{1,0:T(8,128)S(1)} %fusion.10), channel_id=1, source_target_pairs={{0,8},{8,16},{16,24},{24,32},{32,40},{40,48},{48,56},{56,0},{1,9},... | collective-permute-start | bytes 442376 | tf_op jit(solution)/shard_map/ppermute | solution.py:19
  160.6 3.4 %collective-permute-done.20 = f32[288,128]{1,0:T(8,128)S(1)} collective-permute-done((f32[288,128]{1,0:T(8,128)S(1)}, f32[288,128]{1,0:T(8,128)S(1)}, u32[]{:S(2)}, u32[]{:S(2)}) %collective-permute-start.20) | collective-permute-done | bytes 147488 | tf_op jit(solution)/shard_map/ppermute | solution.py:19
  164.0 1.8 collective-permute-start.24
  166.0 2.7 %collective-permute-start.37 = (f32[224,128]{1,0:T(8,128)S(1)}, f32[224,128]{1,0:T(8,128)S(1)}, u32[]{:S(2)}, u32[]{:S(2)}) collective-permute-start(f32[224,128]{1,0:T(8,128)S(1)} %pad_maximum_fusion.8), channel_id=1, source_target_pairs={{0,6},{2,0},{4,2},{6,4},{1,7},{3,1},{5,3},{7,5},{8,14},{10,8},{12,... | collective-permute-start | bytes 344072 | tf_op jit(solution)/shard_map/ppermute | solution.py:19
  168.8 2.7 %collective-permute-start.25 = (f32[288,128]{1,0:T(8,128)S(1)}, f32[288,128]{1,0:T(8,128)S(1)}, u32[]{:S(2)}, u32[]{:S(2)}) collective-permute-start(f32[288,128]{1,0:T(8,128)S(1)} %fusion.9), channel_id=1, source_target_pairs={{0,56},{8,0},{16,8},{24,16},{32,24},{40,32},{48,40},{56,48},{1,57}... | collective-permute-start | bytes 442376 | tf_op jit(solution)/shard_map/ppermute | solution.py:19
  171.5 2.4 collective-permute-done.21
  173.9 1.2 collective-permute-done.25
  175.1 0.7 pad_maximum_fusion.4
  176.3 1.0 fusion.1
  177.2 6.7 %collective-permute-start.38 = (f32[144,128]{1,0:T(8,128)S(1)}, f32[144,128]{1,0:T(8,128)S(1)}, u32[]{:S(2)}, u32[]{:S(2)}) collective-permute-start(f32[144,128]{1,0:T(8,128)S(1)} %fusion.1), channel_id=1, source_target_pairs={{0,1},{1,0},{2,3},{3,2},{4,5},{5,4},{6,7},{7,6},{8,9},{9,8},{10,11... | collective-permute-start | bytes 221192 | tf_op jit(solution)/shard_map/ppermute | solution.py:19
  184.0 0.9 collective-permute-done.38
  184.9 19.5 %all_to_all.10 = f32[16,72,128]{2,1,0:T(8,128)S(1)} all-to-all(f32[16,72,128]{2,1,0:T(8,128)S(1)} %broadcast_in_dim.7), channel_id=1, replica_groups=mesh['lat'=4,'z'=8,'x'=4,'core'=2] {'lat','x'}, dimensions={0} | all-to-all | bytes 1179648 | tf_op jit(solution)/shard_map/all_to_all | solution.py:343
  204.5 16.3 %all_to_all.11 = f32[8,72,128]{2,1,0:T(8,128)S(1)} all-to-all(f32[8,72,128]{2,1,0:T(8,128)S(1)} %broadcast_in_dim.8), channel_id=1, replica_groups=mesh['lat'=4,'z'=8,'x'=4,'core'=2] {'z'}, dimensions={0} | all-to-all | bytes 589824 | tf_op jit(solution)/shard_map/all_to_all | solution.py:343
  220.9 4.2 %collective-permute-start.39 = (f32[72,128]{1,0:T(8,128)S(1)}, f32[72,128]{1,0:T(8,128)S(1)}, u32[]{:S(2)}, u32[]{:S(2)}) collective-permute-start(f32[72,128]{1,0:T(8,128)S(1)} %reduce_sum.29), channel_id=1, source_target_pairs={{0,1},{1,0},{2,3},{3,2},{4,5},{5,4},{6,7},{7,6},{8,9},{9,8},{10,11... | collective-permute-start | bytes 110600 | tf_op jit(solution)/shard_map/ppermute | solution.py:19
  225.1 0.9 collective-permute-done.39
  226.0 0.6 maximum_select_fusion.products
  226.6 5.8 %shard_map.126 = (bf16[128,128]{1,0:T(8,128)(2,1)S(1)}, bf16[128,128]{1,0:T(8,128)(2,1)S(1)}) custom-call(f32[144,128]{1,0:T(8,128)} %maximum_select_fusion.products), custom_call_target="tpu_custom_call" | custom-call | tf_op jit(solution)/shard_map/pallas_call | solution.py:270
  232.4 0.6 copy-done.2
  233.1 0.6 copy-done.3
  233.7 8.2 %shard_map.127 = (f32[8192,128]{1,0:T(8,128)}, f32[512,128]{1,0:T(8,128)}) custom-call(bf16[128,128]{1,0:T(8,128)(2,1)} %copy-done.2, bf16[128,128]{1,0:T(8,128)(2,1)} %copy-done.3, f32[8192,128]{1,0:T(8,128)} %bitcast.18.second.state, f32[512,128]{1,0:T(8,128)} %get-tuple-element.76.observed), custom_call_target="tpu_custom_call" | custom-call | tf_op jit(solution)/shard_map/pallas_call | solution.py:301
  (108 shorter events, 4.5 us)
Async XLA Ops:
  0.6 18.0 %copy-start.8 = (s32[1,1,64]{2,1,0:T(1,128)S(1)}, s32[1,1,64]{2,1,0:T(1,128)}, u32[]{:S(2)}) copy-start(s32[1,1,64]{2,1,0:T(1,128)} %param.19) | copy-start | bytes 772
  0.6 17.4 %copy-start.4 = (s32[1,1,64,128]{3,2,1,0:T(8,128)S(1)}, s32[1,1,64,128]{3,2,1,0:T(8,128)}, u32[]{:S(2)}) copy-start(s32[1,1,64,128]{3,2,1,0:T(8,128)} %param.16) | copy-start | bytes 98308
  0.7 18.9 %copy-start.5 = (f32[1,1,64,128]{3,2,1,0:T(8,128)S(1)}, f32[1,1,64,128]{3,2,1,0:T(8,128)}, u32[]{:S(2)}) copy-start(f32[1,1,64,128]{3,2,1,0:T(8,128)} %param.18) | copy-start | bytes 98308
  0.7 19.2 %copy-start.1 = (s32[1,1,64,128]{3,2,1,0:T(8,128)S(1)}, s32[1,1,64,128]{3,2,1,0:T(8,128)}, u32[]{:S(2)}) copy-start(s32[1,1,64,128]{3,2,1,0:T(8,128)} %param.17) | copy-start | bytes 98308
  2.5 17.6 %collective-permute-start = (f32[1,256,128]{2,1,0:T(8,128)S(1)}, f32[1,256,128]{2,1,0:T(8,128)S(1)}, u32[]{:S(2)}, u32[]{:S(2)}) collective-permute-start(f32[1,256,128]{2,1,0:T(8,128)S(1)} %get-tuple-element.44), channel_id=1, source_target_pairs={{0,64},{64,128},{128,192},{1,65},{65,129},{129,193},{2,66},{66,130... | collective-permute-start | bytes 393224 | tf_op jit(solution)/shard_map/ppermute | solution.py:40
  6.6 13.6 %collective-permute-start.1 = (f32[1,256,128]{2,1,0:T(8,128)S(1)}, f32[1,256,128]{2,1,0:T(8,128)S(1)}, u32[]{:S(2)}, u32[]{:S(2)}) collective-permute-start(f32[1,256,128]{2,1,0:T(8,128)S(1)} %get-tuple-element.43), channel_id=1, source_target_pairs={{64,0},{128,64},{192,128},{65,1},{129,65},{193,129},{66,2},{130,66... | collective-permute-start | bytes 393224 | tf_op jit(solution)/shard_map/ppermute | solution.py:41
  9.9 10.0 %collective-permute-start.2 = (f32[32,1,128]{2,1,0:T(1,128)S(1)}, f32[32,1,128]{2,1,0:T(1,128)S(1)}, u32[]{:S(2)}, u32[]{:S(2)}) collective-permute-start(f32[32,1,128]{2,1,0:T(1,128)S(1)} %get-tuple-element.42), channel_id=1, source_target_pairs={{0,1},{1,2},{2,3},{3,4},{4,5},{5,6},{6,7},{7,8},{8,9},{9,10},{10,1... | collective-permute-start | bytes 49160 | tf_op jit(solution)/shard_map/ppermute | solution.py:40
  13.9 6.3 %collective-permute-start.3 = (f32[32,1,128]{2,1,0:T(1,128)S(1)}, f32[32,1,128]{2,1,0:T(1,128)S(1)}, u32[]{:S(2)}, u32[]{:S(2)}) collective-permute-start(f32[32,1,128]{2,1,0:T(1,128)S(1)} %get-tuple-element.41), channel_id=1, source_target_pairs={{1,0},{2,1},{3,2},{4,3},{5,4},{6,5},{7,6},{8,7},{9,8},{10,9},{11,1... | collective-permute-start | bytes 49160 | tf_op jit(solution)/shard_map/ppermute | solution.py:41
  15.8 2.3 collective-permute-start.10
  18.1 1.4 collective-permute-start.8
  19.5 26.9 %collective-permute-start.9 = (f32[64,128]{1,0:T(8,128)S(1)}, f32[64,128]{1,0:T(8,128)S(1)}, u32[]{:S(2)}, u32[]{:S(2)}) collective-permute-start(f32[64,128]{1,0:T(8,128)S(1)} %bitcast.132), channel_id=1, source_target_pairs={{0,1},{1,0},{2,3},{3,2},{4,5},{5,4},{6,7},{7,6},{8,9},{9,8},{10,11... | collective-permute-start | bytes 98312 | tf_op jit(solution)/shard_map/ppermute | solution.py:19
  19.9 28.5 %collective-permute-start.11 = (s32[64,128]{1,0:T(8,128)S(1)}, s32[64,128]{1,0:T(8,128)S(1)}, u32[]{:S(2)}, u32[]{:S(2)}) collective-permute-start(s32[64,128]{1,0:T(8,128)S(1)} %bitcast.126), channel_id=1, source_target_pairs={{0,1},{1,0},{2,3},{3,2},{4,5},{5,4},{6,7},{7,6},{8,9},{9,8},{10,11... | collective-permute-start | bytes 98312 | tf_op jit(solution)/shard_map/ppermute | solution.py:19
  20.2 2.2 copy-start
  36.9 14.6 %collective-permute-start.4 = (f32[1,256,128]{2,1,0:T(8,128)S(1)}, f32[1,256,128]{2,1,0:T(8,128)S(1)}, u32[]{:S(2)}, u32[]{:S(2)}) collective-permute-start(f32[1,256,128]{2,1,0:T(8,128)S(1)} %get-tuple-element.40), channel_id=1, source_target_pairs={{0,64},{64,128},{128,192},{1,65},{65,129},{129,193},{2,66},{66,130... | collective-permute-start | bytes 393224 | tf_op jit(solution)/shard_map/ppermute | solution.py:40
  41.2 10.3 %collective-permute-start.5 = (f32[1,256,128]{2,1,0:T(8,128)S(1)}, f32[1,256,128]{2,1,0:T(8,128)S(1)}, u32[]{:S(2)}, u32[]{:S(2)}) collective-permute-start(f32[1,256,128]{2,1,0:T(8,128)S(1)} %get-tuple-element.39), channel_id=1, source_target_pairs={{64,0},{128,64},{192,128},{65,1},{129,65},{193,129},{66,2},{130,66... | collective-permute-start | bytes 393224 | tf_op jit(solution)/shard_map/ppermute | solution.py:41
  42.5 6.0 %collective-permute-start.6 = (f32[32,1,128]{2,1,0:T(1,128)S(1)}, f32[32,1,128]{2,1,0:T(1,128)S(1)}, u32[]{:S(2)}, u32[]{:S(2)}) collective-permute-start(f32[32,1,128]{2,1,0:T(1,128)S(1)} %get-tuple-element.38), channel_id=1, source_target_pairs={{0,1},{1,2},{2,3},{3,4},{4,5},{5,6},{6,7},{7,8},{8,9},{9,10},{10,1... | collective-permute-start | bytes 49160 | tf_op jit(solution)/shard_map/ppermute | solution.py:40
  46.4 5.1 %collective-permute-start.7 = (f32[32,1,128]{2,1,0:T(1,128)S(1)}, f32[32,1,128]{2,1,0:T(1,128)S(1)}, u32[]{:S(2)}, u32[]{:S(2)}) collective-permute-start(f32[32,1,128]{2,1,0:T(1,128)S(1)} %get-tuple-element.37), channel_id=1, source_target_pairs={{1,0},{2,1},{3,2},{4,3},{5,4},{6,5},{7,6},{8,7},{9,8},{10,9},{11,1... | collective-permute-start | bytes 49160 | tf_op jit(solution)/shard_map/ppermute | solution.py:41
  48.4 24.1 %collective-permute-start.12 = (f32[8192,128]{1,0:T(8,128)}, f32[8192,128]{1,0:T(8,128)}, u32[]{:S(2)}, u32[]{:S(2)}) collective-permute-start(f32[8192,128]{1,0:T(8,128)} %bitcast.17.first), channel_id=1, source_target_pairs={{0,1},{1,0},{2,3},{3,2},{4,5},{5,4},{6,7},{7,6},{8,9},{9,8},{10,11... | collective-permute-start | bytes 12582920 | tf_op jit(solution)/shard_map/ppermute | solution.py:19
  63.2 9.3 %collective-permute-start.13 = (f32[8192,128]{1,0:T(8,128)}, f32[8192,128]{1,0:T(8,128)}, u32[]{:S(2)}, u32[]{:S(2)}) collective-permute-start(f32[8192,128]{1,0:T(8,128)} %bitcast.18.second.state), channel_id=1, source_target_pairs={{0,1},{1,0},{2,3},{3,2},{4,5},{5,4},{6,7},{7,6},{8,9},{9,8},{10,11... | collective-permute-start | bytes 12582920 | tf_op jit(solution)/shard_map/ppermute | solution.py:19
  89.6 14.9 %collective-permute-start.26 = (f32[4,112,128]{2,1,0:T(8,128)S(1)}, f32[4,112,128]{2,1,0:T(8,128)S(1)}, u32[]{:S(2)}, u32[]{:S(2)}) collective-permute-start(f32[4,112,128]{2,1,0:T(8,128)S(1)} %get-tuple-element.72), channel_id=1, source_target_pairs={{0,8},{8,16},{16,24},{24,32},{32,40},{40,48},{48,56},{56,0},{1,9},... | collective-permute-start | bytes 688136 | tf_op jit(solution)/shard_map/ppermute | solution.py:19
  94.1 17.3 %collective-permute-start.14 = (f32[8,144,128]{2,1,0:T(8,128)S(1)}, f32[8,144,128]{2,1,0:T(8,128)S(1)}, u32[]{:S(2)}, u32[]{:S(2)}) collective-permute-start(f32[8,144,128]{2,1,0:T(8,128)S(1)} %get-tuple-element.60), channel_id=1, source_target_pairs={{0,2},{2,4},{4,6},{6,0},{1,3},{3,5},{5,7},{7,1},{8,10},{10,12},{12... | collective-permute-start | bytes 1769480 | tf_op jit(solution)/shard_map/ppermute | solution.py:19
  94.2 17.5 %collective-permute-start.16 = (f32[8,144,128]{2,1,0:T(8,128)S(1)}, f32[8,144,128]{2,1,0:T(8,128)S(1)}, u32[]{:S(2)}, u32[]{:S(2)}) collective-permute-start(f32[8,144,128]{2,1,0:T(8,128)S(1)} %get-tuple-element.61), channel_id=1, source_target_pairs={{0,6},{2,0},{4,2},{6,4},{1,7},{3,1},{5,3},{7,5},{8,14},{10,8},{12,... | collective-permute-start | bytes 1769480 | tf_op jit(solution)/shard_map/ppermute | solution.py:19
  98.3 16.5 %collective-permute-start.30 = (f32[4,112,128]{2,1,0:T(8,128)S(1)}, f32[4,112,128]{2,1,0:T(8,128)S(1)}, u32[]{:S(2)}, u32[]{:S(2)}) collective-permute-start(f32[4,112,128]{2,1,0:T(8,128)S(1)} %get-tuple-element.73), channel_id=1, source_target_pairs={{0,56},{8,0},{16,8},{24,16},{32,24},{40,32},{48,40},{56,48},{1,57}... | collective-permute-start | bytes 688136 | tf_op jit(solution)/shard_map/ppermute | solution.py:19
  104.6 14.1 %collective-permute-start.27 = (f32[4,224,128]{2,1,0:T(8,128)S(1)}, f32[4,224,128]{2,1,0:T(8,128)S(1)}, u32[]{:S(2)}, u32[]{:S(2)}) collective-permute-start(f32[4,224,128]{2,1,0:T(8,128)S(1)} %pad_maximum_fusion.2), channel_id=1, source_target_pairs={{0,8},{8,16},{16,24},{24,32},{32,40},{40,48},{48,56},{56,0},{1,9},... | collective-permute-start | bytes 1376264 | tf_op jit(solution)/shard_map/ppermute | solution.py:19
  111.6 27.6 %collective-permute-start.15 = (f32[8,288,128]{2,1,0:T(8,128)S(1)}, f32[8,288,128]{2,1,0:T(8,128)S(1)}, u32[]{:S(2)}, u32[]{:S(2)}) collective-permute-start(f32[8,288,128]{2,1,0:T(8,128)S(1)} %pad_maximum_fusion), channel_id=1, source_target_pairs={{0,2},{2,4},{4,6},{6,0},{1,3},{3,5},{5,7},{7,1},{8,10},{10,12},{12... | collective-permute-start | bytes 3538952 | tf_op jit(solution)/shard_map/ppermute | solution.py:19
  111.9 27.3 %collective-permute-start.17 = (f32[8,288,128]{2,1,0:T(8,128)S(1)}, f32[8,288,128]{2,1,0:T(8,128)S(1)}, u32[]{:S(2)}, u32[]{:S(2)}) collective-permute-start(f32[8,288,128]{2,1,0:T(8,128)S(1)} %pad_maximum_fusion.1), channel_id=1, source_target_pairs={{0,6},{2,0},{4,2},{6,4},{1,7},{3,1},{5,3},{7,5},{8,14},{10,8},{12,... | collective-permute-start | bytes 3538952 | tf_op jit(solution)/shard_map/ppermute | solution.py:19
  114.9 12.5 %collective-permute-start.31 = (f32[4,224,128]{2,1,0:T(8,128)S(1)}, f32[4,224,128]{2,1,0:T(8,128)S(1)}, u32[]{:S(2)}, u32[]{:S(2)}) collective-permute-start(f32[4,224,128]{2,1,0:T(8,128)S(1)} %pad_maximum_fusion.3), channel_id=1, source_target_pairs={{0,56},{8,0},{16,8},{24,16},{32,24},{40,32},{48,40},{56,48},{1,57}... | collective-permute-start | bytes 1376264 | tf_op jit(solution)/shard_map/ppermute | solution.py:19
  118.8 11.9 %collective-permute-start.28 = (f32[4,224,128]{2,1,0:T(8,128)S(1)}, f32[4,224,128]{2,1,0:T(8,128)S(1)}, u32[]{:S(2)}, u32[]{:S(2)}) collective-permute-start(f32[4,224,128]{2,1,0:T(8,128)S(1)} %bitcast_add_fusion.3), channel_id=1, source_target_pairs={{0,8},{8,16},{16,24},{24,32},{32,40},{40,48},{48,56},{56,0},{1,9},... | collective-permute-start | bytes 1376264 | tf_op jit(solution)/shard_map/ppermute | solution.py:19
  130.8 13.2 %collective-permute-start.32 = (f32[4,224,128]{2,1,0:T(8,128)S(1)}, f32[4,224,128]{2,1,0:T(8,128)S(1)}, u32[]{:S(2)}, u32[]{:S(2)}) collective-permute-start(f32[4,224,128]{2,1,0:T(8,128)S(1)} %get-tuple-element.46), channel_id=1, source_target_pairs={{0,56},{8,0},{16,8},{24,16},{32,24},{40,32},{48,40},{56,48},{1,57}... | collective-permute-start | bytes 1376264 | tf_op jit(solution)/shard_map/ppermute | solution.py:19
  131.0 18.5 %collective-permute-start.29 = (f32[4,224,128]{2,1,0:T(8,128)S(1)}, f32[4,224,128]{2,1,0:T(8,128)S(1)}, u32[]{:S(2)}, u32[]{:S(2)}) collective-permute-start(f32[4,224,128]{2,1,0:T(8,128)S(1)} %get-tuple-element.45), channel_id=1, source_target_pairs={{0,8},{8,16},{16,24},{24,32},{32,40},{40,48},{48,56},{56,0},{1,9},... | collective-permute-start | bytes 1376264 | tf_op jit(solution)/shard_map/ppermute | solution.py:19
  139.5 6.2 %collective-permute-start.18 = (f32[144,128]{1,0:T(8,128)S(1)}, f32[144,128]{1,0:T(8,128)S(1)}, u32[]{:S(2)}, u32[]{:S(2)}) collective-permute-start(f32[144,128]{1,0:T(8,128)S(1)} %get-tuple-element.54), channel_id=1, source_target_pairs={{0,8},{8,16},{16,24},{24,32},{32,40},{40,48},{48,56},{56,0},{1,9},... | collective-permute-start | bytes 221192 | tf_op jit(solution)/shard_map/ppermute | solution.py:19
  140.6 6.8 %collective-permute-start.22 = (f32[144,128]{1,0:T(8,128)S(1)}, f32[144,128]{1,0:T(8,128)S(1)}, u32[]{:S(2)}, u32[]{:S(2)}) collective-permute-start(f32[144,128]{1,0:T(8,128)S(1)} %get-tuple-element.55), channel_id=1, source_target_pairs={{0,56},{8,0},{16,8},{24,16},{32,24},{40,32},{48,40},{56,48},{1,57}... | collective-permute-start | bytes 221192 | tf_op jit(solution)/shard_map/ppermute | solution.py:19
  144.1 10.9 %collective-permute-start.33 = (f32[4,224,128]{2,1,0:T(8,128)S(1)}, f32[4,224,128]{2,1,0:T(8,128)S(1)}, u32[]{:S(2)}, u32[]{:S(2)}) collective-permute-start(f32[4,224,128]{2,1,0:T(8,128)S(1)} %bitcast_add_fusion.2), channel_id=1, source_target_pairs={{0,56},{8,0},{16,8},{24,16},{32,24},{40,32},{48,40},{56,48},{1,57}... | collective-permute-start | bytes 1376264 | tf_op jit(solution)/shard_map/ppermute | solution.py:19
  147.4 13.2 %collective-permute-start.23 = (f32[288,128]{1,0:T(8,128)S(1)}, f32[288,128]{1,0:T(8,128)S(1)}, u32[]{:S(2)}, u32[]{:S(2)}) collective-permute-start(f32[288,128]{1,0:T(8,128)S(1)} %pad_maximum_fusion.6), channel_id=1, source_target_pairs={{0,56},{8,0},{16,8},{24,16},{32,24},{40,32},{48,40},{56,48},{1,57}... | collective-permute-start | bytes 442376 | tf_op jit(solution)/shard_map/ppermute | solution.py:19
  148.6 9.3 %collective-permute-start.19 = (f32[288,128]{1,0:T(8,128)S(1)}, f32[288,128]{1,0:T(8,128)S(1)}, u32[]{:S(2)}, u32[]{:S(2)}) collective-permute-start(f32[288,128]{1,0:T(8,128)S(1)} %pad_maximum_fusion.5), channel_id=1, source_target_pairs={{0,8},{8,16},{16,24},{24,32},{32,40},{40,48},{48,56},{56,0},{1,9},... | collective-permute-start | bytes 442376 | tf_op jit(solution)/shard_map/ppermute | solution.py:19
  155.2 5.4 %collective-permute-start.34 = (f32[112,128]{1,0:T(8,128)S(1)}, f32[112,128]{1,0:T(8,128)S(1)}, u32[]{:S(2)}, u32[]{:S(2)}) collective-permute-start(f32[112,128]{1,0:T(8,128)S(1)} %get-tuple-element.66), channel_id=1, source_target_pairs={{0,2},{2,4},{4,6},{6,0},{1,3},{3,5},{5,7},{7,1},{8,10},{10,12},{12... | collective-permute-start | bytes 172040 | tf_op jit(solution)/shard_map/ppermute | solution.py:19
  155.3 5.3 %collective-permute-start.36 = (f32[112,128]{1,0:T(8,128)S(1)}, f32[112,128]{1,0:T(8,128)S(1)}, u32[]{:S(2)}, u32[]{:S(2)}) collective-permute-start(f32[112,128]{1,0:T(8,128)S(1)} %get-tuple-element.67), channel_id=1, source_target_pairs={{0,6},{2,0},{4,2},{6,4},{1,7},{3,1},{5,3},{7,5},{8,14},{10,8},{12,... | collective-permute-start | bytes 172040 | tf_op jit(solution)/shard_map/ppermute | solution.py:19
  157.9 6.0 %collective-permute-start.20 = (f32[288,128]{1,0:T(8,128)S(1)}, f32[288,128]{1,0:T(8,128)S(1)}, u32[]{:S(2)}, u32[]{:S(2)}) collective-permute-start(f32[288,128]{1,0:T(8,128)S(1)} %fusion.10), channel_id=1, source_target_pairs={{0,8},{8,16},{16,24},{24,32},{32,40},{40,48},{48,56},{56,0},{1,9},... | collective-permute-start | bytes 442376 | tf_op jit(solution)/shard_map/ppermute | solution.py:19
  164.0 4.7 %collective-permute-start.24 = (f32[288,128]{1,0:T(8,128)S(1)}, f32[288,128]{1,0:T(8,128)S(1)}, u32[]{:S(2)}, u32[]{:S(2)}) collective-permute-start(f32[288,128]{1,0:T(8,128)S(1)} %get-tuple-element.51), channel_id=1, source_target_pairs={{0,56},{8,0},{16,8},{24,16},{32,24},{40,32},{48,40},{56,48},{1,57}... | collective-permute-start | bytes 442376 | tf_op jit(solution)/shard_map/ppermute | solution.py:19
  165.9 10.0 %copy-start.6 = (f32[2,256]{1,0:T(2,128)S(1)}, f32[2,256]{1,0:T(2,128)}, u32[]{:S(2)}) copy-start(f32[2,256]{1,0:T(2,128)} %param.21) | copy-start | bytes 6148
  165.9 10.0 %copy-start.7 = (f32[2,256]{1,0:T(2,128)S(1)}, f32[2,256]{1,0:T(2,128)}, u32[]{:S(2)}) copy-start(f32[2,256]{1,0:T(2,128)} %param.20) | copy-start | bytes 6148
  165.9 5.6 %collective-permute-start.35 = (f32[224,128]{1,0:T(8,128)S(1)}, f32[224,128]{1,0:T(8,128)S(1)}, u32[]{:S(2)}, u32[]{:S(2)}) collective-permute-start(f32[224,128]{1,0:T(8,128)S(1)} %pad_maximum_fusion.7), channel_id=1, source_target_pairs={{0,2},{2,4},{4,6},{6,0},{1,3},{3,5},{5,7},{7,1},{8,10},{10,12},{12... | collective-permute-start | bytes 344072 | tf_op jit(solution)/shard_map/ppermute | solution.py:19
  166.0 5.5 %collective-permute-start.37 = (f32[224,128]{1,0:T(8,128)S(1)}, f32[224,128]{1,0:T(8,128)S(1)}, u32[]{:S(2)}, u32[]{:S(2)}) collective-permute-start(f32[224,128]{1,0:T(8,128)S(1)} %pad_maximum_fusion.8), channel_id=1, source_target_pairs={{0,6},{2,0},{4,2},{6,4},{1,7},{3,1},{5,3},{7,5},{8,14},{10,8},{12,... | collective-permute-start | bytes 344072 | tf_op jit(solution)/shard_map/ppermute | solution.py:19
  168.7 5.2 %collective-permute-start.21 = (f32[288,128]{1,0:T(8,128)S(1)}, f32[288,128]{1,0:T(8,128)S(1)}, u32[]{:S(2)}, u32[]{:S(2)}) collective-permute-start(f32[288,128]{1,0:T(8,128)S(1)} %get-tuple-element.50), channel_id=1, source_target_pairs={{0,8},{8,16},{16,24},{24,32},{32,40},{40,48},{48,56},{56,0},{1,9},... | collective-permute-start | bytes 442376 | tf_op jit(solution)/shard_map/ppermute | solution.py:19
  168.8 6.3 %collective-permute-start.25 = (f32[288,128]{1,0:T(8,128)S(1)}, f32[288,128]{1,0:T(8,128)S(1)}, u32[]{:S(2)}, u32[]{:S(2)}) collective-permute-start(f32[288,128]{1,0:T(8,128)S(1)} %fusion.9), channel_id=1, source_target_pairs={{0,56},{8,0},{16,8},{24,16},{32,24},{40,32},{48,40},{56,48},{1,57}... | collective-permute-start | bytes 442376 | tf_op jit(solution)/shard_map/ppermute | solution.py:19
  177.2 7.6 %collective-permute-start.38 = (f32[144,128]{1,0:T(8,128)S(1)}, f32[144,128]{1,0:T(8,128)S(1)}, u32[]{:S(2)}, u32[]{:S(2)}) collective-permute-start(f32[144,128]{1,0:T(8,128)S(1)} %fusion.1), channel_id=1, source_target_pairs={{0,1},{1,0},{2,3},{3,2},{4,5},{5,4},{6,7},{7,6},{8,9},{9,8},{10,11... | collective-permute-start | bytes 221192 | tf_op jit(solution)/shard_map/ppermute | solution.py:19
  220.9 5.1 %collective-permute-start.39 = (f32[72,128]{1,0:T(8,128)S(1)}, f32[72,128]{1,0:T(8,128)S(1)}, u32[]{:S(2)}, u32[]{:S(2)}) collective-permute-start(f32[72,128]{1,0:T(8,128)S(1)} %reduce_sum.29), channel_id=1, source_target_pairs={{0,1},{1,0},{2,3},{3,2},{4,5},{5,4},{6,7},{7,6},{8,9},{9,8},{10,11... | collective-permute-start | bytes 110600 | tf_op jit(solution)/shard_map/ppermute | solution.py:19
  232.4 0.6 copy-start.2
  233.0 0.6 copy-start.3

commit v6 on v5

--- a/solution.py
+++ b/solution.py
@@ -168,7 +168,7 @@
 def bin_rows(place, cell, weight, count, station_own, station_pair, states, owned):
     size_z, size_x = lax.axis_size("z"), lax.axis_size("x")
     members, slots = states[0].shape[1], station_own.shape[1]
-    rows_a = owned + owned // 8
+    rows_a = owned + owned // 4
     rows_b = 2 * owned - rows_a
     scalar = pl.BlockSpec(memory_space=pltpu.SMEM)
     whole = pl.BlockSpec(memory_space=pltpu.VMEM)

time: 243 us -> 248 us (1.021)
  starting transfers between devices: 75.9 us -> 80 us
    ppermute x32, starting transfers between devices: 53.3 us -> 57.4 us  [shift(): lax.ppermute(value, axis, [(i, (i + step) % count) for i in range(count)])]
  transfers between devices with their start and end apart: 40 -> 40, of which waited for: 15 -> 17; matrix products, arithmetic and copies ran while one was open for 3% -> 3% of each run, Pallas kernels for 14% -> 14%
where the time goes in v6:
time: 248 us; the launch traced here: 246 us
  starting transfers between devices  80 us (32%)
  Pallas kernels  64.3 us (26%)
  waiting for transfers between devices  49.4 us (20%)
  blocking collectives  35.1 us (14%)
  local copies, waits for them, and re-layouts  9.31 us (4%)
  other arithmetic  6.02 us (2%)
    ppermute x32, starting transfers between devices, shift(): lax.ppermute(value, axis, [(i, (i + step) % count) for i in range(count)])  57.4 us
    ppermute x32, waiting for transfers between devices, shift(): lax.ppermute(value, axis, [(i, (i + step) % count) for i in range(count)])  46.4 us
    all_to_all x2, blocking collectives, spread_sum(): lax.all_to_all(copies, axis, split_axis=0, concat_axis=0, tiled=True)  35.1 us
    pallas_call x2, Pallas kernels, advance(): pl.pallas_call(functools.partial(advance_kernel, adds), in_specs=[whole]...  24.3 us
    pallas_call x1, Pallas kernels, bin_rows(): pl.pallas_call(functools.partial(bin_kernel, size_z, size_x, owned), in_s...  16.8 us
    ppermute x4, starting transfers between devices, edges(): sides.append(lax.ppermute(last, axis, forward))  16.2 us
    pallas_call x1, Pallas kernels, bin_rows(): pl.pallas_call(functools.partial(own_kernel, size_z, size_x), in_specs=[s...  9.12 us
    pallas_call x1, Pallas kernels, analyse(): pl.pallas_call(analysis_kernel, grid=(8,), in_specs=[whole, whole, block,...  8.18 us
  transfers between devices with their start and end apart: 40, of which 17 were waited for; matrix products, arithmetic and copies ran while one was open for 3% of the time, Pallas kernels for 14%

profile of v6, /device:TPU:1, one launch (start us, length us, event | category | flops | bytes accessed | tf_op | source)
XLA Modules:
  0.0 246.3 jit_solution(1219538269908973664)
XLA Ops:
  0.7 0.7 fusion.29
  1.4 1.1 slice_add_fusion.4
  2.5 4.0 %collective-permute-start = (f32[1,256,128]{2,1,0:T(8,128)S(1)}, f32[1,256,128]{2,1,0:T(8,128)S(1)}, u32[]{:S(2)}, u32[]{:S(2)}) collective-permute-start(f32[1,256,128]{2,1,0:T(8,128)S(1)} %get-tuple-element.44), channel_id=1, source_target_pairs={{0,64},{64,128},{128,192},{1,65},{65,129},{129,193},{2,66},{66,130... | collective-permute-start | bytes 393224 | tf_op jit(solution)/shard_map/ppermute | solution.py:40
  6.6 1.3 collective-permute-start.1
  7.9 0.9 slice_reduce_fusion
  8.8 1.1 slice_add_fusion.6
  9.9 4.0 %collective-permute-start.2 = (f32[32,1,128]{2,1,0:T(1,128)S(1)}, f32[32,1,128]{2,1,0:T(1,128)S(1)}, u32[]{:S(2)}, u32[]{:S(2)}) collective-permute-start(f32[32,1,128]{2,1,0:T(1,128)S(1)} %get-tuple-element.42), channel_id=1, source_target_pairs={{0,1},{1,2},{2,3},{3,4},{4,5},{5,6},{6,7},{7,8},{8,9},{9,10},{10,1... | collective-permute-start | bytes 49160 | tf_op jit(solution)/shard_map/ppermute | solution.py:40
  13.9 1.9 collective-permute-start.3
  15.9 0.8 add_bitcast_fusion.1
  16.9 0.8 copy.28
  18.7 0.8 collective-permute-done.8
  20.2 2.2 copy-done
  22.4 12.6 %shard_map.122.block = f32[32,256,128]{2,1,0:T(8,128)} custom-call(f32[2,128,256]{2,1,0:T(8,128)S(1)} %bitcast.124, f32[32,256,128]{2,1,0:T(8,128)S(1)} %copy-done, f32[1,256,128]{2,1,0:T(8,128)S(1)} %collective-permute-done.above, f32[1,256,128]{2,1,0:T(8,128)S(1)} %collective-permute-done.1.below, f32[32,1,128]{2,1,0:T(1,128)S(1)} %collective-permute-done.2.left, ...), custom_call_target="tpu_custom_call" | custom-call | flops 12582912 | bytes 8388608 | tf_op jit(solution)/shard_map/pallas_call | solution.py:82
  34.9 1.0 fusion.24
  35.9 1.0 fusion.23
  36.9 4.3 %collective-permute-start.4 = (f32[1,256,128]{2,1,0:T(8,128)S(1)}, f32[1,256,128]{2,1,0:T(8,128)S(1)}, u32[]{:S(2)}, u32[]{:S(2)}) collective-permute-start(f32[1,256,128]{2,1,0:T(8,128)S(1)} %get-tuple-element.40), channel_id=1, source_target_pairs={{0,64},{64,128},{128,192},{1,65},{65,129},{129,193},{2,66},{66,130... | collective-permute-start | bytes 393224 | tf_op jit(solution)/shard_map/ppermute | solution.py:40
  41.2 1.3 collective-permute-start.5
  42.5 3.9 %collective-permute-start.6 = (f32[32,1,128]{2,1,0:T(1,128)S(1)}, f32[32,1,128]{2,1,0:T(1,128)S(1)}, u32[]{:S(2)}, u32[]{:S(2)}) collective-permute-start(f32[32,1,128]{2,1,0:T(1,128)S(1)} %get-tuple-element.38), channel_id=1, source_target_pairs={{0,1},{1,2},{2,3},{3,4},{4,5},{5,6},{6,7},{7,8},{8,9},{9,10},{10,1... | collective-permute-start | bytes 49160 | tf_op jit(solution)/shard_map/ppermute | solution.py:40
  46.4 1.9 collective-permute-start.7
  48.5 3.0 %collective-permute-done.7.right = f32[32,1,128]{2,1,0:T(1,128)S(1)} collective-permute-done((f32[32,1,128]{2,1,0:T(1,128)S(1)}, f32[32,1,128]{2,1,0:T(1,128)S(1)}, u32[]{:S(2)}, u32[]{:S(2)}) %collective-permute-start.7) | collective-permute-done | bytes 16416 | tf_op jit(solution)/shard_map/ppermute | solution.py:41
  51.5 11.7 %shard_map.123 = f32[32,256,128]{2,1,0:T(8,128)} custom-call(f32[2,128,256]{2,1,0:T(8,128)S(1)} %bitcast.125, f32[32,256,128]{2,1,0:T(8,128)} %shard_map.122.block, f32[1,256,128]{2,1,0:T(8,128)S(1)} %collective-permute-done.4.above, f32[1,256,128]{2,1,0:T(8,128)S(1)} %collective-permute-done.5.below, f32[32,1,128]{2,1,0:T(1,128)S(1)} %collective-permute-done.6.left, ...), custom_call_target="tpu_custom_call" | custom-call | flops 12582912 | bytes 8388608 | tf_op jit(solution)/shard_map/pallas_call | solution.py:82
  63.3 9.1 %shard_map.124.held = f32[32,2,16,8,128]{4,3,2,1,0:T(8,128)S(1)} custom-call(s32[3]{0:T(128)S(1)} %pad_add_fusion.place, s32[16384]{0:T(1024)S(1)} %add_bitcast_fusion.cell, f32[16384]{0:T(1024)S(1)} %maximum_bitcast_fusion.weight, s32[128]{0:T(128)S(1)} %pad_add_fusion.1.count, f32[8192,128]{1,0:T(8,128)} %bitcast.17.first, f32[8192,128]{1,0:T(8,128)} %bitcast.18.second.state), custom_call_target="tpu_custom_call" | custom-call | flops 100000000 | bytes 20971520 | tf_op jit(solution)/shard_map/pallas_call | solution.py:175
  72.5 16.8 %shard_map.125 = (f32[4,8,320,128]{3,2,1,0:T(8,128)S(1)}, f32[8,4,192,128]{3,2,1,0:T(8,128)S(1)}) custom-call(s32[3]{0:T(128)S(1)} %pad_add_fusion.place, s32[16384]{0:T(1024)S(1)} %add_bitcast_fusion.cell, f32[16384]{0:T(1024)S(1)} %maximum_bitcast_fusion.weight, s32[128]{0:T(128)S(1)} %pad_add_fusion.1.count, s32[64,128]{1,0:T(8,128)S(1)} %bitcast.127, ...), custom_call_target="tpu_custom_call" | custom-call | flops 1000000000 | bytes 31457280 | tf_op jit(solution)/shard_map/pallas_call | solution.py:185
  89.8 4.9 %collective-permute-start.26 = (f32[4,96,128]{2,1,0:T(8,128)S(1)}, f32[4,96,128]{2,1,0:T(8,128)S(1)}, u32[]{:S(2)}, u32[]{:S(2)}) collective-permute-start(f32[4,96,128]{2,1,0:T(8,128)S(1)} %get-tuple-element.72), channel_id=1, source_target_pairs={{0,8},{8,16},{16,24},{24,32},{32,40},{40,48},{48,56},{56,0},{1,9},... | collective-permute-start | bytes 589832 | tf_op jit(solution)/shard_map/ppermute | solution.py:19
  94.9 3.0 %collective-permute-start.30 = (f32[4,96,128]{2,1,0:T(8,128)S(1)}, f32[4,96,128]{2,1,0:T(8,128)S(1)}, u32[]{:S(2)}, u32[]{:S(2)}) collective-permute-start(f32[4,96,128]{2,1,0:T(8,128)S(1)} %get-tuple-element.73), channel_id=1, source_target_pairs={{0,56},{8,0},{16,8},{24,16},{32,24},{40,32},{48,40},{56,48},{1,57}... | collective-permute-start | bytes 589832 | tf_op jit(solution)/shard_map/ppermute | solution.py:19
  97.9 4.1 %collective-permute-done.26 = f32[4,96,128]{2,1,0:T(8,128)S(1)} collective-permute-done((f32[4,96,128]{2,1,0:T(8,128)S(1)}, f32[4,96,128]{2,1,0:T(8,128)S(1)}, u32[]{:S(2)}, u32[]{:S(2)}) %collective-permute-start.26) | collective-permute-done | bytes 196640 | tf_op jit(solution)/shard_map/ppermute | solution.py:19
  102.2 3.3 %collective-permute-start.16 = (f32[8,160,128]{2,1,0:T(8,128)S(1)}, f32[8,160,128]{2,1,0:T(8,128)S(1)}, u32[]{:S(2)}, u32[]{:S(2)}) collective-permute-start(f32[8,160,128]{2,1,0:T(8,128)S(1)} %get-tuple-element.61), channel_id=1, source_target_pairs={{0,6},{2,0},{4,2},{6,4},{1,7},{3,1},{5,3},{7,5},{8,14},{10,8},{12,... | collective-permute-start | bytes 1966088 | tf_op jit(solution)/shard_map/ppermute | solution.py:19
  105.6 2.5 %collective-permute-start.31 = (f32[4,192,128]{2,1,0:T(8,128)S(1)}, f32[4,192,128]{2,1,0:T(8,128)S(1)}, u32[]{:S(2)}, u32[]{:S(2)}) collective-permute-start(f32[4,192,128]{2,1,0:T(8,128)S(1)} %pad_maximum_fusion.3), channel_id=1, source_target_pairs={{0,56},{8,0},{16,8},{24,16},{32,24},{40,32},{48,40},{56,48},{1,57}... | collective-permute-start | bytes 1179656 | tf_op jit(solution)/shard_map/ppermute | solution.py:19
  108.1 4.4 %collective-permute-done.27 = f32[4,192,128]{2,1,0:T(8,128)S(1)} collective-permute-done((f32[4,192,128]{2,1,0:T(8,128)S(1)}, f32[4,192,128]{2,1,0:T(8,128)S(1)}, u32[]{:S(2)}, u32[]{:S(2)}) %collective-permute-start.27) | collective-permute-done | bytes 393248 | tf_op jit(solution)/shard_map/ppermute | solution.py:19
  112.6 1.3 collective-permute-done.14
  114.4 4.3 %collective-permute-done.16 = f32[8,160,128]{2,1,0:T(8,128)S(1)} collective-permute-done((f32[8,160,128]{2,1,0:T(8,128)S(1)}, f32[8,160,128]{2,1,0:T(8,128)S(1)}, u32[]{:S(2)}, u32[]{:S(2)}) %collective-permute-start.16) | collective-permute-done | bytes 655392 | tf_op jit(solution)/shard_map/ppermute | solution.py:19
  118.9 3.5 %collective-permute-start.17 = (f32[8,320,128]{2,1,0:T(8,128)S(1)}, f32[8,320,128]{2,1,0:T(8,128)S(1)}, u32[]{:S(2)}, u32[]{:S(2)}) collective-permute-start(f32[8,320,128]{2,1,0:T(8,128)S(1)} %pad_maximum_fusion.1), channel_id=1, source_target_pairs={{0,6},{2,0},{4,2},{6,4},{1,7},{3,1},{5,3},{7,5},{8,14},{10,8},{12,... | collective-permute-start | bytes 3932168 | tf_op jit(solution)/shard_map/ppermute | solution.py:19
  122.5 4.7 %collective-permute-start.32 = (f32[4,192,128]{2,1,0:T(8,128)S(1)}, f32[4,192,128]{2,1,0:T(8,128)S(1)}, u32[]{:S(2)}, u32[]{:S(2)}) collective-permute-start(f32[4,192,128]{2,1,0:T(8,128)S(1)} %get-tuple-element.46), channel_id=1, source_target_pairs={{0,56},{8,0},{16,8},{24,16},{32,24},{40,32},{48,40},{56,48},{1,57}... | collective-permute-start | bytes 1179656 | tf_op jit(solution)/shard_map/ppermute | solution.py:19
  127.3 7.1 %collective-permute-done.32 = f32[4,192,128]{2,1,0:T(8,128)S(1)} collective-permute-done((f32[4,192,128]{2,1,0:T(8,128)S(1)}, f32[4,192,128]{2,1,0:T(8,128)S(1)}, u32[]{:S(2)}, u32[]{:S(2)}) %collective-permute-start.32) | collective-permute-done | bytes 393248 | tf_op jit(solution)/shard_map/ppermute | solution.py:19
  134.4 3.5 %collective-permute-start.33 = (f32[4,192,128]{2,1,0:T(8,128)S(1)}, f32[4,192,128]{2,1,0:T(8,128)S(1)}, u32[]{:S(2)}, u32[]{:S(2)}) collective-permute-start(f32[4,192,128]{2,1,0:T(8,128)S(1)} %bitcast_add_fusion.2), channel_id=1, source_target_pairs={{0,56},{8,0},{16,8},{24,16},{32,24},{40,32},{48,40},{56,48},{1,57}... | collective-permute-start | bytes 1179656 | tf_op jit(solution)/shard_map/ppermute | solution.py:19
  137.9 7.6 %collective-permute-done.15 = f32[8,320,128]{2,1,0:T(8,128)S(1)} collective-permute-done((f32[8,320,128]{2,1,0:T(8,128)S(1)}, f32[8,320,128]{2,1,0:T(8,128)S(1)}, u32[]{:S(2)}, u32[]{:S(2)}) %collective-permute-start.15) | collective-permute-done | bytes 1310752 | tf_op jit(solution)/shard_map/ppermute | solution.py:19
  145.5 3.1 %collective-permute-done.17 = f32[8,320,128]{2,1,0:T(8,128)S(1)} collective-permute-done((f32[8,320,128]{2,1,0:T(8,128)S(1)}, f32[8,320,128]{2,1,0:T(8,128)S(1)}, u32[]{:S(2)}, u32[]{:S(2)}) %collective-permute-start.17) | collective-permute-done | bytes 1310752 | tf_op jit(solution)/shard_map/ppermute | solution.py:19
  148.8 4.3 %collective-permute-start.18 = (f32[160,128]{1,0:T(8,128)S(1)}, f32[160,128]{1,0:T(8,128)S(1)}, u32[]{:S(2)}, u32[]{:S(2)}) collective-permute-start(f32[160,128]{1,0:T(8,128)S(1)} %get-tuple-element.54), channel_id=1, source_target_pairs={{0,8},{8,16},{16,24},{24,32},{32,40},{40,48},{48,56},{56,0},{1,9},... | collective-permute-start | bytes 245768 | tf_op jit(solution)/shard_map/ppermute | solution.py:19
  153.2 1.4 collective-permute-done.18
  154.6 2.5 %collective-permute-done.22 = f32[160,128]{1,0:T(8,128)S(1)} collective-permute-done((f32[160,128]{1,0:T(8,128)S(1)}, f32[160,128]{1,0:T(8,128)S(1)}, u32[]{:S(2)}, u32[]{:S(2)}) %collective-permute-start.22) | collective-permute-done | bytes 81952 | tf_op jit(solution)/shard_map/ppermute | solution.py:19
  157.2 2.2 collective-permute-start.19
  159.5 3.5 %collective-permute-start.36 = (f32[96,128]{1,0:T(8,128)S(1)}, f32[96,128]{1,0:T(8,128)S(1)}, u32[]{:S(2)}, u32[]{:S(2)}) collective-permute-start(f32[96,128]{1,0:T(8,128)S(1)} %get-tuple-element.67), channel_id=1, source_target_pairs={{0,6},{2,0},{4,2},{6,4},{1,7},{3,1},{5,3},{7,5},{8,14},{10,8},{12,... | collective-permute-start | bytes 147464 | tf_op jit(solution)/shard_map/ppermute | solution.py:19
  163.0 0.6 collective-permute-start.23
  163.7 1.0 collective-permute-start.20
  164.7 2.7 %collective-permute-done.23 = f32[320,128]{1,0:T(8,128)S(1)} collective-permute-done((f32[320,128]{1,0:T(8,128)S(1)}, f32[320,128]{1,0:T(8,128)S(1)}, u32[]{:S(2)}, u32[]{:S(2)}) %collective-permute-start.23) | collective-permute-done | bytes 163872 | tf_op jit(solution)/shard_map/ppermute | solution.py:19
  167.4 1.7 collective-permute-done.20
  169.6 3.1 %collective-permute-start.37 = (f32[192,128]{1,0:T(8,128)S(1)}, f32[192,128]{1,0:T(8,128)S(1)}, u32[]{:S(2)}, u32[]{:S(2)}) collective-permute-start(f32[192,128]{1,0:T(8,128)S(1)} %pad_maximum_fusion.8), channel_id=1, source_target_pairs={{0,6},{2,0},{4,2},{6,4},{1,7},{3,1},{5,3},{7,5},{8,14},{10,8},{12,... | collective-permute-start | bytes 294920 | tf_op jit(solution)/shard_map/ppermute | solution.py:19
  172.7 1.4 collective-permute-start.21
  174.1 1.8 collective-permute-start.25
  175.9 2.1 collective-permute-done.21
  178.0 1.5 collective-permute-done.25
  179.6 0.7 pad_maximum_fusion.4
  180.7 1.0 fusion.1
  181.7 7.4 %collective-permute-start.38 = (f32[144,128]{1,0:T(8,128)S(1)}, f32[144,128]{1,0:T(8,128)S(1)}, u32[]{:S(2)}, u32[]{:S(2)}) collective-permute-start(f32[144,128]{1,0:T(8,128)S(1)} %fusion.1), channel_id=1, source_target_pairs={{0,1},{1,0},{2,3},{3,2},{4,5},{5,4},{6,7},{7,6},{8,9},{9,8},{10,11... | collective-permute-start | bytes 221192 | tf_op jit(solution)/shard_map/ppermute | solution.py:19
  189.2 0.9 collective-permute-done.38
  190.1 18.9 %all_to_all.10 = f32[16,72,128]{2,1,0:T(8,128)S(1)} all-to-all(f32[16,72,128]{2,1,0:T(8,128)S(1)} %broadcast_in_dim.7), channel_id=1, replica_groups=mesh['lat'=4,'z'=8,'x'=4,'core'=2] {'lat','x'}, dimensions={0} | all-to-all | bytes 1179648 | tf_op jit(solution)/shard_map/all_to_all | solution.py:343
  209.1 16.2 %all_to_all.11 = f32[8,72,128]{2,1,0:T(8,128)S(1)} all-to-all(f32[8,72,128]{2,1,0:T(8,128)S(1)} %broadcast_in_dim.8), channel_id=1, replica_groups=mesh['lat'=4,'z'=8,'x'=4,'core'=2] {'z'}, dimensions={0} | all-to-all | bytes 589824 | tf_op jit(solution)/shard_map/all_to_all | solution.py:343
  225.4 4.2 %collective-permute-start.39 = (f32[72,128]{1,0:T(8,128)S(1)}, f32[72,128]{1,0:T(8,128)S(1)}, u32[]{:S(2)}, u32[]{:S(2)}) collective-permute-start(f32[72,128]{1,0:T(8,128)S(1)} %reduce_sum.29), channel_id=1, source_target_pairs={{0,1},{1,0},{2,3},{3,2},{4,5},{5,4},{6,7},{7,6},{8,9},{9,8},{10,11... | collective-permute-start | bytes 110600 | tf_op jit(solution)/shard_map/ppermute | solution.py:19
  229.6 0.9 collective-permute-done.39
  230.5 0.6 maximum_select_fusion.products
  231.1 5.8 %shard_map.126 = (bf16[128,128]{1,0:T(8,128)(2,1)S(1)}, bf16[128,128]{1,0:T(8,128)(2,1)S(1)}) custom-call(f32[144,128]{1,0:T(8,128)} %maximum_select_fusion.products), custom_call_target="tpu_custom_call" | custom-call | tf_op jit(solution)/shard_map/pallas_call | solution.py:270
  236.9 0.6 copy-done.2
  237.6 0.6 copy-done.3
  238.2 8.2 %shard_map.127 = (f32[8192,128]{1,0:T(8,128)}, f32[512,128]{1,0:T(8,128)}) custom-call(bf16[128,128]{1,0:T(8,128)(2,1)} %copy-done.2, bf16[128,128]{1,0:T(8,128)(2,1)} %copy-done.3, f32[8192,128]{1,0:T(8,128)} %bitcast.18.second.state, f32[512,128]{1,0:T(8,128)} %get-tuple-element.76.observed), custom_call_target="tpu_custom_call" | custom-call | tf_op jit(solution)/shard_map/pallas_call | solution.py:301
  (108 shorter events, 5.5 us)
Async XLA Ops:
  0.6 18.0 %copy-start.8 = (s32[1,1,64]{2,1,0:T(1,128)S(1)}, s32[1,1,64]{2,1,0:T(1,128)}, u32[]{:S(2)}) copy-start(s32[1,1,64]{2,1,0:T(1,128)} %param.19) | copy-start | bytes 772
  0.6 17.4 %copy-start.4 = (s32[1,1,64,128]{3,2,1,0:T(8,128)S(1)}, s32[1,1,64,128]{3,2,1,0:T(8,128)}, u32[]{:S(2)}) copy-start(s32[1,1,64,128]{3,2,1,0:T(8,128)} %param.16) | copy-start | bytes 98308
  0.7 18.9 %copy-start.5 = (f32[1,1,64,128]{3,2,1,0:T(8,128)S(1)}, f32[1,1,64,128]{3,2,1,0:T(8,128)}, u32[]{:S(2)}) copy-start(f32[1,1,64,128]{3,2,1,0:T(8,128)} %param.18) | copy-start | bytes 98308
  0.7 19.2 %copy-start.1 = (s32[1,1,64,128]{3,2,1,0:T(8,128)S(1)}, s32[1,1,64,128]{3,2,1,0:T(8,128)}, u32[]{:S(2)}) copy-start(s32[1,1,64,128]{3,2,1,0:T(8,128)} %param.17) | copy-start | bytes 98308
  2.5 17.6 %collective-permute-start = (f32[1,256,128]{2,1,0:T(8,128)S(1)}, f32[1,256,128]{2,1,0:T(8,128)S(1)}, u32[]{:S(2)}, u32[]{:S(2)}) collective-permute-start(f32[1,256,128]{2,1,0:T(8,128)S(1)} %get-tuple-element.44), channel_id=1, source_target_pairs={{0,64},{64,128},{128,192},{1,65},{65,129},{129,193},{2,66},{66,130... | collective-permute-start | bytes 393224 | tf_op jit(solution)/shard_map/ppermute | solution.py:40
  6.6 13.6 %collective-permute-start.1 = (f32[1,256,128]{2,1,0:T(8,128)S(1)}, f32[1,256,128]{2,1,0:T(8,128)S(1)}, u32[]{:S(2)}, u32[]{:S(2)}) collective-permute-start(f32[1,256,128]{2,1,0:T(8,128)S(1)} %get-tuple-element.43), channel_id=1, source_target_pairs={{64,0},{128,64},{192,128},{65,1},{129,65},{193,129},{66,2},{130,66... | collective-permute-start | bytes 393224 | tf_op jit(solution)/shard_map/ppermute | solution.py:41
  9.9 10.0 %collective-permute-start.2 = (f32[32,1,128]{2,1,0:T(1,128)S(1)}, f32[32,1,128]{2,1,0:T(1,128)S(1)}, u32[]{:S(2)}, u32[]{:S(2)}) collective-permute-start(f32[32,1,128]{2,1,0:T(1,128)S(1)} %get-tuple-element.42), channel_id=1, source_target_pairs={{0,1},{1,2},{2,3},{3,4},{4,5},{5,6},{6,7},{7,8},{8,9},{9,10},{10,1... | collective-permute-start | bytes 49160 | tf_op jit(solution)/shard_map/ppermute | solution.py:40
  13.9 6.3 %collective-permute-start.3 = (f32[32,1,128]{2,1,0:T(1,128)S(1)}, f32[32,1,128]{2,1,0:T(1,128)S(1)}, u32[]{:S(2)}, u32[]{:S(2)}) collective-permute-start(f32[32,1,128]{2,1,0:T(1,128)S(1)} %get-tuple-element.41), channel_id=1, source_target_pairs={{1,0},{2,1},{3,2},{4,3},{5,4},{6,5},{7,6},{8,7},{9,8},{10,9},{11,1... | collective-permute-start | bytes 49160 | tf_op jit(solution)/shard_map/ppermute | solution.py:41
  15.8 2.3 collective-permute-start.10
  18.1 1.4 collective-permute-start.8
  19.5 26.9 %collective-permute-start.9 = (f32[64,128]{1,0:T(8,128)S(1)}, f32[64,128]{1,0:T(8,128)S(1)}, u32[]{:S(2)}, u32[]{:S(2)}) collective-permute-start(f32[64,128]{1,0:T(8,128)S(1)} %bitcast.132), channel_id=1, source_target_pairs={{0,1},{1,0},{2,3},{3,2},{4,5},{5,4},{6,7},{7,6},{8,9},{9,8},{10,11... | collective-permute-start | bytes 98312 | tf_op jit(solution)/shard_map/ppermute | solution.py:19
  19.9 28.5 %collective-permute-start.11 = (s32[64,128]{1,0:T(8,128)S(1)}, s32[64,128]{1,0:T(8,128)S(1)}, u32[]{:S(2)}, u32[]{:S(2)}) collective-permute-start(s32[64,128]{1,0:T(8,128)S(1)} %bitcast.126), channel_id=1, source_target_pairs={{0,1},{1,0},{2,3},{3,2},{4,5},{5,4},{6,7},{7,6},{8,9},{9,8},{10,11... | collective-permute-start | bytes 98312 | tf_op jit(solution)/shard_map/ppermute | solution.py:19
  20.2 2.2 copy-start
  36.9 14.6 %collective-permute-start.4 = (f32[1,256,128]{2,1,0:T(8,128)S(1)}, f32[1,256,128]{2,1,0:T(8,128)S(1)}, u32[]{:S(2)}, u32[]{:S(2)}) collective-permute-start(f32[1,256,128]{2,1,0:T(8,128)S(1)} %get-tuple-element.40), channel_id=1, source_target_pairs={{0,64},{64,128},{128,192},{1,65},{65,129},{129,193},{2,66},{66,130... | collective-permute-start | bytes 393224 | tf_op jit(solution)/shard_map/ppermute | solution.py:40
  41.2 10.3 %collective-permute-start.5 = (f32[1,256,128]{2,1,0:T(8,128)S(1)}, f32[1,256,128]{2,1,0:T(8,128)S(1)}, u32[]{:S(2)}, u32[]{:S(2)}) collective-permute-start(f32[1,256,128]{2,1,0:T(8,128)S(1)} %get-tuple-element.39), channel_id=1, source_target_pairs={{64,0},{128,64},{192,128},{65,1},{129,65},{193,129},{66,2},{130,66... | collective-permute-start | bytes 393224 | tf_op jit(solution)/shard_map/ppermute | solution.py:41
  42.5 6.0 %collective-permute-start.6 = (f32[32,1,128]{2,1,0:T(1,128)S(1)}, f32[32,1,128]{2,1,0:T(1,128)S(1)}, u32[]{:S(2)}, u32[]{:S(2)}) collective-permute-start(f32[32,1,128]{2,1,0:T(1,128)S(1)} %get-tuple-element.38), channel_id=1, source_target_pairs={{0,1},{1,2},{2,3},{3,4},{4,5},{5,6},{6,7},{7,8},{8,9},{9,10},{10,1... | collective-permute-start | bytes 49160 | tf_op jit(solution)/shard_map/ppermute | solution.py:40
  46.4 5.1 %collective-permute-start.7 = (f32[32,1,128]{2,1,0:T(1,128)S(1)}, f32[32,1,128]{2,1,0:T(1,128)S(1)}, u32[]{:S(2)}, u32[]{:S(2)}) collective-permute-start(f32[32,1,128]{2,1,0:T(1,128)S(1)} %get-tuple-element.37), channel_id=1, source_target_pairs={{1,0},{2,1},{3,2},{4,3},{5,4},{6,5},{7,6},{8,7},{9,8},{10,9},{11,1... | collective-permute-start | bytes 49160 | tf_op jit(solution)/shard_map/ppermute | solution.py:41
  48.4 24.1 %collective-permute-start.12 = (f32[8192,128]{1,0:T(8,128)}, f32[8192,128]{1,0:T(8,128)}, u32[]{:S(2)}, u32[]{:S(2)}) collective-permute-start(f32[8192,128]{1,0:T(8,128)} %bitcast.17.first), channel_id=1, source_target_pairs={{0,1},{1,0},{2,3},{3,2},{4,5},{5,4},{6,7},{7,6},{8,9},{9,8},{10,11... | collective-permute-start | bytes 12582920 | tf_op jit(solution)/shard_map/ppermute | solution.py:19
  63.2 9.2 %collective-permute-start.13 = (f32[8192,128]{1,0:T(8,128)}, f32[8192,128]{1,0:T(8,128)}, u32[]{:S(2)}, u32[]{:S(2)}) collective-permute-start(f32[8192,128]{1,0:T(8,128)} %bitcast.18.second.state), channel_id=1, source_target_pairs={{0,1},{1,0},{2,3},{3,2},{4,5},{5,4},{6,7},{7,6},{8,9},{9,8},{10,11... | collective-permute-start | bytes 12582920 | tf_op jit(solution)/shard_map/ppermute | solution.py:19
  89.8 12.2 %collective-permute-start.26 = (f32[4,96,128]{2,1,0:T(8,128)S(1)}, f32[4,96,128]{2,1,0:T(8,128)S(1)}, u32[]{:S(2)}, u32[]{:S(2)}) collective-permute-start(f32[4,96,128]{2,1,0:T(8,128)S(1)} %get-tuple-element.72), channel_id=1, source_target_pairs={{0,8},{8,16},{16,24},{24,32},{32,40},{40,48},{48,56},{56,0},{1,9},... | collective-permute-start | bytes 589832 | tf_op jit(solution)/shard_map/ppermute | solution.py:19
  94.8 19.1 %collective-permute-start.14 = (f32[8,160,128]{2,1,0:T(8,128)S(1)}, f32[8,160,128]{2,1,0:T(8,128)S(1)}, u32[]{:S(2)}, u32[]{:S(2)}) collective-permute-start(f32[8,160,128]{2,1,0:T(8,128)S(1)} %get-tuple-element.60), channel_id=1, source_target_pairs={{0,2},{2,4},{4,6},{6,0},{1,3},{3,5},{5,7},{7,1},{8,10},{10,12},{12... | collective-permute-start | bytes 1966088 | tf_op jit(solution)/shard_map/ppermute | solution.py:19
  94.9 10.6 %collective-permute-start.30 = (f32[4,96,128]{2,1,0:T(8,128)S(1)}, f32[4,96,128]{2,1,0:T(8,128)S(1)}, u32[]{:S(2)}, u32[]{:S(2)}) collective-permute-start(f32[4,96,128]{2,1,0:T(8,128)S(1)} %get-tuple-element.73), channel_id=1, source_target_pairs={{0,56},{8,0},{16,8},{24,16},{32,24},{40,32},{48,40},{56,48},{1,57}... | collective-permute-start | bytes 589832 | tf_op jit(solution)/shard_map/ppermute | solution.py:19
  102.1 10.4 %collective-permute-start.27 = (f32[4,192,128]{2,1,0:T(8,128)S(1)}, f32[4,192,128]{2,1,0:T(8,128)S(1)}, u32[]{:S(2)}, u32[]{:S(2)}) collective-permute-start(f32[4,192,128]{2,1,0:T(8,128)S(1)} %pad_maximum_fusion.2), channel_id=1, source_target_pairs={{0,8},{8,16},{16,24},{24,32},{32,40},{40,48},{48,56},{56,0},{1,9},... | collective-permute-start | bytes 1179656 | tf_op jit(solution)/shard_map/ppermute | solution.py:19
  102.2 16.5 %collective-permute-start.16 = (f32[8,160,128]{2,1,0:T(8,128)S(1)}, f32[8,160,128]{2,1,0:T(8,128)S(1)}, u32[]{:S(2)}, u32[]{:S(2)}) collective-permute-start(f32[8,160,128]{2,1,0:T(8,128)S(1)} %get-tuple-element.61), channel_id=1, source_target_pairs={{0,6},{2,0},{4,2},{6,4},{1,7},{3,1},{5,3},{7,5},{8,14},{10,8},{12,... | collective-permute-start | bytes 1966088 | tf_op jit(solution)/shard_map/ppermute | solution.py:19
  105.6 16.8 %collective-permute-start.31 = (f32[4,192,128]{2,1,0:T(8,128)S(1)}, f32[4,192,128]{2,1,0:T(8,128)S(1)}, u32[]{:S(2)}, u32[]{:S(2)}) collective-permute-start(f32[4,192,128]{2,1,0:T(8,128)S(1)} %pad_maximum_fusion.3), channel_id=1, source_target_pairs={{0,56},{8,0},{16,8},{24,16},{32,24},{40,32},{48,40},{56,48},{1,57}... | collective-permute-start | bytes 1179656 | tf_op jit(solution)/shard_map/ppermute | solution.py:19
  112.5 9.8 %collective-permute-start.28 = (f32[4,192,128]{2,1,0:T(8,128)S(1)}, f32[4,192,128]{2,1,0:T(8,128)S(1)}, u32[]{:S(2)}, u32[]{:S(2)}) collective-permute-start(f32[4,192,128]{2,1,0:T(8,128)S(1)} %bitcast_add_fusion.3), channel_id=1, source_target_pairs={{0,8},{8,16},{16,24},{24,32},{32,40},{40,48},{48,56},{56,0},{1,9},... | collective-permute-start | bytes 1179656 | tf_op jit(solution)/shard_map/ppermute | solution.py:19
  114.1 31.4 %collective-permute-start.15 = (f32[8,320,128]{2,1,0:T(8,128)S(1)}, f32[8,320,128]{2,1,0:T(8,128)S(1)}, u32[]{:S(2)}, u32[]{:S(2)}) collective-permute-start(f32[8,320,128]{2,1,0:T(8,128)S(1)} %pad_maximum_fusion), channel_id=1, source_target_pairs={{0,2},{2,4},{4,6},{6,0},{1,3},{3,5},{5,7},{7,1},{8,10},{10,12},{12... | collective-permute-start | bytes 3932168 | tf_op jit(solution)/shard_map/ppermute | solution.py:19
  118.9 29.7 %collective-permute-start.17 = (f32[8,320,128]{2,1,0:T(8,128)S(1)}, f32[8,320,128]{2,1,0:T(8,128)S(1)}, u32[]{:S(2)}, u32[]{:S(2)}) collective-permute-start(f32[8,320,128]{2,1,0:T(8,128)S(1)} %pad_maximum_fusion.1), channel_id=1, source_target_pairs={{0,6},{2,0},{4,2},{6,4},{1,7},{3,1},{5,3},{7,5},{8,14},{10,8},{12,... | collective-permute-start | bytes 3932168 | tf_op jit(solution)/shard_map/ppermute | solution.py:19
  122.5 11.9 %collective-permute-start.32 = (f32[4,192,128]{2,1,0:T(8,128)S(1)}, f32[4,192,128]{2,1,0:T(8,128)S(1)}, u32[]{:S(2)}, u32[]{:S(2)}) collective-permute-start(f32[4,192,128]{2,1,0:T(8,128)S(1)} %get-tuple-element.46), channel_id=1, source_target_pairs={{0,56},{8,0},{16,8},{24,16},{32,24},{40,32},{48,40},{56,48},{1,57}... | collective-permute-start | bytes 1179656 | tf_op jit(solution)/shard_map/ppermute | solution.py:19
  127.3 25.9 %collective-permute-start.29 = (f32[4,192,128]{2,1,0:T(8,128)S(1)}, f32[4,192,128]{2,1,0:T(8,128)S(1)}, u32[]{:S(2)}, u32[]{:S(2)}) collective-permute-start(f32[4,192,128]{2,1,0:T(8,128)S(1)} %get-tuple-element.45), channel_id=1, source_target_pairs={{0,8},{8,16},{16,24},{24,32},{32,40},{40,48},{48,56},{56,0},{1,9},... | collective-permute-start | bytes 1179656 | tf_op jit(solution)/shard_map/ppermute | solution.py:19
  134.4 18.7 %collective-permute-start.33 = (f32[4,192,128]{2,1,0:T(8,128)S(1)}, f32[4,192,128]{2,1,0:T(8,128)S(1)}, u32[]{:S(2)}, u32[]{:S(2)}) collective-permute-start(f32[4,192,128]{2,1,0:T(8,128)S(1)} %bitcast_add_fusion.2), channel_id=1, source_target_pairs={{0,56},{8,0},{16,8},{24,16},{32,24},{40,32},{48,40},{56,48},{1,57}... | collective-permute-start | bytes 1179656 | tf_op jit(solution)/shard_map/ppermute | solution.py:19
  148.8 5.8 %collective-permute-start.18 = (f32[160,128]{1,0:T(8,128)S(1)}, f32[160,128]{1,0:T(8,128)S(1)}, u32[]{:S(2)}, u32[]{:S(2)}) collective-permute-start(f32[160,128]{1,0:T(8,128)S(1)} %get-tuple-element.54), channel_id=1, source_target_pairs={{0,8},{8,16},{16,24},{24,32},{32,40},{40,48},{48,56},{56,0},{1,9},... | collective-permute-start | bytes 245768 | tf_op jit(solution)/shard_map/ppermute | solution.py:19
  153.1 4.0 %collective-permute-start.22 = (f32[160,128]{1,0:T(8,128)S(1)}, f32[160,128]{1,0:T(8,128)S(1)}, u32[]{:S(2)}, u32[]{:S(2)}) collective-permute-start(f32[160,128]{1,0:T(8,128)S(1)} %get-tuple-element.55), channel_id=1, source_target_pairs={{0,56},{8,0},{16,8},{24,16},{32,24},{40,32},{48,40},{56,48},{1,57}... | collective-permute-start | bytes 245768 | tf_op jit(solution)/shard_map/ppermute | solution.py:19
  157.2 6.4 %collective-permute-start.19 = (f32[320,128]{1,0:T(8,128)S(1)}, f32[320,128]{1,0:T(8,128)S(1)}, u32[]{:S(2)}, u32[]{:S(2)}) collective-permute-start(f32[320,128]{1,0:T(8,128)S(1)} %pad_maximum_fusion.5), channel_id=1, source_target_pairs={{0,8},{8,16},{16,24},{24,32},{32,40},{40,48},{48,56},{56,0},{1,9},... | collective-permute-start | bytes 491528 | tf_op jit(solution)/shard_map/ppermute | solution.py:19
  159.4 5.2 %collective-permute-start.34 = (f32[96,128]{1,0:T(8,128)S(1)}, f32[96,128]{1,0:T(8,128)S(1)}, u32[]{:S(2)}, u32[]{:S(2)}) collective-permute-start(f32[96,128]{1,0:T(8,128)S(1)} %get-tuple-element.66), channel_id=1, source_target_pairs={{0,2},{2,4},{4,6},{6,0},{1,3},{3,5},{5,7},{7,1},{8,10},{10,12},{12... | collective-permute-start | bytes 147464 | tf_op jit(solution)/shard_map/ppermute | solution.py:19
  159.5 5.2 %collective-permute-start.36 = (f32[96,128]{1,0:T(8,128)S(1)}, f32[96,128]{1,0:T(8,128)S(1)}, u32[]{:S(2)}, u32[]{:S(2)}) collective-permute-start(f32[96,128]{1,0:T(8,128)S(1)} %get-tuple-element.67), channel_id=1, source_target_pairs={{0,6},{2,0},{4,2},{6,4},{1,7},{3,1},{5,3},{7,5},{8,14},{10,8},{12,... | collective-permute-start | bytes 147464 | tf_op jit(solution)/shard_map/ppermute | solution.py:19
  163.0 4.4 %collective-permute-start.23 = (f32[320,128]{1,0:T(8,128)S(1)}, f32[320,128]{1,0:T(8,128)S(1)}, u32[]{:S(2)}, u32[]{:S(2)}) collective-permute-start(f32[320,128]{1,0:T(8,128)S(1)} %pad_maximum_fusion.6), channel_id=1, source_target_pairs={{0,56},{8,0},{16,8},{24,16},{32,24},{40,32},{48,40},{56,48},{1,57}... | collective-permute-start | bytes 491528 | tf_op jit(solution)/shard_map/ppermute | solution.py:19
  163.7 5.5 %collective-permute-start.20 = (f32[320,128]{1,0:T(8,128)S(1)}, f32[320,128]{1,0:T(8,128)S(1)}, u32[]{:S(2)}, u32[]{:S(2)}) collective-permute-start(f32[320,128]{1,0:T(8,128)S(1)} %fusion.10), channel_id=1, source_target_pairs={{0,8},{8,16},{16,24},{24,32},{32,40},{40,48},{48,56},{56,0},{1,9},... | collective-permute-start | bytes 491528 | tf_op jit(solution)/shard_map/ppermute | solution.py:19
  169.2 11.2 %copy-start.6 = (f32[2,256]{1,0:T(2,128)S(1)}, f32[2,256]{1,0:T(2,128)}, u32[]{:S(2)}) copy-start(f32[2,256]{1,0:T(2,128)} %param.21) | copy-start | bytes 6148
  169.2 11.2 %copy-start.7 = (f32[2,256]{1,0:T(2,128)S(1)}, f32[2,256]{1,0:T(2,128)}, u32[]{:S(2)}) copy-start(f32[2,256]{1,0:T(2,128)} %param.20) | copy-start | bytes 6148
  169.2 4.9 %collective-permute-start.24 = (f32[320,128]{1,0:T(8,128)S(1)}, f32[320,128]{1,0:T(8,128)S(1)}, u32[]{:S(2)}, u32[]{:S(2)}) collective-permute-start(f32[320,128]{1,0:T(8,128)S(1)} %get-tuple-element.51), channel_id=1, source_target_pairs={{0,56},{8,0},{16,8},{24,16},{32,24},{40,32},{48,40},{56,48},{1,57}... | collective-permute-start | bytes 491528 | tf_op jit(solution)/shard_map/ppermute | solution.py:19
  169.5 6.4 %collective-permute-start.35 = (f32[192,128]{1,0:T(8,128)S(1)}, f32[192,128]{1,0:T(8,128)S(1)}, u32[]{:S(2)}, u32[]{:S(2)}) collective-permute-start(f32[192,128]{1,0:T(8,128)S(1)} %pad_maximum_fusion.7), channel_id=1, source_target_pairs={{0,2},{2,4},{4,6},{6,0},{1,3},{3,5},{5,7},{7,1},{8,10},{10,12},{12... | collective-permute-start | bytes 294920 | tf_op jit(solution)/shard_map/ppermute | solution.py:19
  169.6 6.3 %collective-permute-start.37 = (f32[192,128]{1,0:T(8,128)S(1)}, f32[192,128]{1,0:T(8,128)S(1)}, u32[]{:S(2)}, u32[]{:S(2)}) collective-permute-start(f32[192,128]{1,0:T(8,128)S(1)} %pad_maximum_fusion.8), channel_id=1, source_target_pairs={{0,6},{2,0},{4,2},{6,4},{1,7},{3,1},{5,3},{7,5},{8,14},{10,8},{12,... | collective-permute-start | bytes 294920 | tf_op jit(solution)/shard_map/ppermute | solution.py:19
  172.7 5.4 %collective-permute-start.21 = (f32[320,128]{1,0:T(8,128)S(1)}, f32[320,128]{1,0:T(8,128)S(1)}, u32[]{:S(2)}, u32[]{:S(2)}) collective-permute-start(f32[320,128]{1,0:T(8,128)S(1)} %get-tuple-element.50), channel_id=1, source_target_pairs={{0,8},{8,16},{16,24},{24,32},{32,40},{40,48},{48,56},{56,0},{1,9},... | collective-permute-start | bytes 491528 | tf_op jit(solution)/shard_map/ppermute | solution.py:19
  174.1 5.4 %collective-permute-start.25 = (f32[320,128]{1,0:T(8,128)S(1)}, f32[320,128]{1,0:T(8,128)S(1)}, u32[]{:S(2)}, u32[]{:S(2)}) collective-permute-start(f32[320,128]{1,0:T(8,128)S(1)} %fusion.9), channel_id=1, source_target_pairs={{0,56},{8,0},{16,8},{24,16},{32,24},{40,32},{48,40},{56,48},{1,57}... | collective-permute-start | bytes 491528 | tf_op jit(solution)/shard_map/ppermute | solution.py:19
  181.7 8.4 %collective-permute-start.38 = (f32[144,128]{1,0:T(8,128)S(1)}, f32[144,128]{1,0:T(8,128)S(1)}, u32[]{:S(2)}, u32[]{:S(2)}) collective-permute-start(f32[144,128]{1,0:T(8,128)S(1)} %fusion.1), channel_id=1, source_target_pairs={{0,1},{1,0},{2,3},{3,2},{4,5},{5,4},{6,7},{7,6},{8,9},{9,8},{10,11... | collective-permute-start | bytes 221192 | tf_op jit(solution)/shard_map/ppermute | solution.py:19
  225.4 5.1 %collective-permute-start.39 = (f32[72,128]{1,0:T(8,128)S(1)}, f32[72,128]{1,0:T(8,128)S(1)}, u32[]{:S(2)}, u32[]{:S(2)}) collective-permute-start(f32[72,128]{1,0:T(8,128)S(1)} %reduce_sum.29), channel_id=1, source_target_pairs={{0,1},{1,0},{2,3},{3,2},{4,5},{5,4},{6,7},{7,6},{8,9},{9,8},{10,11... | collective-permute-start | bytes 110600 | tf_op jit(solution)/shard_map/ppermute | solution.py:19
  236.9 0.6 copy-start.2
  237.6 0.6 copy-start.3
